TPU v7x, 32 devices: a whole 2x2x4 slice. The times are simulated.
32 devices in a mesh: dp: 4 (over y, core), expert: 8 (over z, x).
Axes of the slice: x: 2, y: 2, z: 4, core: 2. Of those that a mesh axis runs over, the one named last changes fastest.
Arguments:
- tokens: bfloat16 [2, 32, 128, 2048], P(None, ('dp', 'expert')), may hold values from -6 to 6
- out_cotangent: bfloat16 [2, 32, 128, 2048], P(None, ('dp', 'expert')), may hold values from -6 to 6
- lengths: int32 [2, 32], P(None, ('dp', 'expert')), may hold values from 32 to 128
- routes: int32 [2, 32, 128, 8], P(None, ('dp', 'expert')), may hold values from 0 to 15, all different within a row
- priority: int32 [2, 32, 1024], P(None, ('dp', 'expert')), may hold values from 0 to 1023, each once within a row
- attn_gain: bfloat16 [2048], P(('dp', 'expert')), may hold values from 0.5 to 2
- query_weight: bfloat16 [2048, 2048], P(('dp', 'expert')), may hold values from -0.125 to 0.125
- key_weight: bfloat16 [2048, 2048], P(('dp', 'expert')), may hold values from -0.125 to 0.125
- value_weight: bfloat16 [2048, 2048], P(('dp', 'expert')), may hold values from -0.125 to 0.125
- output_weight: bfloat16 [2048, 2048], P(('dp', 'expert')), may hold values from -1 to 1
- query_gain: bfloat16 [128], P(('dp', 'expert')), may hold values from 0.5 to 2
- key_gain: bfloat16 [128], P(('dp', 'expert')), may hold values from 0.5 to 2
- ffn_gain: bfloat16 [2048], P(('dp', 'expert')), may hold values from 0.5 to 2
- router_weight: bfloat16 [2048, 16], P(('dp', 'expert')), may hold values from -0.0625 to 0.0625
- gate_weight: bfloat16 [16, 2048, 1024], P('expert', 'dp'), may hold values from -0.125 to 0.125
- up_weight: bfloat16 [16, 2048, 1024], P('expert', 'dp'), may hold values from -0.125 to 0.125
- down_weight: bfloat16 [16, 1024, 2048], P('expert', 'dp'), may hold values from -1.5 to 1.5
Outputs:
- layer_out: bfloat16 [2, 32, 128, 2048], P(None, ('dp', 'expert'))
- tokens_grad: float32 [2, 32, 128, 2048], P(None, ('dp', 'expert'))
- attn_gain_grad: float32 [2048], P(('dp', 'expert'))
- query_weight_grad: float32 [2048, 2048], P(('dp', 'expert'))
- key_weight_grad: float32 [2048, 2048], P(('dp', 'expert'))
- value_weight_grad: float32 [2048, 2048], P(('dp', 'expert'))
- output_weight_grad: float32 [2048, 2048], P(('dp', 'expert'))
- query_gain_grad: float32 [128], P(('dp', 'expert'))
- key_gain_grad: float32 [128], P(('dp', 'expert'))
- ffn_gain_grad: float32 [2048], P(('dp', 'expert'))
- router_weight_grad: float32 [2048, 16], P(('dp', 'expert'))
- gate_weight_grad: float32 [16, 2048, 1024], P('expert', 'dp')
- up_weight_grad: float32 [16, 2048, 1024], P('expert', 'dp')
- down_weight_grad: float32 [16, 1024, 2048], P('expert', 'dp')
Inputs may be any that keep to these rules, and one draw needn't show every extreme that they name: `routes`: each token names 8 different experts. `priority`: for each sequence a permutation of its 1024 pairs, pair t * 8 + k being token t's k-th route.
All inputs are finite; a program needn't handle non-finite values.
Results may differ from a plain program's by a relative error of at most 0.023.
Values may be sent and summed in bfloat16 or wider, within the bound.
No kernel may reach another device: no remote copies, remote signals or barrier semaphores. Data moves between devices by JAX's collectives and lax.ppermute only.
A program may use at most 320 MiB of HBM per device.

v0:
```python
import math

import jax
import jax.numpy as jnp
from jax import lax
from jax.sharding import PartitionSpec as P

D = 2048
HEADS = 16
HD = 128
TOP = 8


EPSILON = 1e-06
THETA = 50000.0
NEGATIVE = -1e30


def norm_rows(values, gain_row):
    return (
        values * lax.rsqrt(jnp.mean(values * values, axis=-1, keepdims=True) + EPSILON) * gain_row
    )


def rotate(values):
    row_count = values.shape[0]
    half_size = values.shape[-1] // 2
    frequency = THETA ** (-jnp.arange(half_size, dtype=jnp.float32) / half_size)
    angles = jnp.arange(row_count, dtype=jnp.float32)[:, None] * frequency[None, :]
    cosine = jnp.cos(angles)[:, None, :]
    sine_part = jnp.sin(angles)[:, None, :]
    first_half = values[..., :half_size]
    second = values[..., half_size:]
    return jnp.concatenate(
        [first_half * cosine - second * sine_part, second * cosine + first_half * sine_part],
        axis=-1,
    )


def head_norm(values, gain_row):
    row_count = values.shape[0]
    split_heads = values.reshape(row_count, HEADS, HD)
    return rotate(norm_rows(split_heads, gain_row)).reshape(row_count, HEADS * HD)


def plain(left, right):
    return jnp.dot(left, right, preferred_element_type=jnp.float32)


def inner(left, right):
    return lax.dot_general(
        left, right, (((0,), (0,)), ((), ())), preferred_element_type=jnp.float32
    )


def times_t(left, right):
    return lax.dot_general(
        left, right, (((1,), (1,)), ((), ())), preferred_element_type=jnp.float32
    )


def slot_plan(route, priority, experts, capacity):
    pair_count = route.shape[0] * route.shape[1]
    slot_count = experts * capacity
    flat_route = route.reshape(-1)
    onehot = (flat_route[:, None] == jnp.arange(experts, dtype=jnp.int32)[None, :]).astype(
        jnp.bfloat16
    )
    before = (priority[None, :] < priority[:, None]).astype(jnp.bfloat16)
    counts = jnp.dot(before, onehot, preferred_element_type=jnp.float32)
    pair_rank = jnp.sum(counts * onehot.astype(jnp.float32), axis=1).astype(jnp.int32)
    kept_pair = pair_rank < capacity
    column = jnp.where(kept_pair, flat_route * capacity + pair_rank, slot_count)
    source = (
        jnp.full((slot_count,), pair_count, jnp.int32)
        .at[column]
        .set(jnp.arange(pair_count, dtype=jnp.int32), mode="drop")
    )
    filled = source < pair_count
    return (
        kept_pair,
        jnp.minimum(column, slot_count - 1),
        filled,
        jnp.minimum(source, pair_count - 1),
    )


def fetch_dense(shard):
    return (
        lax.all_gather(shard[0], ("dp", "expert"), axis=0, tiled=True),
        lax.all_gather(shard[1], ("dp", "expert"), axis=0, tiled=True),
        lax.all_gather(shard[2], ("dp", "expert"), axis=0, tiled=True),
        lax.all_gather(shard[3], ("dp", "expert"), axis=0, tiled=True),
        lax.all_gather(shard[4], ("dp", "expert"), axis=0, tiled=True),
        lax.all_gather(shard[5], ("dp", "expert"), axis=0, tiled=True),
        lax.all_gather(shard[6], ("dp", "expert"), axis=0, tiled=True),
        lax.all_gather(shard[7], ("dp", "expert"), axis=0, tiled=True),
        lax.all_gather(shard[8], ("dp", "expert"), axis=0, tiled=True),
    )


def fetch_expert(shard):
    return (
        lax.all_gather(shard[0], "dp", axis=1, tiled=True),
        lax.all_gather(shard[1], "dp", axis=1, tiled=True),
        lax.all_gather(shard[2], "dp", axis=1, tiled=True),
    )


def forward_pass(token_rows, length, route, priority, dense_full, expert_full):
    (
        attn_gain,
        query_weight,
        key_weight,
        value_weight,
        output_weight,
        query_gain,
        key_gain,
        ffn_gain,
        router_weight,
    ) = dense_full
    gate_weight, up_weight, down_weight = expert_full
    row_count = token_rows.shape[0]
    experts = router_weight.shape[1]
    capacity = 5 * row_count * TOP // (4 * experts)
    expert_count = lax.axis_size("expert")
    local_experts = gate_weight.shape[0]
    score_scale = 1.0 / math.sqrt(HD)
    rows_float = token_rows.astype(jnp.float32)
    attn_gain_f = attn_gain.astype(jnp.float32)
    normed = norm_rows(rows_float, attn_gain_f).astype(jnp.bfloat16)
    query_raw = plain(normed, query_weight)
    key_raw = plain(normed, key_weight)
    value_heads = plain(normed, value_weight).astype(jnp.bfloat16).reshape(row_count, HEADS, HD)
    query_gain_f = query_gain.astype(jnp.float32)
    key_gain_f = key_gain.astype(jnp.float32)
    query_heads = (
        head_norm(query_raw, query_gain_f).astype(jnp.bfloat16).reshape(row_count, HEADS, HD)
    )
    key_heads = head_norm(key_raw, key_gain_f).astype(jnp.bfloat16).reshape(row_count, HEADS, HD)
    valid_key = jnp.arange(row_count, dtype=jnp.int32) < length
    scores = (
        jnp.einsum("qhd,khd->hqk", query_heads, key_heads, preferred_element_type=jnp.float32)
        * score_scale
    )
    scores = jnp.where(valid_key[None, None, :], scores, NEGATIVE)
    score_top = jnp.max(scores, axis=-1, keepdims=True)
    exp_total = jnp.sum(jnp.exp(scores - score_top), axis=-1, keepdims=True)
    log_total = score_top + jnp.log(exp_total)
    attention = jnp.exp(scores - score_top) / exp_total
    mixed_rows = (
        jnp.einsum(
            "hqk,khd->qhd",
            attention.astype(jnp.bfloat16),
            value_heads,
            preferred_element_type=jnp.float32,
        )
        .reshape(row_count, D)
        .astype(jnp.bfloat16)
    )
    hidden = rows_float + plain(mixed_rows, output_weight)
    ffn_gain_f = ffn_gain.astype(jnp.float32)
    routed_in = norm_rows(hidden, ffn_gain_f).astype(jnp.bfloat16)
    gate_probs = jax.nn.softmax(plain(routed_in, router_weight), axis=-1)
    choose = (route[:, :, None] == jnp.arange(experts, dtype=jnp.int32)[None, None, :]).astype(
        jnp.float32
    )
    gate_values = jnp.sum(choose * gate_probs[:, None, :], axis=-1)
    kept_pair, column, filled, source = slot_plan(route, priority, experts, capacity)
    sent_rows = jnp.where(filled[:, None], routed_in[source // TOP], 0)
    received = lax.all_to_all(
        sent_rows.reshape(expert_count, -1, D), "expert", split_axis=0, concat_axis=0, tiled=True
    )
    received = received.reshape(expert_count, local_experts, capacity, D)
    gate_hidden = jnp.einsum(
        "secd,edf->secf", received, gate_weight, preferred_element_type=jnp.float32
    )
    up_hidden = jnp.einsum(
        "secd,edf->secf", received, up_weight, preferred_element_type=jnp.float32
    )
    active = (jax.nn.silu(gate_hidden) * up_hidden).astype(jnp.bfloat16)
    expert_out = jnp.einsum(
        "secf,efd->secd", active, down_weight, preferred_element_type=jnp.float32
    ).astype(jnp.bfloat16)
    returned = lax.all_to_all(
        expert_out.reshape(expert_count, -1, D), "expert", split_axis=0, concat_axis=0, tiled=True
    ).reshape(-1, D)
    picked = jnp.where(kept_pair[:, None], returned[column].astype(jnp.float32), 0.0).reshape(
        row_count, TOP, D
    )
    output = hidden + jnp.sum(gate_values[:, :, None] * picked, axis=1)
    stored = (
        rows_float,
        normed,
        query_raw,
        key_raw,
        query_heads,
        key_heads,
        value_heads,
        valid_key,
        log_total,
        mixed_rows,
        hidden,
        routed_in,
        gate_probs,
        choose,
        gate_values,
        kept_pair,
        column,
        filled,
        source,
        received,
        gate_hidden,
        up_hidden,
        active,
        picked,
    )
    return (output.astype(jnp.bfloat16), stored)


def backward_pass(row_grad, stored, dense_full, expert_full):
    (
        rows_float,
        normed,
        query_raw,
        key_raw,
        query_heads,
        key_heads,
        value_heads,
        valid_key,
        log_total,
        mixed_rows,
        hidden,
        routed_in,
        gate_probs,
        choose,
        gate_values,
        kept_pair,
        column,
        filled,
        source,
        received,
        gate_hidden,
        up_hidden,
        active,
        picked,
    ) = stored
    (
        attn_gain,
        query_weight,
        key_weight,
        value_weight,
        output_weight,
        query_gain,
        key_gain,
        ffn_gain,
        router_weight,
    ) = dense_full
    gate_weight, up_weight, down_weight = expert_full
    row_count = row_grad.shape[0]
    expert_count = lax.axis_size("expert")
    local_experts = gate_weight.shape[0]
    capacity = received.shape[2]
    score_scale = 1.0 / math.sqrt(HD)
    gates_grad = jnp.sum(picked * row_grad[:, None, :], axis=-1)
    returned_grad = jnp.where(
        filled[:, None], gate_values.reshape(-1)[source][:, None] * row_grad[source // TOP], 0.0
    ).astype(jnp.bfloat16)
    expert_out_grad = lax.all_to_all(
        returned_grad.reshape(expert_count, -1, D),
        "expert",
        split_axis=0,
        concat_axis=0,
        tiled=True,
    )
    expert_out_grad = expert_out_grad.reshape(expert_count, local_experts, capacity, D)
    down_grad = jnp.einsum(
        "secf,secd->efd", active, expert_out_grad, preferred_element_type=jnp.float32
    )
    active_grad = jnp.einsum(
        "secd,efd->secf", expert_out_grad, down_weight, preferred_element_type=jnp.float32
    )
    sigmoid_gate = jax.nn.sigmoid(gate_hidden)
    gate_hidden_grad = (
        active_grad * up_hidden * sigmoid_gate * (1.0 + gate_hidden * (1.0 - sigmoid_gate))
    ).astype(jnp.bfloat16)
    up_hidden_grad = (active_grad * gate_hidden * sigmoid_gate).astype(jnp.bfloat16)
    gate_grad = jnp.einsum(
        "secd,secf->edf", received, gate_hidden_grad, preferred_element_type=jnp.float32
    )
    up_grad = jnp.einsum(
        "secd,secf->edf", received, up_hidden_grad, preferred_element_type=jnp.float32
    )
    sent_local = jnp.einsum(
        "secf,edf->secd", gate_hidden_grad, gate_weight, preferred_element_type=jnp.float32
    ) + jnp.einsum("secf,edf->secd", up_hidden_grad, up_weight, preferred_element_type=jnp.float32)
    sent_grad = lax.all_to_all(
        sent_local.astype(jnp.bfloat16).reshape(expert_count, -1, D),
        "expert",
        split_axis=0,
        concat_axis=0,
        tiled=True,
    ).reshape(-1, D)
    routed_grad = jnp.sum(
        jnp.where(kept_pair[:, None], sent_grad[column].astype(jnp.float32), 0.0).reshape(
            row_count, TOP, D
        ),
        axis=1,
    )
    probs_grad = jnp.sum(choose * gates_grad[:, :, None], axis=1)
    logits_grad = (
        gate_probs * (probs_grad - jnp.sum(gate_probs * probs_grad, axis=-1, keepdims=True))
    ).astype(jnp.bfloat16)
    router_grad = inner(routed_in, logits_grad)
    routed_grad = routed_grad + times_t(logits_grad, router_weight)
    ffn_gain_f = ffn_gain.astype(jnp.float32)
    unused_second, second_back = jax.vjp(norm_rows, hidden, ffn_gain_f)
    hidden_add, ffn_gain_grad = second_back(routed_grad)
    hidden_grad = row_grad + hidden_add
    attn_out_grad = hidden_grad.astype(jnp.bfloat16)
    output_grad = inner(mixed_rows, attn_out_grad)
    mixed_grad = (
        times_t(attn_out_grad, output_weight).astype(jnp.bfloat16).reshape(row_count, HEADS, HD)
    )
    scores = (
        jnp.einsum("qhd,khd->hqk", query_heads, key_heads, preferred_element_type=jnp.float32)
        * score_scale
    )
    scores = jnp.where(valid_key[None, None, :], scores, NEGATIVE)
    attention = jnp.exp(scores - log_total)
    value_grad = (
        jnp.einsum(
            "hqk,qhd->khd",
            attention.astype(jnp.bfloat16),
            mixed_grad,
            preferred_element_type=jnp.float32,
        )
        .reshape(row_count, D)
        .astype(jnp.bfloat16)
    )
    attention_grad = jnp.einsum(
        "qhd,khd->hqk", mixed_grad, value_heads, preferred_element_type=jnp.float32
    )
    score_grad = (
        attention * (attention_grad - jnp.sum(attention * attention_grad, axis=-1, keepdims=True))
    ).astype(jnp.bfloat16)
    query_heads_grad = (
        jnp.einsum(
            "hqk,khd->qhd", score_grad, key_heads, preferred_element_type=jnp.float32
        ).reshape(row_count, D)
        * score_scale
    )
    key_heads_grad = (
        jnp.einsum(
            "hqk,qhd->khd", score_grad, query_heads, preferred_element_type=jnp.float32
        ).reshape(row_count, D)
        * score_scale
    )
    unused_query, query_back = jax.vjp(head_norm, query_raw, query_gain.astype(jnp.float32))
    query_raw_grad, query_gain_grad = query_back(query_heads_grad)
    unused_key, key_back = jax.vjp(head_norm, key_raw, key_gain.astype(jnp.float32))
    key_raw_grad, key_gain_grad = key_back(key_heads_grad)
    query_raw_grad = query_raw_grad.astype(jnp.bfloat16)
    key_raw_grad = key_raw_grad.astype(jnp.bfloat16)
    query_grad = inner(normed, query_raw_grad)
    key_grad = inner(normed, key_raw_grad)
    value_weight_grad = inner(normed, value_grad)
    normed_grad = (
        times_t(query_raw_grad, query_weight)
        + times_t(key_raw_grad, key_weight)
        + times_t(value_grad, value_weight)
    )
    unused_first, first_back = jax.vjp(norm_rows, rows_float, attn_gain.astype(jnp.float32))
    tokens_add, attn_gain_grad = first_back(normed_grad)
    tokens_grad = hidden_grad + tokens_add
    dense_part = (
        attn_gain_grad,
        query_grad,
        key_grad,
        value_weight_grad,
        output_grad,
        query_gain_grad,
        key_gain_grad,
        ffn_gain_grad,
        router_grad,
    )
    expert_part = (gate_grad, up_grad, down_grad)
    return (tokens_grad, dense_part, expert_part)


def shards(
    tokens,
    out_cotangent,
    lengths,
    routes,
    priority,
    attn_gain,
    query_weight,
    key_weight,
    value_weight,
    output_weight,
    query_gain,
    key_gain,
    ffn_gain,
    router_weight,
    gate_weight,
    up_weight,
    down_weight,
):
    dense_shard = (
        attn_gain,
        query_weight,
        key_weight,
        value_weight,
        output_weight,
        query_gain,
        key_gain,
        ffn_gain,
        router_weight,
    )
    expert_shard = (gate_weight, up_weight, down_weight)
    outputs = []
    input_grads = []
    dense_total = None
    expert_total = None
    for batch_index in range(tokens.shape[0]):
        dense_full = fetch_dense(dense_shard)
        expert_full = fetch_expert(expert_shard)
        output, stored = forward_pass(
            tokens[batch_index, 0],
            lengths[batch_index, 0],
            routes[batch_index, 0],
            priority[batch_index, 0],
            dense_full,
            expert_full,
        )
        dense_full = fetch_dense(dense_shard)
        expert_full = fetch_expert(expert_shard)
        tokens_grad, dense_part, expert_part = backward_pass(
            out_cotangent[batch_index, 0].astype(jnp.float32), stored, dense_full, expert_full
        )
        outputs.append(output)
        input_grads.append(tokens_grad)
        if dense_total is None:
            dense_total = dense_part
            expert_total = expert_part
        else:
            dense_total = jax.tree.map(jnp.add, dense_total, dense_part)
            expert_total = jax.tree.map(jnp.add, expert_total, expert_part)
    dense_grads = (
        lax.psum_scatter(dense_total[0], ("dp", "expert"), scatter_dimension=0, tiled=True),
        lax.psum_scatter(dense_total[1], ("dp", "expert"), scatter_dimension=0, tiled=True),
        lax.psum_scatter(dense_total[2], ("dp", "expert"), scatter_dimension=0, tiled=True),
        lax.psum_scatter(dense_total[3], ("dp", "expert"), scatter_dimension=0, tiled=True),
        lax.psum_scatter(dense_total[4], ("dp", "expert"), scatter_dimension=0, tiled=True),
        lax.psum_scatter(dense_total[5], ("dp", "expert"), scatter_dimension=0, tiled=True),
        lax.psum_scatter(dense_total[6], ("dp", "expert"), scatter_dimension=0, tiled=True),
        lax.psum_scatter(dense_total[7], ("dp", "expert"), scatter_dimension=0, tiled=True),
        lax.psum_scatter(dense_total[8], ("dp", "expert"), scatter_dimension=0, tiled=True),
    )
    expert_grads = (
        lax.psum_scatter(
            expert_total[0].astype(jnp.bfloat16), "dp", scatter_dimension=1, tiled=True
        ).astype(jnp.float32),
        lax.psum_scatter(
            expert_total[1].astype(jnp.bfloat16), "dp", scatter_dimension=1, tiled=True
        ).astype(jnp.float32),
        lax.psum_scatter(
            expert_total[2].astype(jnp.bfloat16), "dp", scatter_dimension=1, tiled=True
        ).astype(jnp.float32),
    )
    layer_out = jnp.stack(outputs)[:, None]
    tokens_grad_all = jnp.stack(input_grads)[:, None]
    return (
        layer_out,
        tokens_grad_all,
        dense_grads[0],
        dense_grads[1],
        dense_grads[2],
        dense_grads[3],
        dense_grads[4],
        dense_grads[5],
        dense_grads[6],
        dense_grads[7],
        dense_grads[8],
        expert_grads[0],
        expert_grads[1],
        expert_grads[2],
    )


def solution(mesh):
    in_specs = (
        P(None, ("dp", "expert"), None, None),
        P(None, ("dp", "expert"), None, None),
        P(None, ("dp", "expert")),
        P(None, ("dp", "expert"), None, None),
        P(None, ("dp", "expert"), None),
        P(("dp", "expert")),
        P(("dp", "expert"), None),
        P(("dp", "expert"), None),
        P(("dp", "expert"), None),
        P(("dp", "expert"), None),
        P(("dp", "expert")),
        P(("dp", "expert")),
        P(("dp", "expert")),
        P(("dp", "expert"), None),
        P("expert", "dp", None),
        P("expert", "dp", None),
        P("expert", "dp", None),
    )
    out_specs = (
        P(None, ("dp", "expert"), None, None),
        P(None, ("dp", "expert"), None, None),
        P(("dp", "expert")),
        P(("dp", "expert"), None),
        P(("dp", "expert"), None),
        P(("dp", "expert"), None),
        P(("dp", "expert"), None),
        P(("dp", "expert")),
        P(("dp", "expert")),
        P(("dp", "expert")),
        P(("dp", "expert"), None),
        P("expert", "dp", None),
        P("expert", "dp", None),
        P("expert", "dp", None),
    )
    return jax.shard_map(shards, mesh=mesh, in_specs=in_specs, out_specs=out_specs, check_vma=False)
```

profile of v0, /device:TPU:0, one launch (start us, length us, event | category | flops | bytes accessed | tf_op | source)
XLA Modules:
  0.0 3197.1 jit_solution(3459151046256052302)
XLA Ops:
  19.9 42.4 %all-reduce.17 = (bf16[2048]{0:T(1024)(128)(2,1)S(1)}, bf16[128]{0:T(256)(128)(2,1)S(1)}, bf16[128]{0:T(256)(128)(2,1)S(1)}, bf16[2048]{0:T(1024)(128)(2,1)S(1)}) all-reduce(bf16[2048]{0:T(1024)(128)(2,1)S(1)} %dynamic-update-slice, bf16[128]{0:T(256)(128)(2,1)S(1)} %dynamic-update-slice.2, ...), channel_id=1, replica_groups=mesh['dp'=4,'expert'=8] {'dp','expert'}, use_global_device_ids=true, to_apply=%add.8 | all-reduce | flops 4352 | bytes 17408
  64.8 26.5 all-gather.11.cloned.1.call-done
  91.3 12.4 copy.151
  103.7 6.0 multiply_reduce_fusion.19
  112.2 58.1 %all-gather.13.cloned.1.call-done = bf16[2048,2048]{1,0:T(8,128)(2,1)} async-done(((bf16[64,2048]{1,0:T(8,128)(2,1)}), bf16[2048,2048]{1,0:T(8,128)(2,1)}) %all-gather.13.cloned.1.call-update) | async-done | bytes 8388624 | tf_op jit(solution)/shard_map/all_gather | solution.py:92
  170.3 12.6 copy.152
  182.9 6.0 multiply_reduce_fusion.18
  196.0 53.4 %all-gather.9.cloned.1.call-done = bf16[2048,2048]{1,0:T(8,128)(2,1)} async-done(((bf16[64,2048]{1,0:T(8,128)(2,1)}), bf16[2048,2048]{1,0:T(8,128)(2,1)}) %all-gather.9.cloned.1.call-update) | async-done | bytes 8388624 | tf_op jit(solution)/shard_map/all_gather | solution.py:93
  255.3 72.9 %all-gather.15.cloned.1.call-done = bf16[2048,2048]{1,0:T(8,128)(2,1)} async-done(((bf16[64,2048]{1,0:T(8,128)(2,1)}), bf16[2048,2048]{1,0:T(8,128)(2,1)}) %all-gather.15.cloned.1.call-update) | async-done | bytes 8388624 | tf_op jit(solution)/shard_map/all_gather | solution.py:94
  334.2 6.2 gather_fusion
  340.4 5.5 broadcast_select_fusion.1
  345.8 5.4 all-to-all-start
  351.2 35.4 %all-gather.17.cloned.1.call-done = bf16[2,2048,1024]{2,1,0:T(8,128)(2,1)} async-done(((bf16[2,512,1024]{2,1,0:T(8,128)(2,1)}), bf16[2,2048,1024]{2,1,0:T(8,128)(2,1)}) %all-gather.17.cloned.1.call-update) | async-done | bytes 8388624 | tf_op jit(solution)/shard_map/all_gather | solution.py:104
  386.6 80.7 %all-to-all-done = bf16[8,160,2048]{2,1,0:T(8,128)(2,1)} async-done(((bf16[8,160,2048]{2,1,0:T(8,128)(2,1)}), bf16[8,160,2048]{2,1,0:T(8,128)(2,1)}, u32[]{:S(2)}, u32[]{:S(2)}) %all-to-all-start) | async-done | bytes 5242912 | tf_op jit(solution)/shard_map/all_to_all | solution.py:171
  467.3 11.4 fusion.37
  478.8 12.7 fusion.56
  491.5 14.8 all-gather.21.cloned.1.call-done
  506.3 9.2 convert_bitcast_fusion.3
  518.2 5.6 all-to-all-start.1
  525.0 7.0 gather_fusion.5
  532.0 163.7 %all-gather = bf16[32,64,16]{1,2,0:T(8,128)(2,1)S(1)} all-gather(bf16[1,64,16]{1,2,0:T(8,128)(2,1)S(1)} %bitcast.513), channel_id=1, replica_groups=mesh['dp'=4,'expert'=8] {'dp','expert'}, dimensions={0}, use_global_device_ids=true | all-gather | bytes 67584 | tf_op jit(solution)/shard_map/all_gather | solution.py:98
  696.4 12.0 gather_fusion.1
  722.0 116.2 %all_to_all.40 = bf16[8,160,2048]{2,1,0:T(8,128)(2,1)} all-to-all(bf16[8,160,2048]{2,1,0:T(8,128)(2,1)S(1)} %select_convert_fusion.1), channel_id=1, replica_groups=mesh['dp'=4,'expert'=8] {'expert'}, dimensions={0} | all-to-all | bytes 10485760 | tf_op jit(solution)/shard_map/all_to_all | solution.py:269
  838.2 14.1 fusion.48
  852.2 12.7 fusion.25
  864.9 11.2 fusion.39
  903.3 94.1 %all-to-all-done.5 = bf16[8,160,2048]{2,1,0:T(8,128)(2,1)} async-done(((bf16[8,160,2048]{2,1,0:T(8,128)(2,1)}), bf16[8,160,2048]{2,1,0:T(8,128)(2,1)}, u32[]{:S(2)}, u32[]{:S(2)}) %all-to-all-start.5) | async-done | bytes 5242912 | tf_op jit(solution)/shard_map/all_to_all | solution.py:297
  997.5 12.0 gather_fusion.6
  1009.5 10.5 fusion.14
  1022.1 6.1 gather_fusion.2
  1031.1 119.6 %all_to_all.41 = bf16[8,160,2048]{2,1,0:T(8,128)(2,1)S(1)} all-to-all(bf16[8,160,2048]{2,1,0:T(8,128)(2,1)S(1)} %broadcast_select_fusion), channel_id=1, replica_groups=mesh['dp'=4,'expert'=8] {'expert'}, dimensions={0} | all-to-all | bytes 10485760 | tf_op jit(solution)/shard_map/all_to_all | solution.py:171
  1150.7 9.9 fusion.35
  1160.7 11.7 fusion.51
  1172.4 5.8 convert_bitcast_fusion.2
  1186.0 7.0 gather_fusion.8
  1193.4 107.2 %all-to-all-done.3 = bf16[8,160,2048]{2,1,0:T(8,128)(2,1)} async-done(((bf16[8,160,2048]{2,1,0:T(8,128)(2,1)}), bf16[8,160,2048]{2,1,0:T(8,128)(2,1)}, u32[]{:S(2)}, u32[]{:S(2)}) %all-to-all-start.3) | async-done | bytes 5242912 | tf_op jit(solution)/shard_map/all_to_all | solution.py:185
  1300.6 12.0 gather_fusion.3
  1321.3 7.3 select_convert_fusion
  1333.7 13.1 fusion.86
  1348.6 104.6 %all-to-all-done.6 = bf16[8,160,2048]{2,1,0:T(8,128)(2,1)} async-done(((bf16[8,160,2048]{2,1,0:T(8,128)(2,1)}), bf16[8,160,2048]{2,1,0:T(8,128)(2,1)}, u32[]{:S(2)}, u32[]{:S(2)}) %all-to-all-start.6) | async-done | bytes 5242912 | tf_op jit(solution)/shard_map/all_to_all | solution.py:269
  1453.3 14.1 fusion.43
  1467.4 15.0 fusion.2
  1484.2 12.8 fusion.83
  1496.9 14.4 fusion.1
  1513.1 12.8 fusion.63
  1525.9 12.8 fusion.23
  1538.8 12.2 fusion.40
  1558.7 14.2 fusion
  1573.8 100.7 %all-to-all-done.7 = bf16[8,160,2048]{2,1,0:T(8,128)(2,1)} async-done(((bf16[8,160,2048]{2,1,0:T(8,128)(2,1)}), bf16[8,160,2048]{2,1,0:T(8,128)(2,1)}, u32[]{:S(2)}, u32[]{:S(2)}) %all-to-all-start.7) | async-done | bytes 5242912 | tf_op jit(solution)/shard_map/all_to_all | solution.py:297
  1674.4 12.2 gather_fusion.9
  1686.8 11.0 fusion.13
  1704.9 6.5 convolution_convert_fusion
  1725.4 8.4 convolution_add_fusion.3
  1742.7 8.3 convolution_add_fusion.2
  1758.2 8.3 convolution_add_fusion.1
  1771.2 8.1 convolution_add_fusion
  1780.8 6.6 fusion.249
  1787.4 6.5 fusion.248
  1793.9 6.5 convolution_add_fusion.7
  1810.9 46.5 %all-reduce.16 = (f32[2048]{0:T(1024)S(1)}, f32[128]{0:T(128)S(1)}, f32[128]{0:T(128)S(1)}, f32[2048]{0:T(1024)S(1)}) all-reduce(f32[2048]{0:T(1024)S(1)} %add.387, f32[128]{0:T(128)S(1)} %add.392, f32[128]{0:T(128)S(1)} %add.393, f32[2048]{0:T(1024)S(1)} %add.394), channel_id=2, replica_groups=mesh['dp'=4,'expert'=8] {'dp','expert'}, use_global_device_ids=true, to_apply=%region_44.45.clone | all-reduce | flops 4352 | bytes 34816
  1878.0 231.8 %reduce-scatter.11.cloned.1.call-done = f32[64,2048]{1,0:T(8,128)} async-done(((f32[2048,2048]{1,0:T(8,128)}), f32[64,2048]{1,0:T(8,128)}) %reduce-scatter.11.cloned.1.call-update) | async-done | bytes 524304 | tf_op jit(solution)/shard_map/reduce_scatter | solution.py:452
  2109.7 360.2 %reduce-scatter.13.cloned.1.call-done = f32[64,2048]{1,0:T(8,128)} async-done(((f32[2048,2048]{1,0:T(8,128)}), f32[64,2048]{1,0:T(8,128)}) %reduce-scatter.13.cloned.1.call-update) | async-done | bytes 524304 | tf_op jit(solution)/shard_map/reduce_scatter | solution.py:453
  2470.0 360.1 %reduce-scatter.15.cloned.1.call-done = f32[64,2048]{1,0:T(8,128)} async-done(((f32[2048,2048]{1,0:T(8,128)}), f32[64,2048]{1,0:T(8,128)}) %reduce-scatter.15.cloned.1.call-update) | async-done | bytes 524304 | tf_op jit(solution)/shard_map/reduce_scatter | solution.py:454
  2830.1 360.1 %reduce-scatter.17.cloned.1.call-done = f32[64,2048]{1,0:T(8,128)} async-done(((f32[2048,2048]{1,0:T(8,128)}), f32[64,2048]{1,0:T(8,128)}) %reduce-scatter.17.cloned.1.call-update) | async-done | bytes 524304 | tf_op jit(solution)/shard_map/reduce_scatter | solution.py:455
  (556 shorter events, 194.6 us)
Async XLA Ops:
  7.2 12.4 copy-start.156
  7.2 55.0 %copy-start.5 = (bf16[2,1,128,2048]{3,2,1,0:T(8,128)(2,1)S(1)}, bf16[2,1,128,2048]{3,2,1,0:T(8,128)(2,1)}, u32[]{:S(2)}) copy-start(bf16[2,1,128,2048]{3,2,1,0:T(8,128)(2,1)} %param.17) | copy-start | bytes 3145732
  7.3 56.2 %copy-start.147 = (s32[2,1]{0,1:T(1,128)S(1)}, s32[2,1]{0,1:T(1,128)}, u32[]{:S(2)}) copy-start(s32[2,1]{0,1:T(1,128)} %param.19) | copy-start | bytes 28
  7.3 84.1 %all-gather.11.cloned.1.call-start = ((), (), s32[]{:S(2)}) async-start(), calls=%async_computation.17 | async-start | bytes 8650752 | tf_op jit(solution)/shard_map/all_gather | solution.py:91
  8.0 162.3 %all-gather.13.cloned.1.call-start = ((), (), s32[]{:S(2)}) async-start(), calls=%async_computation.18 | async-start | bytes 8650752 | tf_op jit(solution)/shard_map/all_gather | solution.py:92
  8.7 240.6 %all-gather.9.cloned.1.call-start = ((), (), s32[]{:S(2)}) async-start(), calls=%async_computation.16 | async-start | bytes 8650752 | tf_op jit(solution)/shard_map/all_gather | solution.py:93
  9.5 318.8 %all-gather.15.cloned.1.call-start = ((), (), s32[]{:S(2)}) async-start(), calls=%async_computation.19 | async-start | bytes 8650752 | tf_op jit(solution)/shard_map/all_gather | solution.py:94
  10.1 376.6 %all-gather.17.cloned.1.call-start = ((), (), s32[]{:S(2)}) async-start(), calls=%async_computation.20 | async-start | bytes 10485760 | tf_op jit(solution)/shard_map/all_gather | solution.py:104
  10.6 468.1 %all-gather.19.cloned.1.call-start = ((), (), s32[]{:S(2)}) async-start(), calls=%async_computation.21 | async-start | bytes 10485760 | tf_op jit(solution)/shard_map/all_gather | solution.py:105
  11.2 495.0 %all-gather.21.cloned.1.call-start = ((), (), s32[]{:S(2)}) async-start(), calls=%async_computation.22 | async-start | bytes 10485760 | tf_op jit(solution)/shard_map/all_gather | solution.py:106
  62.3 187.1 %copy-start.38 = (f32[2048]{0:T(1024)}, f32[2048]{0:T(1024)S(1)}, u32[]{:S(2)}) copy-start(f32[2048]{0:T(1024)S(1)} %convert_element_type.397) | copy-start | bytes 24580
  62.6 186.8 %copy-start.98 = (f32[128]{0:T(128)}, f32[128]{0:T(128)S(1)}, u32[]{:S(2)}) copy-start(f32[128]{0:T(128)S(1)} %fusion.222) | copy-start | bytes 1540
  63.2 128.5 %copy-start.139 = (f32[128]{0:T(128)}, f32[128]{0:T(128)S(1)}, u32[]{:S(2)}) copy-start(f32[128]{0:T(128)S(1)} %convert_element_type.403) | copy-start | bytes 1540
  63.2 125.8 %copy-start.100 = (f32[128]{0:T(128)}, f32[128]{0:T(128)S(1)}, u32[]{:S(2)}) copy-start(f32[128]{0:T(128)S(1)} %fusion.224) | copy-start | bytes 1540
  63.4 129.1 %copy-start.83 = (f32[128,64]{0,1:T(8,128)}, f32[128,64]{0,1:T(8,128)S(1)}, u32[]{:S(2)}) copy-start(f32[128,64]{0,1:T(8,128)S(1)} %get-tuple-element.177) | copy-start | bytes 98308
  63.4 129.1 %copy-start.85 = (f32[128,64]{0,1:T(8,128)}, f32[128,64]{0,1:T(8,128)S(1)}, u32[]{:S(2)}) copy-start(f32[128,64]{0,1:T(8,128)S(1)} %get-tuple-element.178) | copy-start | bytes 98308
  63.4 128.7 %copy-start.137 = (f32[128]{0:T(128)}, f32[128]{0:T(128)S(1)}, u32[]{:S(2)}) copy-start(f32[128]{0:T(128)S(1)} %convert_element_type.404) | copy-start | bytes 1540
  64.7 268.4 %copy-start.87 = (f32[2048]{0:T(1024)}, f32[2048]{0:T(1024)S(1)}, u32[]{:S(2)}) copy-start(f32[2048]{0:T(1024)S(1)} %convert_element_type.409) | copy-start | bytes 24580
  109.7 81.8 %copy-start.107 = (f32[128,16]{0,1:T(8,128)}, f32[128,16]{0,1:T(8,128)S(1)}, u32[]{:S(2)}) copy-start(f32[128,16]{0,1:T(8,128)S(1)} %get-tuple-element.179) | copy-start | bytes 24580
  109.7 82.0 %copy-start.12 = (f32[128,16,128]{0,2,1:T(8,128)}, f32[128,16,128]{0,2,1:T(8,128)S(1)}, u32[]{:S(2)}) copy-start(f32[128,16,128]{0,2,1:T(8,128)S(1)} %get-tuple-element.180) | copy-start | bytes 3145732
  112.2 79.3 %copy-start.109 = (f32[128,16]{0,1:T(8,128)}, f32[128,16]{0,1:T(8,128)S(1)}, u32[]{:S(2)}) copy-start(f32[128,16]{0,1:T(8,128)S(1)} %get-tuple-element.181) | copy-start | bytes 24580
  112.2 79.4 %copy-start.14 = (f32[128,16,128]{0,2,1:T(8,128)}, f32[128,16,128]{0,2,1:T(8,128)S(1)}, u32[]{:S(2)}) copy-start(f32[128,16,128]{0,2,1:T(8,128)S(1)} %get-tuple-element.182) | copy-start | bytes 3145732
  195.3 58.8 %copy-start.25 = (f32[16,128,128]{2,1,0:T(8,128)}, f32[16,128,128]{2,1,0:T(8,128)S(1)}, u32[]{:S(2)}) copy-start(f32[16,128,128]{2,1,0:T(8,128)S(1)} %get-tuple-element.188) | copy-start | bytes 3145732
  195.3 58.8 %copy-start.116 = (f32[16,128]{1,0:T(8,128)}, f32[16,128]{1,0:T(8,128)S(1)}, u32[]{:S(2)}) copy-start(f32[16,128]{1,0:T(8,128)S(1)} %get-tuple-element.187) | copy-start | bytes 24580
  196.0 58.1 %copy-start.118 = (f32[16,128]{1,0:T(8,128)}, f32[16,128]{1,0:T(8,128)S(1)}, u32[]{:S(2)}) copy-start(f32[16,128]{1,0:T(8,128)S(1)} %fusion.146) | copy-start | bytes 24580
  254.1 78.9 %copy-start.60 = (bf16[16,16,8,128]{3,2,1,0:T(8,128)(2,1)}, bf16[16,16,8,128]{3,2,1,0:T(8,128)(2,1)S(1)}, u32[]{:S(2)}) copy-start(bf16[16,16,8,128]{3,2,1,0:T(8,128)(2,1)S(1)} %fusion.110) | copy-start | bytes 1572868
  255.3 77.7 %copy-start.55 = (bf16[16,128,128]{2,1,0:T(8,128)(2,1)}, bf16[16,128,128]{2,1,0:T(8,128)(2,1)S(1)}, u32[]{:S(2)}) copy-start(bf16[16,128,128]{2,1,0:T(8,128)(2,1)S(1)} %convolution_convert_fusion.7) | copy-start | bytes 1572868
  334.2 361.9 %copy-start.1 = (bf16[128,2048]{1,0:T(8,128)(2,1)}, bf16[128,2048]{1,0:T(8,128)(2,1)S(1)}, u32[]{:S(2)}) copy-start(bf16[128,2048]{1,0:T(8,128)(2,1)S(1)} %multiply_convert_fusion.3) | copy-start | bytes 1572868
  345.8 121.5 %all-to-all-start = ((bf16[8,160,2048]{2,1,0:T(8,128)(2,1)}), bf16[8,160,2048]{2,1,0:T(8,128)(2,1)}, u32[]{:S(2)}, u32[]{:S(2)}) async-start(bf16[8,160,2048]{2,1,0:T(8,128)(2,1)} %broadcast_select_fusion.1), calls=%async_computation | async-start | bytes 10485760 | tf_op jit(solution)/shard_map/all_to_all | solution.py:171
  491.5 24.0 copy-start.31
  518.2 178.2 %all-to-all-start.1 = ((bf16[8,160,2048]{2,1,0:T(8,128)(2,1)}), bf16[8,160,2048]{2,1,0:T(8,128)(2,1)}, u32[]{:S(2)}, u32[]{:S(2)}) async-start(bf16[8,160,2048]{2,1,0:T(8,128)(2,1)} %bitcast.479), calls=%async_computation.1 | async-start | bytes 10485760 | tf_op jit(solution)/shard_map/all_to_all | solution.py:185
  696.0 497.1 %copy-start.63 = (bf16[2048,16]{0,1:T(8,128)(2,1)}, bf16[2048,16]{0,1:T(8,128)(2,1)S(1)}, u32[]{:S(2)}) copy-start(bf16[2048,16]{0,1:T(8,128)(2,1)S(1)} %reshape.897) | copy-start | bytes 196612
  852.2 12.7 copy-start.160
  878.9 118.5 %all-to-all-start.5 = ((bf16[8,160,2048]{2,1,0:T(8,128)(2,1)}), bf16[8,160,2048]{2,1,0:T(8,128)(2,1)}, u32[]{:S(2)}, u32[]{:S(2)}) async-start(bf16[8,160,2048]{2,1,0:T(8,128)(2,1)} %bitcast.477), calls=%async_computation.5 | async-start | bytes 10485760 | tf_op jit(solution)/shard_map/all_to_all | solution.py:297
  902.8 117.2 %copy-start.20 = (f32[128,2048]{1,0:T(8,128)}, f32[128,2048]{1,0:T(8,128)S(1)}, u32[]{:S(2)}) copy-start(f32[128,2048]{1,0:T(8,128)S(1)} %get-tuple-element.198) | copy-start | bytes 3145732
  903.3 116.7 %copy-start.135 = (f32[128]{0:T(128)}, f32[128]{0:T(128)S(1)}, u32[]{:S(2)}) copy-start(f32[128]{0:T(128)S(1)} %fusion.225) | copy-start | bytes 1540
  1150.7 21.6 slice-start.6
  1181.0 119.6 %all-to-all-start.3 = ((bf16[8,160,2048]{2,1,0:T(8,128)(2,1)}), bf16[8,160,2048]{2,1,0:T(8,128)(2,1)}, u32[]{:S(2)}, u32[]{:S(2)}) async-start(bf16[8,160,2048]{2,1,0:T(8,128)(2,1)} %bitcast.480), calls=%async_computation.3 | async-start | bytes 10485760 | tf_op jit(solution)/shard_map/all_to_all | solution.py:185
  1193.0 119.6 %copy-start.128 = (pred[1024]{0:T(1024)(128)(4,1)}, pred[1024]{0:T(1024)(128)(4,1)S(1)}, u32[]{:S(2)}) copy-start(pred[1024]{0:T(1024)(128)(4,1)S(1)} %broadcast_compare_fusion.2) | copy-start | bytes 3076
  1193.1 119.5 %copy-start.111 = (s32[1024]{0:T(1024)}, s32[1024]{0:T(1024)S(1)}, u32[]{:S(2)}) copy-start(s32[1024]{0:T(1024)S(1)} %broadcast_clamp_fusion) | copy-start | bytes 12292
  1328.6 124.6 %all-to-all-start.6 = ((bf16[8,160,2048]{2,1,0:T(8,128)(2,1)}), bf16[8,160,2048]{2,1,0:T(8,128)(2,1)}, u32[]{:S(2)}, u32[]{:S(2)}) async-start(bf16[8,160,2048]{2,1,0:T(8,128)(2,1)} %select_convert_fusion), calls=%async_computation.6 | async-start | bytes 10485760 | tf_op jit(solution)/shard_map/all_to_all | solution.py:269
  1333.4 445.9 %reduce-scatter.25.cloned.1.call-start = ((), (), s32[]{:S(2)}) async-start(), calls=%async_computation.30 | async-start | bytes 1081344
  1346.8 120.6 %copy-start.113 = (bf16[128,16]{0,1:T(8,128)(2,1)}, bf16[128,16]{0,1:T(8,128)(2,1)S(1)}, u32[]{:S(2)}) copy-start(bf16[128,16]{0,1:T(8,128)(2,1)S(1)} %multiply_convert_fusion.4) | copy-start | bytes 12292
  1348.4 517.3 %reduce-scatter.19.cloned.1.call-start = ((), (), s32[]{:S(2)}) async-start(), calls=%async_computation.27 | async-start | bytes 10485760 | tf_op jit(solution)/shard_map/reduce_scatter | solution.py:462
  1467.4 15.0 copy-start.158
  1482.5 387.3 %reduce-scatter.21.cloned.1.call-start = ((), (), s32[]{:S(2)}) async-start(), calls=%async_computation.28 | async-start | bytes 10485760 | tf_op jit(solution)/shard_map/reduce_scatter | solution.py:465
  1513.1 12.8 copy-start.162
  1525.9 12.8 copy-start.159
  1553.7 120.7 %all-to-all-start.7 = ((bf16[8,160,2048]{2,1,0:T(8,128)(2,1)}), bf16[8,160,2048]{2,1,0:T(8,128)(2,1)}, u32[]{:S(2)}, u32[]{:S(2)}) async-start(bf16[8,160,2048]{2,1,0:T(8,128)(2,1)} %bitcast.478), calls=%async_computation.7 | async-start | bytes 10485760 | tf_op jit(solution)/shard_map/all_to_all | solution.py:297
  1558.7 315.2 %reduce-scatter.23.cloned.1.call-start = ((), (), s32[]{:S(2)}) async-start(), calls=%async_computation.29 | async-start | bytes 10485760 | tf_op jit(solution)/shard_map/reduce_scatter | solution.py:468
  1573.0 101.4 %copy-start.112 = (s32[1024]{0:T(1024)S(1)}, s32[1024]{0:T(1024)}, u32[]{:S(2)}) copy-start(s32[1024]{0:T(1024)} %copy-done.111) | copy-start | bytes 12292
  1573.0 536.7 %reduce-scatter.11.cloned.1.call-start = ((), (), s32[]{:S(2)}) async-start(), calls=%async_computation.23 | async-start | bytes 17301504 | tf_op jit(solution)/shard_map/reduce_scatter | solution.py:452
  1686.7 12.3 copy-start.151
  1686.7 12.3 copy-start.24
  1686.7 12.3 copy-start.57
  1686.7 12.3 copy-start.58
  1686.7 12.3 copy-start.59
  1686.8 15.0 slice-start
  1733.8 736.2 %reduce-scatter.13.cloned.1.call-start = ((), (), s32[]{:S(2)}) async-start(), calls=%async_computation.24 | async-start | bytes 17301504 | tf_op jit(solution)/shard_map/reduce_scatter | solution.py:453
  1751.1 1079.0 %reduce-scatter.15.cloned.1.call-start = ((), (), s32[]{:S(2)}) async-start(), calls=%async_computation.25 | async-start | bytes 17301504 | tf_op jit(solution)/shard_map/reduce_scatter | solution.py:454
  1766.5 1423.6 %reduce-scatter.17.cloned.1.call-start = ((), (), s32[]{:S(2)}) async-start(), calls=%async_computation.26 | async-start | bytes 17301504 | tf_op jit(solution)/shard_map/reduce_scatter | solution.py:455
  1787.4 13.1 slice-start.2
  1806.7 53.0 %copy-start.144 = (f32[128]{0:T(128)S(1)}, f32[128]{0:T(128)}, u32[]{:S(2)}) copy-start(f32[128]{0:T(128)} %copy-done.143) | copy-start | bytes 1540
  1806.7 53.0 %copy-start.146 = (f32[128]{0:T(128)S(1)}, f32[128]{0:T(128)}, u32[]{:S(2)}) copy-start(f32[128]{0:T(128)} %copy-done.145) | copy-start | bytes 1540
  (128 other events, 602.6 us)
Sparse Core Ops, SparseCore 0:
  11.1 80.1 all-gather.10
  94.3 75.9 all-gather.12
  173.3 75.9 all-gather.8
  252.2 76.0 all-gather.14
  329.7 56.8 all-gather.16
  388.0 58.2 all-gather.18
  447.9 58.2 all-gather.20
  1348.5 178.4 reduce-scatter.24
  1529.8 69.0 reduce-scatter.18
  1601.3 71.7 reduce-scatter.20
  1675.8 71.6 reduce-scatter.22
  1750.3 359.4 reduce-scatter.10
  2112.6 357.3 reduce-scatter.12
  2472.7 357.3 reduce-scatter.14
  2832.8 357.3 reduce-scatter.16
where the time goes:
time: 3210 us; the launch traced here: 3200 us
  waiting for transfers between devices  2070 us (64%)
  blocking collectives  488 us (15%)
  matrix products  357 us (11%)
  local copies, waits for them, and re-layouts  150 us (5%)
  other arithmetic  86.9 us (3%)
  starting transfers between devices  32.1 us (1%)
    reduce_scatter x1, waiting for transfers between devices, shards(): lax.psum_scatter(dense_total[2], ('dp', 'expert'), scatter_dimension=0, t...  360 us
    reduce_scatter x1, waiting for transfers between devices, shards(): lax.psum_scatter(dense_total[3], ('dp', 'expert'), scatter_dimension=0, t...  360 us
    reduce_scatter x1, waiting for transfers between devices, shards(): lax.psum_scatter(dense_total[4], ('dp', 'expert'), scatter_dimension=0, t...  360 us
    reduce_scatter x1, waiting for transfers between devices, shards(): lax.psum_scatter(dense_total[1], ('dp', 'expert'), scatter_dimension=0, t...  232 us
    all_to_all x2, waiting for transfers between devices, backward_pass(): lax.all_to_all(sent_local.astype(jnp.bfloat16).reshape(expert_count, -1,...  195 us
    all_gather x1, blocking collectives, fetch_dense(): lax.all_gather(shard[8], ('dp', 'expert'), axis=0, tiled=True)  164 us
    all_to_all x1, blocking collectives, forward_pass(): lax.all_to_all(sent_rows.reshape(expert_count, -1, D), 'expert', split_ax...  120 us
    all_to_all x1, blocking collectives, backward_pass(): lax.all_to_all(returned_grad.reshape(expert_count, -1, D), 'expert', spli...  116 us
  transfers between devices with their start and end apart: 21, of which 15 were waited for; matrix products, arithmetic and copies ran while one was open for 13% of the time, Pallas kernels for 0%

commit v1 on v0

v1 whole, which is shorter than its diff:
```python
import functools
import math

import jax
import jax.numpy as jnp
from jax import lax
from jax.experimental import pallas as pl
from jax.experimental.pallas import tpu as pltpu
from jax.sharding import Mesh
from jax.sharding import PartitionSpec as P

D = 2048
HEADS = 16
HD = 128
TOP = 8
EXTRA = 128

EPSILON = 1e-06
THETA = 50000.0
NEGATIVE = -1e30
BF = jnp.bfloat16
F32 = jnp.float32


def plain(left, right):
    return jnp.dot(left, right, preferred_element_type=F32)


def inner(left, right):
    return lax.dot_general(left, right, (((0,), (0,)), ((), ())), preferred_element_type=F32)


def times_t(left, right):
    return lax.dot_general(left, right, (((1,), (1,)), ((), ())), preferred_element_type=F32)


def shift(value, axis, step):
    size = lax.axis_size(axis)
    return lax.ppermute(value, axis, [(i, (i + step) % size) for i in range(size)])


def gather_blocks(block, order):
    held = {(): block}
    for axis in order:
        grown = {}
        for key, value in held.items():
            for k in range(lax.axis_size(axis)):
                if k:
                    value = shift(value, axis, 1)
                grown[key + (k,)] = value
        held = grown
    return held


def reduce_blocks(part, order):
    def reduce_from(key, depth):
        if depth == len(order):
            return part(key)
        axis = order[depth]
        size = lax.axis_size(axis)
        total = reduce_from(key + (size - 1,), depth + 1)
        for k in reversed(range(size - 1)):
            arrived = shift(total.astype(BF), axis, -1)
            total = reduce_from(key + (k,), depth + 1).astype(F32) + arrived.astype(F32)
        return total

    return reduce_from((), 0)


def place_kernel(count, row_axis, rows, offsets_ref, *refs):
    blocks, out, sems = refs[:count], refs[count], refs[count + 1]
    copies = []
    for i in range(count):
        start = pl.multiple_of(offsets_ref[i], 16)
        window = pl.ds(start, rows)
        target = out.at[window] if row_axis == 0 else out.at[:, window]
        copies.append(pltpu.make_async_copy(blocks[i], target, sems.at[i]))
    for copy in copies:
        copy.start()
    for copy in copies:
        copy.wait()


def place(blocks, offsets, row_axis):
    shape = list(blocks[0].shape)
    rows = shape[row_axis]
    shape[row_axis] = rows * len(blocks)
    return pl.pallas_call(
        functools.partial(place_kernel, len(blocks), row_axis, rows),
        out_shape=jax.ShapeDtypeStruct(tuple(shape), blocks[0].dtype),
        grid_spec=pltpu.PrefetchScalarGridSpec(
            num_scalar_prefetch=1,
            in_specs=[pl.BlockSpec(memory_space=pl.ANY)] * len(blocks),
            out_specs=pl.BlockSpec(memory_space=pl.ANY),
            scratch_shapes=[pltpu.SemaphoreType.DMA((len(blocks),))],
        ),
    )(jnp.stack(offsets).astype(jnp.int32), *blocks)


def rope_tables(row_count):
    half = HD // 2
    frequency = THETA ** (-jnp.arange(half, dtype=F32) / half)
    angles = jnp.arange(row_count, dtype=F32)[:, None] * frequency[None, :]
    cosine, sine = jnp.cos(angles), jnp.sin(angles)
    return jnp.concatenate([cosine, cosine], axis=1), jnp.concatenate([-sine, sine], axis=1)


def head_forward(raw, gain, cosine, sine):
    scale = lax.rsqrt(jnp.mean(raw * raw, axis=-1, keepdims=True) + EPSILON)
    unit = raw * scale
    value = unit * gain
    turned = value * cosine + pltpu.roll(value, HD // 2, 1) * sine
    return unit, scale, turned.astype(BF)


def head_backward(grad, unit, scale, gain, cosine, sine):
    grad = grad * cosine - pltpu.roll(grad, HD // 2, 1) * sine
    gain_grad = jnp.sum(grad * unit, axis=0, keepdims=True)
    grad = grad * gain
    grad = scale * (grad - unit * jnp.mean(grad * unit, axis=-1, keepdims=True))
    return grad.astype(BF), gain_grad


def attention_of(query, key, length):
    scores = times_t(query, key) * (1.0 / math.sqrt(HD))
    valid = lax.broadcasted_iota(jnp.int32, scores.shape, 1) < length
    scores = jnp.where(valid, scores, NEGATIVE)
    weight = jnp.exp(scores - jnp.max(scores, axis=-1, keepdims=True))
    return weight / jnp.sum(weight, axis=-1, keepdims=True)


def attend_kernel(heads, lengths_ref, qkv_ref, gains_ref, cosine_ref, sine_ref, mixed_ref):
    length = lengths_ref[pl.program_id(0)]
    cosine, sine = cosine_ref[...], sine_ref[...]
    query_gain, key_gain = gains_ref[0:1, :], gains_ref[1:2, :]
    width = heads * HD
    for h in range(heads):
        lo = h * HD
        query = head_forward(qkv_ref[:, lo : lo + HD], query_gain, cosine, sine)[2]
        key = head_forward(qkv_ref[:, width + lo : width + lo + HD], key_gain, cosine, sine)[2]
        value = qkv_ref[:, 2 * width + lo : 2 * width + lo + HD].astype(BF)
        attention = attention_of(query, key, length)
        mixed_ref[:, lo : lo + HD] = plain(attention.astype(BF), value).astype(BF)


def attend_back_kernel(
    heads, lengths_ref, qkv_ref, mixed_grad_ref, gains_ref, cosine_ref, sine_ref, out_ref, gain_ref
):
    @pl.when(pl.program_id(0) == 0)
    def _():
        gain_ref[...] = jnp.zeros_like(gain_ref)

    length = lengths_ref[pl.program_id(0)]
    cosine, sine = cosine_ref[...], sine_ref[...]
    query_gain, key_gain = gains_ref[0:1, :], gains_ref[1:2, :]
    width = heads * HD
    score_scale = 1.0 / math.sqrt(HD)
    for h in range(heads):
        lo = h * HD
        query_unit, query_scale, query = head_forward(
            qkv_ref[:, lo : lo + HD], query_gain, cosine, sine
        )
        key_unit, key_scale, key = head_forward(
            qkv_ref[:, width + lo : width + lo + HD], key_gain, cosine, sine
        )
        value = qkv_ref[:, 2 * width + lo : 2 * width + lo + HD].astype(BF)
        attention = attention_of(query, key, length)
        mixed_grad = mixed_grad_ref[:, lo : lo + HD]
        value_grad = inner(attention.astype(BF), mixed_grad)
        attention_grad = times_t(mixed_grad, value)
        score_grad = attention * (
            attention_grad - jnp.sum(attention * attention_grad, axis=-1, keepdims=True)
        )
        score_grad = score_grad.astype(BF)
        query_grad, query_gain_grad = head_backward(
            plain(score_grad, key) * score_scale, query_unit, query_scale, query_gain, cosine, sine
        )
        key_grad, key_gain_grad = head_backward(
            inner(score_grad, query) * score_scale, key_unit, key_scale, key_gain, cosine, sine
        )
        out_ref[:, lo : lo + HD] = query_grad
        out_ref[:, width + lo : width + lo + HD] = key_grad
        out_ref[:, 2 * width + lo : 2 * width + lo + HD] = value_grad.astype(BF)
        gain_ref[0:1, :] += query_gain_grad
        gain_ref[1:2, :] += key_gain_grad


def attend(qkv, lengths, gains, cosine, sine, rows, heads):
    sequences = qkv.shape[0] // rows
    width = heads * HD
    whole = pl.BlockSpec((2, HD), lambda s, n: (0, 0))
    table = pl.BlockSpec((rows, HD), lambda s, n: (0, 0))
    return pl.pallas_call(
        functools.partial(attend_kernel, heads),
        out_shape=jax.ShapeDtypeStruct((qkv.shape[0], width), BF),
        grid_spec=pltpu.PrefetchScalarGridSpec(
            num_scalar_prefetch=1,
            grid=(sequences,),
            in_specs=[
                pl.BlockSpec((rows, 3 * width), lambda s, n: (s, 0)),
                whole,
                table,
                table,
            ],
            out_specs=pl.BlockSpec((rows, width), lambda s, n: (s, 0)),
        ),
        compiler_params=pltpu.CompilerParams(vmem_limit_bytes=32 << 20),
    )(lengths, qkv, gains, cosine, sine)


def attend_back(qkv, mixed_grad, lengths, gains, cosine, sine, rows, heads):
    sequences = qkv.shape[0] // rows
    width = heads * HD
    whole = pl.BlockSpec((2, HD), lambda s, n: (0, 0))
    table = pl.BlockSpec((rows, HD), lambda s, n: (0, 0))
    return pl.pallas_call(
        functools.partial(attend_back_kernel, heads),
        out_shape=(
            jax.ShapeDtypeStruct((qkv.shape[0], 3 * width), BF),
            jax.ShapeDtypeStruct((2, HD), F32),
        ),
        grid_spec=pltpu.PrefetchScalarGridSpec(
            num_scalar_prefetch=1,
            grid=(sequences,),
            in_specs=[
                pl.BlockSpec((rows, 3 * width), lambda s, n: (s, 0)),
                pl.BlockSpec((rows, width), lambda s, n: (s, 0)),
                whole,
                table,
                table,
            ],
            out_specs=(
                pl.BlockSpec((rows, 3 * width), lambda s, n: (s, 0)),
                whole,
            ),
        ),
        compiler_params=pltpu.CompilerParams(vmem_limit_bytes=32 << 20),
    )(lengths, qkv, mixed_grad, gains, cosine, sine)


def norm_back(grad, unit, scale, gain):
    scaled = grad * gain
    values_grad = scale * (scaled - unit * jnp.mean(scaled * unit, axis=-1, keepdims=True))
    return values_grad, jnp.sum(grad * unit, axis=0)


def slot_ranks(route, priority, experts, capacity):
    rows = route.shape[0]
    expert = jnp.arange(experts, dtype=jnp.int32)
    chosen = route[:, :, None] == expert[None, None, :]
    order = jnp.sum(jnp.where(chosen, priority.reshape(rows, TOP)[:, :, None], 0), axis=1)
    routed = jnp.any(chosen, axis=1)
    order = jnp.where(routed, order, rows * TOP).T
    rank = jnp.sum((order[:, None, :] < order[:, :, None]).astype(jnp.int32), axis=2).T
    return jnp.where(routed & (rank < capacity), rank, -1)


def in_three(value):
    high = value.astype(BF)
    rest = value - high.astype(F32)
    middle = rest.astype(BF)
    low = (rest - middle.astype(F32)).astype(BF)
    return jnp.concatenate([high, middle, low], axis=-1)


def from_three(columns, count):
    return (
        columns[..., :count].astype(F32)
        + columns[..., count : 2 * count].astype(F32)
        + columns[..., 2 * count : 3 * count].astype(F32)
    )


def widen(columns, width):
    return jnp.pad(columns, ((0, 0), (0, width - columns.shape[-1])))


def shards(
    tokens,
    out_cotangent,
    lengths,
    routes,
    priority,
    attn_gain,
    query_weight,
    key_weight,
    value_weight,
    output_weight,
    query_gain,
    key_gain,
    ffn_gain,
    router_weight,
    gate_weight,
    up_weight,
    down_weight,
):
    batches, rows = tokens.shape[0], tokens.shape[2]
    own = batches * rows
    experts = router_weight.shape[1]
    capacity = 5 * rows * TOP // (4 * experts)
    local = gate_weight.shape[0]
    ys, zs, xs = lax.axis_size("y"), lax.axis_size("z"), lax.axis_size("x")
    y, c, z, x = (lax.axis_index(name) for name in ("y", "c", "z", "x"))
    shard_rows = query_weight.shape[0]
    head_shard = query_gain.shape[0]
    heads = HEADS // 2
    width = heads * HD
    chunk = D // (2 * ys)

    def swap(value):
        return lax.ppermute(value, "c", [(0, 1), (1, 0)])

    def half_columns(weight, core):
        return jnp.concatenate(
            [
                lax.dynamic_slice_in_dim(weight, (2 * i + core) * chunk, chunk, 1)
                for i in range(ys)
            ],
            axis=1,
        )

    token_rows = tokens.reshape(own, D)
    both_tokens = jnp.concatenate([token_rows, swap(token_rows)], axis=0)
    length = lengths.reshape(batches)
    both_lengths = jnp.concatenate([length, swap(length)])
    extra = jnp.concatenate(
        [
            attn_gain[:, None],
            ffn_gain[:, None],
            router_weight,
            jnp.pad(query_gain, (0, shard_rows - head_shard))[:, None],
            jnp.pad(key_gain, (0, shard_rows - head_shard))[:, None],
        ],
        axis=1,
    )
    extra = widen(extra, EXTRA)

    def packed(core):
        return jnp.concatenate(
            [half_columns(w, core) for w in (query_weight, key_weight, value_weight)] + [extra],
            axis=1,
        )

    mine, theirs = packed(c), swap(packed(1 - c))
    first = jnp.where(c == 0, mine, theirs)
    second = jnp.where(c == 0, theirs, mine)

    def row_block(key, order, core):
        at = dict(zip(order, key, strict=True))
        ky = jnp.mod(y - at["y"], ys)
        kz = jnp.mod(z - at["z"], zs)
        kx = jnp.mod(x - at["x"], xs)
        if core is None:
            return (ky * zs + kz) * xs + kx
        return ((ky * 2 + core) * zs + kz) * xs + kx

    ZXY, ZYX = ("z", "x", "y"), ("z", "y", "x")
    blocks, offsets = [], []
    for core, order, block in ((0, ZXY, first), (1, ZYX, second)):
        for key, value in gather_blocks(block, order).items():
            blocks.append(value)
            offsets.append(row_block(key, order, core) * shard_rows)
    qkv_weight = place(blocks, offsets, 0)
    blocks, offsets = [], []
    for key, value in gather_blocks(output_weight, ZYX).items():
        blocks.append(value)
        offsets.append(row_block(key, ZYX, None) * shard_rows)
    out_weight = place(blocks, offsets, 0)

    full_experts = []
    for weight in (gate_weight, up_weight, down_weight):
        blocks, offsets = [], []
        for key, value in gather_blocks(weight, ("y", "c")).items():
            blocks.append(value)
            offsets.append(
                (jnp.mod(y - key[0], ys) * 2 + jnp.mod(c - key[1], 2)) * weight.shape[1]
            )
        full_experts.append(place(blocks, offsets, 1))
    gate_full, up_full, down_full = full_experts

    ranks = jnp.concatenate(
        [
            slot_ranks(routes[b, 0], priority[b, 0], experts, capacity)
            for b in range(batches)
        ],
        axis=0,
    )
    cotangent = out_cotangent.reshape(own, D)
    ZX = ("z", "x")
    cot_blocks = gather_blocks(
        jnp.concatenate([cotangent, widen(ranks.astype(BF), EXTRA)], axis=1), ZX
    )

    small = qkv_weight[:, 3 * width :].astype(F32)
    qkv_weight = qkv_weight[:, : 3 * width]
    attn_gain_f = small[:, 0][None, :]
    ffn_gain_f = small[:, 1][None, :]
    router = small[:, 2 : 2 + experts].astype(BF)
    per_device = small.reshape(-1, shard_rows, EXTRA)[:, :head_shard]
    head_gains = jnp.stack(
        [per_device[:, :, 2 + experts].reshape(HD), per_device[:, :, 3 + experts].reshape(HD)]
    )
    tokens_f = both_tokens.astype(F32)
    token_scale = lax.rsqrt(jnp.mean(tokens_f * tokens_f, axis=-1, keepdims=True) + EPSILON)
    normed = (tokens_f * token_scale * attn_gain_f).astype(BF)
    qkv = plain(normed, qkv_weight)
    cosine, sine = rope_tables(rows)
    mixed = attend(qkv, both_lengths, head_gains, cosine, sine, rows, heads)
    partial = plain(mixed, out_weight)
    rows_f = token_rows.astype(F32)
    hidden = rows_f + (partial[:own] + swap(partial[own:]))
    hidden_scale = lax.rsqrt(jnp.mean(hidden * hidden, axis=-1, keepdims=True) + EPSILON)
    hidden_unit = hidden * hidden_scale
    routed_in = (hidden_unit * ffn_gain_f).astype(BF)
    gate_probs = jax.nn.softmax(plain(routed_in, router), axis=-1)

    row_blocks = gather_blocks(
        jnp.concatenate([routed_in, widen(in_three(gate_probs), EXTRA)], axis=1), ZX
    )
    keys = list(row_blocks)
    group = len(keys) * batches
    all_rows = jnp.concatenate([row_blocks[k] for k in keys], axis=0)
    all_cots = jnp.concatenate([cot_blocks[k] for k in keys], axis=0)
    first_expert = (z * xs + x) * local
    all_probs = from_three(all_rows[:, D:], experts)
    all_probs = lax.dynamic_slice_in_dim(all_probs, first_expert, local, 1)
    all_ranks = lax.dynamic_slice_in_dim(all_cots[:, D:], first_expert, local, 1).astype(F32)
    all_rows = all_rows[:, :D].reshape(group, rows, D)
    all_cots = all_cots[:, :D].reshape(group, rows, D)
    slot = jnp.arange(capacity, dtype=F32)[None, :, None]
    combined = 0.0
    routed_grad = 0.0
    probs_grad = []
    gate_grads, up_grads, down_grads = [], [], []
    dispatch = (((2,), (1,)), ((0,), (0,)))
    collect = (((1,), (1,)), ((0,), (0,)))
    for j in range(local):
        rank = all_ranks[:, j].reshape(group, 1, rows)
        probs = all_probs[:, j].reshape(group, 1, rows)
        chosen = rank == slot
        onehot = chosen.astype(BF)
        gated = jnp.where(chosen, probs, 0.0)
        gate_slot = jnp.sum(gated, axis=2, keepdims=True)
        sent = lax.dot_general(onehot, all_rows, dispatch, preferred_element_type=F32)
        sent = sent.astype(BF).reshape(group * capacity, D)
        cot = lax.dot_general(onehot, all_cots, dispatch, preferred_element_type=F32)
        returned_grad = (cot * gate_slot).astype(BF).reshape(group * capacity, D)
        gate_hidden = plain(sent, gate_full[j])
        up_hidden = plain(sent, up_full[j])
        sigmoid = jax.nn.sigmoid(gate_hidden)
        active = (gate_hidden * sigmoid * up_hidden).astype(BF)
        returned = plain(active, down_full[j]).astype(BF).reshape(group, capacity, D)
        combined = combined + lax.dot_general(
            gated.astype(BF), returned, collect, preferred_element_type=F32
        )
        gates_grad = jnp.sum(cot * returned.astype(F32), axis=2, keepdims=True)
        probs_grad.append(jnp.sum(jnp.where(chosen, gates_grad, 0.0), axis=1).reshape(-1, 1))
        active_grad = times_t(returned_grad, down_full[j])
        gate_hidden_grad = (
            active_grad * up_hidden * sigmoid * (1.0 + gate_hidden * (1.0 - sigmoid))
        ).astype(BF)
        up_hidden_grad = (active_grad * gate_hidden * sigmoid).astype(BF)
        sent_grad = times_t(gate_hidden_grad, gate_full[j]) + times_t(up_hidden_grad, up_full[j])
        sent_grad = sent_grad.astype(BF).reshape(group, capacity, D)
        routed_grad = routed_grad + lax.dot_general(
            onehot, sent_grad, collect, preferred_element_type=F32
        )
        down_grads.append(inner(active, returned_grad))
        gate_grads.append(inner(sent, gate_hidden_grad))
        up_grads.append(inner(sent, up_hidden_grad))
    expert_index = jnp.arange(experts)[None, :]
    probs_part = sum(
        jnp.where(expert_index == first_expert + j, probs_grad[j], 0.0) for j in range(local)
    )
    back = jnp.concatenate(
        [
            routed_grad.reshape(group * rows, D).astype(BF),
            widen(in_three(probs_part), EXTRA),
        ],
        axis=1,
    )
    combined = combined.reshape(group * rows, D).astype(BF)

    def part_of(array):
        return lambda key: array[keys.index(key) * own : (keys.index(key) + 1) * own]

    back = reduce_blocks(part_of(back), ZX)
    combined = reduce_blocks(part_of(combined), ZX)
    layer_out = (hidden + combined).astype(BF)

    probs_grad = from_three(back[:, D:], experts)
    logits_grad = (
        gate_probs * (probs_grad - jnp.sum(gate_probs * probs_grad, axis=-1, keepdims=True))
    ).astype(BF)
    router_grad = inner(routed_in, logits_grad)
    routed_grad = back[:, :D] + times_t(logits_grad, router)
    hidden_add, ffn_gain_grad = norm_back(routed_grad, hidden_unit, hidden_scale, ffn_gain_f)
    hidden_grad = cotangent.astype(F32) + hidden_add
    attn_out_grad = hidden_grad.astype(BF)

    both_grads = jnp.concatenate([attn_out_grad, swap(attn_out_grad)], axis=0)
    mixed_grad = times_t(both_grads, out_weight).astype(BF)
    output_grad = inner(mixed, both_grads).astype(BF)
    qkv_grad, head_gain_grads = attend_back(
        qkv, mixed_grad, both_lengths, head_gains, cosine, sine, rows, heads
    )
    qkv_weight_grad = inner(normed, qkv_grad)
    normed_part = times_t(qkv_grad, qkv_weight)
    normed_grad = normed_part[:own] + swap(normed_part[own:])
    token_unit = rows_f * token_scale[:own]
    tokens_add, attn_gain_grad = norm_back(normed_grad, token_unit, token_scale[:own], attn_gain_f)
    tokens_grad = hidden_grad + tokens_add

    small_grad = jnp.concatenate(
        [
            attn_gain_grad[:, None],
            ffn_gain_grad[:, None],
            router_grad,
            jnp.pad(
                head_gain_grads.reshape(2, -1, head_shard),
                ((0, 0), (0, 0), (0, shard_rows - head_shard)),
            )
            .reshape(2, D)
            .T,
        ],
        axis=1,
    )
    qkv_weight_grad = jnp.concatenate(
        [qkv_weight_grad.astype(BF), widen(small_grad, EXTRA).astype(BF)], axis=1
    )

    def rows_of(array, order, core):
        return lambda key: lax.dynamic_slice_in_dim(
            array, row_block(key, order, core) * shard_rows, shard_rows, 0
        )

    output_weight_grad = reduce_blocks(rows_of(output_grad, ZYX, None), ZYX)
    first = reduce_blocks(rows_of(qkv_weight_grad, ZXY, 0), ZXY)
    second = reduce_blocks(rows_of(qkv_weight_grad, ZYX, 1), ZYX)
    mine = jnp.where(c == 0, first, second)
    theirs = swap(jnp.where(c == 0, second, first).astype(BF)).astype(F32)
    small_total = mine[:, 3 * width :] + theirs[:, 3 * width :]

    def both_halves(at):
        low = jnp.where(c == 0, mine, theirs)[:, at * width : (at + 1) * width]
        high = jnp.where(c == 0, theirs, mine)[:, at * width : (at + 1) * width]
        return jnp.stack(
            [low.reshape(shard_rows, ys, chunk), high.reshape(shard_rows, ys, chunk)], axis=2
        ).reshape(shard_rows, D)

    def expert_total(parts):
        grad = jnp.stack(parts).astype(BF)
        depth = grad.shape[1] // (2 * ys)

        def part(key):
            at = jnp.mod(y - key[0], ys) * 2 + jnp.mod(c - key[1], 2)
            return lax.dynamic_slice_in_dim(grad, at * depth, depth, 1)

        return reduce_blocks(part, ("y", "c")).astype(F32)

    shape = (batches, 1, rows, D)
    return (
        layer_out.reshape(shape),
        tokens_grad.reshape(shape),
        small_total[:, 0],
        both_halves(0),
        both_halves(1),
        both_halves(2),
        output_weight_grad,
        small_total[:head_shard, 2 + experts],
        small_total[:head_shard, 3 + experts],
        small_total[:, 1],
        small_total[:, 2 : 2 + experts],
        expert_total(gate_grads),
        expert_total(up_grads),
        expert_total(down_grads),
    )


def solution(mesh):
    dp, expert = mesh.shape["dp"], mesh.shape["expert"]
    zs = math.gcd(expert, 4)
    grid = Mesh(
        mesh.devices.reshape(dp // 2, 2, zs, expert // zs),
        ("y", "c", "z", "x"),
    )
    every, dps, exps = ("y", "c", "z", "x"), ("y", "c"), ("z", "x")
    in_specs = (
        P(None, every, None, None),
        P(None, every, None, None),
        P(None, every),
        P(None, every, None, None),
        P(None, every, None),
        P(every),
        P(every, None),
        P(every, None),
        P(every, None),
        P(every, None),
        P(every),
        P(every),
        P(every),
        P(every, None),
        P(exps, dps, None),
        P(exps, dps, None),
        P(exps, dps, None),
    )
    out_specs = (
        P(None, every, None, None),
        P(None, every, None, None),
        P(every),
        P(every, None),
        P(every, None),
        P(every, None),
        P(every, None),
        P(every),
        P(every),
        P(every),
        P(every, None),
        P(exps, dps, None),
        P(exps, dps, None),
        P(exps, dps, None),
    )
    return jax.shard_map(shards, mesh=grid, in_specs=in_specs, out_specs=out_specs, check_vma=False)
```

time: 3210 us -> 2600 us (0.81)
  waiting for transfers between devices: 2070 us -> 545 us
  Pallas kernels: 0 us -> 1330 us
  blocking collectives: 488 us -> 0 us
  starting transfers between devices: 32.1 us -> 179 us
  matrix products: 357 us -> 284 us
    pallas_call x0 -> x7, Pallas kernels: none -> 1330 us  [the longest x5 1300 us: place(): pl.pallas_call(functools.partial(place_kernel, len(blocks), row_axis, row...]
    reduce_scatter x7 -> x0, waiting for transfers between devices: 1310 us -> none  [the longest x1 360 us: shards(): lax.psum_scatter(dense_total[2], ('dp', 'expert'), scatter_dimension=0, t...]
    ppermute x0 -> x143, waiting for transfers between devices: none -> 545 us  [the longest x136 544 us: shift(): lax.ppermute(value, axis, [(i, (i + step) % size) for i in range(size)])]
    all_to_all x6 -> x0, waiting for transfers between devices: 487 us -> none  [the longest x2 195 us: backward_pass(): lax.all_to_all(sent_local.astype(jnp.bfloat16).reshape(expert_count, -1,...]
    all_gather x7 -> x0, waiting for transfers between devices: 261 us -> none  [the longest x1 72.9 us: fetch_dense(): lax.all_gather(shard[4], ('dp', 'expert'), axis=0, tiled=True)]
    all_to_all x2 -> x0, blocking collectives: 236 us -> none  [the longest x1 120 us: forward_pass(): lax.all_to_all(sent_rows.reshape(expert_count, -1, D), 'expert', split_ax...]
    ppermute x0 -> x143, starting transfers between devices: none -> 179 us  [the longest x136 178 us: shift(): lax.ppermute(value, axis, [(i, (i + step) % size) for i in range(size)])]
    all_gather x1 -> x0, blocking collectives: 164 us -> none  [fetch_dense(): lax.all_gather(shard[8], ('dp', 'expert'), axis=0, tiled=True)]
  transfers between devices with their start and end apart: 21 -> 143, of which waited for: 15 -> 65; matrix products, arithmetic and copies ran while one was open for 13% -> 12% of each run, Pallas kernels for 0% -> 51%
where the time goes in v1:
time: 2600 us; the launch traced here: 2590 us
  Pallas kernels  1330 us (51%)
  waiting for transfers between devices  545 us (21%)
  matrix products  284 us (11%)
  starting transfers between devices  179 us (7%)
  local copies, waits for them, and re-layouts  146 us (6%)
  other arithmetic  107 us (4%)
    pallas_call x5, Pallas kernels, place(): pl.pallas_call(functools.partial(place_kernel, len(blocks), row_axis, row...  1300 us
    ppermute x136, waiting for transfers between devices, shift(): lax.ppermute(value, axis, [(i, (i + step) % size) for i in range(size)])  544 us
    ppermute x136, starting transfers between devices, shift(): lax.ppermute(value, axis, [(i, (i + step) % size) for i in range(size)])  178 us
    dot_general x9, matrix products, times_t(): lax.dot_general(left, right, (((1,), (1,)), ((), ())), preferred_element_...  87 us
    dot_general x9, matrix products, plain(): return jnp.dot(left, right, preferred_element_type=F32)  72.7 us
    dot_general x9, matrix products, inner(): lax.dot_general(left, right, (((0,), (0,)), ((), ())), preferred_element_...  61.8 us
  transfers between devices with their start and end apart: 143, of which 65 were waited for; matrix products, arithmetic and copies ran while one was open for 12% of the time, Pallas kernels for 51%

profile of v1, /device:TPU:0, one launch (start us, length us, event | category | flops | bytes accessed | tf_op | source)
XLA Modules:
  0.0 2593.7 jit_solution(1703434831109647031)
XLA Ops:
  26.3 8.0 collective-permute-done.35.refs_3_
  90.7 8.0 collective-permute-done.20.refs_19_
  122.4 16.6 collective-permute-done.24.refs_23_
  153.7 7.3 collective-permute-done.16.refs_14_
  164.4 129.0 %shard_map.274 = bf16[1024,2048]{1,0:T(8,128)(2,1)} custom-call(s32[16]{0:T(128)} %stack.283.offsets_ref, bf16[64,2048]{1,0:T(8,128)(2,1)} %refs_0_.4, bf16[64,2048]{1,0:T(8,128)(2,1)} %copy-done.86, bf16[64,2048]{1,0:T(8,128)(2,1)} %copy-done.85, bf16[64,2048]{1,0:T(8,128)(2,1)} %copy-done.87, bf16[64,2048]{1,0:T(8,128)(2,1)} %collective-permute-done.36.refs_4_, ...), custom_call_target="tpu_custom_call" | custom-call | tf_op jit(solution)/shard_map/pallas_call | solution.py:88
  293.5 399.3 %shard_map.272 = bf16[2048,3200]{1,0:T(8,128)(2,1)} custom-call(s32[32]{0:T(128)} %stack.265.offsets_ref, bf16[64,3200]{1,0:T(8,128)(2,1)} %copy-done.60, bf16[64,3200]{1,0:T(8,128)(2,1)} %collective-permute-done.3.refs_1_, bf16[64,3200]{1,0:T(8,128)(2,1)} %collective-permute-done.4.refs_2_, bf16[64,3200]{1,0:T(8,128)(2,1)} %collective-permute-done.5.refs_3_, ...), custom_call_target="tpu_custom_call" | custom-call | tf_op jit(solution)/shard_map/pallas_call | solution.py:88
  695.4 10.1 fusion.4.qkv_ref
  705.5 13.7 shard_map.273
  729.2 23.0 collective-permute-done.49
  764.9 12.7 collective-permute-done.64.refs_2_
  778.2 7.8 collective-permute-done.52
  786.3 36.1 %collective-permute-done.67.refs_2_ = bf16[2,512,1024]{2,1,0:T(8,128)(2,1)S(1)} collective-permute-done((bf16[2,512,1024]{2,1,0:T(8,128)(2,1)}, bf16[2,512,1024]{2,1,0:T(8,128)(2,1)S(1)}, u32[]{:S(2)}, u32[]{:S(2)}) %collective-permute-start.67) | collective-permute-done | bytes 2097184 | tf_op jit(solution)/shard_map/ppermute | solution.py:39
  822.5 43.6 %collective-permute-done.70.refs_2_ = bf16[2,256,2048]{2,1,0:T(8,128)(2,1)} collective-permute-done((bf16[2,256,2048]{2,1,0:T(8,128)(2,1)}, bf16[2,256,2048]{2,1,0:T(8,128)(2,1)}, u32[]{:S(2)}, u32[]{:S(2)}) %collective-permute-start.70) | collective-permute-done | bytes 2097184 | tf_op jit(solution)/shard_map/ppermute | solution.py:39
  870.5 20.7 collective-permute-done.53
  898.4 19.2 collective-permute-done.57
  920.0 255.9 %shard_map.275 = bf16[2,2048,1024]{2,1,0:T(8,128)(2,1)} custom-call(s32[4]{0:T(128)} %pad_add_fusion.1.offsets_ref, bf16[2,512,1024]{2,1,0:T(8,128)(2,1)} %refs_0_.5, bf16[2,512,1024]{2,1,0:T(8,128)(2,1)} %collective-permute-done.63.refs_1_, bf16[2,512,1024]{2,1,0:T(8,128)(2,1)} %collective-permute-done.64.refs_2_, bf16[2,512,1024]{2,1,0:T(8,128)(2,1)} %copy-done.51), custom_call_target="tpu_custom_call" | custom-call | tf_op jit(solution)/shard_map/pallas_call | solution.py:88
  1175.9 255.9 %shard_map.276 = bf16[2,2048,1024]{2,1,0:T(8,128)(2,1)} custom-call(s32[4]{0:T(128)} %pad_add_fusion.1.offsets_ref, bf16[2,512,1024]{2,1,0:T(8,128)(2,1)} %refs_0_.6, bf16[2,512,1024]{2,1,0:T(8,128)(2,1)} %collective-permute-done.66.refs_1_, bf16[2,512,1024]{2,1,0:T(8,128)(2,1)} %copy-done.50, bf16[2,512,1024]{2,1,0:T(8,128)(2,1)} %copy-done.52), custom_call_target="tpu_custom_call" | custom-call | tf_op jit(solution)/shard_map/pallas_call | solution.py:88
  1431.8 255.9 %shard_map.277 = bf16[2,1024,2048]{2,1,0:T(8,128)(2,1)} custom-call(s32[4]{0:T(128)} %pad_add_fusion.2.offsets_ref, bf16[2,256,2048]{2,1,0:T(8,128)(2,1)} %refs_0_.7, bf16[2,256,2048]{2,1,0:T(8,128)(2,1)} %collective-permute-done.69.refs_1_, bf16[2,256,2048]{2,1,0:T(8,128)(2,1)} %collective-permute-done.70.refs_2_, ...), custom_call_target="tpu_custom_call" | custom-call | tf_op jit(solution)/shard_map/pallas_call | solution.py:88
  1690.0 8.4 slice.333
  1698.4 12.3 copy.160
  1718.1 20.4 collective-permute-done.58
  1742.5 19.9 collective-permute-done.60
  1764.6 17.4 collective-permute-done.62
  1784.1 8.2 slice.316
  1792.3 12.3 copy.159
  1810.4 10.4 fusion.9
  1823.0 8.2 multiply_convert_fusion.7
  1831.3 9.1 convolution_convert_fusion.2
  1840.5 6.8 multiply_reduce_fusion.1
  1848.1 6.9 multiply_convert_fusion.1
  1855.0 14.1 multiply_convert_fusion.5
  1869.1 9.8 convert_bitcast_fusion.3
  1879.0 10.7 fusion.10
  1891.2 10.2 fusion.13
  1901.4 11.4 multiply_convert_fusion.6
  1912.8 9.3 convolution_convert_fusion.1
  1922.2 6.8 multiply_reduce_fusion
  1929.5 7.1 multiply_convert_fusion
  1936.6 14.2 multiply_convert_fusion.3
  1956.9 12.2 fusion.14
  1969.2 8.1 fusion.55
  1977.3 7.9 convert_bitcast_fusion.4
  1999.2 10.3 add_convert_fusion.3
  2009.5 9.9 add_convert_fusion.2
  2019.4 13.0 add_convert_fusion.1
  2047.0 8.1 fusion.48
  2055.1 13.0 add_convert_fusion
  2068.1 12.3 copy.157
  2086.4 10.0 convert_bitcast_fusion.1
  2096.4 37.4 %collective-permute-done.82 = bf16[256,2176]{0,1:T(8,128)(2,1)S(1)} collective-permute-done((bf16[256,2176]{0,1:T(8,128)(2,1)S(1)}, bf16[256,2176]{0,1:T(8,128)(2,1)S(1)}, u32[]{:S(2)}, u32[]{:S(2)}) %collective-permute-start.82) | collective-permute-done | bytes 1114144 | tf_op jit(solution)/shard_map/ppermute | solution.py:39
  2137.8 7.5 convert_bitcast_fusion
  2146.9 13.1 collective-permute-done.83
  2194.4 12.9 collective-permute-done.74
  2224.1 7.8 collective-permute-done.79
  2252.4 7.5 collective-permute-done.77
  2267.9 20.7 shard_map.278
  2288.6 9.7 fusion.2
  2300.6 8.0 collective-permute-done.142
  2314.6 11.6 convolution_convert_fusion
  2339.2 14.3 collective-permute-done.139
  2361.3 34.2 %collective-permute-done.136 = bf16[2,512,1024]{2,1,0:T(8,128)(2,1)} collective-permute-done((bf16[2,512,1024]{2,1,0:T(8,128)(2,1)}, bf16[2,512,1024]{2,1,0:T(8,128)(2,1)}, u32[]{:S(2)}, u32[]{:S(2)}) %collective-permute-start.136) | collective-permute-done | bytes 2097184 | tf_op jit(solution)/shard_map/ppermute | solution.py:39
  2407.9 8.8 collective-permute-done.95
  2416.7 7.2 collective-permute-done.92
  2443.9 11.2 collective-permute-done.126
  (748 shorter events, 517.2 us)
Async XLA Ops:
  24.2 29.8 %collective-permute-start.21 = (bf16[64,3200]{1,0:T(8,128)(2,1)S(1)}, bf16[64,3200]{1,0:T(8,128)(2,1)S(1)}, u32[]{:S(2)}, u32[]{:S(2)}) collective-permute-start(bf16[64,3200]{1,0:T(8,128)(2,1)S(1)} %get-tuple-element.185.refs_16_), channel_id=1, source_target_pairs={{0,2},{2,4},{4,6},{6,0},{1,3},{3,5},{5,7},{7,1},{8,10},{10,12},{12... | collective-permute-start | bytes 1228808 | tf_op jit(solution)/shard_map/ppermute | solution.py:39
  37.3 45.4 %collective-permute-start.1 = (bf16[256,2048]{0,1:T(8,128)(2,1)S(1)}, bf16[256,2048]{0,1:T(8,128)(2,1)S(1)}, u32[]{:S(2)}, u32[]{:S(2)}) collective-permute-start(bf16[256,2048]{0,1:T(8,128)(2,1)S(1)} %copy.146), channel_id=1, source_target_pairs={{0,8},{8,0},{1,9},{9,1},{2,10},{10,2},{3,11},{11,3},{4,12},{12,4},... | collective-permute-start | bytes 3145736 | tf_op jit(solution)/shard_map/ppermute | solution.py:311
  109.6 29.9 %collective-permute-start.14 = (bf16[64,3200]{1,0:T(8,128)(2,1)}, bf16[64,3200]{1,0:T(8,128)(2,1)}, u32[]{:S(2)}, u32[]{:S(2)}) collective-permute-start(bf16[64,3200]{1,0:T(8,128)(2,1)} %collective-permute-done.10.refs_8_), channel_id=1, source_target_pairs={{0,2},{2,4},{4,6},{6,0},{1,3},{3,5},{5,7},{7,1},{8,10},{10,12},{12... | collective-permute-start | bytes 1228808 | tf_op jit(solution)/shard_map/ppermute | solution.py:39
  113.2 27.8 %collective-permute-start.12 = (bf16[64,3200]{1,0:T(8,128)(2,1)}, bf16[64,3200]{1,0:T(8,128)(2,1)}, u32[]{:S(2)}, u32[]{:S(2)}) collective-permute-start(bf16[64,3200]{1,0:T(8,128)(2,1)} %collective-permute-done.10.refs_8_), channel_id=1, source_target_pairs={{0,1},{1,0},{2,3},{3,2},{4,5},{5,4},{6,7},{7,6},{8,9},{9,8},{10,11... | collective-permute-start | bytes 1228808 | tf_op jit(solution)/shard_map/ppermute | solution.py:39
  114.7 24.3 collective-permute-start.24
  141.9 151.6 %collective-permute-start.15 = (bf16[64,3200]{1,0:T(8,128)(2,1)}, bf16[64,3200]{1,0:T(8,128)(2,1)}, u32[]{:S(2)}, u32[]{:S(2)}) collective-permute-start(bf16[64,3200]{1,0:T(8,128)(2,1)} %collective-permute-done.14.refs_12_), channel_id=1, source_target_pairs={{0,16},{16,0},{1,17},{17,1},{2,18},{18,2},{3,19},{19,3},{4,20},{20... | collective-permute-start | bytes 1228808 | tf_op jit(solution)/shard_map/ppermute | solution.py:39
  143.5 149.9 %collective-permute-start.28 = (bf16[64,3200]{1,0:T(8,128)(2,1)}, bf16[64,3200]{1,0:T(8,128)(2,1)}, u32[]{:S(2)}, u32[]{:S(2)}) collective-permute-start(bf16[64,3200]{1,0:T(8,128)(2,1)} %collective-permute-done.27.refs_26_), channel_id=1, source_target_pairs={{0,1},{1,0},{2,3},{3,2},{4,5},{5,4},{6,7},{7,6},{8,9},{9,8},{10,11... | collective-permute-start | bytes 1228808 | tf_op jit(solution)/shard_map/ppermute | solution.py:39
  151.7 141.8 %collective-permute-start.13 = (bf16[64,3200]{1,0:T(8,128)(2,1)}, bf16[64,3200]{1,0:T(8,128)(2,1)}, u32[]{:S(2)}, u32[]{:S(2)}) collective-permute-start(bf16[64,3200]{1,0:T(8,128)(2,1)} %collective-permute-done.12.refs_10_), channel_id=1, source_target_pairs={{0,16},{16,0},{1,17},{17,1},{2,18},{18,2},{3,19},{19,3},{4,20},{20... | collective-permute-start | bytes 1228808 | tf_op jit(solution)/shard_map/ppermute | solution.py:39
  152.2 141.3 %collective-permute-start.32 = (bf16[64,3200]{1,0:T(8,128)(2,1)}, bf16[64,3200]{1,0:T(8,128)(2,1)}, u32[]{:S(2)}, u32[]{:S(2)}) collective-permute-start(bf16[64,3200]{1,0:T(8,128)(2,1)} %collective-permute-done.31.refs_30_), channel_id=1, source_target_pairs={{0,1},{1,0},{2,3},{3,2},{4,5},{5,4},{6,7},{7,6},{8,9},{9,8},{10,11... | collective-permute-start | bytes 1228808 | tf_op jit(solution)/shard_map/ppermute | solution.py:39
  161.0 132.5 %collective-permute-start.17 = (bf16[64,3200]{1,0:T(8,128)(2,1)}, bf16[64,3200]{1,0:T(8,128)(2,1)}, u32[]{:S(2)}, u32[]{:S(2)}) collective-permute-start(bf16[64,3200]{1,0:T(8,128)(2,1)} %collective-permute-done.16.refs_14_), channel_id=1, source_target_pairs={{0,16},{16,0},{1,17},{17,1},{2,18},{18,2},{3,19},{19,3},{4,20},{20... | collective-permute-start | bytes 1228808 | tf_op jit(solution)/shard_map/ppermute | solution.py:39
  293.4 462.6 %collective-permute-start.63 = (bf16[2,512,1024]{2,1,0:T(8,128)(2,1)}, bf16[2,512,1024]{2,1,0:T(8,128)(2,1)}, u32[]{:S(2)}, u32[]{:S(2)}) collective-permute-start(bf16[2,512,1024]{2,1,0:T(8,128)(2,1)} %refs_0_.5), channel_id=1, source_target_pairs={{0,8},{8,0},{1,9},{9,1},{2,10},{10,2},{3,11},{11,3},{4,12},{12,4},... | collective-permute-start | bytes 6291464 | tf_op jit(solution)/shard_map/ppermute | solution.py:39
  723.4 35.8 %collective-permute-start.48 = (f32[256,2048]{0,1:T(8,128)}, f32[256,2048]{0,1:T(8,128)}, u32[]{:S(2)}, u32[]{:S(2)}) collective-permute-start(f32[256,2048]{0,1:T(8,128)} %slice.307), channel_id=1, source_target_pairs={{0,8},{8,0},{1,9},{9,1},{2,10},{10,2},{3,11},{11,3},{4,12},{12,4},... | collective-permute-start | bytes 6291464 | tf_op jit(solution)/shard_map/ppermute | solution.py:311
  725.3 27.0 %collective-permute-start.49 = (bf16[256,2176]{0,1:T(8,128)(2,1)}, bf16[256,2176]{0,1:T(8,128)(2,1)}, u32[]{:S(2)}, u32[]{:S(2)}) collective-permute-start(bf16[256,2176]{0,1:T(8,128)(2,1)} %get-tuple-element.175), channel_id=1, source_target_pairs={{0,1},{1,0},{2,3},{3,2},{4,5},{5,4},{6,7},{7,6},{8,9},{9,8},{10,11... | collective-permute-start | bytes 3342344 | tf_op jit(solution)/shard_map/ppermute | solution.py:39
  726.8 28.7 %collective-permute-start.50 = (bf16[256,2176]{0,1:T(8,128)(2,1)}, bf16[256,2176]{0,1:T(8,128)(2,1)S(1)}, u32[]{:S(2)}, u32[]{:S(2)}) collective-permute-start(bf16[256,2176]{0,1:T(8,128)(2,1)} %get-tuple-element.175), channel_id=1, source_target_pairs={{0,2},{2,4},{4,6},{6,0},{1,3},{3,5},{5,7},{7,1},{8,10},{10,12},{12... | collective-permute-start | bytes 3342344 | tf_op jit(solution)/shard_map/ppermute | solution.py:39
  728.7 48.9 %collective-permute-start.64 = (bf16[2,512,1024]{2,1,0:T(8,128)(2,1)}, bf16[2,512,1024]{2,1,0:T(8,128)(2,1)}, u32[]{:S(2)}, u32[]{:S(2)}) collective-permute-start(bf16[2,512,1024]{2,1,0:T(8,128)(2,1)} %refs_0_.5), channel_id=1, source_target_pairs={{0,16},{16,0},{1,17},{17,1},{2,18},{18,2},{3,19},{19,3},{4,20},{20... | collective-permute-start | bytes 6291464 | tf_op jit(solution)/shard_map/ppermute | solution.py:39
  752.2 25.9 collective-permute-start.66
  755.5 66.9 %collective-permute-start.67 = (bf16[2,512,1024]{2,1,0:T(8,128)(2,1)}, bf16[2,512,1024]{2,1,0:T(8,128)(2,1)S(1)}, u32[]{:S(2)}, u32[]{:S(2)}) collective-permute-start(bf16[2,512,1024]{2,1,0:T(8,128)(2,1)} %refs_0_.6), channel_id=1, source_target_pairs={{0,16},{16,0},{1,17},{17,1},{2,18},{18,2},{3,19},{19,3},{4,20},{20... | collective-permute-start | bytes 6291464 | tf_op jit(solution)/shard_map/ppermute | solution.py:39
  756.0 110.0 %collective-permute-start.70 = (bf16[2,256,2048]{2,1,0:T(8,128)(2,1)}, bf16[2,256,2048]{2,1,0:T(8,128)(2,1)}, u32[]{:S(2)}, u32[]{:S(2)}) collective-permute-start(bf16[2,256,2048]{2,1,0:T(8,128)(2,1)} %refs_0_.7), channel_id=1, source_target_pairs={{0,16},{16,0},{1,17},{17,1},{2,18},{18,2},{3,19},{19,3},{4,20},{20... | collective-permute-start | bytes 6291464 | tf_op jit(solution)/shard_map/ppermute | solution.py:39
  759.2 26.7 %collective-permute-start.52 = (bf16[256,2176]{0,1:T(8,128)(2,1)S(1)}, bf16[256,2176]{0,1:T(8,128)(2,1)S(1)}, u32[]{:S(2)}, u32[]{:S(2)}) collective-permute-start(bf16[256,2176]{0,1:T(8,128)(2,1)S(1)} %collective-permute-done.50), channel_id=1, source_target_pairs={{0,2},{2,4},{4,6},{6,0},{1,3},{3,5},{5,7},{7,1},{8,10},{10,12},{12... | collective-permute-start | bytes 3342344 | tf_op jit(solution)/shard_map/ppermute | solution.py:39
  777.6 90.7 %collective-permute-start.51 = (bf16[256,2176]{0,1:T(8,128)(2,1)S(1)}, bf16[256,2176]{0,1:T(8,128)(2,1)S(1)}, u32[]{:S(2)}, u32[]{:S(2)}) collective-permute-start(bf16[256,2176]{0,1:T(8,128)(2,1)S(1)} %collective-permute-done.50), channel_id=1, source_target_pairs={{0,1},{1,0},{2,3},{3,2},{4,5},{5,4},{6,7},{7,6},{8,9},{9,8},{10,11... | collective-permute-start | bytes 3342344 | tf_op jit(solution)/shard_map/ppermute | solution.py:39
  778.1 115.8 %collective-permute-start.65 = (bf16[2,512,1024]{2,1,0:T(8,128)(2,1)}, bf16[2,512,1024]{2,1,0:T(8,128)(2,1)S(1)}, u32[]{:S(2)}, u32[]{:S(2)}) collective-permute-start(bf16[2,512,1024]{2,1,0:T(8,128)(2,1)} %collective-permute-done.64.refs_2_), channel_id=1, source_target_pairs={{0,8},{8,0},{1,9},{9,1},{2,10},{10,2},{3,11},{11,3},{4,12},{12,4},... | collective-permute-start | bytes 6291464 | tf_op jit(solution)/shard_map/ppermute | solution.py:39
  785.9 82.5 %collective-permute-start.54 = (bf16[256,2176]{0,1:T(8,128)(2,1)S(1)}, bf16[256,2176]{0,1:T(8,128)(2,1)}, u32[]{:S(2)}, u32[]{:S(2)}) collective-permute-start(bf16[256,2176]{0,1:T(8,128)(2,1)S(1)} %collective-permute-done.52), channel_id=1, source_target_pairs={{0,2},{2,4},{4,6},{6,0},{1,3},{3,5},{5,7},{7,1},{8,10},{10,12},{12... | collective-permute-start | bytes 3342344 | tf_op jit(solution)/shard_map/ppermute | solution.py:39
  822.4 74.4 %collective-permute-start.68 = (bf16[2,512,1024]{2,1,0:T(8,128)(2,1)S(1)}, bf16[2,512,1024]{2,1,0:T(8,128)(2,1)S(1)}, u32[]{:S(2)}, u32[]{:S(2)}) collective-permute-start(bf16[2,512,1024]{2,1,0:T(8,128)(2,1)S(1)} %collective-permute-done.67.refs_2_), channel_id=1, source_target_pairs={{0,8},{8,0},{1,9},{9,1},{2,10},{10,2},{3,11},{11,3},{4,12},{12,4},... | collective-permute-start | bytes 6291464 | tf_op jit(solution)/shard_map/ppermute | solution.py:39
  866.1 25.2 collective-permute-start.53
  868.3 563.5 %collective-permute-start.69 = (bf16[2,256,2048]{2,1,0:T(8,128)(2,1)S(1)}, bf16[2,256,2048]{2,1,0:T(8,128)(2,1)}, u32[]{:S(2)}, u32[]{:S(2)}) collective-permute-start(bf16[2,256,2048]{2,1,0:T(8,128)(2,1)S(1)} %copy-done.49), channel_id=1, source_target_pairs={{0,8},{8,0},{1,9},{9,1},{2,10},{10,2},{3,11},{11,3},{4,12},{12,4},... | collective-permute-start | bytes 6291464 | tf_op jit(solution)/shard_map/ppermute | solution.py:39
  868.4 563.4 %collective-permute-start.71 = (bf16[2,256,2048]{2,1,0:T(8,128)(2,1)}, bf16[2,256,2048]{2,1,0:T(8,128)(2,1)}, u32[]{:S(2)}, u32[]{:S(2)}) collective-permute-start(bf16[2,256,2048]{2,1,0:T(8,128)(2,1)} %collective-permute-done.70.refs_2_), channel_id=1, source_target_pairs={{0,8},{8,0},{1,9},{9,1},{2,10},{10,2},{3,11},{11,3},{4,12},{12,4},... | collective-permute-start | bytes 6291464 | tf_op jit(solution)/shard_map/ppermute | solution.py:39
  891.3 26.4 %collective-permute-start.57 = (bf16[256,2176]{0,1:T(8,128)(2,1)}, bf16[256,2176]{0,1:T(8,128)(2,1)}, u32[]{:S(2)}, u32[]{:S(2)}) collective-permute-start(bf16[256,2176]{0,1:T(8,128)(2,1)} %get-tuple-element.177), channel_id=1, source_target_pairs={{0,2},{2,4},{4,6},{6,0},{1,3},{3,5},{5,7},{7,1},{8,10},{10,12},{12... | collective-permute-start | bytes 3342344 | tf_op jit(solution)/shard_map/ppermute | solution.py:39
  893.9 793.8 %collective-permute-start.55 = (bf16[256,2176]{0,1:T(8,128)(2,1)}, bf16[256,2176]{0,1:T(8,128)(2,1)S(1)}, u32[]{:S(2)}, u32[]{:S(2)}) collective-permute-start(bf16[256,2176]{0,1:T(8,128)(2,1)} %collective-permute-done.54), channel_id=1, source_target_pairs={{0,1},{1,0},{2,3},{3,2},{4,5},{5,4},{6,7},{7,6},{8,9},{9,8},{10,11... | collective-permute-start | bytes 3342344 | tf_op jit(solution)/shard_map/ppermute | solution.py:39
  896.9 815.0 %collective-permute-start.56 = (bf16[256,2176]{0,1:T(8,128)(2,1)}, bf16[256,2176]{0,1:T(8,128)(2,1)}, u32[]{:S(2)}, u32[]{:S(2)}) collective-permute-start(bf16[256,2176]{0,1:T(8,128)(2,1)} %get-tuple-element.177), channel_id=1, source_target_pairs={{0,1},{1,0},{2,3},{3,2},{4,5},{5,4},{6,7},{7,6},{8,9},{9,8},{10,11... | collective-permute-start | bytes 3342344 | tf_op jit(solution)/shard_map/ppermute | solution.py:39
  917.6 793.7 %collective-permute-start.59 = (bf16[256,2176]{0,1:T(8,128)(2,1)}, bf16[256,2176]{0,1:T(8,128)(2,1)}, u32[]{:S(2)}, u32[]{:S(2)}) collective-permute-start(bf16[256,2176]{0,1:T(8,128)(2,1)} %collective-permute-done.57), channel_id=1, source_target_pairs={{0,2},{2,4},{4,6},{6,0},{1,3},{3,5},{5,7},{7,1},{8,10},{10,12},{12... | collective-permute-start | bytes 3342344 | tf_op jit(solution)/shard_map/ppermute | solution.py:39
  1710.7 27.8 %collective-permute-start.58 = (bf16[256,2176]{0,1:T(8,128)(2,1)}, bf16[256,2176]{0,1:T(8,128)(2,1)S(1)}, u32[]{:S(2)}, u32[]{:S(2)}) collective-permute-start(bf16[256,2176]{0,1:T(8,128)(2,1)} %collective-permute-done.57), channel_id=1, source_target_pairs={{0,1},{1,0},{2,3},{3,2},{4,5},{5,4},{6,7},{7,6},{8,9},{9,8},{10,11... | collective-permute-start | bytes 3342344 | tf_op jit(solution)/shard_map/ppermute | solution.py:39
  1711.3 28.3 %collective-permute-start.61 = (bf16[256,2176]{0,1:T(8,128)(2,1)}, bf16[256,2176]{0,1:T(8,128)(2,1)S(1)}, u32[]{:S(2)}, u32[]{:S(2)}) collective-permute-start(bf16[256,2176]{0,1:T(8,128)(2,1)} %collective-permute-done.59), channel_id=1, source_target_pairs={{0,2},{2,4},{4,6},{6,0},{1,3},{3,5},{5,7},{7,1},{8,10},{10,12},{12... | collective-permute-start | bytes 3342344 | tf_op jit(solution)/shard_map/ppermute | solution.py:39
  1714.2 48.1 %collective-permute-start.60 = (bf16[256,2176]{0,1:T(8,128)(2,1)}, bf16[256,2176]{0,1:T(8,128)(2,1)S(1)}, u32[]{:S(2)}, u32[]{:S(2)}) collective-permute-start(bf16[256,2176]{0,1:T(8,128)(2,1)} %collective-permute-done.59), channel_id=1, source_target_pairs={{0,1},{1,0},{2,3},{3,2},{4,5},{5,4},{6,7},{7,6},{8,9},{9,8},{10,11... | collective-permute-start | bytes 3342344 | tf_op jit(solution)/shard_map/ppermute | solution.py:39
  1739.6 42.5 %collective-permute-start.62 = (bf16[256,2176]{0,1:T(8,128)(2,1)S(1)}, bf16[256,2176]{0,1:T(8,128)(2,1)S(1)}, u32[]{:S(2)}, u32[]{:S(2)}) collective-permute-start(bf16[256,2176]{0,1:T(8,128)(2,1)S(1)} %collective-permute-done.61), channel_id=1, source_target_pairs={{0,1},{1,0},{2,3},{3,2},{4,5},{5,4},{6,7},{7,6},{8,9},{9,8},{10,11... | collective-permute-start | bytes 3342344 | tf_op jit(solution)/shard_map/ppermute | solution.py:39
  1993.9 221.5 %collective-permute-start.138 = (bf16[2,512,1024]{2,1,0:T(8,128)(2,1)}, bf16[2,512,1024]{2,1,0:T(8,128)(2,1)}, u32[]{:S(2)}, u32[]{:S(2)}) collective-permute-start(bf16[2,512,1024]{2,1,0:T(8,128)(2,1)} %get-tuple-element.150), channel_id=1, source_target_pairs={{0,8},{8,0},{1,9},{9,1},{2,10},{10,2},{3,11},{11,3},{4,12},{12,4},... | collective-permute-start | bytes 6291464 | tf_op jit(solution)/shard_map/ppermute | solution.py:39
  1998.1 221.5 %collective-permute-start.135 = (bf16[2,512,1024]{2,1,0:T(8,128)(2,1)}, bf16[2,512,1024]{2,1,0:T(8,128)(2,1)}, u32[]{:S(2)}, u32[]{:S(2)}) collective-permute-start(bf16[2,512,1024]{2,1,0:T(8,128)(2,1)} %get-tuple-element.152), channel_id=1, source_target_pairs={{0,8},{8,0},{1,9},{9,1},{2,10},{10,2},{3,11},{11,3},{4,12},{12,4},... | collective-permute-start | bytes 6291464 | tf_op jit(solution)/shard_map/ppermute | solution.py:39
  2040.2 143.6 %collective-permute-start.75 = (bf16[256,2048]{0,1:T(8,128)(2,1)}, bf16[256,2048]{0,1:T(8,128)(2,1)}, u32[]{:S(2)}, u32[]{:S(2)}) collective-permute-start(bf16[256,2048]{0,1:T(8,128)(2,1)} %copy.155), channel_id=1, source_target_pairs={{0,1},{1,0},{2,3},{3,2},{4,5},{5,4},{6,7},{7,6},{8,9},{9,8},{10,11... | collective-permute-start | bytes 3145736 | tf_op jit(solution)/shard_map/ppermute | solution.py:39
  2084.4 61.0 %collective-permute-start.81 = (bf16[256,2176]{0,1:T(8,128)(2,1)S(1)}, bf16[256,2176]{0,1:T(8,128)(2,1)S(1)}, u32[]{:S(2)}, u32[]{:S(2)}) collective-permute-start(bf16[256,2176]{0,1:T(8,128)(2,1)S(1)} %get-tuple-element.142), channel_id=1, source_target_pairs={{0,1},{1,0},{2,3},{3,2},{4,5},{5,4},{6,7},{7,6},{8,9},{9,8},{10,11... | collective-permute-start | bytes 3342344 | tf_op jit(solution)/shard_map/ppermute | solution.py:39
  2085.9 47.9 %collective-permute-start.82 = (bf16[256,2176]{0,1:T(8,128)(2,1)S(1)}, bf16[256,2176]{0,1:T(8,128)(2,1)S(1)}, u32[]{:S(2)}, u32[]{:S(2)}) collective-permute-start(bf16[256,2176]{0,1:T(8,128)(2,1)S(1)} %get-tuple-element.143), channel_id=1, source_target_pairs={{0,1},{1,0},{2,3},{3,2},{4,5},{5,4},{6,7},{7,6},{8,9},{9,8},{10,11... | collective-permute-start | bytes 3342344 | tf_op jit(solution)/shard_map/ppermute | solution.py:39
  2134.2 25.8 collective-permute-start.83
  2145.4 42.2 %collective-permute-start.80 = (bf16[256,2176]{0,1:T(8,128)(2,1)}, bf16[256,2176]{0,1:T(8,128)(2,1)}, u32[]{:S(2)}, u32[]{:S(2)}) collective-permute-start(bf16[256,2176]{0,1:T(8,128)(2,1)} %get-tuple-element.141), channel_id=1, source_target_pairs={{0,1},{1,0},{2,3},{3,2},{4,5},{5,4},{6,7},{7,6},{8,9},{9,8},{10,11... | collective-permute-start | bytes 3342344 | tf_op jit(solution)/shard_map/ppermute | solution.py:39
  2161.5 30.5 %collective-permute-start.84 = (bf16[256,2176]{0,1:T(8,128)(2,1)}, bf16[256,2176]{0,1:T(8,128)(2,1)}, u32[]{:S(2)}, u32[]{:S(2)}) collective-permute-start(bf16[256,2176]{0,1:T(8,128)(2,1)} %add_convert_fusion.8), channel_id=1, source_target_pairs={{0,6},{2,0},{4,2},{6,4},{1,7},{3,1},{5,3},{7,5},{8,14},{10,8},{12,... | collective-permute-start | bytes 3342344 | tf_op jit(solution)/shard_map/ppermute | solution.py:39
  2192.0 108.1 %collective-permute-start.140 = (bf16[2,256,2048]{2,1,0:T(8,128)(2,1)}, bf16[2,256,2048]{2,1,0:T(8,128)(2,1)}, u32[]{:S(2)}, u32[]{:S(2)}) collective-permute-start(bf16[2,256,2048]{2,1,0:T(8,128)(2,1)} %get-tuple-element.147), channel_id=1, source_target_pairs={{0,8},{8,0},{1,9},{9,1},{2,10},{10,2},{3,11},{11,3},{4,12},{12,4},... | collective-permute-start | bytes 6291464 | tf_op jit(solution)/shard_map/ppermute | solution.py:39
  2207.3 24.5 collective-permute-start.79
  2209.7 26.0 %collective-permute-start.85 = (bf16[256,2176]{0,1:T(8,128)(2,1)S(1)}, bf16[256,2176]{0,1:T(8,128)(2,1)S(1)}, u32[]{:S(2)}, u32[]{:S(2)}) collective-permute-start(bf16[256,2176]{0,1:T(8,128)(2,1)S(1)} %add_convert_fusion.7), channel_id=1, source_target_pairs={{0,6},{2,0},{4,2},{6,4},{1,7},{3,1},{5,3},{7,5},{8,14},{10,8},{12,... | collective-permute-start | bytes 3342344 | tf_op jit(solution)/shard_map/ppermute | solution.py:39
  2215.3 28.3 %collective-permute-start.141 = (bf16[2,256,2048]{2,1,0:T(8,128)(2,1)}, bf16[2,256,2048]{2,1,0:T(8,128)(2,1)}, u32[]{:S(2)}, u32[]{:S(2)}) collective-permute-start(bf16[2,256,2048]{2,1,0:T(8,128)(2,1)} %get-tuple-element.148), channel_id=1, source_target_pairs={{0,8},{8,0},{1,9},{9,1},{2,10},{10,2},{3,11},{11,3},{4,12},{12,4},... | collective-permute-start | bytes 6291464 | tf_op jit(solution)/shard_map/ppermute | solution.py:39
  2219.6 117.6 %collective-permute-start.137 = (bf16[2,512,1024]{2,1,0:T(8,128)(2,1)}, bf16[2,512,1024]{2,1,0:T(8,128)(2,1)}, u32[]{:S(2)}, u32[]{:S(2)}) collective-permute-start(bf16[2,512,1024]{2,1,0:T(8,128)(2,1)} %get-tuple-element.149), channel_id=1, source_target_pairs={{0,8},{8,0},{1,9},{9,1},{2,10},{10,2},{3,11},{11,3},{4,12},{12,4},... | collective-permute-start | bytes 6291464 | tf_op jit(solution)/shard_map/ppermute | solution.py:39
  2252.4 107.0 %collective-permute-start.134 = (bf16[2,512,1024]{2,1,0:T(8,128)(2,1)}, bf16[2,512,1024]{2,1,0:T(8,128)(2,1)}, u32[]{:S(2)}, u32[]{:S(2)}) collective-permute-start(bf16[2,512,1024]{2,1,0:T(8,128)(2,1)} %get-tuple-element.151), channel_id=1, source_target_pairs={{0,8},{8,0},{1,9},{9,1},{2,10},{10,2},{3,11},{11,3},{4,12},{12,4},... | collective-permute-start | bytes 6291464 | tf_op jit(solution)/shard_map/ppermute | solution.py:39
  2259.8 48.7 %collective-permute-start.142 = (bf16[2,256,2048]{2,1,0:T(8,128)(2,1)S(1)}, bf16[2,256,2048]{2,1,0:T(8,128)(2,1)}, u32[]{:S(2)}, u32[]{:S(2)}) collective-permute-start(bf16[2,256,2048]{2,1,0:T(8,128)(2,1)S(1)} %add_convert_fusion.4), channel_id=1, source_target_pairs={{0,16},{16,0},{1,17},{17,1},{2,18},{18,2},{3,19},{19,3},{4,20},{20... | collective-permute-start | bytes 6291464 | tf_op jit(solution)/shard_map/ppermute | solution.py:39
  2262.6 90.8 %collective-permute-start.139 = (bf16[2,512,1024]{2,1,0:T(8,128)(2,1)}, bf16[2,512,1024]{2,1,0:T(8,128)(2,1)}, u32[]{:S(2)}, u32[]{:S(2)}) collective-permute-start(bf16[2,512,1024]{2,1,0:T(8,128)(2,1)} %add_convert_fusion.5), channel_id=1, source_target_pairs={{0,16},{16,0},{1,17},{17,1},{2,18},{18,2},{3,19},{19,3},{4,20},{20... | collective-permute-start | bytes 6291464 | tf_op jit(solution)/shard_map/ppermute | solution.py:39
  2300.0 95.5 %collective-permute-start.136 = (bf16[2,512,1024]{2,1,0:T(8,128)(2,1)}, bf16[2,512,1024]{2,1,0:T(8,128)(2,1)}, u32[]{:S(2)}, u32[]{:S(2)}) collective-permute-start(bf16[2,512,1024]{2,1,0:T(8,128)(2,1)} %add_convert_fusion.6), channel_id=1, source_target_pairs={{0,16},{16,0},{1,17},{17,1},{2,18},{18,2},{3,19},{19,3},{4,20},{20... | collective-permute-start | bytes 6291464 | tf_op jit(solution)/shard_map/ppermute | solution.py:39
  2337.2 58.8 %collective-permute-start.113 = (bf16[64,3200]{1,0:T(8,128)(2,1)}, bf16[64,3200]{1,0:T(8,128)(2,1)S(1)}, u32[]{:S(2)}, u32[]{:S(2)}) collective-permute-start(bf16[64,3200]{1,0:T(8,128)(2,1)} %get-tuple-element.111), channel_id=1, source_target_pairs={{0,1},{1,0},{2,3},{3,2},{4,5},{5,4},{6,7},{7,6},{8,9},{9,8},{10,11... | collective-permute-start | bytes 1228808 | tf_op jit(solution)/shard_map/ppermute | solution.py:39
  2337.2 60.4 %collective-permute-start.110 = (bf16[64,3200]{1,0:T(8,128)(2,1)}, bf16[64,3200]{1,0:T(8,128)(2,1)S(1)}, u32[]{:S(2)}, u32[]{:S(2)}) collective-permute-start(bf16[64,3200]{1,0:T(8,128)(2,1)} %get-tuple-element.113), channel_id=1, source_target_pairs={{0,1},{1,0},{2,3},{3,2},{4,5},{5,4},{6,7},{7,6},{8,9},{9,8},{10,11... | collective-permute-start | bytes 1228808 | tf_op jit(solution)/shard_map/ppermute | solution.py:39
  2353.5 44.6 %collective-permute-start.107 = (bf16[64,3200]{1,0:T(8,128)(2,1)}, bf16[64,3200]{1,0:T(8,128)(2,1)}, u32[]{:S(2)}, u32[]{:S(2)}) collective-permute-start(bf16[64,3200]{1,0:T(8,128)(2,1)} %get-tuple-element.115), channel_id=1, source_target_pairs={{0,1},{1,0},{2,3},{3,2},{4,5},{5,4},{6,7},{7,6},{8,9},{9,8},{10,11... | collective-permute-start | bytes 1228808 | tf_op jit(solution)/shard_map/ppermute | solution.py:39
  2359.4 45.9 %collective-permute-start.104 = (bf16[64,3200]{1,0:T(8,128)(2,1)}, bf16[64,3200]{1,0:T(8,128)(2,1)S(1)}, u32[]{:S(2)}, u32[]{:S(2)}) collective-permute-start(bf16[64,3200]{1,0:T(8,128)(2,1)} %get-tuple-element.117), channel_id=1, source_target_pairs={{0,1},{1,0},{2,3},{3,2},{4,5},{5,4},{6,7},{7,6},{8,9},{9,8},{10,11... | collective-permute-start | bytes 1228808 | tf_op jit(solution)/shard_map/ppermute | solution.py:39
  2397.6 26.3 %collective-permute-start.92 = (bf16[64,3200]{1,0:T(8,128)(2,1)S(1)}, bf16[64,3200]{1,0:T(8,128)(2,1)S(1)}, u32[]{:S(2)}, u32[]{:S(2)}) collective-permute-start(bf16[64,3200]{1,0:T(8,128)(2,1)S(1)} %copy-done.81), channel_id=1, source_target_pairs={{0,16},{16,0},{1,17},{17,1},{2,18},{18,2},{3,19},{19,3},{4,20},{20... | collective-permute-start | bytes 1228808 | tf_op jit(solution)/shard_map/ppermute | solution.py:39
  2398.1 31.3 %collective-permute-start.89 = (bf16[64,3200]{1,0:T(8,128)(2,1)S(1)}, bf16[64,3200]{1,0:T(8,128)(2,1)S(1)}, u32[]{:S(2)}, u32[]{:S(2)}) collective-permute-start(bf16[64,3200]{1,0:T(8,128)(2,1)S(1)} %get-tuple-element.124), channel_id=1, source_target_pairs={{0,16},{16,0},{1,17},{17,1},{2,18},{18,2},{3,19},{19,3},{4,20},{20... | collective-permute-start | bytes 1228808 | tf_op jit(solution)/shard_map/ppermute | solution.py:39
  2405.3 31.5 %collective-permute-start.112 = (bf16[64,3200]{1,0:T(8,128)(2,1)}, bf16[64,3200]{1,0:T(8,128)(2,1)S(1)}, u32[]{:S(2)}, u32[]{:S(2)}) collective-permute-start(bf16[64,3200]{1,0:T(8,128)(2,1)} %get-tuple-element.112), channel_id=1, source_target_pairs={{0,1},{1,0},{2,3},{3,2},{4,5},{5,4},{6,7},{7,6},{8,9},{9,8},{10,11... | collective-permute-start | bytes 1228808 | tf_op jit(solution)/shard_map/ppermute | solution.py:39
  2434.7 40.0 %collective-permute-start.128 = (bf16[64,2048]{1,0:T(8,128)(2,1)S(1)}, bf16[64,2048]{1,0:T(8,128)(2,1)S(1)}, u32[]{:S(2)}, u32[]{:S(2)}) collective-permute-start(bf16[64,2048]{1,0:T(8,128)(2,1)S(1)} %get-tuple-element.163), channel_id=1, source_target_pairs={{0,1},{1,0},{2,3},{3,2},{4,5},{5,4},{6,7},{7,6},{8,9},{9,8},{10,11... | collective-permute-start | bytes 786440 | tf_op jit(solution)/shard_map/ppermute | solution.py:39
  2439.4 24.3 collective-permute-start.120
  2443.9 28.5 %collective-permute-start.109 = (bf16[64,3200]{1,0:T(8,128)(2,1)S(1)}, bf16[64,3200]{1,0:T(8,128)(2,1)S(1)}, u32[]{:S(2)}, u32[]{:S(2)}) collective-permute-start(bf16[64,3200]{1,0:T(8,128)(2,1)S(1)} %copy-done.75), channel_id=1, source_target_pairs={{0,1},{1,0},{2,3},{3,2},{4,5},{5,4},{6,7},{7,6},{8,9},{9,8},{10,11... | collective-permute-start | bytes 1228808 | tf_op jit(solution)/shard_map/ppermute | solution.py:39
  2484.8 58.4 %collective-permute-start.119 = (bf16[64,2048]{1,0:T(8,128)(2,1)S(1)}, bf16[64,2048]{1,0:T(8,128)(2,1)S(1)}, u32[]{:S(2)}, u32[]{:S(2)}) collective-permute-start(bf16[64,2048]{1,0:T(8,128)(2,1)S(1)} %get-tuple-element.161), channel_id=1, source_target_pairs={{0,1},{1,0},{2,3},{3,2},{4,5},{5,4},{6,7},{7,6},{8,9},{9,8},{10,11... | collective-permute-start | bytes 786440 | tf_op jit(solution)/shard_map/ppermute | solution.py:39
  2487.6 33.8 %collective-permute-start.122 = (bf16[64,2048]{1,0:T(8,128)(2,1)S(1)}, bf16[64,2048]{1,0:T(8,128)(2,1)S(1)}, u32[]{:S(2)}, u32[]{:S(2)}) collective-permute-start(bf16[64,2048]{1,0:T(8,128)(2,1)S(1)} %get-tuple-element.167), channel_id=1, source_target_pairs={{0,1},{1,0},{2,3},{3,2},{4,5},{5,4},{6,7},{7,6},{8,9},{9,8},{10,11... | collective-permute-start | bytes 786440 | tf_op jit(solution)/shard_map/ppermute | solution.py:39
  2512.8 30.5 %collective-permute-start.121 = (bf16[64,2048]{1,0:T(8,128)(2,1)S(1)}, bf16[64,2048]{1,0:T(8,128)(2,1)S(1)}, u32[]{:S(2)}, u32[]{:S(2)}) collective-permute-start(bf16[64,2048]{1,0:T(8,128)(2,1)S(1)} %get-tuple-element.169), channel_id=1, source_target_pairs={{0,16},{16,0},{1,17},{17,1},{2,18},{18,2},{3,19},{19,3},{4,20},{20... | collective-permute-start | bytes 786440 | tf_op jit(solution)/shard_map/ppermute | solution.py:39
  (229 other events, 7872.7 us)

commit v2 on v1

--- a/solution.py
+++ b/solution.py
@@ -91,9 +91,10 @@
         grid_spec=pltpu.PrefetchScalarGridSpec(
             num_scalar_prefetch=1,
             in_specs=[pl.BlockSpec(memory_space=pl.ANY)] * len(blocks),
-            out_specs=pl.BlockSpec(memory_space=pl.ANY),
+            out_specs=pl.BlockSpec(memory_space=pltpu.VMEM),
             scratch_shapes=[pltpu.SemaphoreType.DMA((len(blocks),))],
         ),
+        compiler_params=pltpu.CompilerParams(vmem_limit_bytes=24 << 20),
     )(jnp.stack(offsets).astype(jnp.int32), *blocks)
 
 

time: 2600 us -> 1360 us (0.52)
  Pallas kernels: 1330 us -> 51.6 us
  local copies, waits for them, and re-layouts: 146 us -> 175 us
    pallas_call x5, Pallas kernels: 1300 us -> 17.3 us  [place(): pl.pallas_call(functools.partial(place_kernel, len(blocks), row_axis, row...]
    unnamed x321 -> x387, local copies, waits for them, and re-layouts: 40.3 us -> 68 us
  transfers between devices with their start and end apart: 143 -> 143, of which waited for: 65 -> 68; matrix products, arithmetic and copies ran while one was open for 12% -> 23% of each run, Pallas kernels for 51% -> 4%
where the time goes in v2:
time: 1360 us; the launch traced here: 1350 us
  waiting for transfers between devices  536 us (39%)
  matrix products  290 us (21%)
  starting transfers between devices  180 us (13%)
  local copies, waits for them, and re-layouts  175 us (13%)
  other arithmetic  110 us (8%)
  Pallas kernels  51.6 us (4%)
    ppermute x136, waiting for transfers between devices, shift(): lax.ppermute(value, axis, [(i, (i + step) % size) for i in range(size)])  535 us
    ppermute x136, starting transfers between devices, shift(): lax.ppermute(value, axis, [(i, (i + step) % size) for i in range(size)])  180 us
    dot_general x9, matrix products, times_t(): lax.dot_general(left, right, (((1,), (1,)), ((), ())), preferred_element_...  83.1 us
    dot_general x9, matrix products, plain(): return jnp.dot(left, right, preferred_element_type=F32)  69.7 us
    unnamed x387, local copies, waits for them, and re-layouts  68 us
    dot_general x9, matrix products, inner(): lax.dot_general(left, right, (((0,), (0,)), ((), ())), preferred_element_...  67.2 us
  transfers between devices with their start and end apart: 143, of which 68 were waited for; matrix products, arithmetic and copies ran while one was open for 23% of the time, Pallas kernels for 4%

profile of v2, /device:TPU:0, one launch (start us, length us, event | category | flops | bytes accessed | tf_op | source)
XLA Modules:
  0.0 1346.8 jit_solution(16070358419495840867)
XLA Ops:
  27.2 7.0 collective-permute-done.35.refs_3_
  92.3 7.2 collective-permute-done.20.refs_19_
  123.5 16.4 %collective-permute-done.24.refs_23_ = bf16[64,3200]{1,0:T(8,128)(2,1)S(1)} collective-permute-done((bf16[64,3200]{1,0:T(8,128)(2,1)}, bf16[64,3200]{1,0:T(8,128)(2,1)S(1)}, u32[]{:S(2)}, u32[]{:S(2)}) %collective-permute-start.24) | collective-permute-done | bytes 409632 | tf_op jit(solution)/shard_map/ppermute | solution.py:39
  145.9 6.6 collective-permute-done.31.refs_30_
  154.7 7.3 collective-permute-done.16.refs_14_
  182.8 7.7 shard_map.272
  196.7 10.6 fusion.4.qkv_ref
  207.3 13.7 %shard_map.273 = bf16[512,1024]{1,0:T(8,128)(2,1)S(1)} custom-call(s32[4]{0:T(128)S(1)} %pad_add_fusion.lengths_ref, f32[512,3072]{1,0:T(8,128)S(1)} %fusion.4.qkv_ref, f32[2,128]{1,0:T(2,128)S(1)} %pad_maximum_fusion.13.gains_ref, f32[128,128]{1,0:T(8,128)S(1)} %get-tuple-element.229.cosine_ref, f32[128,128]{1,0:T(8,128)S(1)} %get-tuple-element.230.sine_ref), custom_call_target="tpu_custom_call" | custom-call | tf_op jit(solution)/shard_map/pallas_call | solution.py:194
  231.0 23.3 %collective-permute-done.49 = bf16[256,2176]{0,1:T(8,128)(2,1)} collective-permute-done((bf16[256,2176]{0,1:T(8,128)(2,1)}, bf16[256,2176]{0,1:T(8,128)(2,1)}, u32[]{:S(2)}, u32[]{:S(2)}) %collective-permute-start.49) | collective-permute-done | bytes 1114144 | tf_op jit(solution)/shard_map/ppermute | solution.py:39
  267.5 11.3 collective-permute-done.64.refs_2_
  279.4 8.3 collective-permute-done.52
  288.0 35.6 %collective-permute-done.67.refs_2_ = bf16[2,512,1024]{2,1,0:T(8,128)(2,1)S(1)} collective-permute-done((bf16[2,512,1024]{2,1,0:T(8,128)(2,1)}, bf16[2,512,1024]{2,1,0:T(8,128)(2,1)S(1)}, u32[]{:S(2)}, u32[]{:S(2)}) %collective-permute-start.67) | collective-permute-done | bytes 2097184 | tf_op jit(solution)/shard_map/ppermute | solution.py:39
  323.7 43.8 %collective-permute-done.70.refs_2_ = bf16[2,256,2048]{2,1,0:T(8,128)(2,1)S(1)} collective-permute-done((bf16[2,256,2048]{2,1,0:T(8,128)(2,1)}, bf16[2,256,2048]{2,1,0:T(8,128)(2,1)S(1)}, u32[]{:S(2)}, u32[]{:S(2)}) %collective-permute-start.70) | collective-permute-done | bytes 2097184 | tf_op jit(solution)/shard_map/ppermute | solution.py:39
  371.9 21.0 %collective-permute-done.53 = bf16[256,2176]{0,1:T(8,128)(2,1)S(1)} collective-permute-done((bf16[256,2176]{0,1:T(8,128)(2,1)S(1)}, bf16[256,2176]{0,1:T(8,128)(2,1)S(1)}, u32[]{:S(2)}, u32[]{:S(2)}) %collective-permute-start.53) | collective-permute-done | bytes 1114144 | tf_op jit(solution)/shard_map/ppermute | solution.py:39
  399.8 19.6 %collective-permute-done.57 = bf16[256,2176]{0,1:T(8,128)(2,1)} collective-permute-done((bf16[256,2176]{0,1:T(8,128)(2,1)}, bf16[256,2176]{0,1:T(8,128)(2,1)}, u32[]{:S(2)}, u32[]{:S(2)}) %collective-permute-start.57) | collective-permute-done | bytes 1114144 | tf_op jit(solution)/shard_map/ppermute | solution.py:39
  439.6 8.4 slice.333
  448.0 12.3 copy.160
  467.8 20.2 %collective-permute-done.58 = bf16[256,2176]{0,1:T(8,128)(2,1)S(1)} collective-permute-done((bf16[256,2176]{0,1:T(8,128)(2,1)}, bf16[256,2176]{0,1:T(8,128)(2,1)S(1)}, u32[]{:S(2)}, u32[]{:S(2)}) %collective-permute-start.58) | collective-permute-done | bytes 1114144 | tf_op jit(solution)/shard_map/ppermute | solution.py:39
  492.2 19.8 %collective-permute-done.60 = bf16[256,2176]{0,1:T(8,128)(2,1)S(1)} collective-permute-done((bf16[256,2176]{0,1:T(8,128)(2,1)}, bf16[256,2176]{0,1:T(8,128)(2,1)S(1)}, u32[]{:S(2)}, u32[]{:S(2)}) %collective-permute-start.60) | collective-permute-done | bytes 1114144 | tf_op jit(solution)/shard_map/ppermute | solution.py:39
  514.2 17.7 %collective-permute-done.62 = bf16[256,2176]{0,1:T(8,128)(2,1)S(1)} collective-permute-done((bf16[256,2176]{0,1:T(8,128)(2,1)S(1)}, bf16[256,2176]{0,1:T(8,128)(2,1)S(1)}, u32[]{:S(2)}, u32[]{:S(2)}) %collective-permute-start.62) | collective-permute-done | bytes 1114144 | tf_op jit(solution)/shard_map/ppermute | solution.py:39
  533.9 8.4 slice.316
  542.2 12.3 copy.159
  560.3 10.8 fusion.9
  571.1 10.0 multiply_convert_fusion.7
  587.1 7.0 multiply_reduce_fusion.1
  595.0 6.9 multiply_convert_fusion.1
  601.9 12.8 multiply_convert_fusion.5
  614.7 9.9 convert_bitcast_fusion.3
  624.6 10.7 fusion.10
  639.2 9.1 fusion.13
  648.4 9.8 multiply_convert_fusion.6
  658.2 9.3 convolution_convert_fusion.1
  667.6 12.0 multiply_reduce_fusion
  680.1 6.9 multiply_convert_fusion
  687.0 14.1 %multiply_convert_fusion.3 = (bf16[1280,1024]{1,0:T(8,128)(2,1)}, bf16[1280,1024]{1,0:T(8,128)(2,1)S(1)}) fusion(f32[1280,1024]{1,0:T(8,128)} %fusion.13, f32[1280,1024]{1,0:T(8,128)} %get-tuple-element.223, bf16[1280,2048]{1,0:T(8,128)(2,1)} %bitcast.257, bf16[2,1024,2048]{2,1,0:T(8,128)(2,1)} %copy-done.4), kind=kOutput, calls=%fused_computation.52 | convolution fusion | flops 5385748480 | bytes 25165824 | tf_op jit(solution)/shard_map/dot_general | solution.py:34
  701.1 8.5 convert_bitcast_fusion.2
  709.7 12.2 fusion.14
  721.9 8.1 fusion.55
  730.0 8.9 convert_bitcast_fusion.4
  750.8 10.3 add_convert_fusion.3
  761.1 9.9 add_convert_fusion.2
  771.0 13.0 add_convert_fusion.1
  798.7 8.1 fusion.48
  806.8 13.0 add_convert_fusion
  819.9 12.4 copy.157
  838.2 10.0 convert_bitcast_fusion.1
  848.2 38.3 %collective-permute-done.82 = bf16[256,2176]{0,1:T(8,128)(2,1)S(1)} collective-permute-done((bf16[256,2176]{0,1:T(8,128)(2,1)S(1)}, bf16[256,2176]{0,1:T(8,128)(2,1)S(1)}, u32[]{:S(2)}, u32[]{:S(2)}) %collective-permute-start.82) | collective-permute-done | bytes 1114144 | tf_op jit(solution)/shard_map/ppermute | solution.py:39
  890.5 7.4 convert_bitcast_fusion
  899.5 14.2 %collective-permute-done.83 = bf16[256,2176]{0,1:T(8,128)(2,1)S(1)} collective-permute-done((bf16[256,2176]{0,1:T(8,128)(2,1)S(1)}, bf16[256,2176]{0,1:T(8,128)(2,1)S(1)}, u32[]{:S(2)}, u32[]{:S(2)}) %collective-permute-start.83) | collective-permute-done | bytes 1114144 | tf_op jit(solution)/shard_map/ppermute | solution.py:39
  947.2 14.0 %collective-permute-done.74 = bf16[256,2048]{0,1:T(8,128)(2,1)S(1)} collective-permute-done((bf16[256,2048]{0,1:T(8,128)(2,1)}, bf16[256,2048]{0,1:T(8,128)(2,1)S(1)}, u32[]{:S(2)}, u32[]{:S(2)}) %collective-permute-start.74) | collective-permute-done | bytes 1048608 | tf_op jit(solution)/shard_map/ppermute | solution.py:39
  1007.4 6.2 collective-permute-done.77
  1020.7 20.6 %shard_map.278 = (bf16[512,3072]{1,0:T(8,128)(2,1)S(1)}, f32[2,128]{1,0:T(2,128)S(1)}) custom-call(s32[4]{0:T(128)S(1)} %pad_add_fusion.lengths_ref, f32[512,3072]{1,0:T(8,128)S(1)} %bitcast.213, bf16[512,1024]{1,0:T(8,128)(2,1)S(1)} %convolution_convert_fusion.7.mixed_grad_ref, f32[2,128]{1,0:T(2,128)S(1)} %pad_maximum_fusion.13.gains_ref, ...), custom_call_target="tpu_custom_call" | custom-call | tf_op jit(solution)/shard_map/pallas_call | solution.py:217
  1041.4 8.2 fusion.2
  1054.2 8.3 collective-permute-done.142
  1069.7 11.5 convolution_convert_fusion
  1084.1 6.4 fusion.1
  1094.4 13.0 collective-permute-done.139
  1109.1 6.3 convert_add_fusion.1
  1115.5 34.0 %collective-permute-done.136 = bf16[2,512,1024]{2,1,0:T(8,128)(2,1)} collective-permute-done((bf16[2,512,1024]{2,1,0:T(8,128)(2,1)}, bf16[2,512,1024]{2,1,0:T(8,128)(2,1)}, u32[]{:S(2)}, u32[]{:S(2)}) %collective-permute-start.136) | collective-permute-done | bytes 2097184 | tf_op jit(solution)/shard_map/ppermute | solution.py:39
  1161.9 8.8 collective-permute-done.95
  1170.7 6.8 collective-permute-done.92
  1200.9 9.7 collective-permute-done.126
  1220.7 7.1 collective-permute-done.109
  1322.4 6.2 collective-permute-done.78
  (816 shorter events, 533.8 us)
Async XLA Ops:
  25.3 30.1 %collective-permute-start.21 = (bf16[64,3200]{1,0:T(8,128)(2,1)S(1)}, bf16[64,3200]{1,0:T(8,128)(2,1)S(1)}, u32[]{:S(2)}, u32[]{:S(2)}) collective-permute-start(bf16[64,3200]{1,0:T(8,128)(2,1)S(1)} %get-tuple-element.185.refs_16_), channel_id=1, source_target_pairs={{0,2},{2,4},{4,6},{6,0},{1,3},{3,5},{5,7},{7,1},{8,10},{10,12},{12... | collective-permute-start | bytes 1228808 | tf_op jit(solution)/shard_map/ppermute | solution.py:39
  37.7 46.4 %collective-permute-start.1 = (bf16[256,2048]{0,1:T(8,128)(2,1)}, bf16[256,2048]{0,1:T(8,128)(2,1)}, u32[]{:S(2)}, u32[]{:S(2)}) collective-permute-start(bf16[256,2048]{0,1:T(8,128)(2,1)} %copy.146), channel_id=1, source_target_pairs={{0,8},{8,0},{1,9},{9,1},{2,10},{10,2},{3,11},{11,3},{4,12},{12,4},... | collective-permute-start | bytes 3145736 | tf_op jit(solution)/shard_map/ppermute | solution.py:312
  110.7 30.0 %collective-permute-start.14 = (bf16[64,3200]{1,0:T(8,128)(2,1)}, bf16[64,3200]{1,0:T(8,128)(2,1)S(1)}, u32[]{:S(2)}, u32[]{:S(2)}) collective-permute-start(bf16[64,3200]{1,0:T(8,128)(2,1)} %copy-done.28), channel_id=1, source_target_pairs={{0,2},{2,4},{4,6},{6,0},{1,3},{3,5},{5,7},{7,1},{8,10},{10,12},{12... | collective-permute-start | bytes 1228808 | tf_op jit(solution)/shard_map/ppermute | solution.py:39
  114.0 28.1 %collective-permute-start.12 = (bf16[64,3200]{1,0:T(8,128)(2,1)}, bf16[64,3200]{1,0:T(8,128)(2,1)S(1)}, u32[]{:S(2)}, u32[]{:S(2)}) collective-permute-start(bf16[64,3200]{1,0:T(8,128)(2,1)} %copy-done.28), channel_id=1, source_target_pairs={{0,1},{1,0},{2,3},{3,2},{4,5},{5,4},{6,7},{7,6},{8,9},{9,8},{10,11... | collective-permute-start | bytes 1228808 | tf_op jit(solution)/shard_map/ppermute | solution.py:39
  115.5 24.3 %collective-permute-start.24 = (bf16[64,3200]{1,0:T(8,128)(2,1)}, bf16[64,3200]{1,0:T(8,128)(2,1)S(1)}, u32[]{:S(2)}, u32[]{:S(2)}) collective-permute-start(bf16[64,3200]{1,0:T(8,128)(2,1)} %copy-done.22), channel_id=1, source_target_pairs={{0,1},{1,0},{2,3},{3,2},{4,5},{5,4},{6,7},{7,6},{8,9},{9,8},{10,11... | collective-permute-start | bytes 1228808 | tf_op jit(solution)/shard_map/ppermute | solution.py:39
  119.3 23.8 %collective-permute-start.11 = (bf16[64,3200]{1,0:T(8,128)(2,1)}, bf16[64,3200]{1,0:T(8,128)(2,1)S(1)}, u32[]{:S(2)}, u32[]{:S(2)}) collective-permute-start(bf16[64,3200]{1,0:T(8,128)(2,1)} %copy-done.28), channel_id=1, source_target_pairs={{0,16},{16,0},{1,17},{17,1},{2,18},{18,2},{3,19},{19,3},{4,20},{20... | collective-permute-start | bytes 1228808 | tf_op jit(solution)/shard_map/ppermute | solution.py:39
  143.1 39.6 %collective-permute-start.15 = (bf16[64,3200]{1,0:T(8,128)(2,1)S(1)}, bf16[64,3200]{1,0:T(8,128)(2,1)S(1)}, u32[]{:S(2)}, u32[]{:S(2)}) collective-permute-start(bf16[64,3200]{1,0:T(8,128)(2,1)S(1)} %collective-permute-done.14.refs_12_), channel_id=1, source_target_pairs={{0,16},{16,0},{1,17},{17,1},{2,18},{18,2},{3,19},{19,3},{4,20},{20... | collective-permute-start | bytes 1228808 | tf_op jit(solution)/shard_map/ppermute | solution.py:39
  144.4 38.3 %collective-permute-start.28 = (bf16[64,3200]{1,0:T(8,128)(2,1)S(1)}, bf16[64,3200]{1,0:T(8,128)(2,1)S(1)}, u32[]{:S(2)}, u32[]{:S(2)}) collective-permute-start(bf16[64,3200]{1,0:T(8,128)(2,1)S(1)} %collective-permute-done.27.refs_26_), channel_id=1, source_target_pairs={{0,1},{1,0},{2,3},{3,2},{4,5},{5,4},{6,7},{7,6},{8,9},{9,8},{10,11... | collective-permute-start | bytes 1228808 | tf_op jit(solution)/shard_map/ppermute | solution.py:39
  152.4 30.2 %collective-permute-start.13 = (bf16[64,3200]{1,0:T(8,128)(2,1)S(1)}, bf16[64,3200]{1,0:T(8,128)(2,1)S(1)}, u32[]{:S(2)}, u32[]{:S(2)}) collective-permute-start(bf16[64,3200]{1,0:T(8,128)(2,1)S(1)} %collective-permute-done.12.refs_10_), channel_id=1, source_target_pairs={{0,16},{16,0},{1,17},{17,1},{2,18},{18,2},{3,19},{19,3},{4,20},{20... | collective-permute-start | bytes 1228808 | tf_op jit(solution)/shard_map/ppermute | solution.py:39
  153.2 29.4 %collective-permute-start.32 = (bf16[64,3200]{1,0:T(8,128)(2,1)S(1)}, bf16[64,3200]{1,0:T(8,128)(2,1)S(1)}, u32[]{:S(2)}, u32[]{:S(2)}) collective-permute-start(bf16[64,3200]{1,0:T(8,128)(2,1)S(1)} %collective-permute-done.31.refs_30_), channel_id=1, source_target_pairs={{0,1},{1,0},{2,3},{3,2},{4,5},{5,4},{6,7},{7,6},{8,9},{9,8},{10,11... | collective-permute-start | bytes 1228808 | tf_op jit(solution)/shard_map/ppermute | solution.py:39
  182.6 75.5 %collective-permute-start.63 = (bf16[2,512,1024]{2,1,0:T(8,128)(2,1)S(1)}, bf16[2,512,1024]{2,1,0:T(8,128)(2,1)}, u32[]{:S(2)}, u32[]{:S(2)}) collective-permute-start(bf16[2,512,1024]{2,1,0:T(8,128)(2,1)S(1)} %copy-done.8), channel_id=1, source_target_pairs={{0,8},{8,0},{1,9},{9,1},{2,10},{10,2},{3,11},{11,3},{4,12},{12,4},... | collective-permute-start | bytes 6291464 | tf_op jit(solution)/shard_map/ppermute | solution.py:39
  225.1 35.4 %collective-permute-start.48 = (f32[256,2048]{0,1:T(8,128)}, f32[256,2048]{0,1:T(8,128)}, u32[]{:S(2)}, u32[]{:S(2)}) collective-permute-start(f32[256,2048]{0,1:T(8,128)} %slice.307), channel_id=1, source_target_pairs={{0,8},{8,0},{1,9},{9,1},{2,10},{10,2},{3,11},{11,3},{4,12},{12,4},... | collective-permute-start | bytes 6291464 | tf_op jit(solution)/shard_map/ppermute | solution.py:312
  227.1 27.2 %collective-permute-start.49 = (bf16[256,2176]{0,1:T(8,128)(2,1)}, bf16[256,2176]{0,1:T(8,128)(2,1)}, u32[]{:S(2)}, u32[]{:S(2)}) collective-permute-start(bf16[256,2176]{0,1:T(8,128)(2,1)} %get-tuple-element.175), channel_id=1, source_target_pairs={{0,1},{1,0},{2,3},{3,2},{4,5},{5,4},{6,7},{7,6},{8,9},{9,8},{10,11... | collective-permute-start | bytes 3342344 | tf_op jit(solution)/shard_map/ppermute | solution.py:39
  228.6 28.7 %collective-permute-start.50 = (bf16[256,2176]{0,1:T(8,128)(2,1)}, bf16[256,2176]{0,1:T(8,128)(2,1)}, u32[]{:S(2)}, u32[]{:S(2)}) collective-permute-start(bf16[256,2176]{0,1:T(8,128)(2,1)} %get-tuple-element.175), channel_id=1, source_target_pairs={{0,2},{2,4},{4,6},{6,0},{1,3},{3,5},{5,7},{7,1},{8,10},{10,12},{12... | collective-permute-start | bytes 3342344 | tf_op jit(solution)/shard_map/ppermute | solution.py:39
  230.2 48.6 %collective-permute-start.64 = (bf16[2,512,1024]{2,1,0:T(8,128)(2,1)S(1)}, bf16[2,512,1024]{2,1,0:T(8,128)(2,1)}, u32[]{:S(2)}, u32[]{:S(2)}) collective-permute-start(bf16[2,512,1024]{2,1,0:T(8,128)(2,1)S(1)} %copy-done.8), channel_id=1, source_target_pairs={{0,16},{16,0},{1,17},{17,1},{2,18},{18,2},{3,19},{19,3},{4,20},{20... | collective-permute-start | bytes 6291464 | tf_op jit(solution)/shard_map/ppermute | solution.py:39
  254.3 25.1 %collective-permute-start.66 = (bf16[2,512,1024]{2,1,0:T(8,128)(2,1)}, bf16[2,512,1024]{2,1,0:T(8,128)(2,1)}, u32[]{:S(2)}, u32[]{:S(2)}) collective-permute-start(bf16[2,512,1024]{2,1,0:T(8,128)(2,1)} %refs_0_.6), channel_id=1, source_target_pairs={{0,8},{8,0},{1,9},{9,1},{2,10},{10,2},{3,11},{11,3},{4,12},{12,4},... | collective-permute-start | bytes 6291464 | tf_op jit(solution)/shard_map/ppermute | solution.py:39
  257.3 66.4 %collective-permute-start.67 = (bf16[2,512,1024]{2,1,0:T(8,128)(2,1)}, bf16[2,512,1024]{2,1,0:T(8,128)(2,1)S(1)}, u32[]{:S(2)}, u32[]{:S(2)}) collective-permute-start(bf16[2,512,1024]{2,1,0:T(8,128)(2,1)} %refs_0_.6), channel_id=1, source_target_pairs={{0,16},{16,0},{1,17},{17,1},{2,18},{18,2},{3,19},{19,3},{4,20},{20... | collective-permute-start | bytes 6291464 | tf_op jit(solution)/shard_map/ppermute | solution.py:39
  258.1 109.3 %collective-permute-start.70 = (bf16[2,256,2048]{2,1,0:T(8,128)(2,1)}, bf16[2,256,2048]{2,1,0:T(8,128)(2,1)S(1)}, u32[]{:S(2)}, u32[]{:S(2)}) collective-permute-start(bf16[2,256,2048]{2,1,0:T(8,128)(2,1)} %refs_0_.7), channel_id=1, source_target_pairs={{0,16},{16,0},{1,17},{17,1},{2,18},{18,2},{3,19},{19,3},{4,20},{20... | collective-permute-start | bytes 6291464 | tf_op jit(solution)/shard_map/ppermute | solution.py:39
  260.5 27.2 %collective-permute-start.52 = (bf16[256,2176]{0,1:T(8,128)(2,1)}, bf16[256,2176]{0,1:T(8,128)(2,1)S(1)}, u32[]{:S(2)}, u32[]{:S(2)}) collective-permute-start(bf16[256,2176]{0,1:T(8,128)(2,1)} %collective-permute-done.50), channel_id=1, source_target_pairs={{0,2},{2,4},{4,6},{6,0},{1,3},{3,5},{5,7},{7,1},{8,10},{10,12},{12... | collective-permute-start | bytes 3342344 | tf_op jit(solution)/shard_map/ppermute | solution.py:39
  278.8 90.8 %collective-permute-start.51 = (bf16[256,2176]{0,1:T(8,128)(2,1)}, bf16[256,2176]{0,1:T(8,128)(2,1)S(1)}, u32[]{:S(2)}, u32[]{:S(2)}) collective-permute-start(bf16[256,2176]{0,1:T(8,128)(2,1)} %collective-permute-done.50), channel_id=1, source_target_pairs={{0,1},{1,0},{2,3},{3,2},{4,5},{5,4},{6,7},{7,6},{8,9},{9,8},{10,11... | collective-permute-start | bytes 3342344 | tf_op jit(solution)/shard_map/ppermute | solution.py:39
  279.4 116.1 %collective-permute-start.65 = (bf16[2,512,1024]{2,1,0:T(8,128)(2,1)}, bf16[2,512,1024]{2,1,0:T(8,128)(2,1)S(1)}, u32[]{:S(2)}, u32[]{:S(2)}) collective-permute-start(bf16[2,512,1024]{2,1,0:T(8,128)(2,1)} %collective-permute-done.64.refs_2_), channel_id=1, source_target_pairs={{0,8},{8,0},{1,9},{9,1},{2,10},{10,2},{3,11},{11,3},{4,12},{12,4},... | collective-permute-start | bytes 6291464 | tf_op jit(solution)/shard_map/ppermute | solution.py:39
  287.7 82.1 %collective-permute-start.54 = (bf16[256,2176]{0,1:T(8,128)(2,1)S(1)}, bf16[256,2176]{0,1:T(8,128)(2,1)S(1)}, u32[]{:S(2)}, u32[]{:S(2)}) collective-permute-start(bf16[256,2176]{0,1:T(8,128)(2,1)S(1)} %collective-permute-done.52), channel_id=1, source_target_pairs={{0,2},{2,4},{4,6},{6,0},{1,3},{3,5},{5,7},{7,1},{8,10},{10,12},{12... | collective-permute-start | bytes 3342344 | tf_op jit(solution)/shard_map/ppermute | solution.py:39
  323.7 74.6 %collective-permute-start.68 = (bf16[2,512,1024]{2,1,0:T(8,128)(2,1)S(1)}, bf16[2,512,1024]{2,1,0:T(8,128)(2,1)S(1)}, u32[]{:S(2)}, u32[]{:S(2)}) collective-permute-start(bf16[2,512,1024]{2,1,0:T(8,128)(2,1)S(1)} %collective-permute-done.67.refs_2_), channel_id=1, source_target_pairs={{0,8},{8,0},{1,9},{9,1},{2,10},{10,2},{3,11},{11,3},{4,12},{12,4},... | collective-permute-start | bytes 6291464 | tf_op jit(solution)/shard_map/ppermute | solution.py:39
  367.4 25.4 %collective-permute-start.53 = (bf16[256,2176]{0,1:T(8,128)(2,1)S(1)}, bf16[256,2176]{0,1:T(8,128)(2,1)S(1)}, u32[]{:S(2)}, u32[]{:S(2)}) collective-permute-start(bf16[256,2176]{0,1:T(8,128)(2,1)S(1)} %collective-permute-done.52), channel_id=1, source_target_pairs={{0,1},{1,0},{2,3},{3,2},{4,5},{5,4},{6,7},{7,6},{8,9},{9,8},{10,11... | collective-permute-start | bytes 3342344 | tf_op jit(solution)/shard_map/ppermute | solution.py:39
  369.7 63.3 %collective-permute-start.69 = (bf16[2,256,2048]{2,1,0:T(8,128)(2,1)S(1)}, bf16[2,256,2048]{2,1,0:T(8,128)(2,1)S(1)}, u32[]{:S(2)}, u32[]{:S(2)}) collective-permute-start(bf16[2,256,2048]{2,1,0:T(8,128)(2,1)S(1)} %copy-done.9), channel_id=1, source_target_pairs={{0,8},{8,0},{1,9},{9,1},{2,10},{10,2},{3,11},{11,3},{4,12},{12,4},... | collective-permute-start | bytes 6291464 | tf_op jit(solution)/shard_map/ppermute | solution.py:39
  369.8 63.2 %collective-permute-start.71 = (bf16[2,256,2048]{2,1,0:T(8,128)(2,1)S(1)}, bf16[2,256,2048]{2,1,0:T(8,128)(2,1)S(1)}, u32[]{:S(2)}, u32[]{:S(2)}) collective-permute-start(bf16[2,256,2048]{2,1,0:T(8,128)(2,1)S(1)} %collective-permute-done.70.refs_2_), channel_id=1, source_target_pairs={{0,8},{8,0},{1,9},{9,1},{2,10},{10,2},{3,11},{11,3},{4,12},{12,4},... | collective-permute-start | bytes 6291464 | tf_op jit(solution)/shard_map/ppermute | solution.py:39
  392.8 26.6 %collective-permute-start.57 = (bf16[256,2176]{0,1:T(8,128)(2,1)}, bf16[256,2176]{0,1:T(8,128)(2,1)}, u32[]{:S(2)}, u32[]{:S(2)}) collective-permute-start(bf16[256,2176]{0,1:T(8,128)(2,1)} %get-tuple-element.177), channel_id=1, source_target_pairs={{0,2},{2,4},{4,6},{6,0},{1,3},{3,5},{5,7},{7,1},{8,10},{10,12},{12... | collective-permute-start | bytes 3342344 | tf_op jit(solution)/shard_map/ppermute | solution.py:39
  395.5 41.9 %collective-permute-start.55 = (bf16[256,2176]{0,1:T(8,128)(2,1)S(1)}, bf16[256,2176]{0,1:T(8,128)(2,1)S(1)}, u32[]{:S(2)}, u32[]{:S(2)}) collective-permute-start(bf16[256,2176]{0,1:T(8,128)(2,1)S(1)} %collective-permute-done.54), channel_id=1, source_target_pairs={{0,1},{1,0},{2,3},{3,2},{4,5},{5,4},{6,7},{7,6},{8,9},{9,8},{10,11... | collective-permute-start | bytes 3342344 | tf_op jit(solution)/shard_map/ppermute | solution.py:39
  398.3 63.3 %collective-permute-start.56 = (bf16[256,2176]{0,1:T(8,128)(2,1)}, bf16[256,2176]{0,1:T(8,128)(2,1)}, u32[]{:S(2)}, u32[]{:S(2)}) collective-permute-start(bf16[256,2176]{0,1:T(8,128)(2,1)} %get-tuple-element.177), channel_id=1, source_target_pairs={{0,1},{1,0},{2,3},{3,2},{4,5},{5,4},{6,7},{7,6},{8,9},{9,8},{10,11... | collective-permute-start | bytes 3342344 | tf_op jit(solution)/shard_map/ppermute | solution.py:39
  419.4 41.5 %collective-permute-start.59 = (bf16[256,2176]{0,1:T(8,128)(2,1)}, bf16[256,2176]{0,1:T(8,128)(2,1)}, u32[]{:S(2)}, u32[]{:S(2)}) collective-permute-start(bf16[256,2176]{0,1:T(8,128)(2,1)} %collective-permute-done.57), channel_id=1, source_target_pairs={{0,2},{2,4},{4,6},{6,0},{1,3},{3,5},{5,7},{7,1},{8,10},{10,12},{12... | collective-permute-start | bytes 3342344 | tf_op jit(solution)/shard_map/ppermute | solution.py:39
  460.3 27.8 %collective-permute-start.58 = (bf16[256,2176]{0,1:T(8,128)(2,1)}, bf16[256,2176]{0,1:T(8,128)(2,1)S(1)}, u32[]{:S(2)}, u32[]{:S(2)}) collective-permute-start(bf16[256,2176]{0,1:T(8,128)(2,1)} %collective-permute-done.57), channel_id=1, source_target_pairs={{0,1},{1,0},{2,3},{3,2},{4,5},{5,4},{6,7},{7,6},{8,9},{9,8},{10,11... | collective-permute-start | bytes 3342344 | tf_op jit(solution)/shard_map/ppermute | solution.py:39
  460.9 28.3 %collective-permute-start.61 = (bf16[256,2176]{0,1:T(8,128)(2,1)}, bf16[256,2176]{0,1:T(8,128)(2,1)S(1)}, u32[]{:S(2)}, u32[]{:S(2)}) collective-permute-start(bf16[256,2176]{0,1:T(8,128)(2,1)} %collective-permute-done.59), channel_id=1, source_target_pairs={{0,2},{2,4},{4,6},{6,0},{1,3},{3,5},{5,7},{7,1},{8,10},{10,12},{12... | collective-permute-start | bytes 3342344 | tf_op jit(solution)/shard_map/ppermute | solution.py:39
  463.9 48.0 %collective-permute-start.60 = (bf16[256,2176]{0,1:T(8,128)(2,1)}, bf16[256,2176]{0,1:T(8,128)(2,1)S(1)}, u32[]{:S(2)}, u32[]{:S(2)}) collective-permute-start(bf16[256,2176]{0,1:T(8,128)(2,1)} %collective-permute-done.59), channel_id=1, source_target_pairs={{0,1},{1,0},{2,3},{3,2},{4,5},{5,4},{6,7},{7,6},{8,9},{9,8},{10,11... | collective-permute-start | bytes 3342344 | tf_op jit(solution)/shard_map/ppermute | solution.py:39
  489.2 42.7 %collective-permute-start.62 = (bf16[256,2176]{0,1:T(8,128)(2,1)S(1)}, bf16[256,2176]{0,1:T(8,128)(2,1)S(1)}, u32[]{:S(2)}, u32[]{:S(2)}) collective-permute-start(bf16[256,2176]{0,1:T(8,128)(2,1)S(1)} %collective-permute-done.61), channel_id=1, source_target_pairs={{0,1},{1,0},{2,3},{3,2},{4,5},{5,4},{6,7},{7,6},{8,9},{9,8},{10,11... | collective-permute-start | bytes 3342344 | tf_op jit(solution)/shard_map/ppermute | solution.py:39
  747.8 222.3 %collective-permute-start.138 = (bf16[2,512,1024]{2,1,0:T(8,128)(2,1)}, bf16[2,512,1024]{2,1,0:T(8,128)(2,1)}, u32[]{:S(2)}, u32[]{:S(2)}) collective-permute-start(bf16[2,512,1024]{2,1,0:T(8,128)(2,1)} %get-tuple-element.150), channel_id=1, source_target_pairs={{0,8},{8,0},{1,9},{9,1},{2,10},{10,2},{3,11},{11,3},{4,12},{12,4},... | collective-permute-start | bytes 6291464 | tf_op jit(solution)/shard_map/ppermute | solution.py:39
  750.8 223.5 %collective-permute-start.135 = (bf16[2,512,1024]{2,1,0:T(8,128)(2,1)}, bf16[2,512,1024]{2,1,0:T(8,128)(2,1)}, u32[]{:S(2)}, u32[]{:S(2)}) collective-permute-start(bf16[2,512,1024]{2,1,0:T(8,128)(2,1)} %get-tuple-element.152), channel_id=1, source_target_pairs={{0,8},{8,0},{1,9},{9,1},{2,10},{10,2},{3,11},{11,3},{4,12},{12,4},... | collective-permute-start | bytes 6291464 | tf_op jit(solution)/shard_map/ppermute | solution.py:39
  791.8 145.9 %collective-permute-start.75 = (bf16[256,2048]{0,1:T(8,128)(2,1)}, bf16[256,2048]{0,1:T(8,128)(2,1)}, u32[]{:S(2)}, u32[]{:S(2)}) collective-permute-start(bf16[256,2048]{0,1:T(8,128)(2,1)} %copy.155), channel_id=1, source_target_pairs={{0,1},{1,0},{2,3},{3,2},{4,5},{5,4},{6,7},{7,6},{8,9},{9,8},{10,11... | collective-permute-start | bytes 3145736 | tf_op jit(solution)/shard_map/ppermute | solution.py:39
  836.1 61.8 %collective-permute-start.81 = (bf16[256,2176]{0,1:T(8,128)(2,1)S(1)}, bf16[256,2176]{0,1:T(8,128)(2,1)S(1)}, u32[]{:S(2)}, u32[]{:S(2)}) collective-permute-start(bf16[256,2176]{0,1:T(8,128)(2,1)S(1)} %get-tuple-element.142), channel_id=1, source_target_pairs={{0,1},{1,0},{2,3},{3,2},{4,5},{5,4},{6,7},{7,6},{8,9},{9,8},{10,11... | collective-permute-start | bytes 3342344 | tf_op jit(solution)/shard_map/ppermute | solution.py:39
  837.7 48.9 %collective-permute-start.82 = (bf16[256,2176]{0,1:T(8,128)(2,1)S(1)}, bf16[256,2176]{0,1:T(8,128)(2,1)S(1)}, u32[]{:S(2)}, u32[]{:S(2)}) collective-permute-start(bf16[256,2176]{0,1:T(8,128)(2,1)S(1)} %get-tuple-element.143), channel_id=1, source_target_pairs={{0,1},{1,0},{2,3},{3,2},{4,5},{5,4},{6,7},{7,6},{8,9},{9,8},{10,11... | collective-permute-start | bytes 3342344 | tf_op jit(solution)/shard_map/ppermute | solution.py:39
  886.9 26.8 %collective-permute-start.83 = (bf16[256,2176]{0,1:T(8,128)(2,1)S(1)}, bf16[256,2176]{0,1:T(8,128)(2,1)S(1)}, u32[]{:S(2)}, u32[]{:S(2)}) collective-permute-start(bf16[256,2176]{0,1:T(8,128)(2,1)S(1)} %add_convert_fusion.9), channel_id=1, source_target_pairs={{0,6},{2,0},{4,2},{6,4},{1,7},{3,1},{5,3},{7,5},{8,14},{10,8},{12,... | collective-permute-start | bytes 3342344 | tf_op jit(solution)/shard_map/ppermute | solution.py:39
  898.0 42.9 %collective-permute-start.80 = (bf16[256,2176]{0,1:T(8,128)(2,1)}, bf16[256,2176]{0,1:T(8,128)(2,1)}, u32[]{:S(2)}, u32[]{:S(2)}) collective-permute-start(bf16[256,2176]{0,1:T(8,128)(2,1)} %get-tuple-element.141), channel_id=1, source_target_pairs={{0,1},{1,0},{2,3},{3,2},{4,5},{5,4},{6,7},{7,6},{8,9},{9,8},{10,11... | collective-permute-start | bytes 3342344 | tf_op jit(solution)/shard_map/ppermute | solution.py:39
  915.2 29.6 %collective-permute-start.84 = (bf16[256,2176]{0,1:T(8,128)(2,1)}, bf16[256,2176]{0,1:T(8,128)(2,1)}, u32[]{:S(2)}, u32[]{:S(2)}) collective-permute-start(bf16[256,2176]{0,1:T(8,128)(2,1)} %add_convert_fusion.8), channel_id=1, source_target_pairs={{0,6},{2,0},{4,2},{6,4},{1,7},{3,1},{5,3},{7,5},{8,14},{10,8},{12,... | collective-permute-start | bytes 3342344 | tf_op jit(solution)/shard_map/ppermute | solution.py:39
  944.9 108.0 %collective-permute-start.140 = (bf16[2,256,2048]{2,1,0:T(8,128)(2,1)}, bf16[2,256,2048]{2,1,0:T(8,128)(2,1)}, u32[]{:S(2)}, u32[]{:S(2)}) collective-permute-start(bf16[2,256,2048]{2,1,0:T(8,128)(2,1)} %get-tuple-element.147), channel_id=1, source_target_pairs={{0,8},{8,0},{1,9},{9,1},{2,10},{10,2},{3,11},{11,3},{4,12},{12,4},... | collective-permute-start | bytes 6291464 | tf_op jit(solution)/shard_map/ppermute | solution.py:39
  961.2 24.7 %collective-permute-start.79 = (bf16[256,2176]{0,1:T(8,128)(2,1)S(1)}, bf16[256,2176]{0,1:T(8,128)(2,1)}, u32[]{:S(2)}, u32[]{:S(2)}) collective-permute-start(bf16[256,2176]{0,1:T(8,128)(2,1)S(1)} %copy-done.109), channel_id=1, source_target_pairs={{0,1},{1,0},{2,3},{3,2},{4,5},{5,4},{6,7},{7,6},{8,9},{9,8},{10,11... | collective-permute-start | bytes 3342344 | tf_op jit(solution)/shard_map/ppermute | solution.py:39
  964.5 25.7 %collective-permute-start.85 = (bf16[256,2176]{0,1:T(8,128)(2,1)S(1)}, bf16[256,2176]{0,1:T(8,128)(2,1)}, u32[]{:S(2)}, u32[]{:S(2)}) collective-permute-start(bf16[256,2176]{0,1:T(8,128)(2,1)S(1)} %add_convert_fusion.7), channel_id=1, source_target_pairs={{0,6},{2,0},{4,2},{6,4},{1,7},{3,1},{5,3},{7,5},{8,14},{10,8},{12,... | collective-permute-start | bytes 3342344 | tf_op jit(solution)/shard_map/ppermute | solution.py:39
  970.2 30.1 %collective-permute-start.141 = (bf16[2,256,2048]{2,1,0:T(8,128)(2,1)S(1)}, bf16[2,256,2048]{2,1,0:T(8,128)(2,1)}, u32[]{:S(2)}, u32[]{:S(2)}) collective-permute-start(bf16[2,256,2048]{2,1,0:T(8,128)(2,1)S(1)} %get-tuple-element.148), channel_id=1, source_target_pairs={{0,8},{8,0},{1,9},{9,1},{2,10},{10,2},{3,11},{11,3},{4,12},{12,4},... | collective-permute-start | bytes 6291464 | tf_op jit(solution)/shard_map/ppermute | solution.py:39
  974.3 119.7 %collective-permute-start.137 = (bf16[2,512,1024]{2,1,0:T(8,128)(2,1)}, bf16[2,512,1024]{2,1,0:T(8,128)(2,1)}, u32[]{:S(2)}, u32[]{:S(2)}) collective-permute-start(bf16[2,512,1024]{2,1,0:T(8,128)(2,1)} %get-tuple-element.149), channel_id=1, source_target_pairs={{0,8},{8,0},{1,9},{9,1},{2,10},{10,2},{3,11},{11,3},{4,12},{12,4},... | collective-permute-start | bytes 6291464 | tf_op jit(solution)/shard_map/ppermute | solution.py:39
  1007.4 108.0 %collective-permute-start.134 = (bf16[2,512,1024]{2,1,0:T(8,128)(2,1)}, bf16[2,512,1024]{2,1,0:T(8,128)(2,1)}, u32[]{:S(2)}, u32[]{:S(2)}) collective-permute-start(bf16[2,512,1024]{2,1,0:T(8,128)(2,1)} %get-tuple-element.151), channel_id=1, source_target_pairs={{0,8},{8,0},{1,9},{9,1},{2,10},{10,2},{3,11},{11,3},{4,12},{12,4},... | collective-permute-start | bytes 6291464 | tf_op jit(solution)/shard_map/ppermute | solution.py:39
  1013.6 48.9 %collective-permute-start.142 = (bf16[2,256,2048]{2,1,0:T(8,128)(2,1)}, bf16[2,256,2048]{2,1,0:T(8,128)(2,1)}, u32[]{:S(2)}, u32[]{:S(2)}) collective-permute-start(bf16[2,256,2048]{2,1,0:T(8,128)(2,1)} %add_convert_fusion.4), channel_id=1, source_target_pairs={{0,16},{16,0},{1,17},{17,1},{2,18},{18,2},{3,19},{19,3},{4,20},{20... | collective-permute-start | bytes 6291464 | tf_op jit(solution)/shard_map/ppermute | solution.py:39
  1015.8 91.7 %collective-permute-start.139 = (bf16[2,512,1024]{2,1,0:T(8,128)(2,1)}, bf16[2,512,1024]{2,1,0:T(8,128)(2,1)}, u32[]{:S(2)}, u32[]{:S(2)}) collective-permute-start(bf16[2,512,1024]{2,1,0:T(8,128)(2,1)} %add_convert_fusion.5), channel_id=1, source_target_pairs={{0,16},{16,0},{1,17},{17,1},{2,18},{18,2},{3,19},{19,3},{4,20},{20... | collective-permute-start | bytes 6291464 | tf_op jit(solution)/shard_map/ppermute | solution.py:39
  1052.9 96.6 %collective-permute-start.136 = (bf16[2,512,1024]{2,1,0:T(8,128)(2,1)}, bf16[2,512,1024]{2,1,0:T(8,128)(2,1)}, u32[]{:S(2)}, u32[]{:S(2)}) collective-permute-start(bf16[2,512,1024]{2,1,0:T(8,128)(2,1)} %add_convert_fusion.6), channel_id=1, source_target_pairs={{0,16},{16,0},{1,17},{17,1},{2,18},{18,2},{3,19},{19,3},{4,20},{20... | collective-permute-start | bytes 6291464 | tf_op jit(solution)/shard_map/ppermute | solution.py:39
  1092.4 57.9 %collective-permute-start.113 = (bf16[64,3200]{1,0:T(8,128)(2,1)}, bf16[64,3200]{1,0:T(8,128)(2,1)S(1)}, u32[]{:S(2)}, u32[]{:S(2)}) collective-permute-start(bf16[64,3200]{1,0:T(8,128)(2,1)} %get-tuple-element.111), channel_id=1, source_target_pairs={{0,1},{1,0},{2,3},{3,2},{4,5},{5,4},{6,7},{7,6},{8,9},{9,8},{10,11... | collective-permute-start | bytes 1228808 | tf_op jit(solution)/shard_map/ppermute | solution.py:39
  1093.9 57.6 %collective-permute-start.110 = (bf16[64,3200]{1,0:T(8,128)(2,1)}, bf16[64,3200]{1,0:T(8,128)(2,1)S(1)}, u32[]{:S(2)}, u32[]{:S(2)}) collective-permute-start(bf16[64,3200]{1,0:T(8,128)(2,1)} %get-tuple-element.113), channel_id=1, source_target_pairs={{0,1},{1,0},{2,3},{3,2},{4,5},{5,4},{6,7},{7,6},{8,9},{9,8},{10,11... | collective-permute-start | bytes 1228808 | tf_op jit(solution)/shard_map/ppermute | solution.py:39
  1107.5 44.9 %collective-permute-start.107 = (bf16[64,3200]{1,0:T(8,128)(2,1)}, bf16[64,3200]{1,0:T(8,128)(2,1)}, u32[]{:S(2)}, u32[]{:S(2)}) collective-permute-start(bf16[64,3200]{1,0:T(8,128)(2,1)} %get-tuple-element.115), channel_id=1, source_target_pairs={{0,1},{1,0},{2,3},{3,2},{4,5},{5,4},{6,7},{7,6},{8,9},{9,8},{10,11... | collective-permute-start | bytes 1228808 | tf_op jit(solution)/shard_map/ppermute | solution.py:39
  1115.4 43.8 %collective-permute-start.104 = (bf16[64,3200]{1,0:T(8,128)(2,1)}, bf16[64,3200]{1,0:T(8,128)(2,1)S(1)}, u32[]{:S(2)}, u32[]{:S(2)}) collective-permute-start(bf16[64,3200]{1,0:T(8,128)(2,1)} %get-tuple-element.117), channel_id=1, source_target_pairs={{0,1},{1,0},{2,3},{3,2},{4,5},{5,4},{6,7},{7,6},{8,9},{9,8},{10,11... | collective-permute-start | bytes 1228808 | tf_op jit(solution)/shard_map/ppermute | solution.py:39
  1151.5 26.0 %collective-permute-start.92 = (bf16[64,3200]{1,0:T(8,128)(2,1)S(1)}, bf16[64,3200]{1,0:T(8,128)(2,1)S(1)}, u32[]{:S(2)}, u32[]{:S(2)}) collective-permute-start(bf16[64,3200]{1,0:T(8,128)(2,1)S(1)} %copy-done.117), channel_id=1, source_target_pairs={{0,16},{16,0},{1,17},{17,1},{2,18},{18,2},{3,19},{19,3},{4,20},{20... | collective-permute-start | bytes 1228808 | tf_op jit(solution)/shard_map/ppermute | solution.py:39
  1152.3 31.2 %collective-permute-start.89 = (bf16[64,3200]{1,0:T(8,128)(2,1)S(1)}, bf16[64,3200]{1,0:T(8,128)(2,1)S(1)}, u32[]{:S(2)}, u32[]{:S(2)}) collective-permute-start(bf16[64,3200]{1,0:T(8,128)(2,1)S(1)} %get-tuple-element.124), channel_id=1, source_target_pairs={{0,16},{16,0},{1,17},{17,1},{2,18},{18,2},{3,19},{19,3},{4,20},{20... | collective-permute-start | bytes 1228808 | tf_op jit(solution)/shard_map/ppermute | solution.py:39
  1159.2 34.5 %collective-permute-start.112 = (bf16[64,3200]{1,0:T(8,128)(2,1)}, bf16[64,3200]{1,0:T(8,128)(2,1)S(1)}, u32[]{:S(2)}, u32[]{:S(2)}) collective-permute-start(bf16[64,3200]{1,0:T(8,128)(2,1)} %get-tuple-element.112), channel_id=1, source_target_pairs={{0,1},{1,0},{2,3},{3,2},{4,5},{5,4},{6,7},{7,6},{8,9},{9,8},{10,11... | collective-permute-start | bytes 1228808 | tf_op jit(solution)/shard_map/ppermute | solution.py:39
  1191.7 40.0 %collective-permute-start.128 = (bf16[64,2048]{1,0:T(8,128)(2,1)S(1)}, bf16[64,2048]{1,0:T(8,128)(2,1)S(1)}, u32[]{:S(2)}, u32[]{:S(2)}) collective-permute-start(bf16[64,2048]{1,0:T(8,128)(2,1)S(1)} %get-tuple-element.163), channel_id=1, source_target_pairs={{0,1},{1,0},{2,3},{3,2},{4,5},{5,4},{6,7},{7,6},{8,9},{9,8},{10,11... | collective-permute-start | bytes 786440 | tf_op jit(solution)/shard_map/ppermute | solution.py:39
  1194.2 24.9 %collective-permute-start.120 = (bf16[64,2048]{1,0:T(8,128)(2,1)S(1)}, bf16[64,2048]{1,0:T(8,128)(2,1)S(1)}, u32[]{:S(2)}, u32[]{:S(2)}) collective-permute-start(bf16[64,2048]{1,0:T(8,128)(2,1)S(1)} %get-tuple-element.168), channel_id=1, source_target_pairs={{0,1},{1,0},{2,3},{3,2},{4,5},{5,4},{6,7},{7,6},{8,9},{9,8},{10,11... | collective-permute-start | bytes 786440 | tf_op jit(solution)/shard_map/ppermute | solution.py:39
  1199.4 28.5 %collective-permute-start.109 = (bf16[64,3200]{1,0:T(8,128)(2,1)S(1)}, bf16[64,3200]{1,0:T(8,128)(2,1)S(1)}, u32[]{:S(2)}, u32[]{:S(2)}) collective-permute-start(bf16[64,3200]{1,0:T(8,128)(2,1)S(1)} %copy-done.116), channel_id=1, source_target_pairs={{0,1},{1,0},{2,3},{3,2},{4,5},{5,4},{6,7},{7,6},{8,9},{9,8},{10,11... | collective-permute-start | bytes 1228808 | tf_op jit(solution)/shard_map/ppermute | solution.py:39
  1240.3 56.8 %collective-permute-start.119 = (bf16[64,2048]{1,0:T(8,128)(2,1)S(1)}, bf16[64,2048]{1,0:T(8,128)(2,1)S(1)}, u32[]{:S(2)}, u32[]{:S(2)}) collective-permute-start(bf16[64,2048]{1,0:T(8,128)(2,1)S(1)} %get-tuple-element.161), channel_id=1, source_target_pairs={{0,1},{1,0},{2,3},{3,2},{4,5},{5,4},{6,7},{7,6},{8,9},{9,8},{10,11... | collective-permute-start | bytes 786440 | tf_op jit(solution)/shard_map/ppermute | solution.py:39
  1246.1 31.2 %collective-permute-start.122 = (bf16[64,2048]{1,0:T(8,128)(2,1)S(1)}, bf16[64,2048]{1,0:T(8,128)(2,1)S(1)}, u32[]{:S(2)}, u32[]{:S(2)}) collective-permute-start(bf16[64,2048]{1,0:T(8,128)(2,1)S(1)} %get-tuple-element.167), channel_id=1, source_target_pairs={{0,1},{1,0},{2,3},{3,2},{4,5},{5,4},{6,7},{7,6},{8,9},{9,8},{10,11... | collective-permute-start | bytes 786440 | tf_op jit(solution)/shard_map/ppermute | solution.py:39
  1268.2 29.3 %collective-permute-start.121 = (bf16[64,2048]{1,0:T(8,128)(2,1)S(1)}, bf16[64,2048]{1,0:T(8,128)(2,1)S(1)}, u32[]{:S(2)}, u32[]{:S(2)}) collective-permute-start(bf16[64,2048]{1,0:T(8,128)(2,1)S(1)} %get-tuple-element.169), channel_id=1, source_target_pairs={{0,16},{16,0},{1,17},{17,1},{2,18},{18,2},{3,19},{19,3},{4,20},{20... | collective-permute-start | bytes 786440 | tf_op jit(solution)/shard_map/ppermute | solution.py:39
  (262 other events, 5401.0 us)

commit v3 on v2

--- a/solution.py
+++ b/solution.py
@@ -34,9 +34,23 @@
     return lax.dot_general(left, right, (((1,), (1,)), ((), ())), preferred_element_type=F32)
 
 
+def tied(values, others):
+    return lax.optimization_barrier((values, others))[0]
+
+
+def ring_place(axis, at):
+    return at ^ (at >> 1) if axis == "z" and lax.axis_size(axis) == 4 else at
+
+
 def shift(value, axis, step):
     size = lax.axis_size(axis)
-    return lax.ppermute(value, axis, [(i, (i + step) % size) for i in range(size)])
+    pairs = [(ring_place(axis, i), ring_place(axis, (i + step) % size)) for i in range(size)]
+    return lax.ppermute(value, axis, pairs)
+
+
+def came_from(axis, k):
+    at = ring_place(axis, lax.axis_index(axis))
+    return ring_place(axis, jnp.mod(at - k, lax.axis_size(axis)))
 
 
 def gather_blocks(block, order):
@@ -58,44 +72,83 @@
             return part(key)
         axis = order[depth]
         size = lax.axis_size(axis)
-        total = reduce_from(key + (size - 1,), depth + 1)
-        for k in reversed(range(size - 1)):
-            arrived = shift(total.astype(BF), axis, -1)
+        total = reduce_from(key + (1,), depth + 1)
+        for k in [*range(2, size), 0]:
+            arrived = shift(total.astype(BF), axis, 1)
             total = reduce_from(key + (k,), depth + 1).astype(F32) + arrived.astype(F32)
         return total
 
     return reduce_from((), 0)
 
 
-def place_kernel(count, row_axis, rows, offsets_ref, *refs):
-    blocks, out, sems = refs[:count], refs[count], refs[count + 1]
+def gather_pieces(block, order, merges):
+    held = [(block, [()])]
+    for depth, axis in enumerate(order):
+        grown, level = [], held
+        for k in range(lax.axis_size(axis)):
+            if k:
+                level = [(shift(value, axis, 1), keys) for value, keys in level]
+            grown += [(value, [key + (k,) for key in keys]) for value, keys in level]
+        if depth < len(merges):
+            size = max(1, len(grown) // merges[depth])
+            grown = [grown[i : i + size] for i in range(0, len(grown), size)]
+            grown = [
+                (
+                    jnp.concatenate([value for value, _ in some], axis=0),
+                    [key for _, keys in some for key in keys],
+                )
+                for some in grown
+            ]
+        held = grown
+    return held
+
+
+def reduce_axis(value, axis, dim):
+    def part(k):
+        return lax.dynamic_index_in_dim(value, came_from(axis, k), dim, keepdims=False)
+
+    total = part(1)
+    for k in [*range(2, lax.axis_size(axis)), 0]:
+        arrived = shift(total.astype(BF), axis, 1)
+        total = part(k).astype(F32) + arrived.astype(F32)
+    return total
+
+
+def place_kernel(plan, rows, offsets_ref, *refs):
+    blocks, out, sems = refs[:-2], refs[-2], refs[-1]
     copies = []
-    for i in range(count):
+    for i, (array, sub, column, width) in enumerate(plan):
         start = pl.multiple_of(offsets_ref[i], 16)
-        window = pl.ds(start, rows)
-        target = out.at[window] if row_axis == 0 else out.at[:, window]
-        copies.append(pltpu.make_async_copy(blocks[i], target, sems.at[i]))
+        copies.append(
+            pltpu.make_async_copy(
+                blocks[array].at[sub * rows : (sub + 1) * rows],
+                out.at[pl.ds(start, rows), column : column + width],
+                sems.at[i],
+            )
+        )
     for copy in copies:
         copy.start()
     for copy in copies:
         copy.wait()
 
 
-def place(blocks, offsets, row_axis):
-    shape = list(blocks[0].shape)
-    rows = shape[row_axis]
-    shape[row_axis] = rows * len(blocks)
+def place(pieces, rows, shape):
+    plan, offsets = [], []
+    for array, (value, starts, column) in enumerate(pieces):
+        for sub, start in enumerate(starts):
+            plan.append((array, sub, column, value.shape[1]))
+            offsets.append(start)
     return pl.pallas_call(
-        functools.partial(place_kernel, len(blocks), row_axis, rows),
-        out_shape=jax.ShapeDtypeStruct(tuple(shape), blocks[0].dtype),
+        functools.partial(place_kernel, plan, rows),
+        out_shape=jax.ShapeDtypeStruct(shape, BF),
         grid_spec=pltpu.PrefetchScalarGridSpec(
             num_scalar_prefetch=1,
-            in_specs=[pl.BlockSpec(memory_space=pl.ANY)] * len(blocks),
+            in_specs=[pl.BlockSpec(memory_space=pl.ANY)] * len(pieces),
             out_specs=pl.BlockSpec(memory_space=pltpu.VMEM),
-            scratch_shapes=[pltpu.SemaphoreType.DMA((len(blocks),))],
+            scratch_shapes=[pltpu.SemaphoreType.DMA((len(plan),))],
         ),
         compiler_params=pltpu.CompilerParams(vmem_limit_bytes=24 << 20),
-    )(jnp.stack(offsets).astype(jnp.int32), *blocks)
+    )(jnp.stack(offsets).astype(jnp.int32), *[value for value, _, _ in pieces])
 
 
 def rope_tables(row_count):
@@ -206,6 +259,7 @@
             out_specs=pl.BlockSpec((rows, width), lambda s, n: (s, 0)),
         ),
         compiler_params=pltpu.CompilerParams(vmem_limit_bytes=32 << 20),
+        cost_estimate=pl.CostEstimate(flops=14 * 10**9, bytes_accessed=14 << 20, transcendentals=0),
     )(lengths, qkv, gains, cosine, sine)
 
 
@@ -236,7 +290,227 @@
             ),
         ),
         compiler_params=pltpu.CompilerParams(vmem_limit_bytes=32 << 20),
+        cost_estimate=pl.CostEstimate(flops=20 * 10**9, bytes_accessed=20 << 20, transcendentals=0),
     )(lengths, qkv, mixed_grad, gains, cosine, sine)
+
+
+TILE = 256
+
+
+def experts_kernel(sizes, places_ref, *refs):
+    part, groups, rows, experts, slots, local, ff = sizes
+    take = iter(refs)
+    row_refs = [next(take) for _ in range(groups)]
+    cots_ref = next(take)
+    weight_refs = [next(take) for _ in range(3)]
+    if part:
+        for _ in range(5):
+            next(take)
+    combined_refs = [next(take) for _ in range(groups)]
+    back_refs = [next(take) for _ in range(groups)]
+    kept_refs = [next(take) for _ in range(5)]
+    (rows_v, cots_v, gate_v, up_v, down_v, sent_v, grad_v, active_v, gate_grad_v, up_grad_v) = (
+        next(take) for _ in range(10)
+    )
+    (cot_slots_v, returned_v, sent_grad_v, rank_v, prob_v, onehot_v, gated_v, sum_v) = (
+        next(take) for _ in range(8)
+    )
+    in_sems, weight_sems, out_sems = (next(take) for _ in range(3))
+    own = row_refs[0].shape[0]
+    batches = own // rows
+    sequences = groups * batches
+    count = sequences * slots
+    first = places_ref[0]
+
+    loads = []
+    for i in range(groups):
+        loads.append(pltpu.make_async_copy(row_refs[i], rows_v.at[i], in_sems.at[2 * i]))
+        start = pl.multiple_of(places_ref[1 + i], 16)
+        loads.append(
+            pltpu.make_async_copy(
+                cots_ref.at[pl.ds(start, own)], cots_v.at[i], in_sems.at[2 * i + 1]
+            )
+        )
+    for copy in loads:
+        copy.start()
+    weight_loads = [[] for _ in range(local)]
+    for j in range(local):
+        for w, target in enumerate((gate_v, up_v, down_v)):
+            copy = pltpu.make_async_copy(
+                weight_refs[w].at[j], target.at[j], weight_sems.at[j * 3 + w]
+            )
+            copy.start()
+            weight_loads[j].append(copy)
+    for copy in loads:
+        copy.wait()
+
+    slot = lax.broadcasted_iota(jnp.int32, (slots, rows), 0).astype(F32)
+    for q in range(sequences):
+        i, lo = q // batches, (q % batches) * rows
+        rank_v[q] = cots_v[i, lo : lo + rows, D:].astype(F32).T
+        prob_v[q] = rows_v[i, lo : lo + rows, D:].astype(F32).T
+        onehots, gates = [], []
+        for j in range(local):
+            rank = rank_v[q, pl.ds(first + j, 1), :]
+            prob = (
+                prob_v[q, pl.ds(first + j, 1), :]
+                + prob_v[q, pl.ds(experts + first + j, 1), :]
+                + prob_v[q, pl.ds(2 * experts + first + j, 1), :]
+            )
+            chosen = rank == slot
+            gated = jnp.where(chosen, prob, 0.0)
+            onehot = jnp.where(chosen, 1.0, 0.0).astype(BF)
+            onehot_v[q, j * slots : (j + 1) * slots, :] = onehot
+            gated_v[q, j * slots : (j + 1) * slots, :] = gated.astype(BF)
+            gates.append(jnp.sum(gated, axis=1, keepdims=True))
+        gate_slots = jnp.concatenate(gates, axis=0)
+        onehots = onehot_v[q]
+
+        @pl.loop(0, D // TILE)
+        def _(n):
+            at = pl.ds(pl.multiple_of(n * TILE, TILE), TILE)
+            sent = plain(onehots, rows_v[i, lo : lo + rows, at]).astype(BF)
+            cots = plain(onehots, cots_v[i, lo : lo + rows, at])
+            grads = (cots * gate_slots).astype(BF)
+            cots = cots.astype(BF)
+            for j in range(local):
+                window = slice(j * slots, (j + 1) * slots)
+                place = slice(q * slots, (q + 1) * slots)
+                sent_v[j, place, at] = sent[window]
+                cot_slots_v[j, place, at] = cots[window]
+                grad_v[j, place, at] = grads[window]
+
+    stores = []
+
+    def store(index, source, j):
+        target = kept_refs[index].at[j, pl.ds(part * count, count)]
+        copy = pltpu.make_async_copy(source.at[j], target, out_sems.at[index * local + j])
+        copy.start()
+        stores.append(copy)
+
+    for j in range(local):
+        store(0, sent_v, j)
+        store(1, grad_v, j)
+    for j in range(local):
+        for copy in weight_loads[j]:
+            copy.wait()
+
+        @pl.loop(0, ff // TILE)
+        def _(n):
+            at = pl.ds(pl.multiple_of(n * TILE, TILE), TILE)
+            gate_hidden = plain(sent_v[j], gate_v[j, :, at])
+            up_hidden = plain(sent_v[j], up_v[j, :, at])
+            active_grad = times_t(grad_v[j], down_v[j, at, :])
+            sigmoid = jax.nn.sigmoid(gate_hidden)
+            silu = gate_hidden * sigmoid
+            active_v[j, :, at] = (silu * up_hidden).astype(BF)
+            gate_grad_v[j, :, at] = (
+                active_grad * up_hidden * sigmoid * (1.0 + gate_hidden * (1.0 - sigmoid))
+            ).astype(BF)
+            up_grad_v[j, :, at] = (active_grad * silu).astype(BF)
+
+        store(2, active_v, j)
+        store(3, gate_grad_v, j)
+        store(4, up_grad_v, j)
+        sum_v[j] = jnp.zeros_like(sum_v[j])
+
+        @pl.loop(0, D // TILE)
+        def _(n):
+            at = pl.ds(pl.multiple_of(n * TILE, TILE), TILE)
+            returned = plain(active_v[j], down_v[j, :, at]).astype(BF)
+            returned_v[j, :, at] = returned
+            product = cot_slots_v[j, :, at].astype(F32) * returned.astype(F32)
+            folded = product[:, :128]
+            for m in range(1, TILE // 128):
+                folded = folded + product[:, m * 128 : (m + 1) * 128]
+            sum_v[j] += folded
+            sent_grad = times_t(gate_grad_v[j], gate_v[j, at, :])
+            sent_grad = sent_grad + times_t(up_grad_v[j], up_v[j, at, :])
+            sent_grad_v[j, :, at] = sent_grad.astype(BF)
+
+    column = lax.broadcasted_iota(jnp.int32, (EXTRA, rows), 0)
+    for q in range(sequences):
+        i, lo = q // batches, (q % batches) * rows
+        place = slice(q * slots, (q + 1) * slots)
+        table = jnp.zeros((EXTRA, rows), F32)
+        for j in range(local):
+            gates_grad = jnp.sum(sum_v[j, place, :], axis=1, keepdims=True)
+            onehot = onehot_v[q, j * slots : (j + 1) * slots, :].astype(F32)
+            value = jnp.sum(onehot * gates_grad, axis=0, keepdims=True)
+            for m in range(3):
+                high = value.astype(BF).astype(F32)
+                table = table + jnp.where(column == m * experts + first + j, high, 0.0)
+                value = value - high
+        back_refs[i][lo : lo + rows, D:] = table.T.astype(BF)
+        onehots, gates = onehot_v[q], gated_v[q]
+
+        @pl.loop(0, D // TILE)
+        def _(n):
+            at = pl.ds(pl.multiple_of(n * TILE, TILE), TILE)
+            returned = jnp.concatenate([returned_v[j, place, at] for j in range(local)], axis=0)
+            sent_grad = jnp.concatenate([sent_grad_v[j, place, at] for j in range(local)], axis=0)
+            combined_refs[i][lo : lo + rows, at] = inner(gates, returned).astype(BF)
+            back_refs[i][lo : lo + rows, at] = inner(onehots, sent_grad).astype(BF)
+
+    for copy in stores:
+        copy.wait()
+
+
+def run_experts(
+    places, row_blocks, cots, weights, kept, part, parts, experts, rows, capacity
+):
+    groups = len(row_blocks)
+    own = row_blocks[0].shape[0]
+    sequences = groups * (own // rows)
+    slots = (capacity + 15) // 16 * 16
+    count = sequences * slots
+    local, _, ff = weights[0].shape
+    any_space = pl.BlockSpec(memory_space=pl.ANY)
+    in_vmem = pl.BlockSpec(memory_space=pltpu.VMEM)
+    widths = (D, D, ff, ff, ff)
+    operands = [*row_blocks, cots, *weights]
+    aliases = {}
+    if kept is not None:
+        aliases = {1 + len(operands) + i: 2 * groups + i for i in range(5)}
+        operands = operands + list(kept)
+    scratch = [
+        pltpu.VMEM((groups, own, D + EXTRA), BF),
+        pltpu.VMEM((groups, own, D + EXTRA), BF),
+        *[pltpu.VMEM(w.shape, BF) for w in weights],
+        *[pltpu.VMEM((local, count, w), BF) for w in widths],
+        pltpu.VMEM((local, count, D), BF),
+        pltpu.VMEM((local, count, D), BF),
+        pltpu.VMEM((local, count, D), BF),
+        pltpu.VMEM((sequences, EXTRA, rows), F32),
+        pltpu.VMEM((sequences, EXTRA, rows), F32),
+        pltpu.VMEM((sequences, local * slots, rows), BF),
+        pltpu.VMEM((sequences, local * slots, rows), BF),
+        pltpu.VMEM((local, count, 128), F32),
+        pltpu.SemaphoreType.DMA((2 * groups,)),
+        pltpu.SemaphoreType.DMA((3 * local,)),
+        pltpu.SemaphoreType.DMA((5 * local,)),
+    ]
+    sizes = (part, groups, rows, experts, slots, local, ff)
+    results = pl.pallas_call(
+        functools.partial(experts_kernel, sizes),
+        out_shape=(
+            *[jax.ShapeDtypeStruct((own, D), BF)] * groups,
+            *[jax.ShapeDtypeStruct((own, D + EXTRA), BF)] * groups,
+            *[jax.ShapeDtypeStruct((local, parts * count, w), BF) for w in widths],
+        ),
+        grid_spec=pltpu.PrefetchScalarGridSpec(
+            num_scalar_prefetch=1,
+            in_specs=[any_space] * len(operands),
+            out_specs=(*[in_vmem] * (2 * groups), *[any_space] * 5),
+            scratch_shapes=scratch,
+        ),
+        input_output_aliases=aliases,
+        compiler_params=pltpu.CompilerParams(vmem_limit_bytes=60 << 20),
+        cost_estimate=pl.CostEstimate(
+            flops=40 * local * count * D * ff, bytes_accessed=40 << 20, transcendentals=0
+        ),
+    )(places, *operands)
+    return results[:groups], results[groups : 2 * groups], results[2 * groups :]
 
 
 def norm_back(grad, unit, scale, gain):
@@ -304,26 +578,28 @@
     y, c, z, x = (lax.axis_index(name) for name in ("y", "c", "z", "x"))
     shard_rows = query_weight.shape[0]
     head_shard = query_gain.shape[0]
-    heads = HEADS // 2
+    heads = HEADS // (2 * xs)
     width = heads * HD
+    half_width = D // 2
     chunk = D // (2 * ys)
 
     def swap(value):
         return lax.ppermute(value, "c", [(0, 1), (1, 0)])
 
-    def half_columns(weight, core):
-        return jnp.concatenate(
-            [
-                lax.dynamic_slice_in_dim(weight, (2 * i + core) * chunk, chunk, 1)
-                for i in range(ys)
-            ],
-            axis=1,
-        )
+    def sent_along(axis, piece_for):
+        at, size = lax.axis_index(axis), lax.axis_size(axis)
+        return [
+            shift(piece_for(jnp.mod(at + k, size)), axis, k) if k else piece_for(at)
+            for k in range(size)
+        ]
 
     token_rows = tokens.reshape(own, D)
-    both_tokens = jnp.concatenate([token_rows, swap(token_rows)], axis=0)
     length = lengths.reshape(batches)
-    both_lengths = jnp.concatenate([length, swap(length)])
+    group_keys = [(kx, kc) for kx in range(xs) for kc in range(2)]
+    held = gather_blocks(token_rows, ("x", "c"))
+    group_tokens = jnp.concatenate([held[key] for key in group_keys], axis=0)
+    held = gather_blocks(length, ("x", "c"))
+    group_lengths = jnp.concatenate([held[key] for key in group_keys])
     extra = jnp.concatenate(
         [
             attn_gain[:, None],
@@ -336,48 +612,67 @@
     )
     extra = widen(extra, EXTRA)
 
-    def packed(core):
+    def row_offset(ky, kc, kz, kx):
+        sources = (came_from("y", ky), came_from("c", kc), came_from("z", kz), came_from("x", kx))
+        return (
+            ((sources[0] * 2 + sources[1]) * zs + sources[2]) * xs + sources[3]
+        ) * shard_rows
+
+    def half_columns(weight, core):
         return jnp.concatenate(
-            [half_columns(w, core) for w in (query_weight, key_weight, value_weight)] + [extra],
+            [
+                lax.dynamic_slice_in_dim(weight, (2 * i + core) * chunk, chunk, 1)
+                for i in range(ys)
+            ],
             axis=1,
         )
 
-    mine, theirs = packed(c), swap(packed(1 - c))
-    first = jnp.where(c == 0, mine, theirs)
-    second = jnp.where(c == 0, theirs, mine)
-
-    def row_block(key, order, core):
-        at = dict(zip(order, key, strict=True))
-        ky = jnp.mod(y - at["y"], ys)
-        kz = jnp.mod(z - at["z"], zs)
-        kx = jnp.mod(x - at["x"], xs)
-        if core is None:
-            return (ky * zs + kz) * xs + kx
-        return ((ky * 2 + core) * zs + kz) * xs + kx
-
-    ZXY, ZYX = ("z", "x", "y"), ("z", "y", "x")
-    blocks, offsets = [], []
-    for core, order, block in ((0, ZXY, first), (1, ZYX, second)):
-        for key, value in gather_blocks(block, order).items():
-            blocks.append(value)
-            offsets.append(row_block(key, order, core) * shard_rows)
-    qkv_weight = place(blocks, offsets, 0)
-    blocks, offsets = [], []
-    for key, value in gather_blocks(output_weight, ZYX).items():
-        blocks.append(value)
-        offsets.append(row_block(key, ZYX, None) * shard_rows)
-    out_weight = place(blocks, offsets, 0)
-
-    full_experts = []
-    for weight in (gate_weight, up_weight, down_weight):
-        blocks, offsets = [], []
-        for key, value in gather_blocks(weight, ("y", "c")).items():
-            blocks.append(value)
-            offsets.append(
-                (jnp.mod(y - key[0], ys) * 2 + jnp.mod(c - key[1], 2)) * weight.shape[1]
-            )
-        full_experts.append(place(blocks, offsets, 1))
-    gate_full, up_full, down_full = full_experts
+    def packed(core):
+        halves = [half_columns(w, core) for w in (query_weight, key_weight, value_weight)]
+        return jnp.stack(
+            [
+                jnp.concatenate(
+                    [half[:, i * width : (i + 1) * width] for half in halves] + [extra], axis=1
+                )
+                for i in range(xs)
+            ]
+        )
+
+    block = jnp.concatenate(sent_along("c", packed), axis=1)
+    block = jnp.concatenate(
+        sent_along("x", lambda i: lax.dynamic_index_in_dim(block, i, 0, keepdims=False)), axis=0
+    )
+    block = jnp.concatenate(list(gather_blocks(block, ("y",)).values()), axis=0)
+    out_blocks = gather_blocks(output_weight, ("z",))
+    out_rows = jnp.concatenate(list(out_blocks.values()), axis=0)
+    block = tied(block, out_rows)
+    qkv_pieces, hops = [], []
+    for (kz,), value in gather_blocks(block, ("z",)).items():
+        starts = [
+            row_offset(ky, kc, kz, kx)
+            for ky in range(ys)
+            for kx in range(xs)
+            for kc in range(2)
+        ]
+        qkv_pieces.append((value, starts, 0))
+        hops.append(value)
+    qkv_weight = place(qkv_pieces, shard_rows, (D, 3 * width + EXTRA))
+    out_rows = jnp.concatenate(list(gather_blocks(out_rows, ("y",)).values()), axis=0)
+    out_pieces = []
+    for (kx,), value in gather_blocks(out_rows, ("x",)).items():
+        starts = [
+            ((came_from("y", ky) * zs + came_from("z", kz)) * xs + came_from("x", kx)) * shard_rows
+            for ky in range(ys)
+            for kz in range(zs)
+        ]
+        out_pieces.append((value, starts, 0))
+    out_weight = place(out_pieces, shard_rows, (half_width, D))
+    ZX = ("z", "x")
+
+    weights = [
+        lax.all_gather(w, ("y", "c"), axis=1, tiled=True)
+        for w in (gate_weight, up_weight, down_weight)
+    ]
 
     ranks = jnp.concatenate(
         [
@@ -387,10 +682,8 @@
         axis=0,
     )
     cotangent = out_cotangent.reshape(own, D)
-    ZX = ("z", "x")
-    cot_blocks = gather_blocks(
-        jnp.concatenate([cotangent, widen(ranks.astype(BF), EXTRA)], axis=1), ZX
-    )
+    cot_rows = jnp.concatenate([cotangent, widen(ranks.astype(BF), EXTRA)], axis=1)
+    all_cots = lax.all_gather(tied(cot_rows, hops[1]), ZX, axis=0, tiled=True)
 
     small = qkv_weight[:, 3 * width :].astype(F32)
     qkv_weight = qkv_weight[:, : 3 * width]
@@ -401,12 +694,20 @@
     head_gains = jnp.stack(
         [per_device[:, :, 2 + experts].reshape(HD), per_device[:, :, 3 + experts].reshape(HD)]
     )
-    tokens_f = both_tokens.astype(F32)
+    tokens_f = group_tokens.astype(F32)
     token_scale = lax.rsqrt(jnp.mean(tokens_f * tokens_f, axis=-1, keepdims=True) + EPSILON)
     normed = (tokens_f * token_scale * attn_gain_f).astype(BF)
     qkv = plain(normed, qkv_weight)
     cosine, sine = rope_tables(rows)
-    mixed = attend(qkv, both_lengths, head_gains, cosine, sine, rows, heads)
+    mixed = attend(qkv, group_lengths, head_gains, cosine, sine, rows, heads)
+    chip_rows = 2 * own
+    parts = [mixed[:chip_rows]]
+    for k in range(1, xs):
+        parts.append(shift(mixed[k * chip_rows : (k + 1) * chip_rows], "x", -k))
+    mixed = jnp.zeros((chip_rows, half_width), BF)
+    for k, part in enumerate(parts):
+        place_at = jnp.mod(x + k, xs) * width
+        mixed = lax.dynamic_update_slice(mixed, part, (0, place_at))
     partial = plain(mixed, out_weight)
     rows_f = token_rows.astype(F32)
     hidden = rows_f + (partial[:own] + swap(partial[own:]))
@@ -418,76 +719,58 @@
     row_blocks = gather_blocks(
         jnp.concatenate([routed_in, widen(in_three(gate_probs), EXTRA)], axis=1), ZX
     )
-    keys = list(row_blocks)
-    group = len(keys) * batches
-    all_rows = jnp.concatenate([row_blocks[k] for k in keys], axis=0)
-    all_cots = jnp.concatenate([cot_blocks[k] for k in keys], axis=0)
     first_expert = (z * xs + x) * local
-    all_probs = from_three(all_rows[:, D:], experts)
-    all_probs = lax.dynamic_slice_in_dim(all_probs, first_expert, local, 1)
-    all_ranks = lax.dynamic_slice_in_dim(all_cots[:, D:], first_expert, local, 1).astype(F32)
-    all_rows = all_rows[:, :D].reshape(group, rows, D)
-    all_cots = all_cots[:, :D].reshape(group, rows, D)
-    slot = jnp.arange(capacity, dtype=F32)[None, :, None]
-    combined = 0.0
-    routed_grad = 0.0
-    probs_grad = []
-    gate_grads, up_grads, down_grads = [], [], []
-    dispatch = (((2,), (1,)), ((0,), (0,)))
-    collect = (((1,), (1,)), ((0,), (0,)))
-    for j in range(local):
-        rank = all_ranks[:, j].reshape(group, 1, rows)
-        probs = all_probs[:, j].reshape(group, 1, rows)
-        chosen = rank == slot
-        onehot = chosen.astype(BF)
-        gated = jnp.where(chosen, probs, 0.0)
-        gate_slot = jnp.sum(gated, axis=2, keepdims=True)
-        sent = lax.dot_general(onehot, all_rows, dispatch, preferred_element_type=F32)
-        sent = sent.astype(BF).reshape(group * capacity, D)
-        cot = lax.dot_general(onehot, all_cots, dispatch, preferred_element_type=F32)
-        returned_grad = (cot * gate_slot).astype(BF).reshape(group * capacity, D)
-        gate_hidden = plain(sent, gate_full[j])
-        up_hidden = plain(sent, up_full[j])
-        sigmoid = jax.nn.sigmoid(gate_hidden)
-        active = (gate_hidden * sigmoid * up_hidden).astype(BF)
-        returned = plain(active, down_full[j]).astype(BF).reshape(group, capacity, D)
-        combined = combined + lax.dot_general(
-            gated.astype(BF), returned, collect, preferred_element_type=F32
-        )
-        gates_grad = jnp.sum(cot * returned.astype(F32), axis=2, keepdims=True)
-        probs_grad.append(jnp.sum(jnp.where(chosen, gates_grad, 0.0), axis=1).reshape(-1, 1))
-        active_grad = times_t(returned_grad, down_full[j])
-        gate_hidden_grad = (
-            active_grad * up_hidden * sigmoid * (1.0 + gate_hidden * (1.0 - sigmoid))
-        ).astype(BF)
-        up_hidden_grad = (active_grad * gate_hidden * sigmoid).astype(BF)
-        sent_grad = times_t(gate_hidden_grad, gate_full[j]) + times_t(up_hidden_grad, up_full[j])
-        sent_grad = sent_grad.astype(BF).reshape(group, capacity, D)
-        routed_grad = routed_grad + lax.dot_general(
-            onehot, sent_grad, collect, preferred_element_type=F32
-        )
-        down_grads.append(inner(active, returned_grad))
-        gate_grads.append(inner(sent, gate_hidden_grad))
-        up_grads.append(inner(sent, up_hidden_grad))
-    expert_index = jnp.arange(experts)[None, :]
-    probs_part = sum(
-        jnp.where(expert_index == first_expert + j, probs_grad[j], 0.0) for j in range(local)
-    )
-    back = jnp.concatenate(
-        [
-            routed_grad.reshape(group * rows, D).astype(BF),
-            widen(in_three(probs_part), EXTRA),
-        ],
-        axis=1,
-    )
-    combined = combined.reshape(group * rows, D).astype(BF)
-
-    def part_of(array):
-        return lambda key: array[keys.index(key) * own : (keys.index(key) + 1) * own]
-
-    back = reduce_blocks(part_of(back), ZX)
-    combined = reduce_blocks(part_of(combined), ZX)
+    kept = None
+    per_call = math.gcd(xs, 2)
+    steps = [*range(1, zs), 0]
+    chains = [[], []]
+    arrived = [None, None]
+    for n, kz in enumerate(steps):
+        parts = [{}, {}]
+        for some in range(0, xs, per_call):
+            keys = [(kz, kx) for kx in range(some, some + per_call)]
+            places = [(came_from("z", kz) * xs + came_from("x", kx)) * own for kz, kx in keys]
+            places = [first_expert, *places]
+            blocks = [row_blocks[key] for key in keys]
+            if n >= 2:
+                blocks = tied(blocks, [chain[n - 2] for chain in chains])
+                if n >= 3:
+                    blocks = tied(blocks, arrived)
+            combined_part, back_part, kept = run_experts(
+                jnp.stack(places).astype(jnp.int32),
+                blocks,
+                all_cots,
+                weights,
+                kept,
+                (n * xs + some) // per_call,
+                zs * xs // per_call,
+                experts,
+                rows,
+                capacity,
+            )
+            parts[0].update(zip(keys, back_part, strict=True))
+            parts[1].update(zip(keys, combined_part, strict=True))
+        for i in range(2):
+            if n:
+                total = chains[i][n - 1]
+                if arrived[i] is not None:
+                    total = total + arrived[i].astype(F32)
+                arrived[i] = shift(total.astype(BF), "z", 1)
+            if kz == 0 and i == 1:
+                back = chains[0][n] + arrived[0].astype(F32)
+                parts[1] = tied(parts[1], back)
+            part = {(kx,): value for (kz, kx), value in parts[i].items()}
+            chains[i].append(reduce_blocks(part.get, ("x",)))
+    combined = chains[1][-1] + arrived[1].astype(F32)
     layer_out = (hidden + combined).astype(BF)
+    sent, returned_grad, active, gate_hidden_grad, up_hidden_grad = kept
+
+    def weight_grads(left, right):
+        return [inner(left[j], right[j]) for j in range(local)]
+
+    down_grads = weight_grads(active, returned_grad)
+    gate_grads = weight_grads(sent, gate_hidden_grad)
+    up_grads = weight_grads(sent, up_hidden_grad)
 
     probs_grad = from_three(back[:, D:], experts)
     logits_grad = (
@@ -502,12 +785,16 @@
     both_grads = jnp.concatenate([attn_out_grad, swap(attn_out_grad)], axis=0)
     mixed_grad = times_t(both_grads, out_weight).astype(BF)
     output_grad = inner(mixed, both_grads).astype(BF)
+    mixed_grad = jnp.concatenate(
+        sent_along("x", lambda i: lax.dynamic_slice_in_dim(mixed_grad, i * width, width, 1)), axis=0
+    )
     qkv_grad, head_gain_grads = attend_back(
-        qkv, mixed_grad, both_lengths, head_gains, cosine, sine, rows, heads
-    )
-    qkv_weight_grad = inner(normed, qkv_grad)
+        qkv, mixed_grad, group_lengths, head_gains, cosine, sine, rows, heads
+    )
     normed_part = times_t(qkv_grad, qkv_weight)
-    normed_grad = normed_part[:own] + swap(normed_part[own:])
+    normed_grad = reduce_blocks(
+        lambda key: normed_part[(key[0] * 2 + key[1]) * own :][:own], ("x", "c")
+    )
     token_unit = rows_f * token_scale[:own]
     tokens_add, attn_gain_grad = norm_back(normed_grad, token_unit, token_scale[:own], attn_gain_f)
     tokens_grad = hidden_grad + tokens_add
@@ -527,46 +814,44 @@
         axis=1,
     )
     qkv_weight_grad = jnp.concatenate(
-        [qkv_weight_grad.astype(BF), widen(small_grad, EXTRA).astype(BF)], axis=1
-    )
-
-    def rows_of(array, order, core):
-        return lambda key: lax.dynamic_slice_in_dim(
-            array, row_block(key, order, core) * shard_rows, shard_rows, 0
-        )
-
-    output_weight_grad = reduce_blocks(rows_of(output_grad, ZYX, None), ZYX)
-    first = reduce_blocks(rows_of(qkv_weight_grad, ZXY, 0), ZXY)
-    second = reduce_blocks(rows_of(qkv_weight_grad, ZYX, 1), ZYX)
-    mine = jnp.where(c == 0, first, second)
-    theirs = swap(jnp.where(c == 0, second, first).astype(BF)).astype(F32)
-    small_total = mine[:, 3 * width :] + theirs[:, 3 * width :]
-
-    def both_halves(at):
-        low = jnp.where(c == 0, mine, theirs)[:, at * width : (at + 1) * width]
-        high = jnp.where(c == 0, theirs, mine)[:, at * width : (at + 1) * width]
-        return jnp.stack(
-            [low.reshape(shard_rows, ys, chunk), high.reshape(shard_rows, ys, chunk)], axis=2
-        ).reshape(shard_rows, D)
+        [inner(normed, qkv_grad).astype(BF), widen(small_grad, EXTRA).astype(BF)], axis=1
+    )
+    output_grad = output_grad.reshape(ys, zs, xs, shard_rows, D)
+    output_weight_grad = reduce_axis(output_grad, "x", 2).astype(BF)
+    output_weight_grad = reduce_axis(output_weight_grad, "y", 0).astype(BF)
+    output_weight_grad = reduce_axis(output_weight_grad, "z", 0)
+    total = qkv_weight_grad.reshape(ys, 2, zs, xs, shard_rows, -1)
+    total = reduce_axis(total, "z", 2).astype(BF)
+    total = reduce_axis(total, "y", 0).astype(BF)
+    columns = sent_along("x", lambda i: lax.dynamic_index_in_dim(total, i, 1, keepdims=False))
+    columns = jnp.stack(columns)
+    columns = sent_along("c", lambda i: lax.dynamic_index_in_dim(columns, i, 1, keepdims=False))
+    small_total = sum(jnp.sum(some[:, :, 3 * width :].astype(F32), axis=0) for some in columns)
+
+    def all_heads(at):
+        halves = []
+        for some in columns:
+            half = jnp.zeros((shard_rows, half_width), BF)
+            for k in range(xs):
+                part = some[k][:, at * width : (at + 1) * width]
+                half = lax.dynamic_update_slice(half, part, (0, jnp.mod(x - k, xs) * width))
+            halves.append(half)
+        low = jnp.where(c == 0, halves[0], halves[1]).reshape(shard_rows, ys, chunk)
+        high = jnp.where(c == 0, halves[1], halves[0]).reshape(shard_rows, ys, chunk)
+        return jnp.stack([low, high], axis=2).reshape(shard_rows, D).astype(F32)
 
     def expert_total(parts):
         grad = jnp.stack(parts).astype(BF)
-        depth = grad.shape[1] // (2 * ys)
-
-        def part(key):
-            at = jnp.mod(y - key[0], ys) * 2 + jnp.mod(c - key[1], 2)
-            return lax.dynamic_slice_in_dim(grad, at * depth, depth, 1)
-
-        return reduce_blocks(part, ("y", "c")).astype(F32)
+        return lax.psum_scatter(grad, ("y", "c"), scatter_dimension=1, tiled=True).astype(F32)
 
     shape = (batches, 1, rows, D)
     return (
         layer_out.reshape(shape),
         tokens_grad.reshape(shape),
         small_total[:, 0],
-        both_halves(0),
-        both_halves(1),
-        both_halves(2),
+        all_heads(0),
+        all_heads(1),
+        all_heads(2),
         output_weight_grad,
         small_total[:head_shard, 2 + experts],
         small_total[:head_shard, 3 + experts],

time: 1360 us -> 1110 us (0.82)
  Pallas kernels: 51.6 us -> 241 us
  matrix products: 290 us -> 104 us
  local copies, waits for them, and re-layouts: 175 us -> 41.9 us
  starting transfers between devices: 180 us -> 47.1 us
  waiting for transfers between devices: 536 us -> 564 us
  other arithmetic: 110 us -> 91.2 us
    pallas_call x5 -> x6, Pallas kernels: 17.3 us -> 205 us  [the longest x4 195 us: run_experts(): pl.pallas_call(functools.partial(experts_kernel, sizes), out_shape=(*[jax...]
    ppermute x136 -> x54, starting transfers between devices: 180 us -> 46.8 us  [shift(): return lax.ppermute(value, axis, pairs)]
    dot_general x8 -> x0, matrix products: 70.1 us -> none  [the longest x2 21.2 us: shards(): lax.dot_general(onehot, sent_grad, collect, preferred_element_type=F32)]
    dot_general x9 -> x3, matrix products: 83.1 us -> 16.9 us  [times_t(): lax.dot_general(left, right, (((1,), (1,)), ((), ())), preferred_element_...]
    unnamed x387 -> x142, local copies, waits for them, and re-layouts: 68 us -> 12.4 us
    dot_general x9 -> x3, matrix products: 69.7 us -> 15.3 us  [plain(): return jnp.dot(left, right, preferred_element_type=F32)]
    slice x14 -> x2, local copies, waits for them, and re-layouts: 37.2 us -> 2.49 us  [the longest x1 1.57 us: shards(): normed_part[(key[0] * 2 + key[1]) * own:][:own]]
    reshape x7 -> x0, local copies, waits for them, and re-layouts: 32.8 us -> none  [the longest x1 12.3 us: shards(): all_rows = all_rows[:, :D].reshape(group, rows, D)]
  transfers between devices with their start and end apart: 143 -> 63, of which waited for: 68 -> 34; matrix products, arithmetic and copies ran while one was open for 23% -> 18% of each run, Pallas kernels for 4% -> 17%
where the time goes in v3:
time: 1110 us
  waiting for transfers between devices  564 us (51%)
  Pallas kernels  241 us (22%)
  matrix products  104 us (9%)
  other arithmetic  91.2 us (8%)
  starting transfers between devices  47.1 us (4%)
  local copies, waits for them, and re-layouts  41.9 us (4%)
  between operations  16.2 us (1%)
    ppermute x54, waiting for transfers between devices, shift(): return lax.ppermute(value, axis, pairs)  555 us
    pallas_call x4, Pallas kernels, run_experts(): pl.pallas_call(functools.partial(experts_kernel, sizes), out_shape=(*[jax...  195 us
    dot_general x9, matrix products, inner(): lax.dot_general(left, right, (((0,), (0,)), ((), ())), preferred_element_...  72.2 us
    ppermute x54, starting transfers between devices, shift(): return lax.ppermute(value, axis, pairs)  46.8 us
  transfers between devices with their start and end apart: 63, of which 34 were waited for; matrix products, arithmetic and copies ran while one was open for 18% of the time, Pallas kernels for 17%

profile of v3, /device:TPU:0, one launch (start us, length us, event | category | flops | bytes accessed | tf_op | source)
XLA Modules:
  0.0 1106.4 jit_solution(7230470354565572552)
XLA Ops:
  12.2 2.9 collective-permute-start.7
  16.7 7.4 collective-permute-done.9
  27.2 5.0 collective-permute-done.10
  33.1 6.4 collective-permute-done.11
  41.8 23.2 %collective-permute-done.8 = bf16[256,1664]{1,0:T(8,128)(2,1)S(1)} collective-permute-done((bf16[256,1664]{1,0:T(8,128)(2,1)S(1)}, bf16[256,1664]{1,0:T(8,128)(2,1)S(1)}, u32[]{:S(2)}, u32[]{:S(2)}) %collective-permute-start.8) | collective-permute-done | bytes 852000 | tf_op jit(solution)/shard_map/ppermute | solution.py:48
  65.2 2.7 collective-permute-start.12
  69.0 35.2 %collective-permute-done.12.refs_1_ = bf16[512,1664]{1,0:T(8,128)(2,1)S(1)} collective-permute-done((bf16[512,1664]{1,0:T(8,128)(2,1)S(1)}, bf16[512,1664]{1,0:T(8,128)(2,1)S(1)}, u32[]{:S(2)}, u32[]{:S(2)}) %collective-permute-start.12) | collective-permute-done | bytes 1703968 | tf_op jit(solution)/shard_map/ppermute | solution.py:48
  111.0 31.4 %collective-permute-done.13.refs_2_ = bf16[512,1664]{1,0:T(8,128)(2,1)} collective-permute-done((bf16[512,1664]{1,0:T(8,128)(2,1)S(1)}, bf16[512,1664]{1,0:T(8,128)(2,1)}, u32[]{:S(2)}, u32[]{:S(2)}) %collective-permute-start.13) | collective-permute-done | bytes 1703968 | tf_op jit(solution)/shard_map/ppermute | solution.py:48
  148.6 5.5 collective-permute-done.16
  157.8 2.7 fusion
  160.5 19.5 %collective-permute-done.14.refs_3_ = bf16[512,1664]{1,0:T(8,128)(2,1)} collective-permute-done((bf16[512,1664]{1,0:T(8,128)(2,1)}, bf16[512,1664]{1,0:T(8,128)(2,1)}, u32[]{:S(2)}, u32[]{:S(2)}) %collective-permute-start.14) | collective-permute-done | bytes 1703968 | tf_op jit(solution)/shard_map/ppermute | solution.py:48
  180.0 7.4 shard_map.272
  187.5 2.7 copy-done
  191.7 10.8 fusion.5.qkv_ref
  202.5 14.6 %shard_map.273 = bf16[1024,512]{1,0:T(8,128)(2,1)S(1)} custom-call(s32[8]{0:T(128)S(1)} %pad_add_fusion.lengths_ref, f32[1024,1536]{1,0:T(8,128)S(1)} %fusion.5.qkv_ref, f32[2,128]{1,0:T(2,128)S(1)} %pad_maximum_fusion.17.gains_ref, f32[128,128]{1,0:T(8,128)S(1)} %get-tuple-element.298.cosine_ref, f32[128,128]{1,0:T(8,128)S(1)} %get-tuple-element.299.sine_ref), custom_call_target="tpu_custom_call" | custom-call | flops 14000000000 | bytes 14680064 | tf_op jit(solution)/shard_map/pallas_call | solution.py:247
  222.5 7.5 collective-permute-done.15
  233.7 4.1 collective-permute-done.18
  243.7 62.9 %collective-permute-done.20.refs_0_ = bf16[256,2176]{1,0:T(8,128)(2,1)} collective-permute-done((bf16[256,2176]{1,0:T(8,128)(2,1)S(1)}, bf16[256,2176]{1,0:T(8,128)(2,1)}, u32[]{:S(2)}, u32[]{:S(2)}) %collective-permute-start.20) | collective-permute-done | bytes 1114144 | tf_op jit(solution)/shard_map/ppermute | solution.py:48
  306.7 73.3 %collective-permute-done.21.refs_0_ = bf16[256,2176]{1,0:T(8,128)(2,1)S(1)} collective-permute-done((bf16[256,2176]{1,0:T(8,128)(2,1)}, bf16[256,2176]{1,0:T(8,128)(2,1)S(1)}, u32[]{:S(2)}, u32[]{:S(2)}) %collective-permute-start.21) | collective-permute-done | bytes 1114144 | tf_op jit(solution)/shard_map/ppermute | solution.py:48
  383.3 46.8 %collective-permute-done.32.refs_0_ = bf16[256,2176]{1,0:T(8,128)(2,1)} collective-permute-done((bf16[256,2176]{1,0:T(8,128)(2,1)S(1)}, bf16[256,2176]{1,0:T(8,128)(2,1)}, u32[]{:S(2)}, u32[]{:S(2)}) %collective-permute-start.32) | collective-permute-done | bytes 1114144 | tf_op jit(solution)/shard_map/ppermute | solution.py:48
  431.3 48.8 %shard_map.275 = (bf16[256,2048]{1,0:T(8,128)(2,1)}, bf16[256,2048]{1,0:T(8,128)(2,1)}, bf16[256,2176]{1,0:T(8,128)(2,1)}, bf16[256,2176]{1,0:T(8,128)(2,1)}, bf...) custom-call(s32[3]{0:T(128)} %pad_add_fusion.3.places_ref, ...), custom_call_target="tpu_custom_call" | custom-call | flops 53687091200 | bytes 41943040 | tf_op jit(solution)/shard_map/pallas_call | solution.py:494
  482.2 48.7 %shard_map.276 = (bf16[256,2048]{1,0:T(8,128)(2,1)}, bf16[256,2048]{1,0:T(8,128)(2,1)}, bf16[256,2176]{1,0:T(8,128)(2,1)}, bf16[256,2176]{1,0:T(8,128)(2,1)}, bf...) custom-call(s32[3]{0:T(128)} %pad_add_fusion.2.places_ref, ...), custom_call_target="tpu_custom_call", output_to_operand_aliasing={{4}: (7, {}), {5}: (8, {}), {6}: (9, {}), {7}: (10, {}), {8... | custom-call | flops 53687091200 | bytes 41943040 | tf_op jit(solution)/shard_map/pallas_call | solution.py:494
  533.0 2.9 fusion.112
  541.6 36.3 %collective-permute-done.25 = bf16[256,2048]{1,0:T(8,128)(2,1)} collective-permute-done((bf16[256,2048]{1,0:T(8,128)(2,1)}, bf16[256,2048]{1,0:T(8,128)(2,1)}, u32[]{:S(2)}, u32[]{:S(2)}) %collective-permute-start.25) | collective-permute-done | bytes 1048608 | tf_op jit(solution)/shard_map/ppermute | solution.py:48
  577.9 3.4 add_convert_fusion.4
  581.6 2.8 collective-permute-done.27
  585.7 49.0 %shard_map.277 = (bf16[256,2048]{1,0:T(8,128)(2,1)}, bf16[256,2048]{1,0:T(8,128)(2,1)}, bf16[256,2176]{1,0:T(8,128)(2,1)}, bf16[256,2176]{1,0:T(8,128)(2,1)}, bf...) custom-call(s32[3]{0:T(128)} %pad_add_fusion.4.places_ref, ...), custom_call_target="tpu_custom_call", output_to_operand_aliasing={{4}: (7, {}), {5}: (8, {}), {6}: (9, {}), {7}: (10, {}), {8... | custom-call | flops 53687091200 | bytes 41943040 | tf_op jit(solution)/shard_map/pallas_call | solution.py:494
  634.7 48.8 %shard_map.278 = (bf16[256,2048]{1,0:T(8,128)(2,1)}, bf16[256,2048]{1,0:T(8,128)(2,1)}, bf16[256,2176]{1,0:T(8,128)(2,1)}, bf16[256,2176]{1,0:T(8,128)(2,1)}, bf...) custom-call(s32[3]{0:T(128)} %pad_add_fusion.1.places_ref, ...), custom_call_target="tpu_custom_call", output_to_operand_aliasing={{4}: (7, {}), {5}: (8, {}), {6}: (9, {}), {7}: (10, {}), {8... | custom-call | flops 53687091200 | bytes 41943040 | tf_op jit(solution)/shard_map/pallas_call | solution.py:494
  683.5 8.9 convert_bitcast_fusion.4
  692.5 7.8 convert_bitcast_fusion.5
  700.2 6.3 pad_maximum_fusion
  706.6 8.8 convert_bitcast_fusion.2
  715.4 11.5 %convert_bitcast_fusion.3 = bf16[1,2048,1024]{2,1,0:T(8,128)(2,1)} fusion(bf16[2,1280,2048]{2,1,0:T(8,128)(2,1)} %get-tuple-element.105, bf16[2,1280,1024]{2,1,0:T(8,128)(2,1)} %get-tuple-element.107), kind=kOutput, calls=%fused_computation.38 | convolution fusion | flops 5370806272 | bytes 12058624 | tf_op jit(solution)/shard_map/dot_general | solution.py:30
  726.9 6.3 pad_maximum_fusion.1
  734.2 22.6 %collective-permute-done.35 = bf16[256,2176]{1,0:T(8,128)(2,1)S(1)} collective-permute-done((bf16[256,2176]{1,0:T(8,128)(2,1)}, bf16[256,2176]{1,0:T(8,128)(2,1)S(1)}, u32[]{:S(2)}, u32[]{:S(2)}) %collective-permute-start.35) | collective-permute-done | bytes 1114144 | tf_op jit(solution)/shard_map/ppermute | solution.py:48
  758.7 18.2 %collective-permute-done.36 = bf16[256,2176]{1,0:T(8,128)(2,1)S(1)} collective-permute-done((bf16[256,2176]{1,0:T(8,128)(2,1)S(1)}, bf16[256,2176]{1,0:T(8,128)(2,1)S(1)}, u32[]{:S(2)}, u32[]{:S(2)}) %collective-permute-start.36) | collective-permute-done | bytes 1114144 | tf_op jit(solution)/shard_map/ppermute | solution.py:48
  783.9 2.6 collective-permute-done.40
  787.6 5.8 convolution_convert_fusion.3
  793.9 10.8 convert_bitcast_fusion
  804.7 2.8 collective-permute-done.41
  807.6 22.0 %shard_map.279 = (bf16[1024,1536]{1,0:T(8,128)(2,1)S(1)}, f32[2,128]{1,0:T(2,128)S(1)}) custom-call(s32[8]{0:T(128)S(1)} %pad_add_fusion.lengths_ref, f32[1024,1536]{1,0:T(8,128)S(1)} %bitcast.254, bf16[1024,512]{1,0:T(8,128)(2,1)S(1)} %pad_maximum_fusion.10.mixed_grad_ref, f32[2,128]{1,0:T(2,128)S(1)} %copy-done.5, ...), custom_call_target="tpu_custom_call" | custom-call | flops 20000000000 | bytes 20971520 | tf_op jit(solution)/shard_map/pallas_call | solution.py:271
  829.6 9.0 fusion.120
  840.2 9.0 convert_bitcast_fusion.1
  849.2 7.6 pad_maximum_fusion.2
  858.9 3.1 fusion.62
  862.2 11.5 %convolution_convert_fusion = bf16[2048,1536]{0,1:T(8,128)(2,1)} fusion(bf16[1024,1536]{1,0:T(8,128)(2,1)S(1)} %get-tuple-element.103, f32[2048]{0:T(1024)S(1)} %copy-done.38, f32[1024]{0:T(1024)S(1)} %copy-done.45, bf16[256,2048]{1,0:T(8,128)(2,1)} %collective-permute-done.5, bf16[256,2048]{1,0:T(8,128)(2,1)} %collective-permute-done.4, ...), kind=kOutput, calls=%fused_computation.8 | convolution fusion | flops 6468665344 | bytes 13643776 | tf_op jit(solution)/shard_map/dot_general | solution.py:30
  873.9 13.5 %collective-permute-done.44 = bf16[256,2048]{1,0:T(8,128)(2,1)} collective-permute-done((bf16[256,2048]{1,0:T(8,128)(2,1)}, bf16[256,2048]{1,0:T(8,128)(2,1)}, u32[]{:S(2)}, u32[]{:S(2)}) %collective-permute-start.44) | collective-permute-done | bytes 1048608 | tf_op jit(solution)/shard_map/ppermute | solution.py:48
  887.4 3.5 fusion.61
  891.0 6.8 pad_maximum_fusion.3
  897.8 9.8 copy.184
  907.7 2.9 dynamic-slice_bitcast_fusion.1
  917.3 32.9 %collective-permute-done.45 = bf16[2,2,2,64,1664]{4,3,2,1,0:T(8,128)(2,1)} collective-permute-done((bf16[2,2,2,64,1664]{4,3,2,1,0:T(8,128)(2,1)}, bf16[2,2,2,64,1664]{4,3,2,1,0:T(8,128)(2,1)}, u32[]{:S(2)}, u32[]{:S(2)}) %collective-permute-start.45) | collective-permute-done | bytes 1703968 | tf_op jit(solution)/shard_map/ppermute | solution.py:48
  950.2 3.6 fusion.38
  953.7 8.5 collective-permute-done.51
  962.2 3.0 fusion.25
  965.4 3.7 collective-permute-start.52
  970.9 21.5 %collective-permute-done.46 = bf16[2,2,2,64,1664]{4,3,2,1,0:T(8,128)(2,1)} collective-permute-done((bf16[2,2,2,64,1664]{4,3,2,1,0:T(8,128)(2,1)}, bf16[2,2,2,64,1664]{4,3,2,1,0:T(8,128)(2,1)}, u32[]{:S(2)}, u32[]{:S(2)}) %collective-permute-start.46) | collective-permute-done | bytes 1703968 | tf_op jit(solution)/shard_map/ppermute | solution.py:48
  1002.3 39.2 %collective-permute-done.53 = bf16[64,2048]{1,0:T(8,128)(2,1)S(1)} collective-permute-done((bf16[64,2048]{1,0:T(8,128)(2,1)S(1)}, bf16[64,2048]{1,0:T(8,128)(2,1)S(1)}, u32[]{:S(2)}, u32[]{:S(2)}) %collective-permute-start.53) | collective-permute-done | bytes 262176 | tf_op jit(solution)/shard_map/ppermute | solution.py:48
  1045.6 17.6 %collective-permute-done.39 = bf16[256,2048]{1,0:T(8,128)(2,1)S(1)} collective-permute-done((bf16[256,2048]{1,0:T(8,128)(2,1)S(1)}, bf16[256,2048]{1,0:T(8,128)(2,1)S(1)}, u32[]{:S(2)}, u32[]{:S(2)}) %collective-permute-start.39) | collective-permute-done | bytes 1048608 | tf_op jit(solution)/shard_map/ppermute | solution.py:48
  1063.2 5.1 fusion.60
  1069.7 6.0 collective-permute-done.55
  1087.0 4.1 convert_element_type.406
  1091.1 4.1 convert_element_type.407
  1095.2 4.1 convert_element_type.408
  (393 shorter events, 113.2 us)
Async XLA Ops:
  7.2 424.0 %all-gather.7.cloned.1.call-start = ((), (), s32[]{:S(2)}) async-start(), calls=%async_computation.4 | async-start | bytes 10485760 | tf_op jit(solution)/shard_map/all_gather | solution.py:673
  8.0 423.2 %all-gather.9.cloned.1.call-start = ((), (), s32[]{:S(2)}) async-start(), calls=%async_computation.5 | async-start | bytes 10485760 | tf_op jit(solution)/shard_map/all_gather | solution.py:673
  8.7 422.5 %all-gather.11.cloned.1.call-start = ((), (), s32[]{:S(2)}) async-start(), calls=%async_computation.6 | async-start | bytes 10485760 | tf_op jit(solution)/shard_map/all_gather | solution.py:673
  9.5 421.8 %all-gather.5.cloned.1.call-start = ((), (), s32[]{:S(2)}) async-start(), calls=%async_computation.3 | async-start | bytes 10027008 | tf_op jit(solution)/shard_map/all_gather | solution.py:686
  10.2 1.9 collective-permute-start.6
  12.2 13.0 %collective-permute-start.7 = (bf16[128,1664]{1,0:T(8,128)(2,1)S(1)}, bf16[128,1664]{1,0:T(8,128)(2,1)S(1)}, u32[]{:S(2)}, u32[]{:S(2)}) collective-permute-start(bf16[128,1664]{1,0:T(8,128)(2,1)S(1)} %get-tuple-element.239), channel_id=1, source_target_pairs={{0,1},{1,0},{2,3},{3,2},{4,5},{5,4},{6,7},{7,6},{8,9},{9,8},{10,11... | collective-permute-start | bytes 1277960 | tf_op jit(solution)/shard_map/ppermute | solution.py:48
  15.2 9.0 collective-permute-start.9
  24.1 8.1 collective-permute-start.10
  25.3 39.7 %collective-permute-start.8 = (bf16[256,1664]{1,0:T(8,128)(2,1)S(1)}, bf16[256,1664]{1,0:T(8,128)(2,1)S(1)}, u32[]{:S(2)}, u32[]{:S(2)}) collective-permute-start(bf16[256,1664]{1,0:T(8,128)(2,1)S(1)} %pad_maximum_fusion.12), channel_id=1, source_target_pairs={{0,16},{16,0},{1,17},{17,1},{2,18},{18,2},{3,19},{19,3},{4,20},{20... | collective-permute-start | bytes 2555912 | tf_op jit(solution)/shard_map/ppermute | solution.py:48
  32.2 7.3 collective-permute-start.11
  65.2 39.1 %collective-permute-start.12 = (bf16[512,1664]{1,0:T(8,128)(2,1)S(1)}, bf16[512,1664]{1,0:T(8,128)(2,1)S(1)}, u32[]{:S(2)}, u32[]{:S(2)}) collective-permute-start(bf16[512,1664]{1,0:T(8,128)(2,1)S(1)} %pad_maximum_fusion.6.refs_0_), channel_id=1, source_target_pairs={{0,2},{2,6},{6,4},{4,0},{1,3},{3,7},{7,5},{5,1},{8,10},{10,14},{14... | collective-permute-start | bytes 5111816 | tf_op jit(solution)/shard_map/ppermute | solution.py:48
  67.9 42.6 %collective-permute-start.4 = (bf16[256,2048]{1,0:T(8,128)(2,1)}, bf16[256,2048]{1,0:T(8,128)(2,1)}, u32[]{:S(2)}, u32[]{:S(2)}) collective-permute-start(bf16[256,2048]{1,0:T(8,128)(2,1)} %bitcast), channel_id=1, source_target_pairs={{0,1},{1,0},{2,3},{3,2},{4,5},{5,4},{6,7},{7,6},{8,9},{9,8},{10,11... | collective-permute-start | bytes 3145736 | tf_op jit(solution)/shard_map/ppermute | solution.py:48
  104.2 38.2 %collective-permute-start.13 = (bf16[512,1664]{1,0:T(8,128)(2,1)S(1)}, bf16[512,1664]{1,0:T(8,128)(2,1)}, u32[]{:S(2)}, u32[]{:S(2)}) collective-permute-start(bf16[512,1664]{1,0:T(8,128)(2,1)S(1)} %collective-permute-done.12.refs_1_), channel_id=1, source_target_pairs={{0,2},{2,6},{6,4},{4,0},{1,3},{3,7},{7,5},{5,1},{8,10},{10,14},{14... | collective-permute-start | bytes 5111816 | tf_op jit(solution)/shard_map/ppermute | solution.py:48
  106.4 47.6 %collective-permute-start.16 = (bf16[256,2048]{1,0:T(8,128)(2,1)}, bf16[256,2048]{1,0:T(8,128)(2,1)}, u32[]{:S(2)}, u32[]{:S(2)}) collective-permute-start(bf16[256,2048]{1,0:T(8,128)(2,1)} %copy-done.39), channel_id=1, source_target_pairs={{0,16},{16,0},{1,17},{17,1},{2,18},{18,2},{3,19},{19,3},{4,20},{20... | collective-permute-start | bytes 3145736 | tf_op jit(solution)/shard_map/ppermute | solution.py:48
  110.3 976.7 %reduce-scatter.4.cloned.1.call-start = ((), (), s32[]{:S(2)}) async-start(), calls=%async_computation.7 | async-start | bytes 10485760 | tf_op jit(solution)/shard_map/reduce_scatter | solution.py:845
  110.4 47.4 %collective-permute-start.3 = (bf16[256,2048]{1,0:T(8,128)(2,1)}, bf16[256,2048]{1,0:T(8,128)(2,1)}, u32[]{:S(2)}, u32[]{:S(2)}) collective-permute-start(bf16[256,2048]{1,0:T(8,128)(2,1)} %bitcast), channel_id=1, source_target_pairs={{0,8},{8,0},{1,9},{9,1},{2,10},{10,2},{3,11},{11,3},{4,12},{12,4},... | collective-permute-start | bytes 3145736 | tf_op jit(solution)/shard_map/ppermute | solution.py:48
  110.5 47.3 %collective-permute-start.5 = (bf16[256,2048]{1,0:T(8,128)(2,1)}, bf16[256,2048]{1,0:T(8,128)(2,1)}, u32[]{:S(2)}, u32[]{:S(2)}) collective-permute-start(bf16[256,2048]{1,0:T(8,128)(2,1)} %collective-permute-done.4), channel_id=1, source_target_pairs={{0,8},{8,0},{1,9},{9,1},{2,10},{10,2},{3,11},{11,3},{4,12},{12,4},... | collective-permute-start | bytes 3145736 | tf_op jit(solution)/shard_map/ppermute | solution.py:48
  142.4 37.6 %collective-permute-start.14 = (bf16[512,1664]{1,0:T(8,128)(2,1)}, bf16[512,1664]{1,0:T(8,128)(2,1)}, u32[]{:S(2)}, u32[]{:S(2)}) collective-permute-start(bf16[512,1664]{1,0:T(8,128)(2,1)} %collective-permute-done.13.refs_2_), channel_id=1, source_target_pairs={{0,2},{2,6},{6,4},{4,0},{1,3},{3,7},{7,5},{5,1},{8,10},{10,14},{14... | collective-permute-start | bytes 5111816 | tf_op jit(solution)/shard_map/ppermute | solution.py:48
  142.7 3.5 collective-permute-start.1
  146.3 1.1 collective-permute-start
  147.4 1.1 collective-permute-start.2
  156.4 63.8 %collective-permute-start.17 = (bf16[512,2048]{1,0:T(8,128)(2,1)}, bf16[512,2048]{1,0:T(8,128)(2,1)}, u32[]{:S(2)}, u32[]{:S(2)}) collective-permute-start(bf16[512,2048]{1,0:T(8,128)(2,1)} %constant_dynamic-update-slice_fusion.4.refs_0_), channel_id=1, source_target_pairs={{0,1},{1,0},{2,3},{3,2},{4,5},{5,4},{6,7},{7,6},{8,9},{9,8},{10,11... | collective-permute-start | bytes 6291464 | tf_op jit(solution)/shard_map/ppermute | solution.py:48
  219.1 10.8 collective-permute-start.15
  233.6 4.2 collective-permute-start.18
  242.4 237.6 %copy-start.16 = (f32[256,16]{1,0:T(8,128)}, f32[256,16]{1,0:T(8,128)S(1)}, u32[]{:S(2)}) copy-start(f32[256,16]{1,0:T(8,128)S(1)} %get-tuple-element.223) | copy-start | bytes 49156
  242.7 64.0 %collective-permute-start.20 = (bf16[256,2176]{1,0:T(8,128)(2,1)S(1)}, bf16[256,2176]{1,0:T(8,128)(2,1)}, u32[]{:S(2)}, u32[]{:S(2)}) collective-permute-start(bf16[256,2176]{1,0:T(8,128)(2,1)S(1)} %pad_maximum_fusion.9.refs_0_), channel_id=1, source_target_pairs={{0,2},{2,6},{6,4},{4,0},{1,3},{3,7},{7,5},{5,1},{8,10},{10,14},{14... | collective-permute-start | bytes 3342344 | tf_op jit(solution)/shard_map/ppermute | solution.py:48
  306.7 73.3 %collective-permute-start.21 = (bf16[256,2176]{1,0:T(8,128)(2,1)}, bf16[256,2176]{1,0:T(8,128)(2,1)S(1)}, u32[]{:S(2)}, u32[]{:S(2)}) collective-permute-start(bf16[256,2176]{1,0:T(8,128)(2,1)} %collective-permute-done.20.refs_0_), channel_id=1, source_target_pairs={{0,2},{2,6},{6,4},{4,0},{1,3},{3,7},{7,5},{5,1},{8,10},{10,14},{14... | collective-permute-start | bytes 3342344 | tf_op jit(solution)/shard_map/ppermute | solution.py:48
  380.0 50.2 %collective-permute-start.32 = (bf16[256,2176]{1,0:T(8,128)(2,1)S(1)}, bf16[256,2176]{1,0:T(8,128)(2,1)}, u32[]{:S(2)}, u32[]{:S(2)}) collective-permute-start(bf16[256,2176]{1,0:T(8,128)(2,1)S(1)} %collective-permute-done.21.refs_0_), channel_id=1, source_target_pairs={{0,2},{2,6},{6,4},{4,0},{1,3},{3,7},{7,5},{5,1},{8,10},{10,14},{14... | collective-permute-start | bytes 3342344 | tf_op jit(solution)/shard_map/ppermute | solution.py:48
  380.0 51.3 %collective-permute-start.23 = (bf16[256,2176]{1,0:T(8,128)(2,1)}, bf16[256,2176]{1,0:T(8,128)(2,1)}, u32[]{:S(2)}, u32[]{:S(2)}) collective-permute-start(bf16[256,2176]{1,0:T(8,128)(2,1)} %collective-permute-done.20.refs_0_), channel_id=1, source_target_pairs={{0,1},{1,0},{2,3},{3,2},{4,5},{5,4},{6,7},{7,6},{8,9},{9,8},{10,11... | collective-permute-start | bytes 3342344 | tf_op jit(solution)/shard_map/ppermute | solution.py:48
  381.3 157.2 %collective-permute-start.19 = (bf16[256,2176]{1,0:T(8,128)(2,1)S(1)}, bf16[256,2176]{1,0:T(8,128)(2,1)}, u32[]{:S(2)}, u32[]{:S(2)}) collective-permute-start(bf16[256,2176]{1,0:T(8,128)(2,1)S(1)} %pad_maximum_fusion.9.refs_0_), channel_id=1, source_target_pairs={{0,1},{1,0},{2,3},{3,2},{4,5},{5,4},{6,7},{7,6},{8,9},{9,8},{10,11... | collective-permute-start | bytes 3342344 | tf_op jit(solution)/shard_map/ppermute | solution.py:48
  383.2 99.0 %collective-permute-start.22 = (bf16[256,2176]{1,0:T(8,128)(2,1)S(1)}, bf16[256,2176]{1,0:T(8,128)(2,1)}, u32[]{:S(2)}, u32[]{:S(2)}) collective-permute-start(bf16[256,2176]{1,0:T(8,128)(2,1)S(1)} %collective-permute-done.21.refs_0_), channel_id=1, source_target_pairs={{0,1},{1,0},{2,3},{3,2},{4,5},{5,4},{6,7},{7,6},{8,9},{9,8},{10,11... | collective-permute-start | bytes 3342344 | tf_op jit(solution)/shard_map/ppermute | solution.py:48
  430.1 111.4 %collective-permute-start.33 = (bf16[256,2176]{1,0:T(8,128)(2,1)}, bf16[256,2176]{1,0:T(8,128)(2,1)}, u32[]{:S(2)}, u32[]{:S(2)}) collective-permute-start(bf16[256,2176]{1,0:T(8,128)(2,1)} %collective-permute-done.32.refs_0_), channel_id=1, source_target_pairs={{0,1},{1,0},{2,3},{3,2},{4,5},{5,4},{6,7},{7,6},{8,9},{9,8},{10,11... | collective-permute-start | bytes 3342344 | tf_op jit(solution)/shard_map/ppermute | solution.py:48
  480.1 55.8 %collective-permute-start.26 = (bf16[256,2176]{1,0:T(8,128)(2,1)}, bf16[256,2176]{1,0:T(8,128)(2,1)}, u32[]{:S(2)}, u32[]{:S(2)}) collective-permute-start(bf16[256,2176]{1,0:T(8,128)(2,1)} %get-tuple-element.76), channel_id=1, source_target_pairs={{0,1},{1,0},{2,3},{3,2},{4,5},{5,4},{6,7},{7,6},{8,9},{9,8},{10,11... | collective-permute-start | bytes 3342344 | tf_op jit(solution)/shard_map/ppermute | solution.py:48
  481.1 50.8 %collective-permute-start.29 = (bf16[256,2048]{1,0:T(8,128)(2,1)}, bf16[256,2048]{1,0:T(8,128)(2,1)}, u32[]{:S(2)}, u32[]{:S(2)}) collective-permute-start(bf16[256,2048]{1,0:T(8,128)(2,1)} %get-tuple-element.78), channel_id=1, source_target_pairs={{0,1},{1,0},{2,3},{3,2},{4,5},{5,4},{6,7},{7,6},{8,9},{9,8},{10,11... | collective-permute-start | bytes 3145736 | tf_op jit(solution)/shard_map/ppermute | solution.py:48
  530.9 50.6 %collective-permute-start.24 = (bf16[256,2176]{1,0:T(8,128)(2,1)}, bf16[256,2176]{1,0:T(8,128)(2,1)S(1)}, u32[]{:S(2)}, u32[]{:S(2)}) collective-permute-start(bf16[256,2176]{1,0:T(8,128)(2,1)} %get-tuple-element.70), channel_id=1, source_target_pairs={{0,1},{1,0},{2,3},{3,2},{4,5},{5,4},{6,7},{7,6},{8,9},{9,8},{10,11... | collective-permute-start | bytes 3342344 | tf_op jit(solution)/shard_map/ppermute | solution.py:48
  531.9 46.0 %collective-permute-start.25 = (bf16[256,2048]{1,0:T(8,128)(2,1)}, bf16[256,2048]{1,0:T(8,128)(2,1)}, u32[]{:S(2)}, u32[]{:S(2)}) collective-permute-start(bf16[256,2048]{1,0:T(8,128)(2,1)} %get-tuple-element.72), channel_id=1, source_target_pairs={{0,1},{1,0},{2,3},{3,2},{4,5},{5,4},{6,7},{7,6},{8,9},{9,8},{10,11... | collective-permute-start | bytes 3145736 | tf_op jit(solution)/shard_map/ppermute | solution.py:48
  535.9 42.0 %collective-permute-start.30 = (bf16[256,2048]{1,0:T(8,128)(2,1)}, bf16[256,2048]{1,0:T(8,128)(2,1)}, u32[]{:S(2)}, u32[]{:S(2)}) collective-permute-start(bf16[256,2048]{1,0:T(8,128)(2,1)} %fusion.112), channel_id=1, source_target_pairs={{0,2},{2,6},{6,4},{4,0},{1,3},{3,7},{7,5},{5,1},{8,10},{10,14},{14... | collective-permute-start | bytes 3145736 | tf_op jit(solution)/shard_map/ppermute | solution.py:48
  538.4 45.9 %collective-permute-start.27 = (bf16[256,2176]{1,0:T(8,128)(2,1)}, bf16[256,2176]{1,0:T(8,128)(2,1)S(1)}, u32[]{:S(2)}, u32[]{:S(2)}) collective-permute-start(bf16[256,2176]{1,0:T(8,128)(2,1)} %fusion.113), channel_id=1, source_target_pairs={{0,2},{2,6},{6,4},{4,0},{1,3},{3,7},{7,5},{5,1},{8,10},{10,14},{14... | collective-permute-start | bytes 3342344 | tf_op jit(solution)/shard_map/ppermute | solution.py:48
  581.3 53.4 %collective-permute-start.31 = (bf16[256,2048]{1,0:T(8,128)(2,1)}, bf16[256,2048]{1,0:T(8,128)(2,1)}, u32[]{:S(2)}, u32[]{:S(2)}) collective-permute-start(bf16[256,2048]{1,0:T(8,128)(2,1)} %add_convert_fusion.4), channel_id=1, source_target_pairs={{0,2},{2,6},{6,4},{4,0},{1,3},{3,7},{7,5},{5,1},{8,10},{10,14},{14... | collective-permute-start | bytes 3145736 | tf_op jit(solution)/shard_map/ppermute | solution.py:48
  585.7 49.0 %collective-permute-start.28 = (bf16[256,2176]{1,0:T(8,128)(2,1)}, bf16[256,2176]{1,0:T(8,128)(2,1)S(1)}, u32[]{:S(2)}, u32[]{:S(2)}) collective-permute-start(bf16[256,2176]{1,0:T(8,128)(2,1)} %add_convert_fusion.1), channel_id=1, source_target_pairs={{0,2},{2,6},{6,4},{4,0},{1,3},{3,7},{7,5},{5,1},{8,10},{10,14},{14... | collective-permute-start | bytes 3342344 | tf_op jit(solution)/shard_map/ppermute | solution.py:48
  706.5 384.6 %reduce-scatter.6.cloned.1.call-start = ((), (), s32[]{:S(2)}) async-start(), calls=%async_computation.8 | async-start | bytes 10485760 | tf_op jit(solution)/shard_map/reduce_scatter | solution.py:845
  733.2 361.9 %reduce-scatter.8.cloned.1.call-start = ((), (), s32[]{:S(2)}) async-start(), calls=%async_computation.9 | async-start | bytes 10485760 | tf_op jit(solution)/shard_map/reduce_scatter | solution.py:845
  733.3 23.5 %collective-permute-start.35 = (bf16[256,2176]{1,0:T(8,128)(2,1)}, bf16[256,2176]{1,0:T(8,128)(2,1)S(1)}, u32[]{:S(2)}, u32[]{:S(2)}) collective-permute-start(bf16[256,2176]{1,0:T(8,128)(2,1)} %get-tuple-element.98), channel_id=1, source_target_pairs={{0,1},{1,0},{2,3},{3,2},{4,5},{5,4},{6,7},{7,6},{8,9},{9,8},{10,11... | collective-permute-start | bytes 3342344 | tf_op jit(solution)/shard_map/ppermute | solution.py:48
  757.2 19.6 %collective-permute-start.36 = (bf16[256,2176]{1,0:T(8,128)(2,1)S(1)}, bf16[256,2176]{1,0:T(8,128)(2,1)S(1)}, u32[]{:S(2)}, u32[]{:S(2)}) collective-permute-start(bf16[256,2176]{1,0:T(8,128)(2,1)S(1)} %add_convert_fusion), channel_id=1, source_target_pairs={{0,2},{2,6},{6,4},{4,0},{1,3},{3,7},{7,5},{5,1},{8,10},{10,14},{14... | collective-permute-start | bytes 3342344 | tf_op jit(solution)/shard_map/ppermute | solution.py:48
  758.1 20.7 %collective-permute-start.34 = (bf16[256,2176]{1,0:T(8,128)(2,1)S(1)}, bf16[256,2176]{1,0:T(8,128)(2,1)S(1)}, u32[]{:S(2)}, u32[]{:S(2)}) collective-permute-start(bf16[256,2176]{1,0:T(8,128)(2,1)S(1)} %copy-done.53), channel_id=1, source_target_pairs={{0,1},{1,0},{2,3},{3,2},{4,5},{5,4},{6,7},{7,6},{8,9},{9,8},{10,11... | collective-permute-start | bytes 3342344 | tf_op jit(solution)/shard_map/ppermute | solution.py:48
  783.9 2.7 collective-permute-start.40
  793.5 14.0 %collective-permute-start.41 = (bf16[512,512]{1,0:T(8,128)(2,1)S(1)}, bf16[512,512]{1,0:T(8,128)(2,1)S(1)}, u32[]{:S(2)}, u32[]{:S(2)}) collective-permute-start(bf16[512,512]{1,0:T(8,128)(2,1)S(1)} %get-tuple-element.231), channel_id=1, source_target_pairs={{0,1},{1,0},{2,3},{3,2},{4,5},{5,4},{6,7},{7,6},{8,9},{9,8},{10,11... | collective-permute-start | bytes 1572872 | tf_op jit(solution)/shard_map/ppermute | solution.py:48
  840.2 18.7 %collective-permute-start.43 = (bf16[256,2048]{1,0:T(8,128)(2,1)}, bf16[256,2048]{1,0:T(8,128)(2,1)}, u32[]{:S(2)}, u32[]{:S(2)}) collective-permute-start(bf16[256,2048]{1,0:T(8,128)(2,1)} %get-tuple-element.227), channel_id=1, source_target_pairs={{0,8},{8,0},{1,9},{9,1},{2,10},{10,2},{3,11},{11,3},{4,12},{12,4},... | collective-permute-start | bytes 3145736 | tf_op jit(solution)/shard_map/ppermute | solution.py:48
  858.3 15.6 %collective-permute-start.42 = (bf16[256,2048]{1,0:T(8,128)(2,1)}, bf16[256,2048]{1,0:T(8,128)(2,1)}, u32[]{:S(2)}, u32[]{:S(2)}) collective-permute-start(bf16[256,2048]{1,0:T(8,128)(2,1)} %get-tuple-element.226), channel_id=1, source_target_pairs={{0,8},{8,0},{1,9},{9,1},{2,10},{10,2},{3,11},{11,3},{4,12},{12,4},... | collective-permute-start | bytes 3145736 | tf_op jit(solution)/shard_map/ppermute | solution.py:48
  862.0 25.4 %collective-permute-start.44 = (bf16[256,2048]{1,0:T(8,128)(2,1)}, bf16[256,2048]{1,0:T(8,128)(2,1)}, u32[]{:S(2)}, u32[]{:S(2)}) collective-permute-start(bf16[256,2048]{1,0:T(8,128)(2,1)} %fusion.62), channel_id=1, source_target_pairs={{0,1},{1,0},{2,3},{3,2},{4,5},{5,4},{6,7},{7,6},{8,9},{9,8},{10,11... | collective-permute-start | bytes 3145736 | tf_op jit(solution)/shard_map/ppermute | solution.py:48
  910.6 39.6 %collective-permute-start.45 = (bf16[2,2,2,64,1664]{4,3,2,1,0:T(8,128)(2,1)}, bf16[2,2,2,64,1664]{4,3,2,1,0:T(8,128)(2,1)}, u32[]{:S(2)}, u32[]{:S(2)}) collective-permute-start(bf16[2,2,2,64,1664]{4,3,2,1,0:T(8,128)(2,1)} %dynamic-slice_bitcast_fusion.1), channel_id=1, source_target_pairs={{0,2},{2,6},{6,4},{4,0},{1,3},{3,7},{7,5},{5,1},{8,10},{10,14},{14... | collective-permute-start | bytes 5111816 | tf_op jit(solution)/shard_map/ppermute | solution.py:48
  915.4 46.9 %collective-permute-start.51 = (bf16[2,4,64,2048]{3,2,1,0:T(8,128)(2,1)S(1)}, bf16[2,4,64,2048]{3,2,1,0:T(8,128)(2,1)}, u32[]{:S(2)}, u32[]{:S(2)}) collective-permute-start(bf16[2,4,64,2048]{3,2,1,0:T(8,128)(2,1)S(1)} %dynamic-slice_bitcast_fusion), channel_id=1, source_target_pairs={{0,1},{1,0},{2,3},{3,2},{4,5},{5,4},{6,7},{7,6},{8,9},{9,8},{10,11... | collective-permute-start | bytes 6291464 | tf_op jit(solution)/shard_map/ppermute | solution.py:48
  953.7 38.6 %collective-permute-start.46 = (bf16[2,2,2,64,1664]{4,3,2,1,0:T(8,128)(2,1)}, bf16[2,2,2,64,1664]{4,3,2,1,0:T(8,128)(2,1)}, u32[]{:S(2)}, u32[]{:S(2)}) collective-permute-start(bf16[2,2,2,64,1664]{4,3,2,1,0:T(8,128)(2,1)} %fusion.38), channel_id=1, source_target_pairs={{0,2},{2,6},{6,4},{4,0},{1,3},{3,7},{7,5},{5,1},{8,10},{10,14},{14... | collective-permute-start | bytes 5111816 | tf_op jit(solution)/shard_map/ppermute | solution.py:48
  965.4 29.5 %collective-permute-start.52 = (bf16[4,64,2048]{2,1,0:T(8,128)(2,1)S(1)}, bf16[4,64,2048]{2,1,0:T(8,128)(2,1)}, u32[]{:S(2)}, u32[]{:S(2)}) collective-permute-start(bf16[4,64,2048]{2,1,0:T(8,128)(2,1)S(1)} %dynamic-slice_bitcast_fusion.2), channel_id=1, source_target_pairs={{0,16},{16,0},{1,17},{17,1},{2,18},{18,2},{3,19},{19,3},{4,20},{20... | collective-permute-start | bytes 3145736 | tf_op jit(solution)/shard_map/ppermute | solution.py:48
  969.1 29.1 %collective-permute-start.38 = (bf16[256,2048]{1,0:T(8,128)(2,1)}, bf16[256,2048]{1,0:T(8,128)(2,1)S(1)}, u32[]{:S(2)}, u32[]{:S(2)}) collective-permute-start(bf16[256,2048]{1,0:T(8,128)(2,1)} %get-tuple-element.102), channel_id=1, source_target_pairs={{0,1},{1,0},{2,3},{3,2},{4,5},{5,4},{6,7},{7,6},{8,9},{9,8},{10,11... | collective-permute-start | bytes 3145736 | tf_op jit(solution)/shard_map/ppermute | solution.py:48
  994.8 46.9 %collective-permute-start.47 = (bf16[2,2,2,64,1664]{4,3,2,1,0:T(8,128)(2,1)S(1)}, bf16[2,2,2,64,1664]{4,3,2,1,0:T(8,128)(2,1)S(1)}, u32[]{:S(2)}, u32[]{:S(2)}) collective-permute-start(bf16[2,2,2,64,1664]{4,3,2,1,0:T(8,128)(2,1)S(1)} %fusion.39), channel_id=1, source_target_pairs={{0,2},{2,6},{6,4},{4,0},{1,3},{3,7},{7,5},{5,1},{8,10},{10,14},{14... | collective-permute-start | bytes 5111816 | tf_op jit(solution)/shard_map/ppermute | solution.py:48
  996.6 44.9 %collective-permute-start.53 = (bf16[64,2048]{1,0:T(8,128)(2,1)S(1)}, bf16[64,2048]{1,0:T(8,128)(2,1)S(1)}, u32[]{:S(2)}, u32[]{:S(2)}) collective-permute-start(bf16[64,2048]{1,0:T(8,128)(2,1)S(1)} %dynamic-slice_bitcast_fusion.8), channel_id=1, source_target_pairs={{0,2},{2,6},{6,4},{4,0},{1,3},{3,7},{7,5},{5,1},{8,10},{10,14},{14... | collective-permute-start | bytes 786440 | tf_op jit(solution)/shard_map/ppermute | solution.py:48
  999.9 63.2 %collective-permute-start.39 = (bf16[256,2048]{1,0:T(8,128)(2,1)S(1)}, bf16[256,2048]{1,0:T(8,128)(2,1)S(1)}, u32[]{:S(2)}, u32[]{:S(2)}) collective-permute-start(bf16[256,2048]{1,0:T(8,128)(2,1)S(1)} %add_convert_fusion.3), channel_id=1, source_target_pairs={{0,2},{2,6},{6,4},{4,0},{1,3},{3,7},{7,5},{5,1},{8,10},{10,14},{14... | collective-permute-start | bytes 3145736 | tf_op jit(solution)/shard_map/ppermute | solution.py:48
  1001.5 61.6 %collective-permute-start.37 = (bf16[256,2048]{1,0:T(8,128)(2,1)S(1)}, bf16[256,2048]{1,0:T(8,128)(2,1)S(1)}, u32[]{:S(2)}, u32[]{:S(2)}) collective-permute-start(bf16[256,2048]{1,0:T(8,128)(2,1)S(1)} %copy-done.54), channel_id=1, source_target_pairs={{0,1},{1,0},{2,3},{3,2},{4,5},{5,4},{6,7},{7,6},{8,9},{9,8},{10,11... | collective-permute-start | bytes 3145736 | tf_op jit(solution)/shard_map/ppermute | solution.py:48
  1041.6 26.6 %collective-permute-start.54 = (bf16[64,2048]{1,0:T(8,128)(2,1)S(1)}, bf16[64,2048]{1,0:T(8,128)(2,1)S(1)}, u32[]{:S(2)}, u32[]{:S(2)}) collective-permute-start(bf16[64,2048]{1,0:T(8,128)(2,1)S(1)} %fusion.76), channel_id=1, source_target_pairs={{0,2},{2,6},{6,4},{4,0},{1,3},{3,7},{7,5},{5,1},{8,10},{10,14},{14... | collective-permute-start | bytes 786440 | tf_op jit(solution)/shard_map/ppermute | solution.py:48
  1043.8 24.6 %collective-permute-start.48 = (bf16[2,2,64,1664]{3,2,1,0:T(8,128)(2,1)S(1)}, bf16[2,2,64,1664]{3,2,1,0:T(8,128)(2,1)S(1)}, u32[]{:S(2)}, u32[]{:S(2)}) collective-permute-start(bf16[2,2,64,1664]{3,2,1,0:T(8,128)(2,1)S(1)} %dynamic-slice_bitcast_fusion.3), channel_id=1, source_target_pairs={{0,16},{16,0},{1,17},{17,1},{2,18},{18,2},{3,19},{19,3},{4,20},{20... | collective-permute-start | bytes 2555912 | tf_op jit(solution)/shard_map/ppermute | solution.py:48
  1068.3 7.3 collective-permute-start.55
  1068.7 8.2 collective-permute-start.49
  1077.0 1.8 collective-permute-start.50
  (67 other events, 1102.5 us)
Sparse Core Ops, SparseCore 0:
  9.6 79.2 all-gather.6
  90.4 80.7 all-gather.8
  172.8 58.2 all-gather.10
  233.7 193.2 all-gather.4
  706.7 71.2 reduce-scatter.3
  780.5 71.8 reduce-scatter.5
  856.9 72.6 reduce-scatter.7

commit v4 on v3

--- a/solution.py
+++ b/solution.py
@@ -301,7 +301,7 @@
     part, groups, rows, experts, slots, local, ff = sizes
     take = iter(refs)
     row_refs = [next(take) for _ in range(groups)]
-    cots_ref = next(take)
+    cot_refs = [next(take) for _ in range(groups)]
     weight_refs = [next(take) for _ in range(3)]
     if part:
         for _ in range(5):
@@ -325,12 +325,7 @@
     loads = []
     for i in range(groups):
         loads.append(pltpu.make_async_copy(row_refs[i], rows_v.at[i], in_sems.at[2 * i]))
-        start = pl.multiple_of(places_ref[1 + i], 16)
-        loads.append(
-            pltpu.make_async_copy(
-                cots_ref.at[pl.ds(start, own)], cots_v.at[i], in_sems.at[2 * i + 1]
-            )
-        )
+        loads.append(pltpu.make_async_copy(cot_refs[i], cots_v.at[i], in_sems.at[2 * i + 1]))
     for copy in loads:
         copy.start()
     weight_loads = [[] for _ in range(local)]
@@ -457,7 +452,7 @@
 
 
 def run_experts(
-    places, row_blocks, cots, weights, kept, part, parts, experts, rows, capacity
+    places, row_blocks, cot_blocks, weights, kept, part, parts, experts, rows, capacity
 ):
     groups = len(row_blocks)
     own = row_blocks[0].shape[0]
@@ -468,7 +463,7 @@
     any_space = pl.BlockSpec(memory_space=pl.ANY)
     in_vmem = pl.BlockSpec(memory_space=pltpu.VMEM)
     widths = (D, D, ff, ff, ff)
-    operands = [*row_blocks, cots, *weights]
+    operands = [*row_blocks, *cot_blocks, *weights]
     aliases = {}
     if kept is not None:
         aliases = {1 + len(operands) + i: 2 * groups + i for i in range(5)}
@@ -596,8 +591,7 @@
     token_rows = tokens.reshape(own, D)
     length = lengths.reshape(batches)
     group_keys = [(kx, kc) for kx in range(xs) for kc in range(2)]
-    held = gather_blocks(token_rows, ("x", "c"))
-    group_tokens = jnp.concatenate([held[key] for key in group_keys], axis=0)
+    x_tokens = gather_blocks(token_rows, ("x",))
     held = gather_blocks(length, ("x", "c"))
     group_lengths = jnp.concatenate([held[key] for key in group_keys])
     extra = jnp.concatenate(
@@ -638,27 +632,53 @@
             ]
         )
 
+    out_hops = [output_weight]
+    for _ in range(1, zs):
+        out_hops.append(shift(out_hops[-1], "z", 1))
     block = jnp.concatenate(sent_along("c", packed), axis=1)
     block = jnp.concatenate(
         sent_along("x", lambda i: lax.dynamic_index_in_dim(block, i, 0, keepdims=False)), axis=0
     )
-    block = jnp.concatenate(list(gather_blocks(block, ("y",)).values()), axis=0)
-    out_blocks = gather_blocks(output_weight, ("z",))
-    out_rows = jnp.concatenate(list(out_blocks.values()), axis=0)
-    block = tied(block, out_rows)
-    qkv_pieces, hops = [], []
-    for (kz,), value in gather_blocks(block, ("z",)).items():
-        starts = [
+    ZX = ("z", "x")
+    ranks = jnp.concatenate(
+        [
+            slot_ranks(routes[b, 0], priority[b, 0], experts, capacity)
+            for b in range(batches)
+        ],
+        axis=0,
+    )
+    cotangent = out_cotangent.reshape(own, D)
+    cot_rows = jnp.concatenate([cotangent, widen(ranks.astype(BF), EXTRA)], axis=1)
+    cot_blocks = {(0, kx): v for (kx,), v in gather_blocks(cot_rows, ("x",)).items()}
+    block = tied(block, out_hops[1])
+    late = list(gather_blocks(block, ("y",)).values())
+    late = jnp.concatenate(late, axis=0)
+    weight_shards = tied((gate_weight, up_weight, down_weight), late)
+    late = tied(late, out_hops[2:3])
+
+    def offsets_of(kz):
+        return [
             row_offset(ky, kc, kz, kx)
             for ky in range(ys)
             for kx in range(xs)
             for kc in range(2)
         ]
-        qkv_pieces.append((value, starts, 0))
-        hops.append(value)
+
+    qkv_pieces = []
+    hop = late
+    for kz in range(zs):
+        if kz:
+            hop = shift(hop, "z", 1)
+            if kz == 1:
+                hop, out_hops, x_tokens = lax.optimization_barrier((hop, out_hops, x_tokens))
+                out_rows = jnp.concatenate(out_hops, axis=0)
+                out_rows = list(gather_blocks(out_rows, ("y",)).values())
+            if kz == 2:
+                hop, out_rows, cot_blocks = lax.optimization_barrier((hop, out_rows, cot_blocks))
+        qkv_pieces.append((hop, offsets_of(kz), 0))
     qkv_weight = place(qkv_pieces, shard_rows, (D, 3 * width + EXTRA))
-    out_rows = jnp.concatenate(list(gather_blocks(out_rows, ("y",)).values()), axis=0)
     out_pieces = []
+    out_rows = jnp.concatenate(out_rows, axis=0)
     for (kx,), value in gather_blocks(out_rows, ("x",)).items():
         starts = [
             ((came_from("y", ky) * zs + came_from("z", kz)) * xs + came_from("x", kx)) * shard_rows
@@ -666,24 +686,17 @@
             for kz in range(zs)
         ]
         out_pieces.append((value, starts, 0))
-    out_weight = place(out_pieces, shard_rows, (half_width, D))
-    ZX = ("z", "x")
+    cot_hops = [tied(cot_rows, hop)]
+    for _ in range(1, zs):
+        cot_hops.append(shift(cot_hops[-1], "z", 1))
+    for kz in range(1, zs):
+        for (kx,), value in gather_blocks(cot_hops[kz], ("x",)).items():
+            cot_blocks[(kz, kx)] = value
 
     weights = [
         lax.all_gather(w, ("y", "c"), axis=1, tiled=True)
-        for w in (gate_weight, up_weight, down_weight)
+        for w in weight_shards
     ]
-
-    ranks = jnp.concatenate(
-        [
-            slot_ranks(routes[b, 0], priority[b, 0], experts, capacity)
-            for b in range(batches)
-        ],
-        axis=0,
-    )
-    cotangent = out_cotangent.reshape(own, D)
-    cot_rows = jnp.concatenate([cotangent, widen(ranks.astype(BF), EXTRA)], axis=1)
-    all_cots = lax.all_gather(tied(cot_rows, hops[1]), ZX, axis=0, tiled=True)
 
     small = qkv_weight[:, 3 * width :].astype(F32)
     qkv_weight = qkv_weight[:, : 3 * width]
@@ -694,10 +707,14 @@
     head_gains = jnp.stack(
         [per_device[:, :, 2 + experts].reshape(HD), per_device[:, :, 3 + experts].reshape(HD)]
     )
+    held = [value for kx in range(xs) for value in (x_tokens[(kx,)], swap(x_tokens[(kx,)]))]
+    group_tokens = jnp.concatenate(held, axis=0)
     tokens_f = group_tokens.astype(F32)
     token_scale = lax.rsqrt(jnp.mean(tokens_f * tokens_f, axis=-1, keepdims=True) + EPSILON)
     normed = (tokens_f * token_scale * attn_gain_f).astype(BF)
     qkv = plain(normed, qkv_weight)
+    qkv = tied(qkv, (cot_hops[1], [value for value, _, _ in out_pieces]))
+    out_weight = place(out_pieces, shard_rows, (half_width, D))
     cosine, sine = rope_tables(rows)
     mixed = attend(qkv, group_lengths, head_gains, cosine, sine, rows, heads)
     chip_rows = 2 * own
@@ -708,6 +725,8 @@
     for k, part in enumerate(parts):
         place_at = jnp.mod(x + k, xs) * width
         mixed = lax.dynamic_update_slice(mixed, part, (0, place_at))
+    early_swaps = [cot_blocks[(1, kx)] for kx in range(xs)]
+    mixed = tied(mixed, (cot_hops[min(2, zs - 1)], early_swaps))
     partial = plain(mixed, out_weight)
     rows_f = token_rows.astype(F32)
     hidden = rows_f + (partial[:own] + swap(partial[own:]))
@@ -716,61 +735,104 @@
     routed_in = (hidden_unit * ffn_gain_f).astype(BF)
     gate_probs = jax.nn.softmax(plain(routed_in, router), axis=-1)
 
-    row_blocks = gather_blocks(
-        jnp.concatenate([routed_in, widen(in_three(gate_probs), EXTRA)], axis=1), ZX
-    )
-    first_expert = (z * xs + x) * local
-    kept = None
+    routed_rows = jnp.concatenate([routed_in, widen(in_three(gate_probs), EXTRA)], axis=1)
+    swaps = [[cot_blocks[(kz, kx)] for kx in range(xs)] for kz in range(zs)]
+    hop = tied(routed_rows, (cot_hops[-1], swaps[: max(2, zs - 1)]))
+    first_expert = ((z * xs + x) * local).astype(jnp.int32).reshape(1)
     per_call = math.gcd(xs, 2)
-    steps = [*range(1, zs), 0]
-    chains = [[], []]
-    arrived = [None, None]
-    for n, kz in enumerate(steps):
-        parts = [{}, {}]
+    back_parts, combined_parts, kept = {}, {}, None
+
+    def call_experts(kz, swapped, kept):
         for some in range(0, xs, per_call):
             keys = [(kz, kx) for kx in range(some, some + per_call)]
-            places = [(came_from("z", kz) * xs + came_from("x", kx)) * own for kz, kx in keys]
-            places = [first_expert, *places]
-            blocks = [row_blocks[key] for key in keys]
-            if n >= 2:
-                blocks = tied(blocks, [chain[n - 2] for chain in chains])
-                if n >= 3:
-                    blocks = tied(blocks, arrived)
             combined_part, back_part, kept = run_experts(
-                jnp.stack(places).astype(jnp.int32),
-                blocks,
-                all_cots,
+                first_expert,
+                [swapped[(kx,)] for _, kx in keys],
+                [cot_blocks[key] for key in keys],
                 weights,
                 kept,
-                (n * xs + some) // per_call,
+                (kz * xs + some) // per_call,
                 zs * xs // per_call,
                 experts,
                 rows,
                 capacity,
             )
-            parts[0].update(zip(keys, back_part, strict=True))
-            parts[1].update(zip(keys, combined_part, strict=True))
-        for i in range(2):
-            if n:
-                total = chains[i][n - 1]
-                if arrived[i] is not None:
-                    total = total + arrived[i].astype(F32)
-                arrived[i] = shift(total.astype(BF), "z", 1)
-            if kz == 0 and i == 1:
-                back = chains[0][n] + arrived[0].astype(F32)
-                parts[1] = tied(parts[1], back)
-            part = {(kx,): value for (kz, kx), value in parts[i].items()}
-            chains[i].append(reduce_blocks(part.get, ("x",)))
-    combined = chains[1][-1] + arrived[1].astype(F32)
-    layer_out = (hidden + combined).astype(BF)
-    sent, returned_grad, active, gate_hidden_grad, up_hidden_grad = kept
+            back_parts.update(zip(keys, back_part, strict=True))
+            combined_parts.update(zip(keys, combined_part, strict=True))
+        return kept
+
+    def moves(chain, parts, given):
+        started = {}
+        done = len(chain["sums"])
+        if done < given:
+            kz = chain["order"][done]
+            total = parts[(kz, 1)]
+            for kx in range(2, xs):
+                total = parts[(kz, kx)].astype(F32) + shift(total.astype(BF), "x", 1).astype(F32)
+            started["x"] = shift(total.astype(BF), "x", 1)
+        if chain["hops"] < min(zs, done + chain["order"][0]):
+            total = chain["sums"][chain["hops"] - chain["order"][0]]
+            if chain["arrived"] is not None:
+                total = total + chain["arrived"].astype(F32)
+            started["z"] = shift(total.astype(BF), "z", 1)
+        return started
+
+    def settle(chain, parts, started):
+        if "x" in started:
+            kz = chain["order"][len(chain["sums"])]
+            chain["sums"].append(parts[(kz, 0)].astype(F32) + started["x"].astype(F32))
+        if "z" in started:
+            chain["arrived"] = started["z"]
+            chain["hops"] += 1
+
+    def final(chain):
+        return chain["sums"][chain["order"].index(0)] + chain["arrived"].astype(F32)
+
+    back_chain = {"sums": [], "hops": 1, "arrived": None, "order": [*range(zs)]}
+    combined_chain = {"sums": [], "hops": 1, "arrived": None, "order": [*range(1, zs), 0]}
+
+    swapped = gather_blocks(hop, ("x",))
+    hop = shift(hop, "z", 1)
+    ready, hop = lax.optimization_barrier((swapped, hop))
+    for kz in range(zs):
+        coming = []
+        if kz < zs - 1:
+            coming = [gather_blocks(hop, ("x",))]
+        if kz < zs - 2:
+            hop = shift(hop, "z", 1)
+        back_moves = moves(back_chain, back_parts, kz)
+        kept = call_experts(kz, ready, kept)
+        coming, hop, kept, back_moves = lax.optimization_barrier((coming, hop, kept, back_moves))
+        settle(back_chain, back_parts, back_moves)
+        ready = coming[0] if coming else None
 
     def weight_grads(left, right):
-        return [inner(left[j], right[j]) for j in range(local)]
-
-    down_grads = weight_grads(active, returned_grad)
-    gate_grads = weight_grads(sent, gate_hidden_grad)
-    up_grads = weight_grads(sent, up_hidden_grad)
+        return lax.dot_general(
+            kept[left], kept[right], (((1,), (1,)), ((0,), (0,))), preferred_element_type=F32
+        ).astype(BF)
+
+    expert_grads, waiting = [], [(2, 1), (0, 3), (0, 4)]
+    while back_chain["hops"] < zs or waiting:
+        back_moves = moves(back_chain, back_parts, zs)
+        last = back_chain["hops"] == zs - 1 and len(back_chain["sums"]) == zs
+        combined_moves = moves(combined_chain, combined_parts, zs) if last else {}
+        some, waiting = (waiting, []) if last else (waiting[:1], waiting[1:])
+        some = [weight_grads(*pair) for pair in some]
+        some, kept, back_moves, combined_moves = lax.optimization_barrier(
+            (some, kept, back_moves, combined_moves)
+        )
+        expert_grads += some
+        settle(back_chain, back_parts, back_moves)
+        settle(combined_chain, combined_parts, combined_moves)
+    down_grads, gate_grads, up_grads = expert_grads
+    back = final(back_chain)
+
+    def beside(value, others):
+        parts = tied(combined_parts, others)
+        started = moves(combined_chain, parts, zs)
+        value, started = lax.optimization_barrier((value, started))
+        settle(combined_chain, combined_parts, started)
+        return value
 
     probs_grad = from_three(back[:, D:], experts)
     logits_grad = (
@@ -791,38 +853,92 @@
     qkv_grad, head_gain_grads = attend_back(
         qkv, mixed_grad, group_lengths, head_gains, cosine, sine, rows, heads
     )
+    output_grad = output_grad.reshape(ys, zs, xs, shard_rows, D)
+    qkv_grad = beside(qkv_grad, mixed_grad)
     normed_part = times_t(qkv_grad, qkv_weight)
-    normed_grad = reduce_blocks(
-        lambda key: normed_part[(key[0] * 2 + key[1]) * own :][:own], ("x", "c")
-    )
-    token_unit = rows_f * token_scale[:own]
-    tokens_add, attn_gain_grad = norm_back(normed_grad, token_unit, token_scale[:own], attn_gain_f)
-    tokens_grad = hidden_grad + tokens_add
-
-    small_grad = jnp.concatenate(
-        [
-            attn_gain_grad[:, None],
-            ffn_gain_grad[:, None],
-            router_grad,
-            jnp.pad(
-                head_gain_grads.reshape(2, -1, head_shard),
-                ((0, 0), (0, 0), (0, shard_rows - head_shard)),
-            )
-            .reshape(2, D)
-            .T,
-        ],
-        axis=1,
-    )
-    qkv_weight_grad = jnp.concatenate(
-        [inner(normed, qkv_grad).astype(BF), widen(small_grad, EXTRA).astype(BF)], axis=1
-    )
-    output_grad = output_grad.reshape(ys, zs, xs, shard_rows, D)
-    output_weight_grad = reduce_axis(output_grad, "x", 2).astype(BF)
-    output_weight_grad = reduce_axis(output_weight_grad, "y", 0).astype(BF)
-    output_weight_grad = reduce_axis(output_weight_grad, "z", 0)
-    total = qkv_weight_grad.reshape(ys, 2, zs, xs, shard_rows, -1)
-    total = reduce_axis(total, "z", 2).astype(BF)
-    total = reduce_axis(total, "y", 0).astype(BF)
+    qkv_weight_grad = inner(normed, tied(qkv_grad, normed_part)).astype(BF)
+    normed_sums = [
+        reduce_blocks(lambda key: normed_part[(kx * 2 + key[0]) * own :][:own], ("c",)).astype(BF)
+        for kx in range(xs)
+    ]
+    qkv_weight_grad, normed_sums = beside((qkv_weight_grad, normed_sums), qkv_grad)
+    late = qkv_weight_grad.reshape(ys, 2, zs, xs, shard_rows, -1)
+
+    def finish(normed_grad):
+        token_unit = rows_f * token_scale[:own]
+        tokens_add, attn_gain_grad = norm_back(
+            normed_grad, token_unit, token_scale[:own], attn_gain_f
+        )
+        small_grad = jnp.concatenate(
+            [
+                attn_gain_grad[:, None],
+                ffn_gain_grad[:, None],
+                router_grad,
+                jnp.pad(
+                    head_gain_grads.reshape(2, -1, head_shard),
+                    ((0, 0), (0, 0), (0, shard_rows - head_shard)),
+                )
+                .reshape(2, D)
+                .T,
+            ],
+            axis=1,
+        )
+        small = widen(small_grad, EXTRA).astype(BF)
+        return hidden_grad + tokens_add, small.reshape(ys, 2, zs, xs, shard_rows, EXTRA)
+
+    def part_of(value, axis, dim, k):
+        return lax.dynamic_index_in_dim(value, came_from(axis, k), dim, keepdims=False)
+
+    ring = [*range(2, zs), 0]
+    late_total = part_of(late, "z", 2, 1)
+    output_x = output_y = output_total = None
+    small_hops, output_hops = 0, 0
+    for n, k in enumerate(ring):
+        arrived = {"late": shift(late_total.astype(BF), "z", 1)}
+        if n == 0:
+            combined_parts = tied(combined_parts, late)
+            arrived["combined"] = moves(combined_chain, combined_parts, zs)
+            arrived["normed"] = reduce_blocks(lambda key: normed_sums[key[0]], ("x",))
+        if n == 1:
+            arrived["x"] = reduce_axis(tied(output_grad, late_total), "x", 2).astype(BF)
+        if n == 2:
+            arrived["y"] = reduce_axis(output_x, "y", 0).astype(BF)
+        if n >= 1:
+            arrived["small"] = shift(small_total.astype(BF), "z", 1)
+        arrived = lax.optimization_barrier(arrived)
+        late_total = part_of(late, "z", 2, k) + arrived["late"].astype(F32)
+        if n == 0:
+            settle(combined_chain, combined_parts, arrived["combined"])
+            tokens_grad, small = finish(arrived["normed"])
+            small_total = part_of(small, "z", 2, 1)
+        if n == 1:
+            output_x = arrived["x"]
+        if n == 2:
+            output_y = arrived["y"]
+            output_total = part_of(output_y, "z", 0, 1)
+        if n >= 1:
+            part = part_of(small, "z", 2, ring[small_hops])
+            small_total = part + arrived["small"].astype(F32)
+            small_hops += 1
+    combined = final(combined_chain)
+    layer_out = (hidden + combined).astype(BF)
+    expert_totals = [
+        lax.psum_scatter(grad, ("y", "c"), scatter_dimension=1, tiled=True).astype(F32)
+        for grad in (down_grads, gate_grads, up_grads)
+    ]
+    late = reduce_axis(late_total.astype(BF), "y", 0).astype(BF)
+    arrived = [shift(small_total.astype(BF), "z", 1), shift(output_total.astype(BF), "z", 1)]
+    late, arrived, expert_totals = lax.optimization_barrier((late, arrived, expert_totals))
+    small = part_of(small, "z", 2, 0) + arrived[0].astype(F32)
+    small = reduce_axis(small.astype(BF), "y", 0).astype(BF)
+    output_total = part_of(output_y, "z", 0, ring[output_hops]) + arrived[1].astype(F32)
+    output_hops += 1
+    while output_hops < zs - 1:
+        output_total = shift(output_total.astype(BF), "z", 1).astype(F32)
+        output_total = part_of(output_y, "z", 0, ring[output_hops]) + output_total
+        output_hops += 1
+    output_weight_grad = output_total
+    total = jnp.concatenate([late, small], axis=-1)
     columns = sent_along("x", lambda i: lax.dynamic_index_in_dim(total, i, 1, keepdims=False))
     columns = jnp.stack(columns)
     columns = sent_along("c", lambda i: lax.dynamic_index_in_dim(columns, i, 1, keepdims=False))
@@ -839,10 +955,6 @@
         low = jnp.where(c == 0, halves[0], halves[1]).reshape(shard_rows, ys, chunk)
         high = jnp.where(c == 0, halves[1], halves[0]).reshape(shard_rows, ys, chunk)
         return jnp.stack([low, high], axis=2).reshape(shard_rows, D).astype(F32)
-
-    def expert_total(parts):
-        grad = jnp.stack(parts).astype(BF)
-        return lax.psum_scatter(grad, ("y", "c"), scatter_dimension=1, tiled=True).astype(F32)
 
     shape = (batches, 1, rows, D)
     return (
@@ -857,9 +969,9 @@
         small_total[:head_shard, 3 + experts],
         small_total[:, 1],
         small_total[:, 2 : 2 + experts],
-        expert_total(gate_grads),
-        expert_total(up_grads),
-        expert_total(down_grads),
+        expert_totals[1],
+        expert_totals[2],
+        expert_totals[0],
     )
 
 

time: 1110 us -> 886 us (0.80)
  waiting for transfers between devices: 564 us -> 356 us
  other arithmetic: 91.2 us -> 68.2 us
  starting transfers between devices: 47.1 us -> 66 us
    ppermute x54 -> x63, waiting for transfers between devices: 555 us -> 352 us  [shift(): return lax.ppermute(value, axis, pairs)]
    dot_general x9 -> x3, matrix products: 72.2 us -> 13.1 us  [inner(): lax.dot_general(left, right, (((0,), (0,)), ((), ())), preferred_element_...]
    dot_general x0 -> x3, matrix products: none -> 54.4 us  [weight_grads(): lax.dot_general(kept[left], kept[right], (((1,), (1,)), ((0,), (0,))), pr...]
    another operation x10 -> x3, other arithmetic: 22.6 us -> 0.02 us  [the longest x3 20.1 us: expert_total(): grad = jnp.stack(parts).astype(BF)]
    ppermute x54 -> x63, starting transfers between devices: 46.8 us -> 64.8 us  [shift(): return lax.ppermute(value, axis, pairs)]
    convert_element_type x18 -> x21, other arithmetic: 40.7 us -> 42.7 us  [the longest x6 14.6 us: moves(): started['z'] = shift(total.astype(BF), 'z', 1)]
  transfers between devices with their start and end apart: 63 -> 73, of which waited for: 34 -> 30; matrix products, arithmetic and copies ran while one was open for 18% -> 20% of each run, Pallas kernels for 17% -> 27%
where the time goes in v4:
time: 886 us; the launch traced here: 877 us
  waiting for transfers between devices  356 us (40%)
  Pallas kernels  237 us (27%)
  matrix products  97.8 us (11%)
  other arithmetic  68.2 us (8%)
  starting transfers between devices  66 us (7%)
  local copies, waits for them, and re-layouts  36 us (4%)
  between operations  16.3 us (2%)
    ppermute x63, waiting for transfers between devices, shift(): return lax.ppermute(value, axis, pairs)  352 us
    pallas_call x4, Pallas kernels, run_experts(): pl.pallas_call(functools.partial(experts_kernel, sizes), out_shape=(*[jax...  191 us
    ppermute x63, starting transfers between devices, shift(): return lax.ppermute(value, axis, pairs)  64.8 us
    dot_general x3, matrix products, weight_grads(): lax.dot_general(kept[left], kept[right], (((1,), (1,)), ((0,), (0,))), pr...  54.4 us
    pallas_call x1, Pallas kernels, attend_back(): pl.pallas_call(functools.partial(attend_back_kernel, heads), out_shape=(j...  21.9 us
  transfers between devices with their start and end apart: 73, of which 30 were waited for; matrix products, arithmetic and copies ran while one was open for 20% of the time, Pallas kernels for 27%

profile of v4, /device:TPU:0, one launch (start us, length us, event | category | flops | bytes accessed | tf_op | source)
XLA Modules:
  0.0 877.3 jit_solution(7424519750061216428)
XLA Ops:
  13.8 2.9 collective-permute-start.4
  18.3 8.5 collective-permute-done.4
  28.9 18.6 %collective-permute-done.6 = bf16[256,1664]{1,0:T(8,128)(2,1)S(1)} collective-permute-done((bf16[256,1664]{1,0:T(8,128)(2,1)S(1)}, bf16[256,1664]{1,0:T(8,128)(2,1)S(1)}, u32[]{:S(2)}, u32[]{:S(2)}) %collective-permute-start.6) | collective-permute-done | bytes 852000 | tf_op jit(solution)/shard_map/ppermute | solution.py:48
  51.9 5.7 collective-permute-done.7
  59.9 3.4 collective-permute-start.9
  63.4 2.3 fusion.25.refs_2_
  66.2 34.3 %collective-permute-done.9 = bf16[64,2048]{1,0:T(8,128)(2,1)S(1)} collective-permute-done((bf16[64,2048]{1,0:T(8,128)(2,1)}, bf16[64,2048]{1,0:T(8,128)(2,1)S(1)}, u32[]{:S(2)}, u32[]{:S(2)}) %collective-permute-start.9) | collective-permute-done | bytes 262176 | tf_op jit(solution)/shard_map/ppermute | solution.py:48
  104.4 27.3 %collective-permute-done.14 = bf16[256,2048]{1,0:T(8,128)(2,1)} collective-permute-done((bf16[256,2048]{1,0:T(8,128)(2,1)S(1)}, bf16[256,2048]{1,0:T(8,128)(2,1)}, u32[]{:S(2)}, u32[]{:S(2)}) %collective-permute-start.14) | collective-permute-done | bytes 1048608 | tf_op jit(solution)/shard_map/ppermute | solution.py:48
  131.8 5.6 collective-permute-done.13.refs_2_
  140.2 2.6 fusion
  146.3 27.1 %collective-permute-done.16.refs_3_ = bf16[512,1664]{1,0:T(8,128)(2,1)} collective-permute-done((bf16[512,1664]{1,0:T(8,128)(2,1)}, bf16[512,1664]{1,0:T(8,128)(2,1)}, u32[]{:S(2)}, u32[]{:S(2)}) %collective-permute-start.16) | collective-permute-done | bytes 1703968 | tf_op jit(solution)/shard_map/ppermute | solution.py:48
  173.3 7.3 shard_map.272
  180.6 3.0 copy-done
  185.8 12.1 %fusion.5.qkv_ref = f32[1024,1536]{1,0:T(8,128)S(1)} fusion(bf16[2048,1664]{1,0:T(8,128)(2,1)} %copy-done, f32[2048]{0:T(1024)S(1)} %get-tuple-element.385, f32[1024]{0:T(1024)S(1)} %add_rsqrt_fusion, bf16[256,2048]{1,0:T(8,128)(2,1)} %collective-permute-done.12, bf16[256,2048]{1,0:T(8,128)(2,1)} %collective-permute-done.10, ...), kind=kOutput, calls=%fused_computation.8 | convolution fusion | flops 6465519616 | bytes 16789504 | tf_op jit(solution)/shard_map/dot_general | solution.py:26
  197.9 10.9 %collective-permute-done.17.refs_2_ = bf16[256,2176]{1,0:T(8,128)(2,1)} collective-permute-done((bf16[256,2176]{1,0:T(8,128)(2,1)}, bf16[256,2176]{1,0:T(8,128)(2,1)}, u32[]{:S(2)}, u32[]{:S(2)}) %collective-permute-start.17) | collective-permute-done | bytes 1114144 | tf_op jit(solution)/shard_map/ppermute | solution.py:48
  210.6 14.6 %shard_map.273 = bf16[1024,512]{1,0:T(8,128)(2,1)S(1)} custom-call(s32[8]{0:T(128)S(1)} %pad_add_fusion.lengths_ref, f32[1024,1536]{1,0:T(8,128)S(1)} %fusion.5.qkv_ref, f32[2,128]{1,0:T(2,128)S(1)} %pad_maximum_fusion.13.gains_ref, f32[128,128]{1,0:T(8,128)S(1)} %get-tuple-element.468.cosine_ref, f32[128,128]{1,0:T(8,128)S(1)} %get-tuple-element.469.sine_ref), custom_call_target="tpu_custom_call" | custom-call | flops 14000000000 | bytes 14680064 | tf_op jit(solution)/shard_map/pallas_call | solution.py:247
  227.4 2.4 shard_map.274
  229.8 9.1 %collective-permute-done.19 = bf16[512,512]{1,0:T(8,128)(2,1)} collective-permute-done((bf16[512,512]{1,0:T(8,128)(2,1)}, bf16[512,512]{1,0:T(8,128)(2,1)}, u32[]{:S(2)}, u32[]{:S(2)}) %collective-permute-start.19) | collective-permute-done | bytes 524320 | tf_op jit(solution)/shard_map/ppermute | solution.py:48
  240.0 2.3 fusion.77
  242.6 3.4 collective-permute-start.23
  249.7 2.1 fusion.75
  252.6 18.2 %collective-permute-done.23.refs_2_ = bf16[256,2176]{1,0:T(8,128)(2,1)} collective-permute-done((bf16[256,2176]{1,0:T(8,128)(2,1)}, bf16[256,2176]{1,0:T(8,128)(2,1)}, u32[]{:S(2)}, u32[]{:S(2)}) %collective-permute-start.23) | collective-permute-done | bytes 1114144 | tf_op jit(solution)/shard_map/ppermute | solution.py:48
  270.8 2.2 collective-permute-done.24.refs_3_
  275.4 25.1 %collective-permute-done.25.refs_1_ = bf16[256,2176]{1,0:T(8,128)(2,1)S(1)} collective-permute-done((bf16[256,2176]{1,0:T(8,128)(2,1)S(1)}, bf16[256,2176]{1,0:T(8,128)(2,1)S(1)}, u32[]{:S(2)}, u32[]{:S(2)}) %collective-permute-start.25) | collective-permute-done | bytes 1114144 | tf_op jit(solution)/shard_map/ppermute | solution.py:48
  303.6 47.0 %shard_map.275 = (bf16[256,2048]{1,0:T(8,128)(2,1)}, bf16[256,2048]{1,0:T(8,128)(2,1)}, bf16[256,2176]{1,0:T(8,128)(2,1)}, bf16[256,2176]{1,0:T(8,128)(2,1)}, bf...) custom-call(s32[1]{0:T(128)} %bitcast.68.places_ref, ...), custom_call_target="tpu_custom_call" | custom-call | flops 53687091200 | bytes 41943040 | tf_op jit(solution)/shard_map/pallas_call | solution.py:489
  354.2 48.0 %shard_map.276 = (bf16[256,2048]{1,0:T(8,128)(2,1)}, bf16[256,2048]{1,0:T(8,128)(2,1)}, bf16[256,2176]{1,0:T(8,128)(2,1)}, bf16[256,2176]{1,0:T(8,128)(2,1)}, bf...) custom-call(s32[1]{0:T(128)} %bitcast.68.places_ref, ...), custom_call_target="tpu_custom_call", output_to_operand_aliasing={{4}: (8, {}), {5}: (9, {}), {6}: (10, {}), {7}: (11, {}), {... | custom-call | flops 53687091200 | bytes 41943040 | tf_op jit(solution)/shard_map/pallas_call | solution.py:489
  405.3 48.1 %shard_map.277 = (bf16[256,2048]{1,0:T(8,128)(2,1)}, bf16[256,2048]{1,0:T(8,128)(2,1)}, bf16[256,2176]{1,0:T(8,128)(2,1)}, bf16[256,2176]{1,0:T(8,128)(2,1)}, bf...) custom-call(s32[1]{0:T(128)} %bitcast.68.places_ref, ...), custom_call_target="tpu_custom_call", output_to_operand_aliasing={{4}: (8, {}), {5}: (9, {}), {6}: (10, {}), {7}: (11, {}), {... | custom-call | flops 53687091200 | bytes 41943040 | tf_op jit(solution)/shard_map/pallas_call | solution.py:489
  454.0 2.5 add_convert_fusion.2
  456.8 48.2 %shard_map.278 = (bf16[256,2048]{1,0:T(8,128)(2,1)}, bf16[256,2048]{1,0:T(8,128)(2,1)}, bf16[256,2176]{1,0:T(8,128)(2,1)}, bf16[256,2176]{1,0:T(8,128)(2,1)}, bf...) custom-call(s32[1]{0:T(128)} %bitcast.68.places_ref, ...), custom_call_target="tpu_custom_call", output_to_operand_aliasing={{4}: (8, {}), {5}: (9, {}), {6}: (10, {}), {7}: (11, {}), {... | custom-call | flops 53687091200 | bytes 41943040 | tf_op jit(solution)/shard_map/pallas_call | solution.py:489
  508.0 3.3 collective-permute-start.38
  511.3 17.4 %convolution_convert_fusion.3 = bf16[2,1024,2048]{2,1,0:T(8,128)(2,1)} fusion(bf16[2,1280,1024]{2,1,0:T(8,128)(2,1)} %get-tuple-element.230, bf16[2,1280,2048]{2,1,0:T(8,128)(2,1)} %get-tuple-element.231), kind=kOutput, calls=%fused_computation.12 | convolution fusion | flops 10741612544 | bytes 24117248 | tf_op jit(solution)/shard_map/dot_general | solution.py:810
  532.1 2.6 add_convert_fusion
  536.4 19.7 %convolution_convert_fusion.1 = bf16[2,2048,1024]{2,1,0:T(8,128)(2,1)} fusion(bf16[2,1280,2048]{2,1,0:T(8,128)(2,1)} %get-tuple-element.239, bf16[2,1280,1024]{2,1,0:T(8,128)(2,1)} %get-tuple-element.241), kind=kOutput, calls=%fused_computation.10 | convolution fusion | flops 10741612544 | bytes 24117248 | tf_op jit(solution)/shard_map/dot_general | solution.py:810
  556.1 17.3 %convolution_convert_fusion.2 = bf16[2,2048,1024]{2,1,0:T(8,128)(2,1)} fusion(bf16[2,1280,2048]{2,1,0:T(8,128)(2,1)} %get-tuple-element.239, bf16[2,1280,1024]{2,1,0:T(8,128)(2,1)} %get-tuple-element.240), kind=kOutput, calls=%fused_computation.11 | convolution fusion | flops 10741612544 | bytes 24117248 | tf_op jit(solution)/shard_map/dot_general | solution.py:810
  580.2 2.7 collective-permute-done.41
  582.8 5.0 convolution_convert_fusion.6
  589.3 2.6 add_convert_fusion.6
  593.5 9.5 %collective-permute-done.42 = bf16[512,512]{1,0:T(8,128)(2,1)} collective-permute-done((bf16[512,512]{1,0:T(8,128)(2,1)}, bf16[512,512]{1,0:T(8,128)(2,1)}, u32[]{:S(2)}, u32[]{:S(2)}) %collective-permute-start.42) | collective-permute-done | bytes 524320 | tf_op jit(solution)/shard_map/ppermute | solution.py:48
  604.5 3.0 copy-done.9
  607.5 21.9 %shard_map.279 = (bf16[1024,1536]{1,0:T(8,128)(2,1)S(1)}, f32[2,128]{1,0:T(2,128)S(1)}) custom-call(s32[8]{0:T(128)S(1)} %pad_add_fusion.lengths_ref, f32[1024,1536]{1,0:T(8,128)S(1)} %copy-done.9, bf16[1024,512]{1,0:T(8,128)(2,1)S(1)} %pad_maximum_fusion.5.mixed_grad_ref, f32[2,128]{1,0:T(2,128)S(1)} %copy-done.7, ...), custom_call_target="tpu_custom_call" | custom-call | flops 20000000000 | bytes 20971520 | tf_op jit(solution)/shard_map/pallas_call | solution.py:271
  629.5 2.7 add_convert_fusion.5
  635.2 6.7 fusion.76
  642.7 8.9 %convolution_convert_fusion = bf16[2048,1536]{1,0:T(8,128)(2,1)S(1)} fusion(bf16[1024,1536]{1,0:T(8,128)(2,1)S(1)} %get-tuple-element.250, f32[2048]{0:T(1024)S(1)} %copy-done.49, f32[1024]{0:T(1024)S(1)} %copy-done.55, bf16[256,2048]{1,0:T(8,128)(2,1)} %collective-permute-done.12, bf16[256,2048]{1,0:T(8,128)(2,1)} %collective-permute-done.10, ...), kind=kOutput, calls=%fused_computation.5 | convolution fusion | flops 6468665344 | bytes 13643776 | tf_op jit(solution)/shard_map/dot_general | solution.py:30
  651.7 2.1 fusion.19
  653.8 4.0 collective-permute-done.48
  661.3 2.7 add_convert_fusion.4
  666.3 3.9 convolution_convert_fusion.4
  670.3 14.7 %collective-permute-done.52 = bf16[256,2048]{1,0:T(8,128)(2,1)} collective-permute-done((bf16[256,2048]{1,0:T(8,128)(2,1)}, bf16[256,2048]{1,0:T(8,128)(2,1)}, u32[]{:S(2)}, u32[]{:S(2)}) %collective-permute-start.52) | collective-permute-done | bytes 1048608 | tf_op jit(solution)/shard_map/ppermute | solution.py:48
  686.8 31.9 %collective-permute-done.50 = bf16[256,2048]{1,0:T(8,128)(2,1)} collective-permute-done((bf16[256,2048]{1,0:T(8,128)(2,1)}, bf16[256,2048]{1,0:T(8,128)(2,1)}, u32[]{:S(2)}, u32[]{:S(2)}) %collective-permute-start.50) | collective-permute-done | bytes 1048608 | tf_op jit(solution)/shard_map/ppermute | solution.py:48
  718.7 3.5 convert_add_fusion.1
  729.4 39.1 %collective-permute-done.55 = bf16[2,4,64,2048]{3,2,1,0:T(8,128)(2,1)} collective-permute-done((bf16[2,4,64,2048]{3,2,1,0:T(8,128)(2,1)}, bf16[2,4,64,2048]{3,2,1,0:T(8,128)(2,1)}, u32[]{:S(2)}, u32[]{:S(2)}) %collective-permute-start.55) | collective-permute-done | bytes 2097184 | tf_op jit(solution)/shard_map/ppermute | solution.py:48
  768.5 3.0 fusion.7
  771.6 4.2 fusion.8
  778.7 19.6 %collective-permute-done.58 = bf16[4,64,2048]{2,1,0:T(8,128)(2,1)} collective-permute-done((bf16[4,64,2048]{2,1,0:T(8,128)(2,1)}, bf16[4,64,2048]{2,1,0:T(8,128)(2,1)}, u32[]{:S(2)}, u32[]{:S(2)}) %collective-permute-start.58) | collective-permute-done | bytes 1048608 | tf_op jit(solution)/shard_map/ppermute | solution.py:48
  800.3 11.8 %collective-permute-done.57 = bf16[2,2,2,64,128]{4,3,2,1,0:T(8,128)(2,1)S(1)} collective-permute-done((bf16[2,2,2,64,128]{4,3,2,1,0:T(8,128)(2,1)S(1)}, bf16[2,2,2,64,128]{4,3,2,1,0:T(8,128)(2,1)S(1)}, u32[]{:S(2)}, u32[]{:S(2)}) %collective-permute-start.57) | collective-permute-done | bytes 131104 | tf_op jit(solution)/shard_map/ppermute | solution.py:48
  812.1 2.3 fusion.9
  814.6 5.0 fusion.17
  822.3 7.0 collective-permute-done.59
  829.6 4.1 convert_element_type.460
  833.7 4.1 convert_element_type.461
  837.8 4.1 convert_element_type.462
  843.3 3.8 collective-permute-done.62
  848.4 4.8 collective-permute-done.65
  855.8 5.1 collective-permute-done.66
  (400 shorter events, 111.6 us)
Async XLA Ops:
  7.2 296.4 %all-gather.4.cloned.1.call-start = ((), (), s32[]{:S(2)}) async-start(), calls=%async_computation.3 | async-start | bytes 10485760 | tf_op jit(solution)/shard_map/all_gather | solution.py:697
  13.8 13.0 %collective-permute-start.4 = (bf16[128,1664]{1,0:T(8,128)(2,1)S(1)}, bf16[128,1664]{1,0:T(8,128)(2,1)S(1)}, u32[]{:S(2)}, u32[]{:S(2)}) collective-permute-start(bf16[128,1664]{1,0:T(8,128)(2,1)S(1)} %get-tuple-element.413), channel_id=1, source_target_pairs={{0,1},{1,0},{2,3},{3,2},{4,5},{5,4},{6,7},{7,6},{8,9},{9,8},{10,11... | collective-permute-start | bytes 1277960 | tf_op jit(solution)/shard_map/ppermute | solution.py:48
  16.8 10.2 %collective-permute-start.5 = (bf16[64,2048]{1,0:T(8,128)(2,1)S(1)}, bf16[64,2048]{1,0:T(8,128)(2,1)S(1)}, u32[]{:S(2)}, u32[]{:S(2)}) collective-permute-start(bf16[64,2048]{1,0:T(8,128)(2,1)S(1)} %copy-done.40), channel_id=1, source_target_pairs={{0,2},{2,6},{6,4},{4,0},{1,3},{3,7},{7,5},{5,1},{8,10},{10,14},{14... | collective-permute-start | bytes 786440 | tf_op jit(solution)/shard_map/ppermute | solution.py:48
  27.0 20.5 %collective-permute-start.6 = (bf16[256,1664]{1,0:T(8,128)(2,1)S(1)}, bf16[256,1664]{1,0:T(8,128)(2,1)S(1)}, u32[]{:S(2)}, u32[]{:S(2)}) collective-permute-start(bf16[256,1664]{1,0:T(8,128)(2,1)S(1)} %pad_maximum_fusion.7), channel_id=1, source_target_pairs={{0,16},{16,0},{1,17},{17,1},{2,18},{18,2},{3,19},{19,3},{4,20},{20... | collective-permute-start | bytes 2555912 | tf_op jit(solution)/shard_map/ppermute | solution.py:48
  47.7 255.9 %all-gather.6.cloned.1.call-start = ((), (), s32[]{:S(2)}) async-start(), calls=%async_computation.4 | async-start | bytes 10485760 | tf_op jit(solution)/shard_map/all_gather | solution.py:697
  48.4 255.1 %all-gather.8.cloned.1.call-start = ((), (), s32[]{:S(2)}) async-start(), calls=%async_computation.5 | async-start | bytes 10485760 | tf_op jit(solution)/shard_map/all_gather | solution.py:697
  48.5 52.0 %collective-permute-start.10 = (bf16[256,2048]{1,0:T(8,128)(2,1)}, bf16[256,2048]{1,0:T(8,128)(2,1)}, u32[]{:S(2)}, u32[]{:S(2)}) collective-permute-start(bf16[256,2048]{1,0:T(8,128)(2,1)} %bitcast), channel_id=1, source_target_pairs={{0,1},{1,0},{2,3},{3,2},{4,5},{5,4},{6,7},{7,6},{8,9},{9,8},{10,11... | collective-permute-start | bytes 3145736 | tf_op jit(solution)/shard_map/ppermute | solution.py:48
  57.6 42.9 %collective-permute-start.8 = (bf16[512,1664]{1,0:T(8,128)(2,1)S(1)}, bf16[512,1664]{1,0:T(8,128)(2,1)S(1)}, u32[]{:S(2)}, u32[]{:S(2)}) collective-permute-start(bf16[512,1664]{1,0:T(8,128)(2,1)S(1)} %constant_dynamic-update-slice_fusion.refs_0_), channel_id=1, source_target_pairs={{0,2},{2,6},{6,4},{4,0},{1,3},{3,7},{7,5},{5,1},{8,10},{10,14},{14... | collective-permute-start | bytes 5111816 | tf_op jit(solution)/shard_map/ppermute | solution.py:48
  59.9 40.6 %collective-permute-start.9 = (bf16[64,2048]{1,0:T(8,128)(2,1)}, bf16[64,2048]{1,0:T(8,128)(2,1)S(1)}, u32[]{:S(2)}, u32[]{:S(2)}) collective-permute-start(bf16[64,2048]{1,0:T(8,128)(2,1)} %copy-done.44), channel_id=1, source_target_pairs={{0,2},{2,6},{6,4},{4,0},{1,3},{3,7},{7,5},{5,1},{8,10},{10,14},{14... | collective-permute-start | bytes 786440 | tf_op jit(solution)/shard_map/ppermute | solution.py:48
  65.7 38.2 %collective-permute-start.15 = (bf16[256,2176]{1,0:T(8,128)(2,1)}, bf16[256,2176]{1,0:T(8,128)(2,1)}, u32[]{:S(2)}, u32[]{:S(2)}) collective-permute-start(bf16[256,2176]{1,0:T(8,128)(2,1)} %fusion.25.refs_2_), channel_id=1, source_target_pairs={{0,1},{1,0},{2,3},{3,2},{4,5},{5,4},{6,7},{7,6},{8,9},{9,8},{10,11... | collective-permute-start | bytes 3342344 | tf_op jit(solution)/shard_map/ppermute | solution.py:48
  100.5 36.9 %collective-permute-start.13 = (bf16[512,1664]{1,0:T(8,128)(2,1)S(1)}, bf16[512,1664]{1,0:T(8,128)(2,1)}, u32[]{:S(2)}, u32[]{:S(2)}) collective-permute-start(bf16[512,1664]{1,0:T(8,128)(2,1)S(1)} %collective-permute-done.8.refs_1_), channel_id=1, source_target_pairs={{0,2},{2,6},{6,4},{4,0},{1,3},{3,7},{7,5},{5,1},{8,10},{10,14},{14... | collective-permute-start | bytes 5111816 | tf_op jit(solution)/shard_map/ppermute | solution.py:48
  101.6 30.2 %collective-permute-start.14 = (bf16[256,2048]{1,0:T(8,128)(2,1)S(1)}, bf16[256,2048]{1,0:T(8,128)(2,1)}, u32[]{:S(2)}, u32[]{:S(2)}) collective-permute-start(bf16[256,2048]{1,0:T(8,128)(2,1)S(1)} %constant_dynamic-update-slice_fusion.2), channel_id=1, source_target_pairs={{0,16},{16,0},{1,17},{17,1},{2,18},{18,2},{3,19},{19,3},{4,20},{20... | collective-permute-start | bytes 3145736 | tf_op jit(solution)/shard_map/ppermute | solution.py:48
  103.2 37.0 %collective-permute-start.11 = (bf16[256,2048]{1,0:T(8,128)(2,1)}, bf16[256,2048]{1,0:T(8,128)(2,1)}, u32[]{:S(2)}, u32[]{:S(2)}) collective-permute-start(bf16[256,2048]{1,0:T(8,128)(2,1)} %bitcast), channel_id=1, source_target_pairs={{0,8},{8,0},{1,9},{9,1},{2,10},{10,2},{3,11},{11,3},{4,12},{12,4},... | collective-permute-start | bytes 3145736 | tf_op jit(solution)/shard_map/ppermute | solution.py:582
  103.2 37.0 %collective-permute-start.12 = (bf16[256,2048]{1,0:T(8,128)(2,1)}, bf16[256,2048]{1,0:T(8,128)(2,1)}, u32[]{:S(2)}, u32[]{:S(2)}) collective-permute-start(bf16[256,2048]{1,0:T(8,128)(2,1)} %collective-permute-done.10), channel_id=1, source_target_pairs={{0,8},{8,0},{1,9},{9,1},{2,10},{10,2},{3,11},{11,3},{4,12},{12,4},... | collective-permute-start | bytes 3145736 | tf_op jit(solution)/shard_map/ppermute | solution.py:582
  103.8 35.0 %collective-permute-start.1 = (s32[2]{0:T(128)S(1)}, s32[2]{0:T(128)S(1)}, u32[]{:S(2)}, u32[]{:S(2)}) collective-permute-start(s32[2]{0:T(128)S(1)} %bitcast.231), channel_id=1, source_target_pairs={{0,1},{1,0},{2,3},{3,2},{4,5},{5,4},{6,7},{7,6},{8,9},{9,8},{10,11... | collective-permute-start | bytes 32 | tf_op jit(solution)/shard_map/ppermute | solution.py:48
  137.4 35.9 %collective-permute-start.16 = (bf16[512,1664]{1,0:T(8,128)(2,1)}, bf16[512,1664]{1,0:T(8,128)(2,1)}, u32[]{:S(2)}, u32[]{:S(2)}) collective-permute-start(bf16[512,1664]{1,0:T(8,128)(2,1)} %collective-permute-done.13.refs_2_), channel_id=1, source_target_pairs={{0,2},{2,6},{6,4},{4,0},{1,3},{3,7},{7,5},{5,1},{8,10},{10,14},{14... | collective-permute-start | bytes 5111816 | tf_op jit(solution)/shard_map/ppermute | solution.py:48
  140.1 689.4 %reduce-scatter.4.cloned.1.call-start = ((), (), s32[]{:S(2)}) async-start(), calls=%async_computation.6 | async-start | bytes 10485760 | tf_op jit(solution)/shard_map/reduce_scatter | solution.py:926
  145.7 52.2 %collective-permute-start.18 = (bf16[512,2048]{1,0:T(8,128)(2,1)S(1)}, bf16[512,2048]{1,0:T(8,128)(2,1)}, u32[]{:S(2)}, u32[]{:S(2)}) collective-permute-start(bf16[512,2048]{1,0:T(8,128)(2,1)S(1)} %constant_dynamic-update-slice_fusion.6.refs_0_), channel_id=1, source_target_pairs={{0,1},{1,0},{2,3},{3,2},{4,5},{5,4},{6,7},{7,6},{8,9},{9,8},{10,11... | collective-permute-start | bytes 6291464 | tf_op jit(solution)/shard_map/ppermute | solution.py:48
  184.2 24.6 %collective-permute-start.17 = (bf16[256,2176]{1,0:T(8,128)(2,1)}, bf16[256,2176]{1,0:T(8,128)(2,1)}, u32[]{:S(2)}, u32[]{:S(2)}) collective-permute-start(bf16[256,2176]{1,0:T(8,128)(2,1)} %fusion.25.refs_2_), channel_id=1, source_target_pairs={{0,2},{2,6},{6,4},{4,0},{1,3},{3,7},{7,5},{5,1},{8,10},{10,14},{14... | collective-permute-start | bytes 3342344 | tf_op jit(solution)/shard_map/ppermute | solution.py:48
  208.8 31.2 %collective-permute-start.20 = (bf16[256,2176]{1,0:T(8,128)(2,1)}, bf16[256,2176]{1,0:T(8,128)(2,1)}, u32[]{:S(2)}, u32[]{:S(2)}) collective-permute-start(bf16[256,2176]{1,0:T(8,128)(2,1)} %collective-permute-done.17.refs_2_), channel_id=1, source_target_pairs={{0,2},{2,6},{6,4},{4,0},{1,3},{3,7},{7,5},{5,1},{8,10},{10,14},{14... | collective-permute-start | bytes 3342344 | tf_op jit(solution)/shard_map/ppermute | solution.py:48
  209.7 30.3 %collective-permute-start.21 = (bf16[256,2176]{1,0:T(8,128)(2,1)}, bf16[256,2176]{1,0:T(8,128)(2,1)}, u32[]{:S(2)}, u32[]{:S(2)}) collective-permute-start(bf16[256,2176]{1,0:T(8,128)(2,1)} %collective-permute-done.17.refs_2_), channel_id=1, source_target_pairs={{0,1},{1,0},{2,3},{3,2},{4,5},{5,4},{6,7},{7,6},{8,9},{9,8},{10,11... | collective-permute-start | bytes 3342344 | tf_op jit(solution)/shard_map/ppermute | solution.py:48
  226.2 12.7 %collective-permute-start.19 = (bf16[512,512]{1,0:T(8,128)(2,1)}, bf16[512,512]{1,0:T(8,128)(2,1)}, u32[]{:S(2)}, u32[]{:S(2)}) collective-permute-start(bf16[512,512]{1,0:T(8,128)(2,1)} %get-tuple-element.406), channel_id=1, source_target_pairs={{0,1},{1,0},{2,3},{3,2},{4,5},{5,4},{6,7},{7,6},{8,9},{9,8},{10,11... | collective-permute-start | bytes 1572872 | tf_op jit(solution)/shard_map/ppermute | solution.py:48
  242.6 28.2 %collective-permute-start.23 = (bf16[256,2176]{1,0:T(8,128)(2,1)}, bf16[256,2176]{1,0:T(8,128)(2,1)}, u32[]{:S(2)}, u32[]{:S(2)}) collective-permute-start(bf16[256,2176]{1,0:T(8,128)(2,1)} %collective-permute-done.20.refs_2_), channel_id=1, source_target_pairs={{0,2},{2,6},{6,4},{4,0},{1,3},{3,7},{7,5},{5,1},{8,10},{10,14},{14... | collective-permute-start | bytes 3342344 | tf_op jit(solution)/shard_map/ppermute | solution.py:48
  246.1 27.0 %collective-permute-start.24 = (bf16[256,2176]{1,0:T(8,128)(2,1)}, bf16[256,2176]{1,0:T(8,128)(2,1)}, u32[]{:S(2)}, u32[]{:S(2)}) collective-permute-start(bf16[256,2176]{1,0:T(8,128)(2,1)} %collective-permute-done.20.refs_2_), channel_id=1, source_target_pairs={{0,1},{1,0},{2,3},{3,2},{4,5},{5,4},{6,7},{7,6},{8,9},{9,8},{10,11... | collective-permute-start | bytes 3342344 | tf_op jit(solution)/shard_map/ppermute | solution.py:48
  273.0 27.5 %collective-permute-start.25 = (bf16[256,2176]{1,0:T(8,128)(2,1)S(1)}, bf16[256,2176]{1,0:T(8,128)(2,1)S(1)}, u32[]{:S(2)}, u32[]{:S(2)}) collective-permute-start(bf16[256,2176]{1,0:T(8,128)(2,1)S(1)} %pad_maximum_fusion.4.refs_0_), channel_id=1, source_target_pairs={{0,1},{1,0},{2,3},{3,2},{4,5},{5,4},{6,7},{7,6},{8,9},{9,8},{10,11... | collective-permute-start | bytes 3342344 | tf_op jit(solution)/shard_map/ppermute | solution.py:48
  274.7 26.5 %collective-permute-start.26 = (bf16[256,2176]{1,0:T(8,128)(2,1)S(1)}, bf16[256,2176]{1,0:T(8,128)(2,1)}, u32[]{:S(2)}, u32[]{:S(2)}) collective-permute-start(bf16[256,2176]{1,0:T(8,128)(2,1)S(1)} %pad_maximum_fusion.4.refs_0_), channel_id=1, source_target_pairs={{0,2},{2,6},{6,4},{4,0},{1,3},{3,7},{7,5},{5,1},{8,10},{10,14},{14... | collective-permute-start | bytes 3342344 | tf_op jit(solution)/shard_map/ppermute | solution.py:48
  275.1 181.7 %collective-permute-start.34 = (bf16[256,2176]{1,0:T(8,128)(2,1)}, bf16[256,2176]{1,0:T(8,128)(2,1)}, u32[]{:S(2)}, u32[]{:S(2)}) collective-permute-start(bf16[256,2176]{1,0:T(8,128)(2,1)} %collective-permute-done.23.refs_2_), channel_id=1, source_target_pairs={{0,1},{1,0},{2,3},{3,2},{4,5},{5,4},{6,7},{7,6},{8,9},{9,8},{10,11... | collective-permute-start | bytes 3342344 | tf_op jit(solution)/shard_map/ppermute | solution.py:48
  301.5 49.0 %collective-permute-start.27 = (bf16[256,2176]{1,0:T(8,128)(2,1)}, bf16[256,2176]{1,0:T(8,128)(2,1)}, u32[]{:S(2)}, u32[]{:S(2)}) collective-permute-start(bf16[256,2176]{1,0:T(8,128)(2,1)} %collective-permute-done.26.refs_0_), channel_id=1, source_target_pairs={{0,1},{1,0},{2,3},{3,2},{4,5},{5,4},{6,7},{7,6},{8,9},{9,8},{10,11... | collective-permute-start | bytes 3342344 | tf_op jit(solution)/shard_map/ppermute | solution.py:48
  303.2 47.3 %collective-permute-start.28 = (bf16[256,2176]{1,0:T(8,128)(2,1)}, bf16[256,2176]{1,0:T(8,128)(2,1)S(1)}, u32[]{:S(2)}, u32[]{:S(2)}) collective-permute-start(bf16[256,2176]{1,0:T(8,128)(2,1)} %collective-permute-done.26.refs_0_), channel_id=1, source_target_pairs={{0,2},{2,6},{6,4},{4,0},{1,3},{3,7},{7,5},{5,1},{8,10},{10,14},{14... | collective-permute-start | bytes 3342344 | tf_op jit(solution)/shard_map/ppermute | solution.py:48
  350.6 52.2 %collective-permute-start.29 = (bf16[256,2176]{1,0:T(8,128)(2,1)S(1)}, bf16[256,2176]{1,0:T(8,128)(2,1)S(1)}, u32[]{:S(2)}, u32[]{:S(2)}) collective-permute-start(bf16[256,2176]{1,0:T(8,128)(2,1)S(1)} %collective-permute-done.28.refs_0_), channel_id=1, source_target_pairs={{0,1},{1,0},{2,3},{3,2},{4,5},{5,4},{6,7},{7,6},{8,9},{9,8},{10,11... | collective-permute-start | bytes 3342344 | tf_op jit(solution)/shard_map/ppermute | solution.py:48
  351.0 51.8 %collective-permute-start.30 = (bf16[256,2176]{1,0:T(8,128)(2,1)S(1)}, bf16[256,2176]{1,0:T(8,128)(2,1)}, u32[]{:S(2)}, u32[]{:S(2)}) collective-permute-start(bf16[256,2176]{1,0:T(8,128)(2,1)S(1)} %collective-permute-done.28.refs_0_), channel_id=1, source_target_pairs={{0,2},{2,6},{6,4},{4,0},{1,3},{3,7},{7,5},{5,1},{8,10},{10,14},{14... | collective-permute-start | bytes 3342344 | tf_op jit(solution)/shard_map/ppermute | solution.py:48
  352.6 50.1 %collective-permute-start.31 = (bf16[256,2176]{1,0:T(8,128)(2,1)}, bf16[256,2176]{1,0:T(8,128)(2,1)S(1)}, u32[]{:S(2)}, u32[]{:S(2)}) collective-permute-start(bf16[256,2176]{1,0:T(8,128)(2,1)} %get-tuple-element.194), channel_id=1, source_target_pairs={{0,1},{1,0},{2,3},{3,2},{4,5},{5,4},{6,7},{7,6},{8,9},{9,8},{10,11... | collective-permute-start | bytes 3342344 | tf_op jit(solution)/shard_map/ppermute | solution.py:48
  402.2 51.8 %collective-permute-start.33 = (bf16[256,2176]{1,0:T(8,128)(2,1)}, bf16[256,2176]{1,0:T(8,128)(2,1)}, u32[]{:S(2)}, u32[]{:S(2)}) collective-permute-start(bf16[256,2176]{1,0:T(8,128)(2,1)} %get-tuple-element.210), channel_id=1, source_target_pairs={{0,1},{1,0},{2,3},{3,2},{4,5},{5,4},{6,7},{7,6},{8,9},{9,8},{10,11... | collective-permute-start | bytes 3342344 | tf_op jit(solution)/shard_map/ppermute | solution.py:48
  403.8 50.2 %collective-permute-start.32 = (bf16[256,2176]{1,0:T(8,128)(2,1)}, bf16[256,2176]{1,0:T(8,128)(2,1)}, u32[]{:S(2)}, u32[]{:S(2)}) collective-permute-start(bf16[256,2176]{1,0:T(8,128)(2,1)} %collective-permute-done.30.refs_0_), channel_id=1, source_target_pairs={{0,1},{1,0},{2,3},{3,2},{4,5},{5,4},{6,7},{7,6},{8,9},{9,8},{10,11... | collective-permute-start | bytes 3342344 | tf_op jit(solution)/shard_map/ppermute | solution.py:48
  453.4 53.2 %collective-permute-start.35 = (bf16[256,2176]{1,0:T(8,128)(2,1)}, bf16[256,2176]{1,0:T(8,128)(2,1)S(1)}, u32[]{:S(2)}, u32[]{:S(2)}) collective-permute-start(bf16[256,2176]{1,0:T(8,128)(2,1)} %get-tuple-element.227), channel_id=1, source_target_pairs={{0,1},{1,0},{2,3},{3,2},{4,5},{5,4},{6,7},{7,6},{8,9},{9,8},{10,11... | collective-permute-start | bytes 3342344 | tf_op jit(solution)/shard_map/ppermute | solution.py:48
  456.5 50.2 %collective-permute-start.36 = (bf16[256,2176]{1,0:T(8,128)(2,1)}, bf16[256,2176]{1,0:T(8,128)(2,1)S(1)}, u32[]{:S(2)}, u32[]{:S(2)}) collective-permute-start(bf16[256,2176]{1,0:T(8,128)(2,1)} %add_convert_fusion.2), channel_id=1, source_target_pairs={{0,2},{2,6},{6,4},{4,0},{1,3},{3,7},{7,5},{5,1},{8,10},{10,14},{14... | collective-permute-start | bytes 3342344 | tf_op jit(solution)/shard_map/ppermute | solution.py:48
  505.0 23.7 %collective-permute-start.37 = (bf16[256,2176]{1,0:T(8,128)(2,1)}, bf16[256,2176]{1,0:T(8,128)(2,1)}, u32[]{:S(2)}, u32[]{:S(2)}) collective-permute-start(bf16[256,2176]{1,0:T(8,128)(2,1)} %get-tuple-element.235), channel_id=1, source_target_pairs={{0,1},{1,0},{2,3},{3,2},{4,5},{5,4},{6,7},{7,6},{8,9},{9,8},{10,11... | collective-permute-start | bytes 3342344 | tf_op jit(solution)/shard_map/ppermute | solution.py:48
  508.0 22.7 %collective-permute-start.38 = (bf16[256,2176]{1,0:T(8,128)(2,1)}, bf16[256,2176]{1,0:T(8,128)(2,1)S(1)}, u32[]{:S(2)}, u32[]{:S(2)}) collective-permute-start(bf16[256,2176]{1,0:T(8,128)(2,1)} %add_convert_fusion.1), channel_id=1, source_target_pairs={{0,2},{2,6},{6,4},{4,0},{1,3},{3,7},{7,5},{5,1},{8,10},{10,14},{14... | collective-permute-start | bytes 3342344 | tf_op jit(solution)/shard_map/ppermute | solution.py:48
  530.7 303.0 %reduce-scatter.6.cloned.1.call-start = ((), (), s32[]{:S(2)}) async-start(), calls=%async_computation.7 | async-start | bytes 10485760 | tf_op jit(solution)/shard_map/reduce_scatter | solution.py:926
  530.8 42.7 %collective-permute-start.40 = (bf16[256,2048]{1,0:T(8,128)(2,1)}, bf16[256,2048]{1,0:T(8,128)(2,1)}, u32[]{:S(2)}, u32[]{:S(2)}) collective-permute-start(bf16[256,2048]{1,0:T(8,128)(2,1)} %get-tuple-element.187), channel_id=1, source_target_pairs={{0,1},{1,0},{2,3},{3,2},{4,5},{5,4},{6,7},{7,6},{8,9},{9,8},{10,11... | collective-permute-start | bytes 3145736 | tf_op jit(solution)/shard_map/ppermute | solution.py:48
  534.8 38.7 %collective-permute-start.39 = (bf16[256,2176]{1,0:T(8,128)(2,1)}, bf16[256,2176]{1,0:T(8,128)(2,1)S(1)}, u32[]{:S(2)}, u32[]{:S(2)}) collective-permute-start(bf16[256,2176]{1,0:T(8,128)(2,1)} %add_convert_fusion), channel_id=1, source_target_pairs={{0,2},{2,6},{6,4},{4,0},{1,3},{3,7},{7,5},{5,1},{8,10},{10,14},{14... | collective-permute-start | bytes 3342344 | tf_op jit(solution)/shard_map/ppermute | solution.py:48
  573.5 264.3 %reduce-scatter.8.cloned.1.call-start = ((), (), s32[]{:S(2)}) async-start(), calls=%async_computation.8 | async-start | bytes 10485760 | tf_op jit(solution)/shard_map/reduce_scatter | solution.py:926
  588.8 14.3 %collective-permute-start.42 = (bf16[512,512]{1,0:T(8,128)(2,1)}, bf16[512,512]{1,0:T(8,128)(2,1)}, u32[]{:S(2)}, u32[]{:S(2)}) collective-permute-start(bf16[512,512]{1,0:T(8,128)(2,1)} %get-tuple-element.405), channel_id=1, source_target_pairs={{0,1},{1,0},{2,3},{3,2},{4,5},{5,4},{6,7},{7,6},{8,9},{9,8},{10,11... | collective-permute-start | bytes 1572872 | tf_op jit(solution)/shard_map/ppermute | solution.py:48
  591.9 37.5 %collective-permute-start.44 = (bf16[256,2048]{1,0:T(8,128)(2,1)}, bf16[256,2048]{1,0:T(8,128)(2,1)}, u32[]{:S(2)}, u32[]{:S(2)}) collective-permute-start(bf16[256,2048]{1,0:T(8,128)(2,1)} %add_convert_fusion.6), channel_id=1, source_target_pairs={{0,2},{2,6},{6,4},{4,0},{1,3},{3,7},{7,5},{5,1},{8,10},{10,14},{14... | collective-permute-start | bytes 3145736 | tf_op jit(solution)/shard_map/ppermute | solution.py:48
  604.2 25.3 %collective-permute-start.43 = (bf16[256,2048]{1,0:T(8,128)(2,1)S(1)}, bf16[256,2048]{1,0:T(8,128)(2,1)S(1)}, u32[]{:S(2)}, u32[]{:S(2)}) collective-permute-start(bf16[256,2048]{1,0:T(8,128)(2,1)S(1)} %copy-done.60), channel_id=1, source_target_pairs={{0,1},{1,0},{2,3},{3,2},{4,5},{5,4},{6,7},{7,6},{8,9},{9,8},{10,11... | collective-permute-start | bytes 3145736 | tf_op jit(solution)/shard_map/ppermute | solution.py:48
  632.2 25.7 %collective-permute-start.48 = (bf16[256,2048]{1,0:T(8,128)(2,1)}, bf16[256,2048]{1,0:T(8,128)(2,1)S(1)}, u32[]{:S(2)}, u32[]{:S(2)}) collective-permute-start(bf16[256,2048]{1,0:T(8,128)(2,1)} %add_convert_fusion.5), channel_id=1, source_target_pairs={{0,2},{2,6},{6,4},{4,0},{1,3},{3,7},{7,5},{5,1},{8,10},{10,14},{14... | collective-permute-start | bytes 3145736 | tf_op jit(solution)/shard_map/ppermute | solution.py:48
  634.2 24.4 %collective-permute-start.47 = (bf16[256,2048]{1,0:T(8,128)(2,1)}, bf16[256,2048]{1,0:T(8,128)(2,1)}, u32[]{:S(2)}, u32[]{:S(2)}) collective-permute-start(bf16[256,2048]{1,0:T(8,128)(2,1)} %get-tuple-element.251), channel_id=1, source_target_pairs={{0,1},{1,0},{2,3},{3,2},{4,5},{5,4},{6,7},{7,6},{8,9},{9,8},{10,11... | collective-permute-start | bytes 3145736 | tf_op jit(solution)/shard_map/ppermute | solution.py:48
  642.2 9.5 %collective-permute-start.45 = (bf16[256,2048]{1,0:T(8,128)(2,1)S(1)}, bf16[256,2048]{1,0:T(8,128)(2,1)S(1)}, u32[]{:S(2)}, u32[]{:S(2)}) collective-permute-start(bf16[256,2048]{1,0:T(8,128)(2,1)S(1)} %get-tuple-element.401), channel_id=1, source_target_pairs={{0,8},{8,0},{1,9},{9,1},{2,10},{10,2},{3,11},{11,3},{4,12},{12,4},... | collective-permute-start | bytes 3145736 | tf_op jit(solution)/shard_map/ppermute | solution.py:48
  642.2 9.4 %collective-permute-start.46 = (bf16[256,2048]{1,0:T(8,128)(2,1)S(1)}, bf16[256,2048]{1,0:T(8,128)(2,1)S(1)}, u32[]{:S(2)}, u32[]{:S(2)}) collective-permute-start(bf16[256,2048]{1,0:T(8,128)(2,1)S(1)} %get-tuple-element.400), channel_id=1, source_target_pairs={{0,8},{8,0},{1,9},{9,1},{2,10},{10,2},{3,11},{11,3},{4,12},{12,4},... | collective-permute-start | bytes 3145736 | tf_op jit(solution)/shard_map/ppermute | solution.py:48
  658.6 26.4 %collective-permute-start.52 = (bf16[256,2048]{1,0:T(8,128)(2,1)}, bf16[256,2048]{1,0:T(8,128)(2,1)}, u32[]{:S(2)}, u32[]{:S(2)}) collective-permute-start(bf16[256,2048]{1,0:T(8,128)(2,1)} %get-tuple-element.260), channel_id=1, source_target_pairs={{0,1},{1,0},{2,3},{3,2},{4,5},{5,4},{6,7},{7,6},{8,9},{9,8},{10,11... | collective-permute-start | bytes 3145736 | tf_op jit(solution)/shard_map/ppermute | solution.py:48
  660.9 57.8 %collective-permute-start.51 = (bf16[2,2,2,64,1536]{4,3,2,1,0:T(8,128)(2,1)}, bf16[2,2,2,64,1536]{4,3,2,1,0:T(8,128)(2,1)}, u32[]{:S(2)}, u32[]{:S(2)}) collective-permute-start(bf16[2,2,2,64,1536]{4,3,2,1,0:T(8,128)(2,1)} %dynamic-slice_bitcast_fusion.1), channel_id=1, source_target_pairs={{0,2},{2,6},{6,4},{4,0},{1,3},{3,7},{7,5},{5,1},{8,10},{10,14},{14... | collective-permute-start | bytes 4718600 | tf_op jit(solution)/shard_map/ppermute | solution.py:48
  664.0 54.7 %collective-permute-start.50 = (bf16[256,2048]{1,0:T(8,128)(2,1)}, bf16[256,2048]{1,0:T(8,128)(2,1)}, u32[]{:S(2)}, u32[]{:S(2)}) collective-permute-start(bf16[256,2048]{1,0:T(8,128)(2,1)} %add_convert_fusion.4), channel_id=1, source_target_pairs={{0,2},{2,6},{6,4},{4,0},{1,3},{3,7},{7,5},{5,1},{8,10},{10,14},{14... | collective-permute-start | bytes 3145736 | tf_op jit(solution)/shard_map/ppermute | solution.py:48
  665.5 53.2 %collective-permute-start.49 = (bf16[256,2048]{1,0:T(8,128)(2,1)}, bf16[256,2048]{1,0:T(8,128)(2,1)}, u32[]{:S(2)}, u32[]{:S(2)}) collective-permute-start(bf16[256,2048]{1,0:T(8,128)(2,1)} %get-tuple-element.256), channel_id=1, source_target_pairs={{0,1},{1,0},{2,3},{3,2},{4,5},{5,4},{6,7},{7,6},{8,9},{9,8},{10,11... | collective-permute-start | bytes 3145736 | tf_op jit(solution)/shard_map/ppermute | solution.py:48
  723.6 44.9 %collective-permute-start.55 = (bf16[2,4,64,2048]{3,2,1,0:T(8,128)(2,1)}, bf16[2,4,64,2048]{3,2,1,0:T(8,128)(2,1)}, u32[]{:S(2)}, u32[]{:S(2)}) collective-permute-start(bf16[2,4,64,2048]{3,2,1,0:T(8,128)(2,1)} %dynamic-slice_bitcast_fusion), channel_id=1, source_target_pairs={{0,1},{1,0},{2,3},{3,2},{4,5},{5,4},{6,7},{7,6},{8,9},{9,8},{10,11... | collective-permute-start | bytes 6291464 | tf_op jit(solution)/shard_map/ppermute | solution.py:48
  724.6 47.0 %collective-permute-start.53 = (bf16[2,2,2,64,1536]{4,3,2,1,0:T(8,128)(2,1)}, bf16[2,2,2,64,1536]{4,3,2,1,0:T(8,128)(2,1)}, u32[]{:S(2)}, u32[]{:S(2)}) collective-permute-start(bf16[2,2,2,64,1536]{4,3,2,1,0:T(8,128)(2,1)} %convert_add_fusion.1), channel_id=1, source_target_pairs={{0,2},{2,6},{6,4},{4,0},{1,3},{3,7},{7,5},{5,1},{8,10},{10,14},{14... | collective-permute-start | bytes 4718600 | tf_op jit(solution)/shard_map/ppermute | solution.py:48
  727.5 44.0 %collective-permute-start.54 = (bf16[2,2,2,64,128]{4,3,2,1,0:T(8,128)(2,1)S(1)}, bf16[2,2,2,64,128]{4,3,2,1,0:T(8,128)(2,1)S(1)}, u32[]{:S(2)}, u32[]{:S(2)}) collective-permute-start(bf16[2,2,2,64,128]{4,3,2,1,0:T(8,128)(2,1)S(1)} %dynamic-slice_bitcast_fusion.7), channel_id=1, source_target_pairs={{0,2},{2,6},{6,4},{4,0},{1,3},{3,7},{7,5},{5,1},{8,10},{10,14},{14... | collective-permute-start | bytes 393224 | tf_op jit(solution)/shard_map/ppermute | solution.py:48
  775.8 36.3 %collective-permute-start.56 = (bf16[2,2,2,64,1536]{4,3,2,1,0:T(8,128)(2,1)}, bf16[2,2,2,64,1536]{4,3,2,1,0:T(8,128)(2,1)}, u32[]{:S(2)}, u32[]{:S(2)}) collective-permute-start(bf16[2,2,2,64,1536]{4,3,2,1,0:T(8,128)(2,1)} %fusion.8), channel_id=1, source_target_pairs={{0,2},{2,6},{6,4},{4,0},{1,3},{3,7},{7,5},{5,1},{8,10},{10,14},{14... | collective-permute-start | bytes 4718600 | tf_op jit(solution)/shard_map/ppermute | solution.py:48
  776.9 21.5 %collective-permute-start.58 = (bf16[4,64,2048]{2,1,0:T(8,128)(2,1)}, bf16[4,64,2048]{2,1,0:T(8,128)(2,1)}, u32[]{:S(2)}, u32[]{:S(2)}) collective-permute-start(bf16[4,64,2048]{2,1,0:T(8,128)(2,1)} %dynamic-slice_bitcast_fusion.2), channel_id=1, source_target_pairs={{0,16},{16,0},{1,17},{17,1},{2,18},{18,2},{3,19},{19,3},{4,20},{20... | collective-permute-start | bytes 3145736 | tf_op jit(solution)/shard_map/ppermute | solution.py:48
  776.9 35.2 %collective-permute-start.57 = (bf16[2,2,2,64,128]{4,3,2,1,0:T(8,128)(2,1)S(1)}, bf16[2,2,2,64,128]{4,3,2,1,0:T(8,128)(2,1)S(1)}, u32[]{:S(2)}, u32[]{:S(2)}) collective-permute-start(bf16[2,2,2,64,128]{4,3,2,1,0:T(8,128)(2,1)S(1)} %fusion.41), channel_id=1, source_target_pairs={{0,2},{2,6},{6,4},{4,0},{1,3},{3,7},{7,5},{5,1},{8,10},{10,14},{14... | collective-permute-start | bytes 393224 | tf_op jit(solution)/shard_map/ppermute | solution.py:48
  814.5 14.8 %collective-permute-start.59 = (bf16[2,2,64,1536]{3,2,1,0:T(8,128)(2,1)S(1)}, bf16[2,2,64,1536]{3,2,1,0:T(8,128)(2,1)S(1)}, u32[]{:S(2)}, u32[]{:S(2)}) collective-permute-start(bf16[2,2,64,1536]{3,2,1,0:T(8,128)(2,1)S(1)} %dynamic-slice_bitcast_fusion.3), channel_id=1, source_target_pairs={{0,16},{16,0},{1,17},{17,1},{2,18},{18,2},{3,19},{19,3},{4,20},{20... | collective-permute-start | bytes 2359304 | tf_op jit(solution)/shard_map/ppermute | solution.py:48
  820.5 21.3 %collective-permute-start.60 = (bf16[2,2,2,64,128]{4,3,2,1,0:T(8,128)(2,1)S(1)}, bf16[2,2,2,64,128]{4,3,2,1,0:T(8,128)(2,1)S(1)}, u32[]{:S(2)}, u32[]{:S(2)}) collective-permute-start(bf16[2,2,2,64,128]{4,3,2,1,0:T(8,128)(2,1)S(1)} %fusion.40), channel_id=1, source_target_pairs={{0,2},{2,6},{6,4},{4,0},{1,3},{3,7},{7,5},{5,1},{8,10},{10,14},{14... | collective-permute-start | bytes 393224 | tf_op jit(solution)/shard_map/ppermute | solution.py:48
  820.6 21.2 %collective-permute-start.61 = (bf16[64,2048]{1,0:T(8,128)(2,1)S(1)}, bf16[64,2048]{1,0:T(8,128)(2,1)S(1)}, u32[]{:S(2)}, u32[]{:S(2)}) collective-permute-start(bf16[64,2048]{1,0:T(8,128)(2,1)S(1)} %dynamic-slice_bitcast_fusion.6), channel_id=1, source_target_pairs={{0,2},{2,6},{6,4},{4,0},{1,3},{3,7},{7,5},{5,1},{8,10},{10,14},{14... | collective-permute-start | bytes 786440 | tf_op jit(solution)/shard_map/ppermute | solution.py:48
  843.2 10.0 %collective-permute-start.65 = (bf16[64,2048]{1,0:T(8,128)(2,1)S(1)}, bf16[64,2048]{1,0:T(8,128)(2,1)S(1)}, u32[]{:S(2)}, u32[]{:S(2)}) collective-permute-start(bf16[64,2048]{1,0:T(8,128)(2,1)S(1)} %fusion.26), channel_id=1, source_target_pairs={{0,2},{2,6},{6,4},{4,0},{1,3},{3,7},{7,5},{5,1},{8,10},{10,14},{14... | collective-permute-start | bytes 786440 | tf_op jit(solution)/shard_map/ppermute | solution.py:48
  847.2 8.2 collective-permute-start.63
  (73 other events, 1283.7 us)
Sparse Core Ops, SparseCore 0:
  47.8 63.6 all-gather.3
  113.1 61.5 all-gather.5
  176.3 58.2 all-gather.7
  530.8 70.3 reduce-scatter.3
  603.9 71.7 reduce-scatter.5
  678.1 71.7 reduce-scatter.7

commit v5 on v4

--- a/solution.py
+++ b/solution.py
@@ -294,9 +294,6 @@
     )(lengths, qkv, mixed_grad, gains, cosine, sine)
 
 
-TILE = 256
-
-
 def experts_kernel(sizes, places_ref, *refs):
     part, groups, rows, experts, slots, local, ff = sizes
     take = iter(refs)
@@ -361,19 +358,16 @@
         gate_slots = jnp.concatenate(gates, axis=0)
         onehots = onehot_v[q]
 
-        @pl.loop(0, D // TILE)
-        def _(n):
-            at = pl.ds(pl.multiple_of(n * TILE, TILE), TILE)
-            sent = plain(onehots, rows_v[i, lo : lo + rows, at]).astype(BF)
-            cots = plain(onehots, cots_v[i, lo : lo + rows, at])
-            grads = (cots * gate_slots).astype(BF)
-            cots = cots.astype(BF)
-            for j in range(local):
-                window = slice(j * slots, (j + 1) * slots)
-                place = slice(q * slots, (q + 1) * slots)
-                sent_v[j, place, at] = sent[window]
-                cot_slots_v[j, place, at] = cots[window]
-                grad_v[j, place, at] = grads[window]
+        sent = plain(onehots, rows_v[i, lo : lo + rows, :D]).astype(BF)
+        cots = plain(onehots, cots_v[i, lo : lo + rows, :D])
+        grads = (cots * gate_slots).astype(BF)
+        cots = cots.astype(BF)
+        for j in range(local):
+            window = slice(j * slots, (j + 1) * slots)
+            place = slice(q * slots, (q + 1) * slots)
+            sent_v[j, place, :] = sent[window]
+            cot_slots_v[j, place, :] = cots[window]
+            grad_v[j, place, :] = grads[window]
 
     stores = []
 
@@ -390,9 +384,9 @@
         for copy in weight_loads[j]:
             copy.wait()
 
-        @pl.loop(0, ff // TILE)
+        @pl.loop(0, ff // 512)
         def _(n):
-            at = pl.ds(pl.multiple_of(n * TILE, TILE), TILE)
+            at = pl.ds(pl.multiple_of(n * 512, 512), 512)
             gate_hidden = plain(sent_v[j], gate_v[j, :, at])
             up_hidden = plain(sent_v[j], up_v[j, :, at])
             active_grad = times_t(grad_v[j], down_v[j, at, :])
@@ -407,16 +401,17 @@
         store(2, active_v, j)
         store(3, gate_grad_v, j)
         store(4, up_grad_v, j)
+
         sum_v[j] = jnp.zeros_like(sum_v[j])
 
-        @pl.loop(0, D // TILE)
+        @pl.loop(0, D // 1024)
         def _(n):
-            at = pl.ds(pl.multiple_of(n * TILE, TILE), TILE)
+            at = pl.ds(pl.multiple_of(n * 1024, 1024), 1024)
             returned = plain(active_v[j], down_v[j, :, at]).astype(BF)
             returned_v[j, :, at] = returned
             product = cot_slots_v[j, :, at].astype(F32) * returned.astype(F32)
             folded = product[:, :128]
-            for m in range(1, TILE // 128):
+            for m in range(1, 1024 // 128):
                 folded = folded + product[:, m * 128 : (m + 1) * 128]
             sum_v[j] += folded
             sent_grad = times_t(gate_grad_v[j], gate_v[j, at, :])
@@ -439,13 +434,10 @@
         back_refs[i][lo : lo + rows, D:] = table.T.astype(BF)
         onehots, gates = onehot_v[q], gated_v[q]
 
-        @pl.loop(0, D // TILE)
-        def _(n):
-            at = pl.ds(pl.multiple_of(n * TILE, TILE), TILE)
-            returned = jnp.concatenate([returned_v[j, place, at] for j in range(local)], axis=0)
-            sent_grad = jnp.concatenate([sent_grad_v[j, place, at] for j in range(local)], axis=0)
-            combined_refs[i][lo : lo + rows, at] = inner(gates, returned).astype(BF)
-            back_refs[i][lo : lo + rows, at] = inner(onehots, sent_grad).astype(BF)
+        returned = jnp.concatenate([returned_v[j, place, :] for j in range(local)], axis=0)
+        sent_grad = jnp.concatenate([sent_grad_v[j, place, :] for j in range(local)], axis=0)
+        combined_refs[i][lo : lo + rows, :] = inner(gates, returned).astype(BF)
+        back_refs[i][lo : lo + rows, :D] = inner(onehots, sent_grad).astype(BF)
 
     for copy in stores:
         copy.wait()
@@ -652,9 +644,8 @@
     cot_blocks = {(0, kx): v for (kx,), v in gather_blocks(cot_rows, ("x",)).items()}
     block = tied(block, out_hops[1])
     late = list(gather_blocks(block, ("y",)).values())
-    late = jnp.concatenate(late, axis=0)
+    late = jnp.concatenate(tied(late, out_hops[2:3]), axis=0)
     weight_shards = tied((gate_weight, up_weight, down_weight), late)
-    late = tied(late, out_hops[2:3])
 
     def offsets_of(kz):
         return [
@@ -893,6 +884,10 @@
     late_total = part_of(late, "z", 2, 1)
     output_x = output_y = output_total = None
     small_hops, output_hops = 0, 0
+    expert_totals = [
+        lax.psum_scatter(grad, ("y", "c"), scatter_dimension=1, tiled=True).astype(F32)
+        for grad in (down_grads, gate_grads, up_grads)
+    ]
     for n, k in enumerate(ring):
         arrived = {"late": shift(late_total.astype(BF), "z", 1)}
         if n == 0:
@@ -903,6 +898,7 @@
             arrived["x"] = reduce_axis(tied(output_grad, late_total), "x", 2).astype(BF)
         if n == 2:
             arrived["y"] = reduce_axis(output_x, "y", 0).astype(BF)
+            arrived["experts"] = expert_totals
         if n >= 1:
             arrived["small"] = shift(small_total.astype(BF), "z", 1)
         arrived = lax.optimization_barrier(arrived)
@@ -915,6 +911,7 @@
             output_x = arrived["x"]
         if n == 2:
             output_y = arrived["y"]
+            expert_totals = arrived["experts"]
             output_total = part_of(output_y, "z", 0, 1)
         if n >= 1:
             part = part_of(small, "z", 2, ring[small_hops])
@@ -922,13 +919,9 @@
             small_hops += 1
     combined = final(combined_chain)
     layer_out = (hidden + combined).astype(BF)
-    expert_totals = [
-        lax.psum_scatter(grad, ("y", "c"), scatter_dimension=1, tiled=True).astype(F32)
-        for grad in (down_grads, gate_grads, up_grads)
-    ]
     late = reduce_axis(late_total.astype(BF), "y", 0).astype(BF)
     arrived = [shift(small_total.astype(BF), "z", 1), shift(output_total.astype(BF), "z", 1)]
-    late, arrived, expert_totals = lax.optimization_barrier((late, arrived, expert_totals))
+    late, arrived = lax.optimization_barrier((late, arrived))
     small = part_of(small, "z", 2, 0) + arrived[0].astype(F32)
     small = reduce_axis(small.astype(BF), "y", 0).astype(BF)
     output_total = part_of(output_y, "z", 0, ring[output_hops]) + arrived[1].astype(F32)

time: 886 us -> 851 us (0.960)
  Pallas kernels: 237 us -> 186 us
  waiting for transfers between devices: 356 us -> 373 us
    pallas_call x4, Pallas kernels: 191 us -> 140 us  [run_experts(): pl.pallas_call(functools.partial(experts_kernel, sizes), out_shape=(*[jax...]
    ppermute x63, waiting for transfers between devices: 352 us -> 369 us  [shift(): return lax.ppermute(value, axis, pairs)]
  transfers between devices with their start and end apart: 73 -> 73, of which waited for: 30 -> 35; matrix products, arithmetic and copies ran while one was open for 20% -> 20% of each run, Pallas kernels for 27% -> 22%
where the time goes in v5:
time: 851 us; the launch traced here: 837 us
  waiting for transfers between devices  373 us (44%)
  Pallas kernels  186 us (22%)
  matrix products  96.5 us (11%)
  starting transfers between devices  69.6 us (8%)
  other arithmetic  63.4 us (7%)
  local copies, waits for them, and re-layouts  32.4 us (4%)
  between operations  16 us (2%)
    ppermute x63, waiting for transfers between devices, shift(): return lax.ppermute(value, axis, pairs)  369 us
    pallas_call x4, Pallas kernels, run_experts(): pl.pallas_call(functools.partial(experts_kernel, sizes), out_shape=(*[jax...  140 us
    ppermute x63, starting transfers between devices, shift(): return lax.ppermute(value, axis, pairs)  68.5 us
    dot_general x3, matrix products, weight_grads(): lax.dot_general(kept[left], kept[right], (((1,), (1,)), ((0,), (0,))), pr...  54.6 us
    pallas_call x1, Pallas kernels, attend_back(): pl.pallas_call(functools.partial(attend_back_kernel, heads), out_shape=(j...  21.9 us
  transfers between devices with their start and end apart: 73, of which 35 were waited for; matrix products, arithmetic and copies ran while one was open for 20% of the time, Pallas kernels for 22%

profile of v5, /device:TPU:0, one launch (start us, length us, event | category | flops | bytes accessed | tf_op | source)
XLA Modules:
  0.0 836.8 jit_solution(11971551765203927939)
XLA Ops:
  13.8 2.9 collective-permute-start.4
  18.3 8.5 %collective-permute-done.4 = bf16[128,1664]{1,0:T(8,128)(2,1)S(1)} collective-permute-done((bf16[128,1664]{1,0:T(8,128)(2,1)S(1)}, bf16[128,1664]{1,0:T(8,128)(2,1)S(1)}, u32[]{:S(2)}, u32[]{:S(2)}) %collective-permute-start.4) | collective-permute-done | bytes 426016 | tf_op jit(solution)/shard_map/ppermute | solution.py:48
  30.4 6.6 collective-permute-done.7
  37.7 9.9 %collective-permute-done.6 = bf16[256,1664]{1,0:T(8,128)(2,1)S(1)} collective-permute-done((bf16[256,1664]{1,0:T(8,128)(2,1)S(1)}, bf16[256,1664]{1,0:T(8,128)(2,1)S(1)}, u32[]{:S(2)}, u32[]{:S(2)}) %collective-permute-start.6) | collective-permute-done | bytes 852000 | tf_op jit(solution)/shard_map/ppermute | solution.py:48
  53.6 2.6 collective-permute-start.9
  56.2 2.5 fusion.25.refs_2_
  59.2 35.0 %collective-permute-done.9 = bf16[64,2048]{1,0:T(8,128)(2,1)S(1)} collective-permute-done((bf16[64,2048]{1,0:T(8,128)(2,1)}, bf16[64,2048]{1,0:T(8,128)(2,1)S(1)}, u32[]{:S(2)}, u32[]{:S(2)}) %collective-permute-start.9) | collective-permute-done | bytes 262176 | tf_op jit(solution)/shard_map/ppermute | solution.py:48
  98.1 30.0 %collective-permute-done.14 = bf16[256,2048]{1,0:T(8,128)(2,1)} collective-permute-done((bf16[256,2048]{1,0:T(8,128)(2,1)S(1)}, bf16[256,2048]{1,0:T(8,128)(2,1)}, u32[]{:S(2)}, u32[]{:S(2)}) %collective-permute-start.14) | collective-permute-done | bytes 1048608 | tf_op jit(solution)/shard_map/ppermute | solution.py:48
  128.2 3.4 collective-permute-done.13.refs_2_
  134.0 2.6 fusion
  140.2 28.9 %collective-permute-done.16.refs_3_ = bf16[512,1664]{1,0:T(8,128)(2,1)} collective-permute-done((bf16[512,1664]{1,0:T(8,128)(2,1)}, bf16[512,1664]{1,0:T(8,128)(2,1)}, u32[]{:S(2)}, u32[]{:S(2)}) %collective-permute-start.16) | collective-permute-done | bytes 1703968 | tf_op jit(solution)/shard_map/ppermute | solution.py:48
  169.0 7.3 shard_map.272
  176.3 2.8 copy-done
  181.3 10.8 %fusion.5.qkv_ref = f32[1024,1536]{1,0:T(8,128)S(1)} fusion(bf16[2048,1664]{1,0:T(8,128)(2,1)} %copy-done, f32[2048]{0:T(1024)S(1)} %get-tuple-element.387, f32[1024]{0:T(1024)S(1)} %add_rsqrt_fusion, bf16[256,2048]{1,0:T(8,128)(2,1)} %collective-permute-done.12, bf16[256,2048]{1,0:T(8,128)(2,1)} %collective-permute-done.10, ...), kind=kOutput, calls=%fused_computation.8 | convolution fusion | flops 6465519616 | bytes 16789504 | tf_op jit(solution)/shard_map/dot_general | solution.py:26
  192.1 12.1 %collective-permute-done.17.refs_2_ = bf16[256,2176]{1,0:T(8,128)(2,1)} collective-permute-done((bf16[256,2176]{1,0:T(8,128)(2,1)}, bf16[256,2176]{1,0:T(8,128)(2,1)}, u32[]{:S(2)}, u32[]{:S(2)}) %collective-permute-start.17) | collective-permute-done | bytes 1114144 | tf_op jit(solution)/shard_map/ppermute | solution.py:48
  206.8 14.6 %shard_map.273 = bf16[1024,512]{1,0:T(8,128)(2,1)S(1)} custom-call(s32[8]{0:T(128)S(1)} %pad_add_fusion.lengths_ref, f32[1024,1536]{1,0:T(8,128)S(1)} %fusion.5.qkv_ref, f32[2,128]{1,0:T(2,128)S(1)} %pad_maximum_fusion.13.gains_ref, f32[128,128]{1,0:T(8,128)S(1)} %get-tuple-element.470.cosine_ref, f32[128,128]{1,0:T(8,128)S(1)} %get-tuple-element.471.sine_ref), custom_call_target="tpu_custom_call" | custom-call | flops 14000000000 | bytes 14680064 | tf_op jit(solution)/shard_map/pallas_call | solution.py:247
  222.8 2.4 shard_map.274
  225.2 14.7 %collective-permute-done.19 = bf16[512,512]{1,0:T(8,128)(2,1)} collective-permute-done((bf16[512,512]{1,0:T(8,128)(2,1)}, bf16[512,512]{1,0:T(8,128)(2,1)}, u32[]{:S(2)}, u32[]{:S(2)}) %collective-permute-start.19) | collective-permute-done | bytes 524320 | tf_op jit(solution)/shard_map/ppermute | solution.py:48
  240.9 2.4 fusion.77
  252.5 19.2 %collective-permute-done.23.refs_2_ = bf16[256,2176]{1,0:T(8,128)(2,1)} collective-permute-done((bf16[256,2176]{1,0:T(8,128)(2,1)}, bf16[256,2176]{1,0:T(8,128)(2,1)}, u32[]{:S(2)}, u32[]{:S(2)}) %collective-permute-start.23) | collective-permute-done | bytes 1114144 | tf_op jit(solution)/shard_map/ppermute | solution.py:48
  275.1 25.1 %collective-permute-done.25.refs_1_ = bf16[256,2176]{1,0:T(8,128)(2,1)S(1)} collective-permute-done((bf16[256,2176]{1,0:T(8,128)(2,1)S(1)}, bf16[256,2176]{1,0:T(8,128)(2,1)S(1)}, u32[]{:S(2)}, u32[]{:S(2)}) %collective-permute-start.25) | collective-permute-done | bytes 1114144 | tf_op jit(solution)/shard_map/ppermute | solution.py:48
  303.3 31.9 %shard_map.275 = (bf16[256,2048]{1,0:T(8,128)(2,1)}, bf16[256,2048]{1,0:T(8,128)(2,1)}, bf16[256,2176]{1,0:T(8,128)(2,1)}, bf16[256,2176]{1,0:T(8,128)(2,1)}, bf...) custom-call(s32[1]{0:T(128)} %bitcast.68.places_ref, ...), custom_call_target="tpu_custom_call" | custom-call | flops 53687091200 | bytes 41943040 | tf_op jit(solution)/shard_map/pallas_call | solution.py:481
  335.3 11.2 %collective-permute-done.27.refs_1_ = bf16[256,2176]{1,0:T(8,128)(2,1)} collective-permute-done((bf16[256,2176]{1,0:T(8,128)(2,1)}, bf16[256,2176]{1,0:T(8,128)(2,1)}, u32[]{:S(2)}, u32[]{:S(2)}) %collective-permute-start.27) | collective-permute-done | bytes 1114144 | tf_op jit(solution)/shard_map/ppermute | solution.py:48
  349.0 41.7 %shard_map.276 = (bf16[256,2048]{1,0:T(8,128)(2,1)}, bf16[256,2048]{1,0:T(8,128)(2,1)}, bf16[256,2176]{1,0:T(8,128)(2,1)}, bf16[256,2176]{1,0:T(8,128)(2,1)}, bf...) custom-call(s32[1]{0:T(128)} %bitcast.68.places_ref, ...), custom_call_target="tpu_custom_call", output_to_operand_aliasing={{4}: (8, {}), {5}: (9, {}), {6}: (10, {}), {7}: (11, {}), {... | custom-call | flops 53687091200 | bytes 41943040 | tf_op jit(solution)/shard_map/pallas_call | solution.py:481
  392.6 5.2 collective-permute-done.31
  399.5 33.2 %shard_map.277 = (bf16[256,2048]{1,0:T(8,128)(2,1)}, bf16[256,2048]{1,0:T(8,128)(2,1)}, bf16[256,2176]{1,0:T(8,128)(2,1)}, bf16[256,2176]{1,0:T(8,128)(2,1)}, bf...) custom-call(s32[1]{0:T(128)} %bitcast.68.places_ref, ...), custom_call_target="tpu_custom_call", output_to_operand_aliasing={{4}: (8, {}), {5}: (9, {}), {6}: (10, {}), {7}: (11, {}), {... | custom-call | flops 53687091200 | bytes 41943040 | tf_op jit(solution)/shard_map/pallas_call | solution.py:481
  433.5 12.1 %collective-permute-done.32.refs_1_ = bf16[256,2176]{1,0:T(8,128)(2,1)} collective-permute-done((bf16[256,2176]{1,0:T(8,128)(2,1)}, bf16[256,2176]{1,0:T(8,128)(2,1)}, u32[]{:S(2)}, u32[]{:S(2)}) %collective-permute-start.32) | collective-permute-done | bytes 1114144 | tf_op jit(solution)/shard_map/ppermute | solution.py:48
  445.7 2.5 add_convert_fusion.2
  448.8 33.4 %shard_map.278 = (bf16[256,2048]{1,0:T(8,128)(2,1)}, bf16[256,2048]{1,0:T(8,128)(2,1)}, bf16[256,2176]{1,0:T(8,128)(2,1)}, bf16[256,2176]{1,0:T(8,128)(2,1)}, bf...) custom-call(s32[1]{0:T(128)} %bitcast.68.places_ref, ...), custom_call_target="tpu_custom_call", output_to_operand_aliasing={{4}: (8, {}), {5}: (9, {}), {6}: (10, {}), {7}: (11, {}), {... | custom-call | flops 53687091200 | bytes 41943040 | tf_op jit(solution)/shard_map/pallas_call | solution.py:481
  486.7 17.8 %convolution_convert_fusion.3 = bf16[2,1024,2048]{2,1,0:T(8,128)(2,1)} fusion(bf16[2,1280,1024]{2,1,0:T(8,128)(2,1)} %get-tuple-element.232, bf16[2,1280,2048]{2,1,0:T(8,128)(2,1)} %get-tuple-element.233), kind=kOutput, calls=%fused_computation.12 | convolution fusion | flops 10741612544 | bytes 24117248 | tf_op jit(solution)/shard_map/dot_general | solution.py:801
  504.5 3.3 collective-permute-done.38
  508.3 2.6 add_convert_fusion
  511.4 19.4 %convolution_convert_fusion.1 = bf16[2,2048,1024]{2,1,0:T(8,128)(2,1)} fusion(bf16[2,1280,2048]{2,1,0:T(8,128)(2,1)} %get-tuple-element.241, bf16[2,1280,1024]{2,1,0:T(8,128)(2,1)} %get-tuple-element.243), kind=kOutput, calls=%fused_computation.10 | convolution fusion | flops 10741612544 | bytes 24117248 | tf_op jit(solution)/shard_map/dot_general | solution.py:801
  530.8 17.3 %convolution_convert_fusion.2 = bf16[2,2048,1024]{2,1,0:T(8,128)(2,1)} fusion(bf16[2,1280,2048]{2,1,0:T(8,128)(2,1)} %get-tuple-element.241, bf16[2,1280,1024]{2,1,0:T(8,128)(2,1)} %get-tuple-element.242), kind=kOutput, calls=%fused_computation.11 | convolution fusion | flops 10741612544 | bytes 24117248 | tf_op jit(solution)/shard_map/dot_general | solution.py:801
  555.1 2.7 collective-permute-done.41
  557.8 4.9 convolution_convert_fusion.6
  567.9 9.1 %collective-permute-done.42 = bf16[512,512]{1,0:T(8,128)(2,1)S(1)} collective-permute-done((bf16[512,512]{1,0:T(8,128)(2,1)S(1)}, bf16[512,512]{1,0:T(8,128)(2,1)S(1)}, u32[]{:S(2)}, u32[]{:S(2)}) %collective-permute-start.42) | collective-permute-done | bytes 524320 | tf_op jit(solution)/shard_map/ppermute | solution.py:48
  579.0 21.9 %shard_map.279 = (bf16[1024,1536]{1,0:T(8,128)(2,1)S(1)}, f32[2,128]{1,0:T(2,128)S(1)}) custom-call(s32[8]{0:T(128)S(1)} %pad_add_fusion.lengths_ref, f32[1024,1536]{1,0:T(8,128)S(1)} %bitcast.213, bf16[1024,512]{1,0:T(8,128)(2,1)S(1)} %pad_maximum_fusion.5.mixed_grad_ref, f32[2,128]{1,0:T(2,128)S(1)} %copy-done.7, ...), custom_call_target="tpu_custom_call" | custom-call | flops 20000000000 | bytes 20971520 | tf_op jit(solution)/shard_map/pallas_call | solution.py:271
  606.6 6.7 fusion.76
  614.2 8.9 %convolution_convert_fusion = bf16[2048,1536]{1,0:T(8,128)(2,1)S(1)} fusion(bf16[1024,1536]{1,0:T(8,128)(2,1)S(1)} %get-tuple-element.252, f32[2048]{0:T(1024)S(1)} %copy-done.50, f32[1024]{0:T(1024)S(1)} %copy-done.56, bf16[256,2048]{1,0:T(8,128)(2,1)} %collective-permute-done.12, bf16[256,2048]{1,0:T(8,128)(2,1)} %collective-permute-done.10, ...), kind=kOutput, calls=%fused_computation.5 | convolution fusion | flops 6468665344 | bytes 13643776 | tf_op jit(solution)/shard_map/dot_general | solution.py:30
  625.2 3.3 collective-permute-done.48
  632.7 2.8 add_convert_fusion.4
  638.2 3.9 convolution_convert_fusion.4
  642.2 13.2 %collective-permute-done.52 = bf16[256,2048]{1,0:T(8,128)(2,1)} collective-permute-done((bf16[256,2048]{1,0:T(8,128)(2,1)}, bf16[256,2048]{1,0:T(8,128)(2,1)}, u32[]{:S(2)}, u32[]{:S(2)}) %collective-permute-start.52) | collective-permute-done | bytes 1048608 | tf_op jit(solution)/shard_map/ppermute | solution.py:48
  657.0 31.9 %collective-permute-done.50 = bf16[256,2048]{1,0:T(8,128)(2,1)} collective-permute-done((bf16[256,2048]{1,0:T(8,128)(2,1)}, bf16[256,2048]{1,0:T(8,128)(2,1)}, u32[]{:S(2)}, u32[]{:S(2)}) %collective-permute-start.50) | collective-permute-done | bytes 1048608 | tf_op jit(solution)/shard_map/ppermute | solution.py:48
  688.9 3.5 convert_add_fusion.1
  698.0 2.6 collective-permute-start.54
  700.6 37.9 %collective-permute-done.55 = bf16[2,4,64,2048]{3,2,1,0:T(8,128)(2,1)} collective-permute-done((bf16[2,4,64,2048]{3,2,1,0:T(8,128)(2,1)}, bf16[2,4,64,2048]{3,2,1,0:T(8,128)(2,1)}, u32[]{:S(2)}, u32[]{:S(2)}) %collective-permute-start.55) | collective-permute-done | bytes 2097184 | tf_op jit(solution)/shard_map/ppermute | solution.py:48
  738.5 3.0 fusion.7
  741.6 4.2 fusion.8
  746.9 2.8 collective-permute-start.57
  749.8 18.4 %collective-permute-done.58 = bf16[4,64,2048]{2,1,0:T(8,128)(2,1)} collective-permute-done((bf16[4,64,2048]{2,1,0:T(8,128)(2,1)}, bf16[4,64,2048]{2,1,0:T(8,128)(2,1)}, u32[]{:S(2)}, u32[]{:S(2)}) %collective-permute-start.58) | collective-permute-done | bytes 1048608 | tf_op jit(solution)/shard_map/ppermute | solution.py:48
  770.2 4.1 convert_element_type.429
  774.3 4.1 convert_element_type.430
  778.4 4.1 convert_element_type.431
  782.5 2.5 fusion.9
  786.2 5.0 fusion.17
  791.2 2.4 collective-permute-start.60
  793.9 6.4 collective-permute-done.59
  800.5 3.1 collective-permute-done.61
  804.9 3.1 collective-permute-done.62
  808.5 4.6 collective-permute-done.65
  813.5 2.8 collective-permute-done.63
  816.6 4.1 collective-permute-done.66
  (405 shorter events, 116.9 us)
Async XLA Ops:
  7.2 296.1 %all-gather.4.cloned.1.call-start = ((), (), s32[]{:S(2)}) async-start(), calls=%async_computation.3 | async-start | bytes 10485760 | tf_op jit(solution)/shard_map/all_gather | solution.py:688
  13.8 13.0 %collective-permute-start.4 = (bf16[128,1664]{1,0:T(8,128)(2,1)S(1)}, bf16[128,1664]{1,0:T(8,128)(2,1)S(1)}, u32[]{:S(2)}, u32[]{:S(2)}) collective-permute-start(bf16[128,1664]{1,0:T(8,128)(2,1)S(1)} %get-tuple-element.415), channel_id=1, source_target_pairs={{0,1},{1,0},{2,3},{3,2},{4,5},{5,4},{6,7},{7,6},{8,9},{9,8},{10,11... | collective-permute-start | bytes 1277960 | tf_op jit(solution)/shard_map/ppermute | solution.py:48
  16.8 10.2 %collective-permute-start.5 = (bf16[64,2048]{1,0:T(8,128)(2,1)S(1)}, bf16[64,2048]{1,0:T(8,128)(2,1)S(1)}, u32[]{:S(2)}, u32[]{:S(2)}) collective-permute-start(bf16[64,2048]{1,0:T(8,128)(2,1)S(1)} %copy-done.41), channel_id=1, source_target_pairs={{0,2},{2,6},{6,4},{4,0},{1,3},{3,7},{7,5},{5,1},{8,10},{10,14},{14... | collective-permute-start | bytes 786440 | tf_op jit(solution)/shard_map/ppermute | solution.py:48
  27.0 20.5 %collective-permute-start.6 = (bf16[256,1664]{1,0:T(8,128)(2,1)S(1)}, bf16[256,1664]{1,0:T(8,128)(2,1)S(1)}, u32[]{:S(2)}, u32[]{:S(2)}) collective-permute-start(bf16[256,1664]{1,0:T(8,128)(2,1)S(1)} %pad_maximum_fusion.7), channel_id=1, source_target_pairs={{0,16},{16,0},{1,17},{17,1},{2,18},{18,2},{3,19},{19,3},{4,20},{20... | collective-permute-start | bytes 2555912 | tf_op jit(solution)/shard_map/ppermute | solution.py:48
  47.8 255.5 %all-gather.6.cloned.1.call-start = ((), (), s32[]{:S(2)}) async-start(), calls=%async_computation.4 | async-start | bytes 10485760 | tf_op jit(solution)/shard_map/all_gather | solution.py:688
  48.5 254.8 %all-gather.8.cloned.1.call-start = ((), (), s32[]{:S(2)}) async-start(), calls=%async_computation.5 | async-start | bytes 10485760 | tf_op jit(solution)/shard_map/all_gather | solution.py:688
  48.6 45.7 %collective-permute-start.10 = (bf16[256,2048]{1,0:T(8,128)(2,1)}, bf16[256,2048]{1,0:T(8,128)(2,1)}, u32[]{:S(2)}, u32[]{:S(2)}) collective-permute-start(bf16[256,2048]{1,0:T(8,128)(2,1)} %bitcast), channel_id=1, source_target_pairs={{0,1},{1,0},{2,3},{3,2},{4,5},{5,4},{6,7},{7,6},{8,9},{9,8},{10,11... | collective-permute-start | bytes 3145736 | tf_op jit(solution)/shard_map/ppermute | solution.py:48
  50.4 43.8 %collective-permute-start.8 = (bf16[512,1664]{1,0:T(8,128)(2,1)S(1)}, bf16[512,1664]{1,0:T(8,128)(2,1)S(1)}, u32[]{:S(2)}, u32[]{:S(2)}) collective-permute-start(bf16[512,1664]{1,0:T(8,128)(2,1)S(1)} %constant_dynamic-update-slice_fusion.refs_0_), channel_id=1, source_target_pairs={{0,2},{2,6},{6,4},{4,0},{1,3},{3,7},{7,5},{5,1},{8,10},{10,14},{14... | collective-permute-start | bytes 5111816 | tf_op jit(solution)/shard_map/ppermute | solution.py:48
  53.6 40.6 %collective-permute-start.9 = (bf16[64,2048]{1,0:T(8,128)(2,1)}, bf16[64,2048]{1,0:T(8,128)(2,1)S(1)}, u32[]{:S(2)}, u32[]{:S(2)}) collective-permute-start(bf16[64,2048]{1,0:T(8,128)(2,1)} %copy-done.45), channel_id=1, source_target_pairs={{0,2},{2,6},{6,4},{4,0},{1,3},{3,7},{7,5},{5,1},{8,10},{10,14},{14... | collective-permute-start | bytes 786440 | tf_op jit(solution)/shard_map/ppermute | solution.py:48
  58.7 38.8 %collective-permute-start.15 = (bf16[256,2176]{1,0:T(8,128)(2,1)}, bf16[256,2176]{1,0:T(8,128)(2,1)}, u32[]{:S(2)}, u32[]{:S(2)}) collective-permute-start(bf16[256,2176]{1,0:T(8,128)(2,1)} %fusion.25.refs_2_), channel_id=1, source_target_pairs={{0,1},{1,0},{2,3},{3,2},{4,5},{5,4},{6,7},{7,6},{8,9},{9,8},{10,11... | collective-permute-start | bytes 3342344 | tf_op jit(solution)/shard_map/ppermute | solution.py:48
  94.2 37.4 %collective-permute-start.13 = (bf16[512,1664]{1,0:T(8,128)(2,1)S(1)}, bf16[512,1664]{1,0:T(8,128)(2,1)}, u32[]{:S(2)}, u32[]{:S(2)}) collective-permute-start(bf16[512,1664]{1,0:T(8,128)(2,1)S(1)} %collective-permute-done.8.refs_1_), channel_id=1, source_target_pairs={{0,2},{2,6},{6,4},{4,0},{1,3},{3,7},{7,5},{5,1},{8,10},{10,14},{14... | collective-permute-start | bytes 5111816 | tf_op jit(solution)/shard_map/ppermute | solution.py:48
  95.3 32.9 %collective-permute-start.14 = (bf16[256,2048]{1,0:T(8,128)(2,1)S(1)}, bf16[256,2048]{1,0:T(8,128)(2,1)}, u32[]{:S(2)}, u32[]{:S(2)}) collective-permute-start(bf16[256,2048]{1,0:T(8,128)(2,1)S(1)} %constant_dynamic-update-slice_fusion.2), channel_id=1, source_target_pairs={{0,16},{16,0},{1,17},{17,1},{2,18},{18,2},{3,19},{19,3},{4,20},{20... | collective-permute-start | bytes 3145736 | tf_op jit(solution)/shard_map/ppermute | solution.py:48
  96.9 37.1 %collective-permute-start.11 = (bf16[256,2048]{1,0:T(8,128)(2,1)}, bf16[256,2048]{1,0:T(8,128)(2,1)}, u32[]{:S(2)}, u32[]{:S(2)}) collective-permute-start(bf16[256,2048]{1,0:T(8,128)(2,1)} %bitcast), channel_id=1, source_target_pairs={{0,8},{8,0},{1,9},{9,1},{2,10},{10,2},{3,11},{11,3},{4,12},{12,4},... | collective-permute-start | bytes 3145736 | tf_op jit(solution)/shard_map/ppermute | solution.py:574
  96.9 37.1 %collective-permute-start.12 = (bf16[256,2048]{1,0:T(8,128)(2,1)}, bf16[256,2048]{1,0:T(8,128)(2,1)}, u32[]{:S(2)}, u32[]{:S(2)}) collective-permute-start(bf16[256,2048]{1,0:T(8,128)(2,1)} %collective-permute-done.10), channel_id=1, source_target_pairs={{0,8},{8,0},{1,9},{9,1},{2,10},{10,2},{3,11},{11,3},{4,12},{12,4},... | collective-permute-start | bytes 3145736 | tf_op jit(solution)/shard_map/ppermute | solution.py:574
  97.5 35.1 %collective-permute-start.1 = (s32[2]{0:T(128)S(1)}, s32[2]{0:T(128)S(1)}, u32[]{:S(2)}, u32[]{:S(2)}) collective-permute-start(s32[2]{0:T(128)S(1)} %bitcast.233), channel_id=1, source_target_pairs={{0,1},{1,0},{2,3},{3,2},{4,5},{5,4},{6,7},{7,6},{8,9},{9,8},{10,11... | collective-permute-start | bytes 32 | tf_op jit(solution)/shard_map/ppermute | solution.py:48
  131.6 37.4 %collective-permute-start.16 = (bf16[512,1664]{1,0:T(8,128)(2,1)}, bf16[512,1664]{1,0:T(8,128)(2,1)}, u32[]{:S(2)}, u32[]{:S(2)}) collective-permute-start(bf16[512,1664]{1,0:T(8,128)(2,1)} %collective-permute-done.13.refs_2_), channel_id=1, source_target_pairs={{0,2},{2,6},{6,4},{4,0},{1,3},{3,7},{7,5},{5,1},{8,10},{10,14},{14... | collective-permute-start | bytes 5111816 | tf_op jit(solution)/shard_map/ppermute | solution.py:48
  134.0 636.2 %reduce-scatter.4.cloned.1.call-start = ((), (), s32[]{:S(2)}) async-start(), calls=%async_computation.6 | async-start | bytes 10485760 | tf_op jit(solution)/shard_map/reduce_scatter | solution.py:888
  139.5 52.6 %collective-permute-start.18 = (bf16[512,2048]{1,0:T(8,128)(2,1)S(1)}, bf16[512,2048]{1,0:T(8,128)(2,1)}, u32[]{:S(2)}, u32[]{:S(2)}) collective-permute-start(bf16[512,2048]{1,0:T(8,128)(2,1)S(1)} %constant_dynamic-update-slice_fusion.6.refs_0_), channel_id=1, source_target_pairs={{0,1},{1,0},{2,3},{3,2},{4,5},{5,4},{6,7},{7,6},{8,9},{9,8},{10,11... | collective-permute-start | bytes 6291464 | tf_op jit(solution)/shard_map/ppermute | solution.py:48
  179.7 24.5 %collective-permute-start.17 = (bf16[256,2176]{1,0:T(8,128)(2,1)}, bf16[256,2176]{1,0:T(8,128)(2,1)}, u32[]{:S(2)}, u32[]{:S(2)}) collective-permute-start(bf16[256,2176]{1,0:T(8,128)(2,1)} %fusion.25.refs_2_), channel_id=1, source_target_pairs={{0,2},{2,6},{6,4},{4,0},{1,3},{3,7},{7,5},{5,1},{8,10},{10,14},{14... | collective-permute-start | bytes 3342344 | tf_op jit(solution)/shard_map/ppermute | solution.py:48
  204.2 36.7 %collective-permute-start.20 = (bf16[256,2176]{1,0:T(8,128)(2,1)}, bf16[256,2176]{1,0:T(8,128)(2,1)}, u32[]{:S(2)}, u32[]{:S(2)}) collective-permute-start(bf16[256,2176]{1,0:T(8,128)(2,1)} %collective-permute-done.17.refs_2_), channel_id=1, source_target_pairs={{0,2},{2,6},{6,4},{4,0},{1,3},{3,7},{7,5},{5,1},{8,10},{10,14},{14... | collective-permute-start | bytes 3342344 | tf_op jit(solution)/shard_map/ppermute | solution.py:48
  205.1 35.9 %collective-permute-start.21 = (bf16[256,2176]{1,0:T(8,128)(2,1)}, bf16[256,2176]{1,0:T(8,128)(2,1)}, u32[]{:S(2)}, u32[]{:S(2)}) collective-permute-start(bf16[256,2176]{1,0:T(8,128)(2,1)} %collective-permute-done.17.refs_2_), channel_id=1, source_target_pairs={{0,1},{1,0},{2,3},{3,2},{4,5},{5,4},{6,7},{7,6},{8,9},{9,8},{10,11... | collective-permute-start | bytes 3342344 | tf_op jit(solution)/shard_map/ppermute | solution.py:48
  222.4 17.4 %collective-permute-start.19 = (bf16[512,512]{1,0:T(8,128)(2,1)}, bf16[512,512]{1,0:T(8,128)(2,1)}, u32[]{:S(2)}, u32[]{:S(2)}) collective-permute-start(bf16[512,512]{1,0:T(8,128)(2,1)} %get-tuple-element.408), channel_id=1, source_target_pairs={{0,1},{1,0},{2,3},{3,2},{4,5},{5,4},{6,7},{7,6},{8,9},{9,8},{10,11... | collective-permute-start | bytes 1572872 | tf_op jit(solution)/shard_map/ppermute | solution.py:48
  243.6 28.2 %collective-permute-start.23 = (bf16[256,2176]{1,0:T(8,128)(2,1)}, bf16[256,2176]{1,0:T(8,128)(2,1)}, u32[]{:S(2)}, u32[]{:S(2)}) collective-permute-start(bf16[256,2176]{1,0:T(8,128)(2,1)} %collective-permute-done.20.refs_2_), channel_id=1, source_target_pairs={{0,2},{2,6},{6,4},{4,0},{1,3},{3,7},{7,5},{5,1},{8,10},{10,14},{14... | collective-permute-start | bytes 3342344 | tf_op jit(solution)/shard_map/ppermute | solution.py:48
  245.8 27.0 %collective-permute-start.24 = (bf16[256,2176]{1,0:T(8,128)(2,1)}, bf16[256,2176]{1,0:T(8,128)(2,1)}, u32[]{:S(2)}, u32[]{:S(2)}) collective-permute-start(bf16[256,2176]{1,0:T(8,128)(2,1)} %collective-permute-done.20.refs_2_), channel_id=1, source_target_pairs={{0,1},{1,0},{2,3},{3,2},{4,5},{5,4},{6,7},{7,6},{8,9},{9,8},{10,11... | collective-permute-start | bytes 3342344 | tf_op jit(solution)/shard_map/ppermute | solution.py:48
  272.8 27.5 %collective-permute-start.25 = (bf16[256,2176]{1,0:T(8,128)(2,1)S(1)}, bf16[256,2176]{1,0:T(8,128)(2,1)S(1)}, u32[]{:S(2)}, u32[]{:S(2)}) collective-permute-start(bf16[256,2176]{1,0:T(8,128)(2,1)S(1)} %pad_maximum_fusion.4.refs_0_), channel_id=1, source_target_pairs={{0,1},{1,0},{2,3},{3,2},{4,5},{5,4},{6,7},{7,6},{8,9},{9,8},{10,11... | collective-permute-start | bytes 3342344 | tf_op jit(solution)/shard_map/ppermute | solution.py:48
  274.5 26.5 %collective-permute-start.26 = (bf16[256,2176]{1,0:T(8,128)(2,1)S(1)}, bf16[256,2176]{1,0:T(8,128)(2,1)}, u32[]{:S(2)}, u32[]{:S(2)}) collective-permute-start(bf16[256,2176]{1,0:T(8,128)(2,1)S(1)} %pad_maximum_fusion.4.refs_0_), channel_id=1, source_target_pairs={{0,2},{2,6},{6,4},{4,0},{1,3},{3,7},{7,5},{5,1},{8,10},{10,14},{14... | collective-permute-start | bytes 3342344 | tf_op jit(solution)/shard_map/ppermute | solution.py:48
  274.8 173.9 %collective-permute-start.34 = (bf16[256,2176]{1,0:T(8,128)(2,1)}, bf16[256,2176]{1,0:T(8,128)(2,1)}, u32[]{:S(2)}, u32[]{:S(2)}) collective-permute-start(bf16[256,2176]{1,0:T(8,128)(2,1)} %collective-permute-done.23.refs_2_), channel_id=1, source_target_pairs={{0,1},{1,0},{2,3},{3,2},{4,5},{5,4},{6,7},{7,6},{8,9},{9,8},{10,11... | collective-permute-start | bytes 3342344 | tf_op jit(solution)/shard_map/ppermute | solution.py:48
  301.3 45.2 %collective-permute-start.27 = (bf16[256,2176]{1,0:T(8,128)(2,1)}, bf16[256,2176]{1,0:T(8,128)(2,1)}, u32[]{:S(2)}, u32[]{:S(2)}) collective-permute-start(bf16[256,2176]{1,0:T(8,128)(2,1)} %collective-permute-done.26.refs_0_), channel_id=1, source_target_pairs={{0,1},{1,0},{2,3},{3,2},{4,5},{5,4},{6,7},{7,6},{8,9},{9,8},{10,11... | collective-permute-start | bytes 3342344 | tf_op jit(solution)/shard_map/ppermute | solution.py:48
  303.0 43.4 %collective-permute-start.28 = (bf16[256,2176]{1,0:T(8,128)(2,1)}, bf16[256,2176]{1,0:T(8,128)(2,1)S(1)}, u32[]{:S(2)}, u32[]{:S(2)}) collective-permute-start(bf16[256,2176]{1,0:T(8,128)(2,1)} %collective-permute-done.26.refs_0_), channel_id=1, source_target_pairs={{0,2},{2,6},{6,4},{4,0},{1,3},{3,7},{7,5},{5,1},{8,10},{10,14},{14... | collective-permute-start | bytes 3342344 | tf_op jit(solution)/shard_map/ppermute | solution.py:48
  346.4 46.2 %collective-permute-start.29 = (bf16[256,2176]{1,0:T(8,128)(2,1)S(1)}, bf16[256,2176]{1,0:T(8,128)(2,1)S(1)}, u32[]{:S(2)}, u32[]{:S(2)}) collective-permute-start(bf16[256,2176]{1,0:T(8,128)(2,1)S(1)} %collective-permute-done.28.refs_0_), channel_id=1, source_target_pairs={{0,1},{1,0},{2,3},{3,2},{4,5},{5,4},{6,7},{7,6},{8,9},{9,8},{10,11... | collective-permute-start | bytes 3342344 | tf_op jit(solution)/shard_map/ppermute | solution.py:48
  348.1 44.5 %collective-permute-start.30 = (bf16[256,2176]{1,0:T(8,128)(2,1)S(1)}, bf16[256,2176]{1,0:T(8,128)(2,1)}, u32[]{:S(2)}, u32[]{:S(2)}) collective-permute-start(bf16[256,2176]{1,0:T(8,128)(2,1)S(1)} %collective-permute-done.28.refs_0_), channel_id=1, source_target_pairs={{0,2},{2,6},{6,4},{4,0},{1,3},{3,7},{7,5},{5,1},{8,10},{10,14},{14... | collective-permute-start | bytes 3342344 | tf_op jit(solution)/shard_map/ppermute | solution.py:48
  348.7 49.1 %collective-permute-start.31 = (bf16[256,2176]{1,0:T(8,128)(2,1)}, bf16[256,2176]{1,0:T(8,128)(2,1)S(1)}, u32[]{:S(2)}, u32[]{:S(2)}) collective-permute-start(bf16[256,2176]{1,0:T(8,128)(2,1)} %get-tuple-element.196), channel_id=1, source_target_pairs={{0,1},{1,0},{2,3},{3,2},{4,5},{5,4},{6,7},{7,6},{8,9},{9,8},{10,11... | collective-permute-start | bytes 3342344 | tf_op jit(solution)/shard_map/ppermute | solution.py:48
  390.8 42.7 %collective-permute-start.33 = (bf16[256,2176]{1,0:T(8,128)(2,1)}, bf16[256,2176]{1,0:T(8,128)(2,1)}, u32[]{:S(2)}, u32[]{:S(2)}) collective-permute-start(bf16[256,2176]{1,0:T(8,128)(2,1)} %get-tuple-element.212), channel_id=1, source_target_pairs={{0,1},{1,0},{2,3},{3,2},{4,5},{5,4},{6,7},{7,6},{8,9},{9,8},{10,11... | collective-permute-start | bytes 3342344 | tf_op jit(solution)/shard_map/ppermute | solution.py:48
  397.8 47.8 %collective-permute-start.32 = (bf16[256,2176]{1,0:T(8,128)(2,1)}, bf16[256,2176]{1,0:T(8,128)(2,1)}, u32[]{:S(2)}, u32[]{:S(2)}) collective-permute-start(bf16[256,2176]{1,0:T(8,128)(2,1)} %collective-permute-done.30.refs_0_), channel_id=1, source_target_pairs={{0,1},{1,0},{2,3},{3,2},{4,5},{5,4},{6,7},{7,6},{8,9},{9,8},{10,11... | collective-permute-start | bytes 3342344 | tf_op jit(solution)/shard_map/ppermute | solution.py:48
  432.7 51.3 %collective-permute-start.35 = (bf16[256,2176]{1,0:T(8,128)(2,1)}, bf16[256,2176]{1,0:T(8,128)(2,1)S(1)}, u32[]{:S(2)}, u32[]{:S(2)}) collective-permute-start(bf16[256,2176]{1,0:T(8,128)(2,1)} %get-tuple-element.229), channel_id=1, source_target_pairs={{0,1},{1,0},{2,3},{3,2},{4,5},{5,4},{6,7},{7,6},{8,9},{9,8},{10,11... | collective-permute-start | bytes 3342344 | tf_op jit(solution)/shard_map/ppermute | solution.py:48
  448.1 35.8 %collective-permute-start.36 = (bf16[256,2176]{1,0:T(8,128)(2,1)}, bf16[256,2176]{1,0:T(8,128)(2,1)S(1)}, u32[]{:S(2)}, u32[]{:S(2)}) collective-permute-start(bf16[256,2176]{1,0:T(8,128)(2,1)} %add_convert_fusion.2), channel_id=1, source_target_pairs={{0,2},{2,6},{6,4},{4,0},{1,3},{3,7},{7,5},{5,1},{8,10},{10,14},{14... | collective-permute-start | bytes 3342344 | tf_op jit(solution)/shard_map/ppermute | solution.py:48
  482.2 22.3 %collective-permute-start.37 = (bf16[256,2176]{1,0:T(8,128)(2,1)}, bf16[256,2176]{1,0:T(8,128)(2,1)}, u32[]{:S(2)}, u32[]{:S(2)}) collective-permute-start(bf16[256,2176]{1,0:T(8,128)(2,1)} %get-tuple-element.237), channel_id=1, source_target_pairs={{0,1},{1,0},{2,3},{3,2},{4,5},{5,4},{6,7},{7,6},{8,9},{9,8},{10,11... | collective-permute-start | bytes 3342344 | tf_op jit(solution)/shard_map/ppermute | solution.py:48
  485.4 22.4 %collective-permute-start.38 = (bf16[256,2176]{1,0:T(8,128)(2,1)}, bf16[256,2176]{1,0:T(8,128)(2,1)S(1)}, u32[]{:S(2)}, u32[]{:S(2)}) collective-permute-start(bf16[256,2176]{1,0:T(8,128)(2,1)} %add_convert_fusion.1), channel_id=1, source_target_pairs={{0,2},{2,6},{6,4},{4,0},{1,3},{3,7},{7,5},{5,1},{8,10},{10,14},{14... | collective-permute-start | bytes 3342344 | tf_op jit(solution)/shard_map/ppermute | solution.py:48
  507.8 266.5 %reduce-scatter.6.cloned.1.call-start = ((), (), s32[]{:S(2)}) async-start(), calls=%async_computation.7 | async-start | bytes 10485760 | tf_op jit(solution)/shard_map/reduce_scatter | solution.py:888
  507.9 40.3 %collective-permute-start.40 = (bf16[256,2048]{1,0:T(8,128)(2,1)}, bf16[256,2048]{1,0:T(8,128)(2,1)}, u32[]{:S(2)}, u32[]{:S(2)}) collective-permute-start(bf16[256,2048]{1,0:T(8,128)(2,1)} %get-tuple-element.189), channel_id=1, source_target_pairs={{0,1},{1,0},{2,3},{3,2},{4,5},{5,4},{6,7},{7,6},{8,9},{9,8},{10,11... | collective-permute-start | bytes 3145736 | tf_op jit(solution)/shard_map/ppermute | solution.py:48
  510.9 37.2 %collective-permute-start.39 = (bf16[256,2176]{1,0:T(8,128)(2,1)}, bf16[256,2176]{1,0:T(8,128)(2,1)S(1)}, u32[]{:S(2)}, u32[]{:S(2)}) collective-permute-start(bf16[256,2176]{1,0:T(8,128)(2,1)} %add_convert_fusion), channel_id=1, source_target_pairs={{0,2},{2,6},{6,4},{4,0},{1,3},{3,7},{7,5},{5,1},{8,10},{10,14},{14... | collective-permute-start | bytes 3342344 | tf_op jit(solution)/shard_map/ppermute | solution.py:48
  548.2 230.2 %reduce-scatter.8.cloned.1.call-start = ((), (), s32[]{:S(2)}) async-start(), calls=%async_computation.8 | async-start | bytes 10485760 | tf_op jit(solution)/shard_map/reduce_scatter | solution.py:888
  562.8 14.2 %collective-permute-start.42 = (bf16[512,512]{1,0:T(8,128)(2,1)S(1)}, bf16[512,512]{1,0:T(8,128)(2,1)S(1)}, u32[]{:S(2)}, u32[]{:S(2)}) collective-permute-start(bf16[512,512]{1,0:T(8,128)(2,1)S(1)} %get-tuple-element.407), channel_id=1, source_target_pairs={{0,1},{1,0},{2,3},{3,2},{4,5},{5,4},{6,7},{7,6},{8,9},{9,8},{10,11... | collective-permute-start | bytes 1572872 | tf_op jit(solution)/shard_map/ppermute | solution.py:48
  566.5 34.4 %collective-permute-start.44 = (bf16[256,2048]{1,0:T(8,128)(2,1)S(1)}, bf16[256,2048]{1,0:T(8,128)(2,1)S(1)}, u32[]{:S(2)}, u32[]{:S(2)}) collective-permute-start(bf16[256,2048]{1,0:T(8,128)(2,1)S(1)} %add_convert_fusion.6), channel_id=1, source_target_pairs={{0,2},{2,6},{6,4},{4,0},{1,3},{3,7},{7,5},{5,1},{8,10},{10,14},{14... | collective-permute-start | bytes 3145736 | tf_op jit(solution)/shard_map/ppermute | solution.py:48
  577.1 24.6 %collective-permute-start.43 = (bf16[256,2048]{1,0:T(8,128)(2,1)S(1)}, bf16[256,2048]{1,0:T(8,128)(2,1)S(1)}, u32[]{:S(2)}, u32[]{:S(2)}) collective-permute-start(bf16[256,2048]{1,0:T(8,128)(2,1)S(1)} %copy-done.61), channel_id=1, source_target_pairs={{0,1},{1,0},{2,3},{3,2},{4,5},{5,4},{6,7},{7,6},{8,9},{9,8},{10,11... | collective-permute-start | bytes 3145736 | tf_op jit(solution)/shard_map/ppermute | solution.py:48
  603.3 25.2 %collective-permute-start.48 = (bf16[256,2048]{1,0:T(8,128)(2,1)}, bf16[256,2048]{1,0:T(8,128)(2,1)S(1)}, u32[]{:S(2)}, u32[]{:S(2)}) collective-permute-start(bf16[256,2048]{1,0:T(8,128)(2,1)} %add_convert_fusion.5), channel_id=1, source_target_pairs={{0,2},{2,6},{6,4},{4,0},{1,3},{3,7},{7,5},{5,1},{8,10},{10,14},{14... | collective-permute-start | bytes 3145736 | tf_op jit(solution)/shard_map/ppermute | solution.py:48
  605.2 23.8 %collective-permute-start.47 = (bf16[256,2048]{1,0:T(8,128)(2,1)}, bf16[256,2048]{1,0:T(8,128)(2,1)S(1)}, u32[]{:S(2)}, u32[]{:S(2)}) collective-permute-start(bf16[256,2048]{1,0:T(8,128)(2,1)} %get-tuple-element.253), channel_id=1, source_target_pairs={{0,1},{1,0},{2,3},{3,2},{4,5},{5,4},{6,7},{7,6},{8,9},{9,8},{10,11... | collective-permute-start | bytes 3145736 | tf_op jit(solution)/shard_map/ppermute | solution.py:48
  613.6 9.5 %collective-permute-start.45 = (bf16[256,2048]{1,0:T(8,128)(2,1)S(1)}, bf16[256,2048]{1,0:T(8,128)(2,1)S(1)}, u32[]{:S(2)}, u32[]{:S(2)}) collective-permute-start(bf16[256,2048]{1,0:T(8,128)(2,1)S(1)} %get-tuple-element.403), channel_id=1, source_target_pairs={{0,8},{8,0},{1,9},{9,1},{2,10},{10,2},{3,11},{11,3},{4,12},{12,4},... | collective-permute-start | bytes 3145736 | tf_op jit(solution)/shard_map/ppermute | solution.py:48
  613.6 9.4 %collective-permute-start.46 = (bf16[256,2048]{1,0:T(8,128)(2,1)S(1)}, bf16[256,2048]{1,0:T(8,128)(2,1)S(1)}, u32[]{:S(2)}, u32[]{:S(2)}) collective-permute-start(bf16[256,2048]{1,0:T(8,128)(2,1)S(1)} %get-tuple-element.402), channel_id=1, source_target_pairs={{0,8},{8,0},{1,9},{9,1},{2,10},{10,2},{3,11},{11,3},{4,12},{12,4},... | collective-permute-start | bytes 3145736 | tf_op jit(solution)/shard_map/ppermute | solution.py:48
  629.0 26.4 %collective-permute-start.52 = (bf16[256,2048]{1,0:T(8,128)(2,1)}, bf16[256,2048]{1,0:T(8,128)(2,1)}, u32[]{:S(2)}, u32[]{:S(2)}) collective-permute-start(bf16[256,2048]{1,0:T(8,128)(2,1)} %get-tuple-element.262), channel_id=1, source_target_pairs={{0,1},{1,0},{2,3},{3,2},{4,5},{5,4},{6,7},{7,6},{8,9},{9,8},{10,11... | collective-permute-start | bytes 3145736 | tf_op jit(solution)/shard_map/ppermute | solution.py:48
  631.3 57.6 %collective-permute-start.51 = (bf16[2,2,2,64,1536]{4,3,2,1,0:T(8,128)(2,1)}, bf16[2,2,2,64,1536]{4,3,2,1,0:T(8,128)(2,1)}, u32[]{:S(2)}, u32[]{:S(2)}) collective-permute-start(bf16[2,2,2,64,1536]{4,3,2,1,0:T(8,128)(2,1)} %dynamic-slice_bitcast_fusion.1), channel_id=1, source_target_pairs={{0,2},{2,6},{6,4},{4,0},{1,3},{3,7},{7,5},{5,1},{8,10},{10,14},{14... | collective-permute-start | bytes 4718600 | tf_op jit(solution)/shard_map/ppermute | solution.py:48
  635.5 53.4 %collective-permute-start.50 = (bf16[256,2048]{1,0:T(8,128)(2,1)}, bf16[256,2048]{1,0:T(8,128)(2,1)}, u32[]{:S(2)}, u32[]{:S(2)}) collective-permute-start(bf16[256,2048]{1,0:T(8,128)(2,1)} %add_convert_fusion.4), channel_id=1, source_target_pairs={{0,2},{2,6},{6,4},{4,0},{1,3},{3,7},{7,5},{5,1},{8,10},{10,14},{14... | collective-permute-start | bytes 3145736 | tf_op jit(solution)/shard_map/ppermute | solution.py:48
  637.3 51.6 %collective-permute-start.49 = (bf16[256,2048]{1,0:T(8,128)(2,1)}, bf16[256,2048]{1,0:T(8,128)(2,1)}, u32[]{:S(2)}, u32[]{:S(2)}) collective-permute-start(bf16[256,2048]{1,0:T(8,128)(2,1)} %get-tuple-element.258), channel_id=1, source_target_pairs={{0,1},{1,0},{2,3},{3,2},{4,5},{5,4},{6,7},{7,6},{8,9},{9,8},{10,11... | collective-permute-start | bytes 3145736 | tf_op jit(solution)/shard_map/ppermute | solution.py:48
  693.8 44.7 %collective-permute-start.55 = (bf16[2,4,64,2048]{3,2,1,0:T(8,128)(2,1)}, bf16[2,4,64,2048]{3,2,1,0:T(8,128)(2,1)}, u32[]{:S(2)}, u32[]{:S(2)}) collective-permute-start(bf16[2,4,64,2048]{3,2,1,0:T(8,128)(2,1)} %dynamic-slice_bitcast_fusion), channel_id=1, source_target_pairs={{0,1},{1,0},{2,3},{3,2},{4,5},{5,4},{6,7},{7,6},{8,9},{9,8},{10,11... | collective-permute-start | bytes 6291464 | tf_op jit(solution)/shard_map/ppermute | solution.py:48
  694.6 47.0 %collective-permute-start.53 = (bf16[2,2,2,64,1536]{4,3,2,1,0:T(8,128)(2,1)}, bf16[2,2,2,64,1536]{4,3,2,1,0:T(8,128)(2,1)}, u32[]{:S(2)}, u32[]{:S(2)}) collective-permute-start(bf16[2,2,2,64,1536]{4,3,2,1,0:T(8,128)(2,1)} %convert_add_fusion.1), channel_id=1, source_target_pairs={{0,2},{2,6},{6,4},{4,0},{1,3},{3,7},{7,5},{5,1},{8,10},{10,14},{14... | collective-permute-start | bytes 4718600 | tf_op jit(solution)/shard_map/ppermute | solution.py:48
  698.0 43.6 %collective-permute-start.54 = (bf16[2,2,2,64,128]{4,3,2,1,0:T(8,128)(2,1)S(1)}, bf16[2,2,2,64,128]{4,3,2,1,0:T(8,128)(2,1)S(1)}, u32[]{:S(2)}, u32[]{:S(2)}) collective-permute-start(bf16[2,2,2,64,128]{4,3,2,1,0:T(8,128)(2,1)S(1)} %dynamic-slice_bitcast_fusion.7), channel_id=1, source_target_pairs={{0,2},{2,6},{6,4},{4,0},{1,3},{3,7},{7,5},{5,1},{8,10},{10,14},{14... | collective-permute-start | bytes 393224 | tf_op jit(solution)/shard_map/ppermute | solution.py:48
  745.8 36.7 %collective-permute-start.56 = (bf16[2,2,2,64,1536]{4,3,2,1,0:T(8,128)(2,1)}, bf16[2,2,2,64,1536]{4,3,2,1,0:T(8,128)(2,1)}, u32[]{:S(2)}, u32[]{:S(2)}) collective-permute-start(bf16[2,2,2,64,1536]{4,3,2,1,0:T(8,128)(2,1)} %fusion.8), channel_id=1, source_target_pairs={{0,2},{2,6},{6,4},{4,0},{1,3},{3,7},{7,5},{5,1},{8,10},{10,14},{14... | collective-permute-start | bytes 4718600 | tf_op jit(solution)/shard_map/ppermute | solution.py:48
  746.8 21.4 %collective-permute-start.58 = (bf16[4,64,2048]{2,1,0:T(8,128)(2,1)}, bf16[4,64,2048]{2,1,0:T(8,128)(2,1)}, u32[]{:S(2)}, u32[]{:S(2)}) collective-permute-start(bf16[4,64,2048]{2,1,0:T(8,128)(2,1)} %dynamic-slice_bitcast_fusion.2), channel_id=1, source_target_pairs={{0,16},{16,0},{1,17},{17,1},{2,18},{18,2},{3,19},{19,3},{4,20},{20... | collective-permute-start | bytes 3145736 | tf_op jit(solution)/shard_map/ppermute | solution.py:48
  746.9 35.5 %collective-permute-start.57 = (bf16[2,2,2,64,128]{4,3,2,1,0:T(8,128)(2,1)S(1)}, bf16[2,2,2,64,128]{4,3,2,1,0:T(8,128)(2,1)S(1)}, u32[]{:S(2)}, u32[]{:S(2)}) collective-permute-start(bf16[2,2,2,64,128]{4,3,2,1,0:T(8,128)(2,1)S(1)} %fusion.41), channel_id=1, source_target_pairs={{0,2},{2,6},{6,4},{4,0},{1,3},{3,7},{7,5},{5,1},{8,10},{10,14},{14... | collective-permute-start | bytes 393224 | tf_op jit(solution)/shard_map/ppermute | solution.py:48
  785.0 15.3 %collective-permute-start.59 = (bf16[2,2,64,1536]{3,2,1,0:T(8,128)(2,1)S(1)}, bf16[2,2,64,1536]{3,2,1,0:T(8,128)(2,1)S(1)}, u32[]{:S(2)}, u32[]{:S(2)}) collective-permute-start(bf16[2,2,64,1536]{3,2,1,0:T(8,128)(2,1)S(1)} %dynamic-slice_bitcast_fusion.3), channel_id=1, source_target_pairs={{0,16},{16,0},{1,17},{17,1},{2,18},{18,2},{3,19},{19,3},{4,20},{20... | collective-permute-start | bytes 2359304 | tf_op jit(solution)/shard_map/ppermute | solution.py:48
  791.2 9.3 %collective-permute-start.60 = (bf16[2,2,2,64,128]{4,3,2,1,0:T(8,128)(2,1)S(1)}, bf16[2,2,2,64,128]{4,3,2,1,0:T(8,128)(2,1)S(1)}, u32[]{:S(2)}, u32[]{:S(2)}) collective-permute-start(bf16[2,2,2,64,128]{4,3,2,1,0:T(8,128)(2,1)S(1)} %fusion.40), channel_id=1, source_target_pairs={{0,2},{2,6},{6,4},{4,0},{1,3},{3,7},{7,5},{5,1},{8,10},{10,14},{14... | collective-permute-start | bytes 393224 | tf_op jit(solution)/shard_map/ppermute | solution.py:48
  793.6 10.0 %collective-permute-start.61 = (bf16[64,2048]{1,0:T(8,128)(2,1)S(1)}, bf16[64,2048]{1,0:T(8,128)(2,1)S(1)}, u32[]{:S(2)}, u32[]{:S(2)}) collective-permute-start(bf16[64,2048]{1,0:T(8,128)(2,1)S(1)} %dynamic-slice_bitcast_fusion.6), channel_id=1, source_target_pairs={{0,2},{2,6},{6,4},{4,0},{1,3},{3,7},{7,5},{5,1},{8,10},{10,14},{14... | collective-permute-start | bytes 786440 | tf_op jit(solution)/shard_map/ppermute | solution.py:48
  804.4 8.7 %collective-permute-start.65 = (bf16[64,2048]{1,0:T(8,128)(2,1)S(1)}, bf16[64,2048]{1,0:T(8,128)(2,1)S(1)}, u32[]{:S(2)}, u32[]{:S(2)}) collective-permute-start(bf16[64,2048]{1,0:T(8,128)(2,1)S(1)} %fusion.26), channel_id=1, source_target_pairs={{0,2},{2,6},{6,4},{4,0},{1,3},{3,7},{7,5},{5,1},{8,10},{10,14},{14... | collective-permute-start | bytes 786440 | tf_op jit(solution)/shard_map/ppermute | solution.py:48
  808.1 8.2 collective-permute-start.63
  (75 other events, 1239.4 us)
Sparse Core Ops, SparseCore 0:
  47.9 69.0 all-gather.3
  118.6 59.6 all-gather.5
  179.8 58.2 all-gather.7
  508.0 69.1 reduce-scatter.3
  579.8 71.9 reduce-scatter.5
  654.2 71.7 reduce-scatter.7

commit v6 on v5

--- a/solution.py
+++ b/solution.py
@@ -803,11 +803,11 @@
         ).astype(BF)
 
     expert_grads, waiting = [], [(2, 1), (0, 3), (0, 4)]
-    while back_chain["hops"] < zs or waiting:
+    while back_chain["hops"] < zs:
         back_moves = moves(back_chain, back_parts, zs)
         last = back_chain["hops"] == zs - 1 and len(back_chain["sums"]) == zs
         combined_moves = moves(combined_chain, combined_parts, zs) if last else {}
-        some, waiting = (waiting, []) if last else (waiting[:1], waiting[1:])
+        some, waiting = waiting[:1], waiting[1:]
         some = [weight_grads(*pair) for pair in some]
         some, kept, back_moves, combined_moves = lax.optimization_barrier(
             (some, kept, back_moves, combined_moves)
@@ -815,7 +815,6 @@
         expert_grads += some
         settle(back_chain, back_parts, back_moves)
         settle(combined_chain, combined_parts, combined_moves)
-    down_grads, gate_grads, up_grads = expert_grads
     back = final(back_chain)
 
     def beside(value, others):
@@ -884,15 +883,13 @@
     late_total = part_of(late, "z", 2, 1)
     output_x = output_y = output_total = None
     small_hops, output_hops = 0, 0
-    expert_totals = [
-        lax.psum_scatter(grad, ("y", "c"), scatter_dimension=1, tiled=True).astype(F32)
-        for grad in (down_grads, gate_grads, up_grads)
-    ]
     for n, k in enumerate(ring):
         arrived = {"late": shift(late_total.astype(BF), "z", 1)}
         if n == 0:
             combined_parts = tied(combined_parts, late)
             arrived["combined"] = moves(combined_chain, combined_parts, zs)
+            kept = tied(kept, late)
+            arrived["grads"] = [weight_grads(*pair) for pair in waiting]
             arrived["normed"] = reduce_blocks(lambda key: normed_sums[key[0]], ("x",))
         if n == 1:
             arrived["x"] = reduce_axis(tied(output_grad, late_total), "x", 2).astype(BF)
@@ -905,6 +902,10 @@
         late_total = part_of(late, "z", 2, k) + arrived["late"].astype(F32)
         if n == 0:
             settle(combined_chain, combined_parts, arrived["combined"])
+            expert_totals = [
+                lax.psum_scatter(grad, ("y", "c"), scatter_dimension=1, tiled=True).astype(F32)
+                for grad in expert_grads + arrived["grads"]
+            ]
             tokens_grad, small = finish(arrived["normed"])
             small_total = part_of(small, "z", 2, 1)
         if n == 1:

time: 851 us -> 844 us (level); the launches traced: 837 us -> 841 us
  starting transfers between devices: 69.6 us -> 84.9 us
    ppermute x63, starting transfers between devices: 68.5 us -> 83.9 us  [shift(): return lax.ppermute(value, axis, pairs)]
  transfers between devices with their start and end apart: 73 -> 73, of which waited for: 35 -> 35; matrix products, arithmetic and copies ran while one was open for 20% -> 20% of each run, Pallas kernels for 22% -> 21%
where the time goes in v6:
time: 844 us; the launch traced here: 841 us
  waiting for transfers between devices  369 us (44%)
  Pallas kernels  178 us (21%)
  matrix products  96.7 us (11%)
  starting transfers between devices  84.9 us (10%)
  other arithmetic  64.4 us (8%)
  local copies, waits for them, and re-layouts  32.2 us (4%)
  between operations  16 us (2%)
    ppermute x63, waiting for transfers between devices, shift(): return lax.ppermute(value, axis, pairs)  365 us
    pallas_call x4, Pallas kernels, run_experts(): pl.pallas_call(functools.partial(experts_kernel, sizes), out_shape=(*[jax...  132 us
    ppermute x63, starting transfers between devices, shift(): return lax.ppermute(value, axis, pairs)  83.9 us
    dot_general x3, matrix products, weight_grads(): lax.dot_general(kept[left], kept[right], (((1,), (1,)), ((0,), (0,))), pr...  54.6 us
    pallas_call x1, Pallas kernels, attend_back(): pl.pallas_call(functools.partial(attend_back_kernel, heads), out_shape=(j...  21.9 us
  transfers between devices with their start and end apart: 73, of which 35 were waited for; matrix products, arithmetic and copies ran while one was open for 20% of the time, Pallas kernels for 21%

profile of v6, /device:TPU:0, one launch (start us, length us, event | category | flops | bytes accessed | tf_op | source)
XLA Modules:
  0.0 841.2 jit_solution(15770304893235402988)
XLA Ops:
  13.8 2.9 collective-permute-start.4
  18.3 8.5 %collective-permute-done.4 = bf16[128,1664]{1,0:T(8,128)(2,1)S(1)} collective-permute-done((bf16[128,1664]{1,0:T(8,128)(2,1)S(1)}, bf16[128,1664]{1,0:T(8,128)(2,1)S(1)}, u32[]{:S(2)}, u32[]{:S(2)}) %collective-permute-start.4) | collective-permute-done | bytes 426016 | tf_op jit(solution)/shard_map/ppermute | solution.py:48
  30.4 6.6 collective-permute-done.7
  37.7 9.9 %collective-permute-done.6 = bf16[256,1664]{1,0:T(8,128)(2,1)S(1)} collective-permute-done((bf16[256,1664]{1,0:T(8,128)(2,1)S(1)}, bf16[256,1664]{1,0:T(8,128)(2,1)S(1)}, u32[]{:S(2)}, u32[]{:S(2)}) %collective-permute-start.6) | collective-permute-done | bytes 852000 | tf_op jit(solution)/shard_map/ppermute | solution.py:48
  53.6 2.6 collective-permute-start.9
  56.2 2.5 fusion.25.refs_2_
  59.2 35.0 %collective-permute-done.9 = bf16[64,2048]{1,0:T(8,128)(2,1)S(1)} collective-permute-done((bf16[64,2048]{1,0:T(8,128)(2,1)}, bf16[64,2048]{1,0:T(8,128)(2,1)S(1)}, u32[]{:S(2)}, u32[]{:S(2)}) %collective-permute-start.9) | collective-permute-done | bytes 262176 | tf_op jit(solution)/shard_map/ppermute | solution.py:48
  98.1 30.0 %collective-permute-done.14 = bf16[256,2048]{1,0:T(8,128)(2,1)} collective-permute-done((bf16[256,2048]{1,0:T(8,128)(2,1)S(1)}, bf16[256,2048]{1,0:T(8,128)(2,1)}, u32[]{:S(2)}, u32[]{:S(2)}) %collective-permute-start.14) | collective-permute-done | bytes 1048608 | tf_op jit(solution)/shard_map/ppermute | solution.py:48
  128.2 3.4 collective-permute-done.13.refs_2_
  134.0 2.6 fusion
  140.2 28.9 %collective-permute-done.16.refs_3_ = bf16[512,1664]{1,0:T(8,128)(2,1)} collective-permute-done((bf16[512,1664]{1,0:T(8,128)(2,1)}, bf16[512,1664]{1,0:T(8,128)(2,1)}, u32[]{:S(2)}, u32[]{:S(2)}) %collective-permute-start.16) | collective-permute-done | bytes 1703968 | tf_op jit(solution)/shard_map/ppermute | solution.py:48
  169.0 7.3 shard_map.272
  176.3 2.8 copy-done
  181.3 10.8 %fusion.5.qkv_ref = f32[1024,1536]{1,0:T(8,128)S(1)} fusion(bf16[2048,1664]{1,0:T(8,128)(2,1)} %copy-done, f32[2048]{0:T(1024)S(1)} %get-tuple-element.395, f32[1024]{0:T(1024)S(1)} %add_rsqrt_fusion, bf16[256,2048]{1,0:T(8,128)(2,1)} %collective-permute-done.12, bf16[256,2048]{1,0:T(8,128)(2,1)} %collective-permute-done.10, ...), kind=kOutput, calls=%fused_computation.8 | convolution fusion | flops 6465519616 | bytes 16789504 | tf_op jit(solution)/shard_map/dot_general | solution.py:26
  192.1 11.6 %collective-permute-done.17.refs_2_ = bf16[256,2176]{1,0:T(8,128)(2,1)} collective-permute-done((bf16[256,2176]{1,0:T(8,128)(2,1)}, bf16[256,2176]{1,0:T(8,128)(2,1)}, u32[]{:S(2)}, u32[]{:S(2)}) %collective-permute-start.17) | collective-permute-done | bytes 1114144 | tf_op jit(solution)/shard_map/ppermute | solution.py:48
  203.7 12.5 %collective-permute-start.20 = (bf16[256,2176]{1,0:T(8,128)(2,1)}, bf16[256,2176]{1,0:T(8,128)(2,1)}, u32[]{:S(2)}, u32[]{:S(2)}) collective-permute-start(bf16[256,2176]{1,0:T(8,128)(2,1)} %collective-permute-done.17.refs_2_), channel_id=1, source_target_pairs={{0,2},{2,6},{6,4},{4,0},{1,3},{3,7},{7,5},{5,1},{8,10},{10,14},{14... | collective-permute-start | bytes 3342344 | tf_op jit(solution)/shard_map/ppermute | solution.py:48
  216.2 2.4 collective-permute-start.21
  218.5 14.6 %shard_map.273 = bf16[1024,512]{1,0:T(8,128)(2,1)S(1)} custom-call(s32[8]{0:T(128)S(1)} %pad_add_fusion.lengths_ref, f32[1024,1536]{1,0:T(8,128)S(1)} %fusion.5.qkv_ref, f32[2,128]{1,0:T(2,128)S(1)} %pad_maximum_fusion.13.gains_ref, f32[128,128]{1,0:T(8,128)S(1)} %get-tuple-element.478.cosine_ref, f32[128,128]{1,0:T(8,128)S(1)} %get-tuple-element.479.sine_ref), custom_call_target="tpu_custom_call" | custom-call | flops 14000000000 | bytes 14680064 | tf_op jit(solution)/shard_map/pallas_call | solution.py:247
  234.2 2.4 shard_map.274
  236.6 15.0 %collective-permute-done.19 = bf16[512,512]{1,0:T(8,128)(2,1)} collective-permute-done((bf16[512,512]{1,0:T(8,128)(2,1)}, bf16[512,512]{1,0:T(8,128)(2,1)}, u32[]{:S(2)}, u32[]{:S(2)}) %collective-permute-start.19) | collective-permute-done | bytes 524320 | tf_op jit(solution)/shard_map/ppermute | solution.py:48
  252.7 2.4 fusion.77
  255.3 2.2 collective-permute-start.23
  264.3 19.2 %collective-permute-done.23.refs_2_ = bf16[256,2176]{1,0:T(8,128)(2,1)} collective-permute-done((bf16[256,2176]{1,0:T(8,128)(2,1)}, bf16[256,2176]{1,0:T(8,128)(2,1)}, u32[]{:S(2)}, u32[]{:S(2)}) %collective-permute-start.23) | collective-permute-done | bytes 1114144 | tf_op jit(solution)/shard_map/ppermute | solution.py:48
  286.9 25.1 %collective-permute-done.25.refs_1_ = bf16[256,2176]{1,0:T(8,128)(2,1)S(1)} collective-permute-done((bf16[256,2176]{1,0:T(8,128)(2,1)S(1)}, bf16[256,2176]{1,0:T(8,128)(2,1)S(1)}, u32[]{:S(2)}, u32[]{:S(2)}) %collective-permute-start.25) | collective-permute-done | bytes 1114144 | tf_op jit(solution)/shard_map/ppermute | solution.py:48
  315.1 31.9 %shard_map.275 = (bf16[256,2048]{1,0:T(8,128)(2,1)}, bf16[256,2048]{1,0:T(8,128)(2,1)}, bf16[256,2176]{1,0:T(8,128)(2,1)}, bf16[256,2176]{1,0:T(8,128)(2,1)}, bf...) custom-call(s32[1]{0:T(128)} %bitcast.68.places_ref, ...), custom_call_target="tpu_custom_call" | custom-call | flops 53687091200 | bytes 41943040 | tf_op jit(solution)/shard_map/pallas_call | solution.py:481
  347.0 11.2 %collective-permute-done.27.refs_1_ = bf16[256,2176]{1,0:T(8,128)(2,1)} collective-permute-done((bf16[256,2176]{1,0:T(8,128)(2,1)}, bf16[256,2176]{1,0:T(8,128)(2,1)}, u32[]{:S(2)}, u32[]{:S(2)}) %collective-permute-start.27) | collective-permute-done | bytes 1114144 | tf_op jit(solution)/shard_map/ppermute | solution.py:48
  360.8 33.4 %shard_map.276 = (bf16[256,2048]{1,0:T(8,128)(2,1)}, bf16[256,2048]{1,0:T(8,128)(2,1)}, bf16[256,2176]{1,0:T(8,128)(2,1)}, bf16[256,2176]{1,0:T(8,128)(2,1)}, bf...) custom-call(s32[1]{0:T(128)} %bitcast.68.places_ref, ...), custom_call_target="tpu_custom_call", output_to_operand_aliasing={{4}: (8, {}), {5}: (9, {}), {6}: (10, {}), {7}: (11, {}), {... | custom-call | flops 53687091200 | bytes 41943040 | tf_op jit(solution)/shard_map/pallas_call | solution.py:481
  396.1 13.5 %collective-permute-done.31 = bf16[256,2176]{1,0:T(8,128)(2,1)S(1)} collective-permute-done((bf16[256,2176]{1,0:T(8,128)(2,1)}, bf16[256,2176]{1,0:T(8,128)(2,1)S(1)}, u32[]{:S(2)}, u32[]{:S(2)}) %collective-permute-start.31) | collective-permute-done | bytes 1114144 | tf_op jit(solution)/shard_map/ppermute | solution.py:48
  411.3 33.2 %shard_map.277 = (bf16[256,2048]{1,0:T(8,128)(2,1)}, bf16[256,2048]{1,0:T(8,128)(2,1)}, bf16[256,2176]{1,0:T(8,128)(2,1)}, bf16[256,2176]{1,0:T(8,128)(2,1)}, bf...) custom-call(s32[1]{0:T(128)} %bitcast.68.places_ref, ...), custom_call_target="tpu_custom_call", output_to_operand_aliasing={{4}: (8, {}), {5}: (9, {}), {6}: (10, {}), {7}: (11, {}), {... | custom-call | flops 53687091200 | bytes 41943040 | tf_op jit(solution)/shard_map/pallas_call | solution.py:481
  445.3 12.2 %collective-permute-done.32.refs_1_ = bf16[256,2176]{1,0:T(8,128)(2,1)} collective-permute-done((bf16[256,2176]{1,0:T(8,128)(2,1)}, bf16[256,2176]{1,0:T(8,128)(2,1)}, u32[]{:S(2)}, u32[]{:S(2)}) %collective-permute-start.32) | collective-permute-done | bytes 1114144 | tf_op jit(solution)/shard_map/ppermute | solution.py:48
  457.4 2.5 add_convert_fusion.2
  460.5 33.4 %shard_map.278 = (bf16[256,2048]{1,0:T(8,128)(2,1)}, bf16[256,2048]{1,0:T(8,128)(2,1)}, bf16[256,2176]{1,0:T(8,128)(2,1)}, bf16[256,2176]{1,0:T(8,128)(2,1)}, bf...) custom-call(s32[1]{0:T(128)} %bitcast.68.places_ref, ...), custom_call_target="tpu_custom_call", output_to_operand_aliasing={{4}: (8, {}), {5}: (9, {}), {6}: (10, {}), {7}: (11, {}), {... | custom-call | flops 53687091200 | bytes 41943040 | tf_op jit(solution)/shard_map/pallas_call | solution.py:481
  498.4 17.8 %convolution_convert_fusion.3 = bf16[2,1024,2048]{2,1,0:T(8,128)(2,1)} fusion(bf16[2,1280,1024]{2,1,0:T(8,128)(2,1)} %get-tuple-element.236, bf16[2,1280,2048]{2,1,0:T(8,128)(2,1)} %get-tuple-element.237), kind=kOutput, calls=%fused_computation.12 | convolution fusion | flops 10741612544 | bytes 24117248 | tf_op jit(solution)/shard_map/dot_general | solution.py:801
  516.2 3.4 collective-permute-done.38
  520.0 2.6 add_convert_fusion
  523.2 19.2 %convolution_convert_fusion.2 = bf16[2,2048,1024]{2,1,0:T(8,128)(2,1)} fusion(bf16[2,1280,2048]{2,1,0:T(8,128)(2,1)} %get-tuple-element.267, bf16[2,1280,1024]{2,1,0:T(8,128)(2,1)} %get-tuple-element.246), kind=kOutput, calls=%fused_computation.11 | convolution fusion | flops 10741612544 | bytes 24117248 | tf_op jit(solution)/shard_map/dot_general | solution.py:801
  549.6 2.9 collective-permute-done.41
  553.5 5.0 convolution_convert_fusion.6
  562.9 9.8 %collective-permute-done.42 = bf16[512,512]{1,0:T(8,128)(2,1)S(1)} collective-permute-done((bf16[512,512]{1,0:T(8,128)(2,1)S(1)}, bf16[512,512]{1,0:T(8,128)(2,1)S(1)}, u32[]{:S(2)}, u32[]{:S(2)}) %collective-permute-start.42) | collective-permute-done | bytes 524320 | tf_op jit(solution)/shard_map/ppermute | solution.py:48
  574.7 21.9 %shard_map.279 = (bf16[1024,1536]{1,0:T(8,128)(2,1)S(1)}, f32[2,128]{1,0:T(2,128)S(1)}) custom-call(s32[8]{0:T(128)S(1)} %pad_add_fusion.lengths_ref, f32[1024,1536]{1,0:T(8,128)S(1)} %bitcast.213, bf16[1024,512]{1,0:T(8,128)(2,1)S(1)} %pad_maximum_fusion.5.mixed_grad_ref, f32[2,128]{1,0:T(2,128)S(1)} %copy-done.7, ...), custom_call_target="tpu_custom_call" | custom-call | flops 20000000000 | bytes 20971520 | tf_op jit(solution)/shard_map/pallas_call | solution.py:271
  600.9 6.7 fusion.76
  609.3 8.9 %convolution_convert_fusion = bf16[2048,1536]{1,0:T(8,128)(2,1)S(1)} fusion(bf16[1024,1536]{1,0:T(8,128)(2,1)S(1)} %get-tuple-element.256, f32[2048]{0:T(1024)S(1)} %copy-done.48, f32[1024]{0:T(1024)S(1)} %copy-done.54, bf16[256,2048]{1,0:T(8,128)(2,1)} %collective-permute-done.12, bf16[256,2048]{1,0:T(8,128)(2,1)} %collective-permute-done.10, ...), kind=kOutput, calls=%fused_computation.5 | convolution fusion | flops 6468665344 | bytes 13643776 | tf_op jit(solution)/shard_map/dot_general | solution.py:30
  620.4 2.4 collective-permute-done.48
  628.7 2.2 collective-permute-start.50
  631.6 17.5 %convolution_convert_fusion.1 = bf16[2,2048,1024]{2,1,0:T(8,128)(2,1)} fusion(bf16[2,1280,2048]{2,1,0:T(8,128)(2,1)} %get-tuple-element.267, bf16[2,1280,1024]{2,1,0:T(8,128)(2,1)} %get-tuple-element.268), kind=kOutput, calls=%fused_computation.10 | convolution fusion | flops 10741612544 | bytes 24117248 | tf_op jit(solution)/shard_map/dot_general | solution.py:801
  651.0 32.1 %collective-permute-done.50 = bf16[256,2048]{1,0:T(8,128)(2,1)} collective-permute-done((bf16[256,2048]{1,0:T(8,128)(2,1)}, bf16[256,2048]{1,0:T(8,128)(2,1)}, u32[]{:S(2)}, u32[]{:S(2)}) %collective-permute-start.50) | collective-permute-done | bytes 1048608 | tf_op jit(solution)/shard_map/ppermute | solution.py:48
  683.2 3.9 convolution_convert_fusion.4
  687.1 5.4 convert_add_fusion.1
  698.0 2.6 collective-permute-start.54
  700.6 37.2 %collective-permute-done.55 = bf16[2,4,64,2048]{3,2,1,0:T(8,128)(2,1)} collective-permute-done((bf16[2,4,64,2048]{3,2,1,0:T(8,128)(2,1)}, bf16[2,4,64,2048]{3,2,1,0:T(8,128)(2,1)}, u32[]{:S(2)}, u32[]{:S(2)}) %collective-permute-start.55) | collective-permute-done | bytes 2097184 | tf_op jit(solution)/shard_map/ppermute | solution.py:48
  737.8 3.0 fusion.7
  740.9 4.2 fusion.8
  746.2 2.9 collective-permute-start.57
  749.1 25.5 %collective-permute-done.58 = bf16[4,64,2048]{2,1,0:T(8,128)(2,1)} collective-permute-done((bf16[4,64,2048]{2,1,0:T(8,128)(2,1)}, bf16[4,64,2048]{2,1,0:T(8,128)(2,1)}, u32[]{:S(2)}, u32[]{:S(2)}) %collective-permute-start.58) | collective-permute-done | bytes 1048608 | tf_op jit(solution)/shard_map/ppermute | solution.py:48
  776.6 4.1 convert_element_type.429
  780.8 4.1 convert_element_type.430
  784.8 4.1 convert_element_type.431
  788.9 2.5 fusion.9
  792.7 5.0 fusion.17
  799.2 2.5 collective-permute-start.61
  801.7 7.4 collective-permute-done.59
  815.4 2.3 collective-permute-done.65
  819.2 2.9 collective-permute-done.63
  822.4 2.7 collective-permute-done.66
  (403 shorter events, 117.9 us)
Async XLA Ops:
  7.2 307.9 %all-gather.4.cloned.1.call-start = ((), (), s32[]{:S(2)}) async-start(), calls=%async_computation.3 | async-start | bytes 10485760 | tf_op jit(solution)/shard_map/all_gather | solution.py:688
  13.8 13.0 %collective-permute-start.4 = (bf16[128,1664]{1,0:T(8,128)(2,1)S(1)}, bf16[128,1664]{1,0:T(8,128)(2,1)S(1)}, u32[]{:S(2)}, u32[]{:S(2)}) collective-permute-start(bf16[128,1664]{1,0:T(8,128)(2,1)S(1)} %get-tuple-element.423), channel_id=1, source_target_pairs={{0,1},{1,0},{2,3},{3,2},{4,5},{5,4},{6,7},{7,6},{8,9},{9,8},{10,11... | collective-permute-start | bytes 1277960 | tf_op jit(solution)/shard_map/ppermute | solution.py:48
  16.8 10.2 %collective-permute-start.5 = (bf16[64,2048]{1,0:T(8,128)(2,1)S(1)}, bf16[64,2048]{1,0:T(8,128)(2,1)S(1)}, u32[]{:S(2)}, u32[]{:S(2)}) collective-permute-start(bf16[64,2048]{1,0:T(8,128)(2,1)S(1)} %copy-done.39), channel_id=1, source_target_pairs={{0,2},{2,6},{6,4},{4,0},{1,3},{3,7},{7,5},{5,1},{8,10},{10,14},{14... | collective-permute-start | bytes 786440 | tf_op jit(solution)/shard_map/ppermute | solution.py:48
  27.0 20.5 %collective-permute-start.6 = (bf16[256,1664]{1,0:T(8,128)(2,1)S(1)}, bf16[256,1664]{1,0:T(8,128)(2,1)S(1)}, u32[]{:S(2)}, u32[]{:S(2)}) collective-permute-start(bf16[256,1664]{1,0:T(8,128)(2,1)S(1)} %pad_maximum_fusion.7), channel_id=1, source_target_pairs={{0,16},{16,0},{1,17},{17,1},{2,18},{18,2},{3,19},{19,3},{4,20},{20... | collective-permute-start | bytes 2555912 | tf_op jit(solution)/shard_map/ppermute | solution.py:48
  28.8 8.1 collective-permute-start.7
  47.8 267.3 %all-gather.6.cloned.1.call-start = ((), (), s32[]{:S(2)}) async-start(), calls=%async_computation.4 | async-start | bytes 10485760 | tf_op jit(solution)/shard_map/all_gather | solution.py:688
  48.5 266.6 %all-gather.8.cloned.1.call-start = ((), (), s32[]{:S(2)}) async-start(), calls=%async_computation.5 | async-start | bytes 10485760 | tf_op jit(solution)/shard_map/all_gather | solution.py:688
  48.6 45.7 %collective-permute-start.10 = (bf16[256,2048]{1,0:T(8,128)(2,1)}, bf16[256,2048]{1,0:T(8,128)(2,1)}, u32[]{:S(2)}, u32[]{:S(2)}) collective-permute-start(bf16[256,2048]{1,0:T(8,128)(2,1)} %bitcast), channel_id=1, source_target_pairs={{0,1},{1,0},{2,3},{3,2},{4,5},{5,4},{6,7},{7,6},{8,9},{9,8},{10,11... | collective-permute-start | bytes 3145736 | tf_op jit(solution)/shard_map/ppermute | solution.py:48
  50.4 43.8 %collective-permute-start.8 = (bf16[512,1664]{1,0:T(8,128)(2,1)S(1)}, bf16[512,1664]{1,0:T(8,128)(2,1)S(1)}, u32[]{:S(2)}, u32[]{:S(2)}) collective-permute-start(bf16[512,1664]{1,0:T(8,128)(2,1)S(1)} %constant_dynamic-update-slice_fusion.refs_0_), channel_id=1, source_target_pairs={{0,2},{2,6},{6,4},{4,0},{1,3},{3,7},{7,5},{5,1},{8,10},{10,14},{14... | collective-permute-start | bytes 5111816 | tf_op jit(solution)/shard_map/ppermute | solution.py:48
  53.6 40.6 %collective-permute-start.9 = (bf16[64,2048]{1,0:T(8,128)(2,1)}, bf16[64,2048]{1,0:T(8,128)(2,1)S(1)}, u32[]{:S(2)}, u32[]{:S(2)}) collective-permute-start(bf16[64,2048]{1,0:T(8,128)(2,1)} %copy-done.43), channel_id=1, source_target_pairs={{0,2},{2,6},{6,4},{4,0},{1,3},{3,7},{7,5},{5,1},{8,10},{10,14},{14... | collective-permute-start | bytes 786440 | tf_op jit(solution)/shard_map/ppermute | solution.py:48
  58.7 38.8 %collective-permute-start.15 = (bf16[256,2176]{1,0:T(8,128)(2,1)}, bf16[256,2176]{1,0:T(8,128)(2,1)}, u32[]{:S(2)}, u32[]{:S(2)}) collective-permute-start(bf16[256,2176]{1,0:T(8,128)(2,1)} %fusion.25.refs_2_), channel_id=1, source_target_pairs={{0,1},{1,0},{2,3},{3,2},{4,5},{5,4},{6,7},{7,6},{8,9},{9,8},{10,11... | collective-permute-start | bytes 3342344 | tf_op jit(solution)/shard_map/ppermute | solution.py:48
  94.2 37.4 %collective-permute-start.13 = (bf16[512,1664]{1,0:T(8,128)(2,1)S(1)}, bf16[512,1664]{1,0:T(8,128)(2,1)}, u32[]{:S(2)}, u32[]{:S(2)}) collective-permute-start(bf16[512,1664]{1,0:T(8,128)(2,1)S(1)} %collective-permute-done.8.refs_1_), channel_id=1, source_target_pairs={{0,2},{2,6},{6,4},{4,0},{1,3},{3,7},{7,5},{5,1},{8,10},{10,14},{14... | collective-permute-start | bytes 5111816 | tf_op jit(solution)/shard_map/ppermute | solution.py:48
  95.3 32.9 %collective-permute-start.14 = (bf16[256,2048]{1,0:T(8,128)(2,1)S(1)}, bf16[256,2048]{1,0:T(8,128)(2,1)}, u32[]{:S(2)}, u32[]{:S(2)}) collective-permute-start(bf16[256,2048]{1,0:T(8,128)(2,1)S(1)} %constant_dynamic-update-slice_fusion.2), channel_id=1, source_target_pairs={{0,16},{16,0},{1,17},{17,1},{2,18},{18,2},{3,19},{19,3},{4,20},{20... | collective-permute-start | bytes 3145736 | tf_op jit(solution)/shard_map/ppermute | solution.py:48
  96.9 37.1 %collective-permute-start.11 = (bf16[256,2048]{1,0:T(8,128)(2,1)}, bf16[256,2048]{1,0:T(8,128)(2,1)}, u32[]{:S(2)}, u32[]{:S(2)}) collective-permute-start(bf16[256,2048]{1,0:T(8,128)(2,1)} %bitcast), channel_id=1, source_target_pairs={{0,8},{8,0},{1,9},{9,1},{2,10},{10,2},{3,11},{11,3},{4,12},{12,4},... | collective-permute-start | bytes 3145736 | tf_op jit(solution)/shard_map/ppermute | solution.py:574
  96.9 37.1 %collective-permute-start.12 = (bf16[256,2048]{1,0:T(8,128)(2,1)}, bf16[256,2048]{1,0:T(8,128)(2,1)}, u32[]{:S(2)}, u32[]{:S(2)}) collective-permute-start(bf16[256,2048]{1,0:T(8,128)(2,1)} %collective-permute-done.10), channel_id=1, source_target_pairs={{0,8},{8,0},{1,9},{9,1},{2,10},{10,2},{3,11},{11,3},{4,12},{12,4},... | collective-permute-start | bytes 3145736 | tf_op jit(solution)/shard_map/ppermute | solution.py:574
  97.5 35.1 %collective-permute-start.1 = (s32[2]{0:T(128)S(1)}, s32[2]{0:T(128)S(1)}, u32[]{:S(2)}, u32[]{:S(2)}) collective-permute-start(s32[2]{0:T(128)S(1)} %bitcast.233), channel_id=1, source_target_pairs={{0,1},{1,0},{2,3},{3,2},{4,5},{5,4},{6,7},{7,6},{8,9},{9,8},{10,11... | collective-permute-start | bytes 32 | tf_op jit(solution)/shard_map/ppermute | solution.py:48
  131.6 37.4 %collective-permute-start.16 = (bf16[512,1664]{1,0:T(8,128)(2,1)}, bf16[512,1664]{1,0:T(8,128)(2,1)}, u32[]{:S(2)}, u32[]{:S(2)}) collective-permute-start(bf16[512,1664]{1,0:T(8,128)(2,1)} %collective-permute-done.13.refs_2_), channel_id=1, source_target_pairs={{0,2},{2,6},{6,4},{4,0},{1,3},{3,7},{7,5},{5,1},{8,10},{10,14},{14... | collective-permute-start | bytes 5111816 | tf_op jit(solution)/shard_map/ppermute | solution.py:48
  134.0 642.7 %reduce-scatter.4.cloned.1.call-start = ((), (), s32[]{:S(2)}) async-start(), calls=%async_computation.6 | async-start | bytes 10485760 | tf_op jit(solution)/shard_map/reduce_scatter | solution.py:906
  139.5 52.6 %collective-permute-start.18 = (bf16[512,2048]{1,0:T(8,128)(2,1)S(1)}, bf16[512,2048]{1,0:T(8,128)(2,1)}, u32[]{:S(2)}, u32[]{:S(2)}) collective-permute-start(bf16[512,2048]{1,0:T(8,128)(2,1)S(1)} %constant_dynamic-update-slice_fusion.6.refs_0_), channel_id=1, source_target_pairs={{0,1},{1,0},{2,3},{3,2},{4,5},{5,4},{6,7},{7,6},{8,9},{9,8},{10,11... | collective-permute-start | bytes 6291464 | tf_op jit(solution)/shard_map/ppermute | solution.py:48
  179.7 24.0 %collective-permute-start.17 = (bf16[256,2176]{1,0:T(8,128)(2,1)}, bf16[256,2176]{1,0:T(8,128)(2,1)}, u32[]{:S(2)}, u32[]{:S(2)}) collective-permute-start(bf16[256,2176]{1,0:T(8,128)(2,1)} %fusion.25.refs_2_), channel_id=1, source_target_pairs={{0,2},{2,6},{6,4},{4,0},{1,3},{3,7},{7,5},{5,1},{8,10},{10,14},{14... | collective-permute-start | bytes 3342344 | tf_op jit(solution)/shard_map/ppermute | solution.py:48
  203.7 49.0 %collective-permute-start.20 = (bf16[256,2176]{1,0:T(8,128)(2,1)}, bf16[256,2176]{1,0:T(8,128)(2,1)}, u32[]{:S(2)}, u32[]{:S(2)}) collective-permute-start(bf16[256,2176]{1,0:T(8,128)(2,1)} %collective-permute-done.17.refs_2_), channel_id=1, source_target_pairs={{0,2},{2,6},{6,4},{4,0},{1,3},{3,7},{7,5},{5,1},{8,10},{10,14},{14... | collective-permute-start | bytes 3342344 | tf_op jit(solution)/shard_map/ppermute | solution.py:48
  216.2 36.5 %collective-permute-start.21 = (bf16[256,2176]{1,0:T(8,128)(2,1)}, bf16[256,2176]{1,0:T(8,128)(2,1)}, u32[]{:S(2)}, u32[]{:S(2)}) collective-permute-start(bf16[256,2176]{1,0:T(8,128)(2,1)} %collective-permute-done.17.refs_2_), channel_id=1, source_target_pairs={{0,1},{1,0},{2,3},{3,2},{4,5},{5,4},{6,7},{7,6},{8,9},{9,8},{10,11... | collective-permute-start | bytes 3342344 | tf_op jit(solution)/shard_map/ppermute | solution.py:48
  234.1 17.4 %collective-permute-start.19 = (bf16[512,512]{1,0:T(8,128)(2,1)}, bf16[512,512]{1,0:T(8,128)(2,1)}, u32[]{:S(2)}, u32[]{:S(2)}) collective-permute-start(bf16[512,512]{1,0:T(8,128)(2,1)} %get-tuple-element.416), channel_id=1, source_target_pairs={{0,1},{1,0},{2,3},{3,2},{4,5},{5,4},{6,7},{7,6},{8,9},{9,8},{10,11... | collective-permute-start | bytes 1572872 | tf_op jit(solution)/shard_map/ppermute | solution.py:48
  255.3 28.2 %collective-permute-start.23 = (bf16[256,2176]{1,0:T(8,128)(2,1)}, bf16[256,2176]{1,0:T(8,128)(2,1)}, u32[]{:S(2)}, u32[]{:S(2)}) collective-permute-start(bf16[256,2176]{1,0:T(8,128)(2,1)} %collective-permute-done.20.refs_2_), channel_id=1, source_target_pairs={{0,2},{2,6},{6,4},{4,0},{1,3},{3,7},{7,5},{5,1},{8,10},{10,14},{14... | collective-permute-start | bytes 3342344 | tf_op jit(solution)/shard_map/ppermute | solution.py:48
  257.6 27.0 %collective-permute-start.24 = (bf16[256,2176]{1,0:T(8,128)(2,1)}, bf16[256,2176]{1,0:T(8,128)(2,1)}, u32[]{:S(2)}, u32[]{:S(2)}) collective-permute-start(bf16[256,2176]{1,0:T(8,128)(2,1)} %collective-permute-done.20.refs_2_), channel_id=1, source_target_pairs={{0,1},{1,0},{2,3},{3,2},{4,5},{5,4},{6,7},{7,6},{8,9},{9,8},{10,11... | collective-permute-start | bytes 3342344 | tf_op jit(solution)/shard_map/ppermute | solution.py:48
  284.5 27.5 %collective-permute-start.25 = (bf16[256,2176]{1,0:T(8,128)(2,1)S(1)}, bf16[256,2176]{1,0:T(8,128)(2,1)S(1)}, u32[]{:S(2)}, u32[]{:S(2)}) collective-permute-start(bf16[256,2176]{1,0:T(8,128)(2,1)S(1)} %pad_maximum_fusion.4.refs_0_), channel_id=1, source_target_pairs={{0,1},{1,0},{2,3},{3,2},{4,5},{5,4},{6,7},{7,6},{8,9},{9,8},{10,11... | collective-permute-start | bytes 3342344 | tf_op jit(solution)/shard_map/ppermute | solution.py:48
  286.2 26.5 %collective-permute-start.26 = (bf16[256,2176]{1,0:T(8,128)(2,1)S(1)}, bf16[256,2176]{1,0:T(8,128)(2,1)}, u32[]{:S(2)}, u32[]{:S(2)}) collective-permute-start(bf16[256,2176]{1,0:T(8,128)(2,1)S(1)} %pad_maximum_fusion.4.refs_0_), channel_id=1, source_target_pairs={{0,2},{2,6},{6,4},{4,0},{1,3},{3,7},{7,5},{5,1},{8,10},{10,14},{14... | collective-permute-start | bytes 3342344 | tf_op jit(solution)/shard_map/ppermute | solution.py:48
  286.6 173.9 %collective-permute-start.34 = (bf16[256,2176]{1,0:T(8,128)(2,1)}, bf16[256,2176]{1,0:T(8,128)(2,1)}, u32[]{:S(2)}, u32[]{:S(2)}) collective-permute-start(bf16[256,2176]{1,0:T(8,128)(2,1)} %collective-permute-done.23.refs_2_), channel_id=1, source_target_pairs={{0,1},{1,0},{2,3},{3,2},{4,5},{5,4},{6,7},{7,6},{8,9},{9,8},{10,11... | collective-permute-start | bytes 3342344 | tf_op jit(solution)/shard_map/ppermute | solution.py:48
  313.0 45.2 %collective-permute-start.27 = (bf16[256,2176]{1,0:T(8,128)(2,1)}, bf16[256,2176]{1,0:T(8,128)(2,1)}, u32[]{:S(2)}, u32[]{:S(2)}) collective-permute-start(bf16[256,2176]{1,0:T(8,128)(2,1)} %collective-permute-done.26.refs_0_), channel_id=1, source_target_pairs={{0,1},{1,0},{2,3},{3,2},{4,5},{5,4},{6,7},{7,6},{8,9},{9,8},{10,11... | collective-permute-start | bytes 3342344 | tf_op jit(solution)/shard_map/ppermute | solution.py:48
  314.7 43.4 %collective-permute-start.28 = (bf16[256,2176]{1,0:T(8,128)(2,1)}, bf16[256,2176]{1,0:T(8,128)(2,1)S(1)}, u32[]{:S(2)}, u32[]{:S(2)}) collective-permute-start(bf16[256,2176]{1,0:T(8,128)(2,1)} %collective-permute-done.26.refs_0_), channel_id=1, source_target_pairs={{0,2},{2,6},{6,4},{4,0},{1,3},{3,7},{7,5},{5,1},{8,10},{10,14},{14... | collective-permute-start | bytes 3342344 | tf_op jit(solution)/shard_map/ppermute | solution.py:48
  358.2 37.9 %collective-permute-start.29 = (bf16[256,2176]{1,0:T(8,128)(2,1)S(1)}, bf16[256,2176]{1,0:T(8,128)(2,1)S(1)}, u32[]{:S(2)}, u32[]{:S(2)}) collective-permute-start(bf16[256,2176]{1,0:T(8,128)(2,1)S(1)} %collective-permute-done.28.refs_0_), channel_id=1, source_target_pairs={{0,1},{1,0},{2,3},{3,2},{4,5},{5,4},{6,7},{7,6},{8,9},{9,8},{10,11... | collective-permute-start | bytes 3342344 | tf_op jit(solution)/shard_map/ppermute | solution.py:48
  359.9 36.2 %collective-permute-start.30 = (bf16[256,2176]{1,0:T(8,128)(2,1)S(1)}, bf16[256,2176]{1,0:T(8,128)(2,1)}, u32[]{:S(2)}, u32[]{:S(2)}) collective-permute-start(bf16[256,2176]{1,0:T(8,128)(2,1)S(1)} %collective-permute-done.28.refs_0_), channel_id=1, source_target_pairs={{0,2},{2,6},{6,4},{4,0},{1,3},{3,7},{7,5},{5,1},{8,10},{10,14},{14... | collective-permute-start | bytes 3342344 | tf_op jit(solution)/shard_map/ppermute | solution.py:48
  360.5 49.1 %collective-permute-start.31 = (bf16[256,2176]{1,0:T(8,128)(2,1)}, bf16[256,2176]{1,0:T(8,128)(2,1)S(1)}, u32[]{:S(2)}, u32[]{:S(2)}) collective-permute-start(bf16[256,2176]{1,0:T(8,128)(2,1)} %get-tuple-element.200), channel_id=1, source_target_pairs={{0,1},{1,0},{2,3},{3,2},{4,5},{5,4},{6,7},{7,6},{8,9},{9,8},{10,11... | collective-permute-start | bytes 3342344 | tf_op jit(solution)/shard_map/ppermute | solution.py:48
  394.3 51.0 %collective-permute-start.33 = (bf16[256,2176]{1,0:T(8,128)(2,1)}, bf16[256,2176]{1,0:T(8,128)(2,1)}, u32[]{:S(2)}, u32[]{:S(2)}) collective-permute-start(bf16[256,2176]{1,0:T(8,128)(2,1)} %get-tuple-element.216), channel_id=1, source_target_pairs={{0,1},{1,0},{2,3},{3,2},{4,5},{5,4},{6,7},{7,6},{8,9},{9,8},{10,11... | collective-permute-start | bytes 3342344 | tf_op jit(solution)/shard_map/ppermute | solution.py:48
  409.6 47.8 %collective-permute-start.32 = (bf16[256,2176]{1,0:T(8,128)(2,1)}, bf16[256,2176]{1,0:T(8,128)(2,1)}, u32[]{:S(2)}, u32[]{:S(2)}) collective-permute-start(bf16[256,2176]{1,0:T(8,128)(2,1)} %collective-permute-done.30.refs_0_), channel_id=1, source_target_pairs={{0,1},{1,0},{2,3},{3,2},{4,5},{5,4},{6,7},{7,6},{8,9},{9,8},{10,11... | collective-permute-start | bytes 3342344 | tf_op jit(solution)/shard_map/ppermute | solution.py:48
  444.5 51.3 %collective-permute-start.35 = (bf16[256,2176]{1,0:T(8,128)(2,1)}, bf16[256,2176]{1,0:T(8,128)(2,1)S(1)}, u32[]{:S(2)}, u32[]{:S(2)}) collective-permute-start(bf16[256,2176]{1,0:T(8,128)(2,1)} %get-tuple-element.233), channel_id=1, source_target_pairs={{0,1},{1,0},{2,3},{3,2},{4,5},{5,4},{6,7},{7,6},{8,9},{9,8},{10,11... | collective-permute-start | bytes 3342344 | tf_op jit(solution)/shard_map/ppermute | solution.py:48
  459.9 35.8 %collective-permute-start.36 = (bf16[256,2176]{1,0:T(8,128)(2,1)}, bf16[256,2176]{1,0:T(8,128)(2,1)S(1)}, u32[]{:S(2)}, u32[]{:S(2)}) collective-permute-start(bf16[256,2176]{1,0:T(8,128)(2,1)} %add_convert_fusion.2), channel_id=1, source_target_pairs={{0,2},{2,6},{6,4},{4,0},{1,3},{3,7},{7,5},{5,1},{8,10},{10,14},{14... | collective-permute-start | bytes 3342344 | tf_op jit(solution)/shard_map/ppermute | solution.py:48
  494.0 22.2 %collective-permute-start.37 = (bf16[256,2176]{1,0:T(8,128)(2,1)}, bf16[256,2176]{1,0:T(8,128)(2,1)}, u32[]{:S(2)}, u32[]{:S(2)}) collective-permute-start(bf16[256,2176]{1,0:T(8,128)(2,1)} %get-tuple-element.241), channel_id=1, source_target_pairs={{0,1},{1,0},{2,3},{3,2},{4,5},{5,4},{6,7},{7,6},{8,9},{9,8},{10,11... | collective-permute-start | bytes 3342344 | tf_op jit(solution)/shard_map/ppermute | solution.py:48
  497.1 22.4 %collective-permute-start.38 = (bf16[256,2176]{1,0:T(8,128)(2,1)}, bf16[256,2176]{1,0:T(8,128)(2,1)S(1)}, u32[]{:S(2)}, u32[]{:S(2)}) collective-permute-start(bf16[256,2176]{1,0:T(8,128)(2,1)} %add_convert_fusion.1), channel_id=1, source_target_pairs={{0,2},{2,6},{6,4},{4,0},{1,3},{3,7},{7,5},{5,1},{8,10},{10,14},{14... | collective-permute-start | bytes 3342344 | tf_op jit(solution)/shard_map/ppermute | solution.py:48
  519.6 261.2 %reduce-scatter.6.cloned.1.call-start = ((), (), s32[]{:S(2)}) async-start(), calls=%async_computation.7 | async-start | bytes 10485760 | tf_op jit(solution)/shard_map/reduce_scatter | solution.py:906
  519.6 22.8 %collective-permute-start.40 = (bf16[256,2048]{1,0:T(8,128)(2,1)}, bf16[256,2048]{1,0:T(8,128)(2,1)}, u32[]{:S(2)}, u32[]{:S(2)}) collective-permute-start(bf16[256,2048]{1,0:T(8,128)(2,1)} %get-tuple-element.193), channel_id=1, source_target_pairs={{0,1},{1,0},{2,3},{3,2},{4,5},{5,4},{6,7},{7,6},{8,9},{9,8},{10,11... | collective-permute-start | bytes 3145736 | tf_op jit(solution)/shard_map/ppermute | solution.py:48
  522.7 21.2 %collective-permute-start.39 = (bf16[256,2176]{1,0:T(8,128)(2,1)}, bf16[256,2176]{1,0:T(8,128)(2,1)S(1)}, u32[]{:S(2)}, u32[]{:S(2)}) collective-permute-start(bf16[256,2176]{1,0:T(8,128)(2,1)} %add_convert_fusion), channel_id=1, source_target_pairs={{0,2},{2,6},{6,4},{4,0},{1,3},{3,7},{7,5},{5,1},{8,10},{10,14},{14... | collective-permute-start | bytes 3342344 | tf_op jit(solution)/shard_map/ppermute | solution.py:48
  543.9 240.9 %reduce-scatter.8.cloned.1.call-start = ((), (), s32[]{:S(2)}) async-start(), calls=%async_computation.8 | async-start | bytes 10485760 | tf_op jit(solution)/shard_map/reduce_scatter | solution.py:906
  558.6 14.1 %collective-permute-start.42 = (bf16[512,512]{1,0:T(8,128)(2,1)S(1)}, bf16[512,512]{1,0:T(8,128)(2,1)S(1)}, u32[]{:S(2)}, u32[]{:S(2)}) collective-permute-start(bf16[512,512]{1,0:T(8,128)(2,1)S(1)} %get-tuple-element.415), channel_id=1, source_target_pairs={{0,1},{1,0},{2,3},{3,2},{4,5},{5,4},{6,7},{7,6},{8,9},{9,8},{10,11... | collective-permute-start | bytes 1572872 | tf_op jit(solution)/shard_map/ppermute | solution.py:48
  562.3 34.2 %collective-permute-start.44 = (bf16[256,2048]{1,0:T(8,128)(2,1)S(1)}, bf16[256,2048]{1,0:T(8,128)(2,1)S(1)}, u32[]{:S(2)}, u32[]{:S(2)}) collective-permute-start(bf16[256,2048]{1,0:T(8,128)(2,1)S(1)} %add_convert_fusion.6), channel_id=1, source_target_pairs={{0,2},{2,6},{6,4},{4,0},{1,3},{3,7},{7,5},{5,1},{8,10},{10,14},{14... | collective-permute-start | bytes 3145736 | tf_op jit(solution)/shard_map/ppermute | solution.py:48
  572.9 24.6 %collective-permute-start.43 = (bf16[256,2048]{1,0:T(8,128)(2,1)S(1)}, bf16[256,2048]{1,0:T(8,128)(2,1)S(1)}, u32[]{:S(2)}, u32[]{:S(2)}) collective-permute-start(bf16[256,2048]{1,0:T(8,128)(2,1)S(1)} %copy-done.59), channel_id=1, source_target_pairs={{0,1},{1,0},{2,3},{3,2},{4,5},{5,4},{6,7},{7,6},{8,9},{9,8},{10,11... | collective-permute-start | bytes 3145736 | tf_op jit(solution)/shard_map/ppermute | solution.py:48
  598.0 24.8 %collective-permute-start.48 = (bf16[256,2048]{1,0:T(8,128)(2,1)S(1)}, bf16[256,2048]{1,0:T(8,128)(2,1)S(1)}, u32[]{:S(2)}, u32[]{:S(2)}) collective-permute-start(bf16[256,2048]{1,0:T(8,128)(2,1)S(1)} %add_convert_fusion.5), channel_id=1, source_target_pairs={{0,2},{2,6},{6,4},{4,0},{1,3},{3,7},{7,5},{5,1},{8,10},{10,14},{14... | collective-permute-start | bytes 3145736 | tf_op jit(solution)/shard_map/ppermute | solution.py:48
  599.2 23.8 %collective-permute-start.47 = (bf16[256,2048]{1,0:T(8,128)(2,1)}, bf16[256,2048]{1,0:T(8,128)(2,1)S(1)}, u32[]{:S(2)}, u32[]{:S(2)}) collective-permute-start(bf16[256,2048]{1,0:T(8,128)(2,1)} %get-tuple-element.257), channel_id=1, source_target_pairs={{0,1},{1,0},{2,3},{3,2},{4,5},{5,4},{6,7},{7,6},{8,9},{9,8},{10,11... | collective-permute-start | bytes 3145736 | tf_op jit(solution)/shard_map/ppermute | solution.py:48
  608.8 9.4 %collective-permute-start.45 = (bf16[256,2048]{1,0:T(8,128)(2,1)}, bf16[256,2048]{1,0:T(8,128)(2,1)S(1)}, u32[]{:S(2)}, u32[]{:S(2)}) collective-permute-start(bf16[256,2048]{1,0:T(8,128)(2,1)} %get-tuple-element.411), channel_id=1, source_target_pairs={{0,8},{8,0},{1,9},{9,1},{2,10},{10,2},{3,11},{11,3},{4,12},{12,4},... | collective-permute-start | bytes 3145736 | tf_op jit(solution)/shard_map/ppermute | solution.py:48
  608.8 9.4 %collective-permute-start.46 = (bf16[256,2048]{1,0:T(8,128)(2,1)S(1)}, bf16[256,2048]{1,0:T(8,128)(2,1)S(1)}, u32[]{:S(2)}, u32[]{:S(2)}) collective-permute-start(bf16[256,2048]{1,0:T(8,128)(2,1)S(1)} %get-tuple-element.410), channel_id=1, source_target_pairs={{0,8},{8,0},{1,9},{9,1},{2,10},{10,2},{3,11},{11,3},{4,12},{12,4},... | collective-permute-start | bytes 3145736 | tf_op jit(solution)/shard_map/ppermute | solution.py:48
  623.0 26.4 %collective-permute-start.52 = (bf16[256,2048]{1,0:T(8,128)(2,1)}, bf16[256,2048]{1,0:T(8,128)(2,1)}, u32[]{:S(2)}, u32[]{:S(2)}) collective-permute-start(bf16[256,2048]{1,0:T(8,128)(2,1)} %get-tuple-element.270), channel_id=1, source_target_pairs={{0,1},{1,0},{2,3},{3,2},{4,5},{5,4},{6,7},{7,6},{8,9},{9,8},{10,11... | collective-permute-start | bytes 3145736 | tf_op jit(solution)/shard_map/ppermute | solution.py:48
  625.8 57.3 %collective-permute-start.51 = (bf16[2,2,2,64,1536]{4,3,2,1,0:T(8,128)(2,1)}, bf16[2,2,2,64,1536]{4,3,2,1,0:T(8,128)(2,1)}, u32[]{:S(2)}, u32[]{:S(2)}) collective-permute-start(bf16[2,2,2,64,1536]{4,3,2,1,0:T(8,128)(2,1)} %dynamic-slice_bitcast_fusion.1), channel_id=1, source_target_pairs={{0,2},{2,6},{6,4},{4,0},{1,3},{3,7},{7,5},{5,1},{8,10},{10,14},{14... | collective-permute-start | bytes 4718600 | tf_op jit(solution)/shard_map/ppermute | solution.py:48
  628.7 54.5 %collective-permute-start.50 = (bf16[256,2048]{1,0:T(8,128)(2,1)}, bf16[256,2048]{1,0:T(8,128)(2,1)}, u32[]{:S(2)}, u32[]{:S(2)}) collective-permute-start(bf16[256,2048]{1,0:T(8,128)(2,1)} %add_convert_fusion.4), channel_id=1, source_target_pairs={{0,2},{2,6},{6,4},{4,0},{1,3},{3,7},{7,5},{5,1},{8,10},{10,14},{14... | collective-permute-start | bytes 3145736 | tf_op jit(solution)/shard_map/ppermute | solution.py:48
  630.9 52.2 %collective-permute-start.49 = (bf16[256,2048]{1,0:T(8,128)(2,1)}, bf16[256,2048]{1,0:T(8,128)(2,1)}, u32[]{:S(2)}, u32[]{:S(2)}) collective-permute-start(bf16[256,2048]{1,0:T(8,128)(2,1)} %get-tuple-element.262), channel_id=1, source_target_pairs={{0,1},{1,0},{2,3},{3,2},{4,5},{5,4},{6,7},{7,6},{8,9},{9,8},{10,11... | collective-permute-start | bytes 3145736 | tf_op jit(solution)/shard_map/ppermute | solution.py:48
  694.0 43.8 %collective-permute-start.55 = (bf16[2,4,64,2048]{3,2,1,0:T(8,128)(2,1)}, bf16[2,4,64,2048]{3,2,1,0:T(8,128)(2,1)}, u32[]{:S(2)}, u32[]{:S(2)}) collective-permute-start(bf16[2,4,64,2048]{3,2,1,0:T(8,128)(2,1)} %dynamic-slice_bitcast_fusion), channel_id=1, source_target_pairs={{0,1},{1,0},{2,3},{3,2},{4,5},{5,4},{6,7},{7,6},{8,9},{9,8},{10,11... | collective-permute-start | bytes 6291464 | tf_op jit(solution)/shard_map/ppermute | solution.py:48
  694.2 46.7 %collective-permute-start.53 = (bf16[2,2,2,64,1536]{4,3,2,1,0:T(8,128)(2,1)}, bf16[2,2,2,64,1536]{4,3,2,1,0:T(8,128)(2,1)}, u32[]{:S(2)}, u32[]{:S(2)}) collective-permute-start(bf16[2,2,2,64,1536]{4,3,2,1,0:T(8,128)(2,1)} %convert_add_fusion.1), channel_id=1, source_target_pairs={{0,2},{2,6},{6,4},{4,0},{1,3},{3,7},{7,5},{5,1},{8,10},{10,14},{14... | collective-permute-start | bytes 4718600 | tf_op jit(solution)/shard_map/ppermute | solution.py:48
  698.0 42.8 %collective-permute-start.54 = (bf16[2,2,2,64,128]{4,3,2,1,0:T(8,128)(2,1)S(1)}, bf16[2,2,2,64,128]{4,3,2,1,0:T(8,128)(2,1)S(1)}, u32[]{:S(2)}, u32[]{:S(2)}) collective-permute-start(bf16[2,2,2,64,128]{4,3,2,1,0:T(8,128)(2,1)S(1)} %dynamic-slice_bitcast_fusion.7), channel_id=1, source_target_pairs={{0,2},{2,6},{6,4},{4,0},{1,3},{3,7},{7,5},{5,1},{8,10},{10,14},{14... | collective-permute-start | bytes 393224 | tf_op jit(solution)/shard_map/ppermute | solution.py:48
  745.1 43.8 %collective-permute-start.56 = (bf16[2,2,2,64,1536]{4,3,2,1,0:T(8,128)(2,1)}, bf16[2,2,2,64,1536]{4,3,2,1,0:T(8,128)(2,1)}, u32[]{:S(2)}, u32[]{:S(2)}) collective-permute-start(bf16[2,2,2,64,1536]{4,3,2,1,0:T(8,128)(2,1)} %fusion.8), channel_id=1, source_target_pairs={{0,2},{2,6},{6,4},{4,0},{1,3},{3,7},{7,5},{5,1},{8,10},{10,14},{14... | collective-permute-start | bytes 4718600 | tf_op jit(solution)/shard_map/ppermute | solution.py:48
  746.1 28.5 %collective-permute-start.58 = (bf16[4,64,2048]{2,1,0:T(8,128)(2,1)}, bf16[4,64,2048]{2,1,0:T(8,128)(2,1)}, u32[]{:S(2)}, u32[]{:S(2)}) collective-permute-start(bf16[4,64,2048]{2,1,0:T(8,128)(2,1)} %dynamic-slice_bitcast_fusion.2), channel_id=1, source_target_pairs={{0,16},{16,0},{1,17},{17,1},{2,18},{18,2},{3,19},{19,3},{4,20},{20... | collective-permute-start | bytes 3145736 | tf_op jit(solution)/shard_map/ppermute | solution.py:48
  746.2 42.7 %collective-permute-start.57 = (bf16[2,2,2,64,128]{4,3,2,1,0:T(8,128)(2,1)S(1)}, bf16[2,2,2,64,128]{4,3,2,1,0:T(8,128)(2,1)S(1)}, u32[]{:S(2)}, u32[]{:S(2)}) collective-permute-start(bf16[2,2,2,64,128]{4,3,2,1,0:T(8,128)(2,1)S(1)} %fusion.41), channel_id=1, source_target_pairs={{0,2},{2,6},{6,4},{4,0},{1,3},{3,7},{7,5},{5,1},{8,10},{10,14},{14... | collective-permute-start | bytes 393224 | tf_op jit(solution)/shard_map/ppermute | solution.py:48
  791.5 17.6 %collective-permute-start.59 = (bf16[2,2,64,1536]{3,2,1,0:T(8,128)(2,1)S(1)}, bf16[2,2,64,1536]{3,2,1,0:T(8,128)(2,1)S(1)}, u32[]{:S(2)}, u32[]{:S(2)}) collective-permute-start(bf16[2,2,64,1536]{3,2,1,0:T(8,128)(2,1)S(1)} %dynamic-slice_bitcast_fusion.3), channel_id=1, source_target_pairs={{0,16},{16,0},{1,17},{17,1},{2,18},{18,2},{3,19},{19,3},{4,20},{20... | collective-permute-start | bytes 2359304 | tf_op jit(solution)/shard_map/ppermute | solution.py:48
  797.7 11.7 %collective-permute-start.60 = (bf16[2,2,2,64,128]{4,3,2,1,0:T(8,128)(2,1)S(1)}, bf16[2,2,2,64,128]{4,3,2,1,0:T(8,128)(2,1)S(1)}, u32[]{:S(2)}, u32[]{:S(2)}) collective-permute-start(bf16[2,2,2,64,128]{4,3,2,1,0:T(8,128)(2,1)S(1)} %fusion.40), channel_id=1, source_target_pairs={{0,2},{2,6},{6,4},{4,0},{1,3},{3,7},{7,5},{5,1},{8,10},{10,14},{14... | collective-permute-start | bytes 393224 | tf_op jit(solution)/shard_map/ppermute | solution.py:48
  799.2 10.1 %collective-permute-start.61 = (bf16[64,2048]{1,0:T(8,128)(2,1)S(1)}, bf16[64,2048]{1,0:T(8,128)(2,1)S(1)}, u32[]{:S(2)}, u32[]{:S(2)}) collective-permute-start(bf16[64,2048]{1,0:T(8,128)(2,1)S(1)} %dynamic-slice_bitcast_fusion.6), channel_id=1, source_target_pairs={{0,2},{2,6},{6,4},{4,0},{1,3},{3,7},{7,5},{5,1},{8,10},{10,14},{14... | collective-permute-start | bytes 786440 | tf_op jit(solution)/shard_map/ppermute | solution.py:48
  813.9 8.2 collective-permute-start.63
  (74 other events, 1251.7 us)
Sparse Core Ops, SparseCore 0:
  47.9 69.0 all-gather.3
  118.6 59.6 all-gather.5
  179.8 58.2 all-gather.7
  519.7 69.2 reduce-scatter.3
  591.6 74.4 reduce-scatter.5
  683.3 76.5 reduce-scatter.7

commit v7 on v6

--- a/solution.py
+++ b/solution.py
@@ -893,9 +893,9 @@
             arrived["normed"] = reduce_blocks(lambda key: normed_sums[key[0]], ("x",))
         if n == 1:
             arrived["x"] = reduce_axis(tied(output_grad, late_total), "x", 2).astype(BF)
+            arrived["experts"] = expert_totals[:2]
         if n == 2:
             arrived["y"] = reduce_axis(output_x, "y", 0).astype(BF)
-            arrived["experts"] = expert_totals
         if n >= 1:
             arrived["small"] = shift(small_total.astype(BF), "z", 1)
         arrived = lax.optimization_barrier(arrived)
@@ -910,9 +910,9 @@
             small_total = part_of(small, "z", 2, 1)
         if n == 1:
             output_x = arrived["x"]
+            expert_totals[:2] = arrived["experts"]
         if n == 2:
             output_y = arrived["y"]
-            expert_totals = arrived["experts"]
             output_total = part_of(output_y, "z", 0, 1)
         if n >= 1:
             part = part_of(small, "z", 2, ring[small_hops])
@@ -922,7 +922,7 @@
     layer_out = (hidden + combined).astype(BF)
     late = reduce_axis(late_total.astype(BF), "y", 0).astype(BF)
     arrived = [shift(small_total.astype(BF), "z", 1), shift(output_total.astype(BF), "z", 1)]
-    late, arrived = lax.optimization_barrier((late, arrived))
+    late, arrived, expert_totals[2] = lax.optimization_barrier((late, arrived, expert_totals[2]))
     small = part_of(small, "z", 2, 0) + arrived[0].astype(F32)
     small = reduce_axis(small.astype(BF), "y", 0).astype(BF)
     output_total = part_of(output_y, "z", 0, ring[output_hops]) + arrived[1].astype(F32)

time: 844 us -> 846 us (level)
  transfers between devices with their start and end apart: 73 -> 73, of which waited for: 35 -> 36; matrix products, arithmetic and copies ran while one was open for 20% -> 21% of each run, Pallas kernels for 21% -> 21%
where the time goes in v7:
time: 846 us; the launch traced here: 843 us
  waiting for transfers between devices  372 us (44%)
  Pallas kernels  178 us (21%)
  matrix products  96.7 us (11%)
  starting transfers between devices  82.2 us (10%)
  other arithmetic  67 us (8%)
  local copies, waits for them, and re-layouts  31.5 us (4%)
  between operations  16 us (2%)
    ppermute x63, waiting for transfers between devices, shift(): return lax.ppermute(value, axis, pairs)  368 us
    pallas_call x4, Pallas kernels, run_experts(): pl.pallas_call(functools.partial(experts_kernel, sizes), out_shape=(*[jax...  132 us
    ppermute x63, starting transfers between devices, shift(): return lax.ppermute(value, axis, pairs)  81.2 us
    dot_general x3, matrix products, weight_grads(): lax.dot_general(kept[left], kept[right], (((1,), (1,)), ((0,), (0,))), pr...  54.5 us
    pallas_call x1, Pallas kernels, attend_back(): pl.pallas_call(functools.partial(attend_back_kernel, heads), out_shape=(j...  21.9 us
  transfers between devices with their start and end apart: 73, of which 36 were waited for; matrix products, arithmetic and copies ran while one was open for 21% of the time, Pallas kernels for 21%

profile of v7, /device:TPU:0, one launch (start us, length us, event | category | flops | bytes accessed | tf_op | source)
XLA Modules:
  0.0 843.4 jit_solution(12554135690764336097)
XLA Ops:
  13.8 2.9 collective-permute-start.4
  18.3 8.5 %collective-permute-done.4 = bf16[128,1664]{1,0:T(8,128)(2,1)S(1)} collective-permute-done((bf16[128,1664]{1,0:T(8,128)(2,1)S(1)}, bf16[128,1664]{1,0:T(8,128)(2,1)S(1)}, u32[]{:S(2)}, u32[]{:S(2)}) %collective-permute-start.4) | collective-permute-done | bytes 426016 | tf_op jit(solution)/shard_map/ppermute | solution.py:48
  30.4 6.6 collective-permute-done.7
  37.7 9.9 %collective-permute-done.6 = bf16[256,1664]{1,0:T(8,128)(2,1)S(1)} collective-permute-done((bf16[256,1664]{1,0:T(8,128)(2,1)S(1)}, bf16[256,1664]{1,0:T(8,128)(2,1)S(1)}, u32[]{:S(2)}, u32[]{:S(2)}) %collective-permute-start.6) | collective-permute-done | bytes 852000 | tf_op jit(solution)/shard_map/ppermute | solution.py:48
  53.6 2.6 collective-permute-start.9
  56.2 2.5 fusion.25.refs_2_
  59.2 35.0 %collective-permute-done.9 = bf16[64,2048]{1,0:T(8,128)(2,1)S(1)} collective-permute-done((bf16[64,2048]{1,0:T(8,128)(2,1)}, bf16[64,2048]{1,0:T(8,128)(2,1)S(1)}, u32[]{:S(2)}, u32[]{:S(2)}) %collective-permute-start.9) | collective-permute-done | bytes 262176 | tf_op jit(solution)/shard_map/ppermute | solution.py:48
  98.1 30.0 %collective-permute-done.14 = bf16[256,2048]{1,0:T(8,128)(2,1)} collective-permute-done((bf16[256,2048]{1,0:T(8,128)(2,1)S(1)}, bf16[256,2048]{1,0:T(8,128)(2,1)}, u32[]{:S(2)}, u32[]{:S(2)}) %collective-permute-start.14) | collective-permute-done | bytes 1048608 | tf_op jit(solution)/shard_map/ppermute | solution.py:48
  128.2 3.4 collective-permute-done.13.refs_2_
  134.0 2.6 fusion
  140.2 28.9 %collective-permute-done.16.refs_3_ = bf16[512,1664]{1,0:T(8,128)(2,1)} collective-permute-done((bf16[512,1664]{1,0:T(8,128)(2,1)}, bf16[512,1664]{1,0:T(8,128)(2,1)}, u32[]{:S(2)}, u32[]{:S(2)}) %collective-permute-start.16) | collective-permute-done | bytes 1703968 | tf_op jit(solution)/shard_map/ppermute | solution.py:48
  169.0 7.3 shard_map.272
  176.3 2.8 copy-done
  181.3 10.8 %fusion.5.qkv_ref = f32[1024,1536]{1,0:T(8,128)S(1)} fusion(bf16[2048,1664]{1,0:T(8,128)(2,1)} %copy-done, f32[2048]{0:T(1024)S(1)} %get-tuple-element.395, f32[1024]{0:T(1024)S(1)} %add_rsqrt_fusion, bf16[256,2048]{1,0:T(8,128)(2,1)} %collective-permute-done.12, bf16[256,2048]{1,0:T(8,128)(2,1)} %collective-permute-done.10, ...), kind=kOutput, calls=%fused_computation.8 | convolution fusion | flops 6465519616 | bytes 16789504 | tf_op jit(solution)/shard_map/dot_general | solution.py:26
  192.1 11.6 %collective-permute-done.17.refs_2_ = bf16[256,2176]{1,0:T(8,128)(2,1)} collective-permute-done((bf16[256,2176]{1,0:T(8,128)(2,1)}, bf16[256,2176]{1,0:T(8,128)(2,1)}, u32[]{:S(2)}, u32[]{:S(2)}) %collective-permute-start.17) | collective-permute-done | bytes 1114144 | tf_op jit(solution)/shard_map/ppermute | solution.py:48
  203.7 12.5 %collective-permute-start.20 = (bf16[256,2176]{1,0:T(8,128)(2,1)}, bf16[256,2176]{1,0:T(8,128)(2,1)}, u32[]{:S(2)}, u32[]{:S(2)}) collective-permute-start(bf16[256,2176]{1,0:T(8,128)(2,1)} %collective-permute-done.17.refs_2_), channel_id=1, source_target_pairs={{0,2},{2,6},{6,4},{4,0},{1,3},{3,7},{7,5},{5,1},{8,10},{10,14},{14... | collective-permute-start | bytes 3342344 | tf_op jit(solution)/shard_map/ppermute | solution.py:48
  216.2 2.4 collective-permute-start.21
  218.5 14.6 %shard_map.273 = bf16[1024,512]{1,0:T(8,128)(2,1)S(1)} custom-call(s32[8]{0:T(128)S(1)} %pad_add_fusion.lengths_ref, f32[1024,1536]{1,0:T(8,128)S(1)} %fusion.5.qkv_ref, f32[2,128]{1,0:T(2,128)S(1)} %pad_maximum_fusion.13.gains_ref, f32[128,128]{1,0:T(8,128)S(1)} %get-tuple-element.478.cosine_ref, f32[128,128]{1,0:T(8,128)S(1)} %get-tuple-element.479.sine_ref), custom_call_target="tpu_custom_call" | custom-call | flops 14000000000 | bytes 14680064 | tf_op jit(solution)/shard_map/pallas_call | solution.py:247
  234.2 2.4 shard_map.274
  236.6 15.0 %collective-permute-done.19 = bf16[512,512]{1,0:T(8,128)(2,1)} collective-permute-done((bf16[512,512]{1,0:T(8,128)(2,1)}, bf16[512,512]{1,0:T(8,128)(2,1)}, u32[]{:S(2)}, u32[]{:S(2)}) %collective-permute-start.19) | collective-permute-done | bytes 524320 | tf_op jit(solution)/shard_map/ppermute | solution.py:48
  252.7 2.4 fusion.77
  264.3 19.2 %collective-permute-done.23.refs_2_ = bf16[256,2176]{1,0:T(8,128)(2,1)} collective-permute-done((bf16[256,2176]{1,0:T(8,128)(2,1)}, bf16[256,2176]{1,0:T(8,128)(2,1)}, u32[]{:S(2)}, u32[]{:S(2)}) %collective-permute-start.23) | collective-permute-done | bytes 1114144 | tf_op jit(solution)/shard_map/ppermute | solution.py:48
  286.9 25.2 %collective-permute-done.25.refs_1_ = bf16[256,2176]{1,0:T(8,128)(2,1)S(1)} collective-permute-done((bf16[256,2176]{1,0:T(8,128)(2,1)S(1)}, bf16[256,2176]{1,0:T(8,128)(2,1)S(1)}, u32[]{:S(2)}, u32[]{:S(2)}) %collective-permute-start.25) | collective-permute-done | bytes 1114144 | tf_op jit(solution)/shard_map/ppermute | solution.py:48
  315.1 31.9 %shard_map.275 = (bf16[256,2048]{1,0:T(8,128)(2,1)}, bf16[256,2048]{1,0:T(8,128)(2,1)}, bf16[256,2176]{1,0:T(8,128)(2,1)}, bf16[256,2176]{1,0:T(8,128)(2,1)}, bf...) custom-call(s32[1]{0:T(128)} %bitcast.68.places_ref, ...), custom_call_target="tpu_custom_call" | custom-call | flops 53687091200 | bytes 41943040 | tf_op jit(solution)/shard_map/pallas_call | solution.py:481
  347.0 11.3 %collective-permute-done.27.refs_1_ = bf16[256,2176]{1,0:T(8,128)(2,1)} collective-permute-done((bf16[256,2176]{1,0:T(8,128)(2,1)}, bf16[256,2176]{1,0:T(8,128)(2,1)}, u32[]{:S(2)}, u32[]{:S(2)}) %collective-permute-start.27) | collective-permute-done | bytes 1114144 | tf_op jit(solution)/shard_map/ppermute | solution.py:48
  360.8 33.4 %shard_map.276 = (bf16[256,2048]{1,0:T(8,128)(2,1)}, bf16[256,2048]{1,0:T(8,128)(2,1)}, bf16[256,2176]{1,0:T(8,128)(2,1)}, bf16[256,2176]{1,0:T(8,128)(2,1)}, bf...) custom-call(s32[1]{0:T(128)} %bitcast.68.places_ref, ...), custom_call_target="tpu_custom_call", output_to_operand_aliasing={{4}: (8, {}), {5}: (9, {}), {6}: (10, {}), {7}: (11, {}), {... | custom-call | flops 53687091200 | bytes 41943040 | tf_op jit(solution)/shard_map/pallas_call | solution.py:481
  396.1 13.6 %collective-permute-done.31 = bf16[256,2176]{1,0:T(8,128)(2,1)S(1)} collective-permute-done((bf16[256,2176]{1,0:T(8,128)(2,1)}, bf16[256,2176]{1,0:T(8,128)(2,1)S(1)}, u32[]{:S(2)}, u32[]{:S(2)}) %collective-permute-start.31) | collective-permute-done | bytes 1114144 | tf_op jit(solution)/shard_map/ppermute | solution.py:48
  411.3 33.2 %shard_map.277 = (bf16[256,2048]{1,0:T(8,128)(2,1)}, bf16[256,2048]{1,0:T(8,128)(2,1)}, bf16[256,2176]{1,0:T(8,128)(2,1)}, bf16[256,2176]{1,0:T(8,128)(2,1)}, bf...) custom-call(s32[1]{0:T(128)} %bitcast.68.places_ref, ...), custom_call_target="tpu_custom_call", output_to_operand_aliasing={{4}: (8, {}), {5}: (9, {}), {6}: (10, {}), {7}: (11, {}), {... | custom-call | flops 53687091200 | bytes 41943040 | tf_op jit(solution)/shard_map/pallas_call | solution.py:481
  445.3 12.2 %collective-permute-done.32.refs_1_ = bf16[256,2176]{1,0:T(8,128)(2,1)} collective-permute-done((bf16[256,2176]{1,0:T(8,128)(2,1)}, bf16[256,2176]{1,0:T(8,128)(2,1)}, u32[]{:S(2)}, u32[]{:S(2)}) %collective-permute-start.32) | collective-permute-done | bytes 1114144 | tf_op jit(solution)/shard_map/ppermute | solution.py:48
  457.5 2.5 add_convert_fusion.2
  460.5 33.4 %shard_map.278 = (bf16[256,2048]{1,0:T(8,128)(2,1)}, bf16[256,2048]{1,0:T(8,128)(2,1)}, bf16[256,2176]{1,0:T(8,128)(2,1)}, bf16[256,2176]{1,0:T(8,128)(2,1)}, bf...) custom-call(s32[1]{0:T(128)} %bitcast.68.places_ref, ...), custom_call_target="tpu_custom_call", output_to_operand_aliasing={{4}: (8, {}), {5}: (9, {}), {6}: (10, {}), {7}: (11, {}), {... | custom-call | flops 53687091200 | bytes 41943040 | tf_op jit(solution)/shard_map/pallas_call | solution.py:481
  498.4 17.8 %convolution_convert_fusion.3 = bf16[2,1024,2048]{2,1,0:T(8,128)(2,1)} fusion(bf16[2,1280,1024]{2,1,0:T(8,128)(2,1)} %get-tuple-element.236, bf16[2,1280,2048]{2,1,0:T(8,128)(2,1)} %get-tuple-element.237), kind=kOutput, calls=%fused_computation.12 | convolution fusion | flops 10741612544 | bytes 24117248 | tf_op jit(solution)/shard_map/dot_general | solution.py:801
  516.2 3.4 collective-permute-done.38
  520.0 2.6 add_convert_fusion
  523.2 19.3 %convolution_convert_fusion.2 = bf16[2,2048,1024]{2,1,0:T(8,128)(2,1)} fusion(bf16[2,1280,2048]{2,1,0:T(8,128)(2,1)} %get-tuple-element.267, bf16[2,1280,1024]{2,1,0:T(8,128)(2,1)} %get-tuple-element.246), kind=kOutput, calls=%fused_computation.11 | convolution fusion | flops 10741612544 | bytes 24117248 | tf_op jit(solution)/shard_map/dot_general | solution.py:801
  549.6 2.9 collective-permute-done.41
  553.4 5.1 convolution_convert_fusion.6
  563.2 9.6 %collective-permute-done.42 = bf16[512,512]{1,0:T(8,128)(2,1)S(1)} collective-permute-done((bf16[512,512]{1,0:T(8,128)(2,1)S(1)}, bf16[512,512]{1,0:T(8,128)(2,1)S(1)}, u32[]{:S(2)}, u32[]{:S(2)}) %collective-permute-start.42) | collective-permute-done | bytes 524320 | tf_op jit(solution)/shard_map/ppermute | solution.py:48
  574.7 21.9 %shard_map.279 = (bf16[1024,1536]{1,0:T(8,128)(2,1)S(1)}, f32[2,128]{1,0:T(2,128)S(1)}) custom-call(s32[8]{0:T(128)S(1)} %pad_add_fusion.lengths_ref, f32[1024,1536]{1,0:T(8,128)S(1)} %bitcast.213, bf16[1024,512]{1,0:T(8,128)(2,1)S(1)} %pad_maximum_fusion.5.mixed_grad_ref, f32[2,128]{1,0:T(2,128)S(1)} %copy-done.7, ...), custom_call_target="tpu_custom_call" | custom-call | flops 20000000000 | bytes 20971520 | tf_op jit(solution)/shard_map/pallas_call | solution.py:271
  600.9 6.7 fusion.76
  609.3 8.9 %convolution_convert_fusion = bf16[2048,1536]{1,0:T(8,128)(2,1)S(1)} fusion(bf16[1024,1536]{1,0:T(8,128)(2,1)S(1)} %get-tuple-element.256, f32[2048]{0:T(1024)S(1)} %copy-done.47, f32[1024]{0:T(1024)S(1)} %copy-done.53, bf16[256,2048]{1,0:T(8,128)(2,1)} %collective-permute-done.12, bf16[256,2048]{1,0:T(8,128)(2,1)} %collective-permute-done.10, ...), kind=kOutput, calls=%fused_computation.5 | convolution fusion | flops 6468665344 | bytes 13643776 | tf_op jit(solution)/shard_map/dot_general | solution.py:30
  620.4 2.5 collective-permute-done.48
  628.4 2.5 collective-permute-start.50
  631.9 17.4 %convolution_convert_fusion.1 = bf16[2,2048,1024]{2,1,0:T(8,128)(2,1)} fusion(bf16[2,1280,2048]{2,1,0:T(8,128)(2,1)} %get-tuple-element.267, bf16[2,1280,1024]{2,1,0:T(8,128)(2,1)} %get-tuple-element.268), kind=kOutput, calls=%fused_computation.10 | convolution fusion | flops 10741612544 | bytes 24117248 | tf_op jit(solution)/shard_map/dot_general | solution.py:801
  651.1 31.9 %collective-permute-done.50 = bf16[256,2048]{1,0:T(8,128)(2,1)} collective-permute-done((bf16[256,2048]{1,0:T(8,128)(2,1)}, bf16[256,2048]{1,0:T(8,128)(2,1)}, u32[]{:S(2)}, u32[]{:S(2)}) %collective-permute-start.50) | collective-permute-done | bytes 1048608 | tf_op jit(solution)/shard_map/ppermute | solution.py:48
  683.1 3.9 convolution_convert_fusion.4
  687.0 5.4 convert_add_fusion.1
  698.1 3.2 collective-permute-start.54
  701.3 36.4 %collective-permute-done.55 = bf16[2,4,64,2048]{3,2,1,0:T(8,128)(2,1)} collective-permute-done((bf16[2,4,64,2048]{3,2,1,0:T(8,128)(2,1)}, bf16[2,4,64,2048]{3,2,1,0:T(8,128)(2,1)}, u32[]{:S(2)}, u32[]{:S(2)}) %collective-permute-start.55) | collective-permute-done | bytes 2097184 | tf_op jit(solution)/shard_map/ppermute | solution.py:48
  737.7 4.4 fusion.7
  742.2 4.2 convert_element_type.431
  746.4 4.1 convert_element_type.432
  750.5 3.6 fusion.8
  755.2 3.0 collective-permute-start.57
  758.2 17.4 %collective-permute-done.58 = bf16[4,64,2048]{2,1,0:T(8,128)(2,1)} collective-permute-done((bf16[4,64,2048]{2,1,0:T(8,128)(2,1)}, bf16[4,64,2048]{2,1,0:T(8,128)(2,1)}, u32[]{:S(2)}, u32[]{:S(2)}) %collective-permute-start.58) | collective-permute-done | bytes 1048608 | tf_op jit(solution)/shard_map/ppermute | solution.py:48
  777.6 11.8 %collective-permute-done.57 = bf16[2,2,2,64,128]{4,3,2,1,0:T(8,128)(2,1)S(1)} collective-permute-done((bf16[2,2,2,64,128]{4,3,2,1,0:T(8,128)(2,1)S(1)}, bf16[2,2,2,64,128]{4,3,2,1,0:T(8,128)(2,1)S(1)}, u32[]{:S(2)}, u32[]{:S(2)}) %collective-permute-start.57) | collective-permute-done | bytes 131104 | tf_op jit(solution)/shard_map/ppermute | solution.py:48
  791.9 5.0 fusion.17
  797.9 3.1 collective-permute-start.61
  801.0 4.5 collective-permute-done.59
  805.7 4.1 convert_element_type.462
  811.2 3.8 collective-permute-done.62
  817.1 2.7 collective-permute-done.65
  820.1 3.3 collective-permute-done.63
  823.8 3.5 collective-permute-done.66
  (401 shorter events, 116.9 us)
Async XLA Ops:
  7.2 307.9 %all-gather.4.cloned.1.call-start = ((), (), s32[]{:S(2)}) async-start(), calls=%async_computation.3 | async-start | bytes 10485760 | tf_op jit(solution)/shard_map/all_gather | solution.py:688
  13.8 13.0 %collective-permute-start.4 = (bf16[128,1664]{1,0:T(8,128)(2,1)S(1)}, bf16[128,1664]{1,0:T(8,128)(2,1)S(1)}, u32[]{:S(2)}, u32[]{:S(2)}) collective-permute-start(bf16[128,1664]{1,0:T(8,128)(2,1)S(1)} %get-tuple-element.423), channel_id=1, source_target_pairs={{0,1},{1,0},{2,3},{3,2},{4,5},{5,4},{6,7},{7,6},{8,9},{9,8},{10,11... | collective-permute-start | bytes 1277960 | tf_op jit(solution)/shard_map/ppermute | solution.py:48
  16.8 10.2 %collective-permute-start.5 = (bf16[64,2048]{1,0:T(8,128)(2,1)S(1)}, bf16[64,2048]{1,0:T(8,128)(2,1)S(1)}, u32[]{:S(2)}, u32[]{:S(2)}) collective-permute-start(bf16[64,2048]{1,0:T(8,128)(2,1)S(1)} %copy-done.38), channel_id=1, source_target_pairs={{0,2},{2,6},{6,4},{4,0},{1,3},{3,7},{7,5},{5,1},{8,10},{10,14},{14... | collective-permute-start | bytes 786440 | tf_op jit(solution)/shard_map/ppermute | solution.py:48
  27.0 20.5 %collective-permute-start.6 = (bf16[256,1664]{1,0:T(8,128)(2,1)S(1)}, bf16[256,1664]{1,0:T(8,128)(2,1)S(1)}, u32[]{:S(2)}, u32[]{:S(2)}) collective-permute-start(bf16[256,1664]{1,0:T(8,128)(2,1)S(1)} %pad_maximum_fusion.7), channel_id=1, source_target_pairs={{0,16},{16,0},{1,17},{17,1},{2,18},{18,2},{3,19},{19,3},{4,20},{20... | collective-permute-start | bytes 2555912 | tf_op jit(solution)/shard_map/ppermute | solution.py:48
  47.8 267.3 %all-gather.6.cloned.1.call-start = ((), (), s32[]{:S(2)}) async-start(), calls=%async_computation.4 | async-start | bytes 10485760 | tf_op jit(solution)/shard_map/all_gather | solution.py:688
  48.5 266.6 %all-gather.8.cloned.1.call-start = ((), (), s32[]{:S(2)}) async-start(), calls=%async_computation.5 | async-start | bytes 10485760 | tf_op jit(solution)/shard_map/all_gather | solution.py:688
  48.6 45.7 %collective-permute-start.10 = (bf16[256,2048]{1,0:T(8,128)(2,1)}, bf16[256,2048]{1,0:T(8,128)(2,1)}, u32[]{:S(2)}, u32[]{:S(2)}) collective-permute-start(bf16[256,2048]{1,0:T(8,128)(2,1)} %bitcast), channel_id=1, source_target_pairs={{0,1},{1,0},{2,3},{3,2},{4,5},{5,4},{6,7},{7,6},{8,9},{9,8},{10,11... | collective-permute-start | bytes 3145736 | tf_op jit(solution)/shard_map/ppermute | solution.py:48
  50.4 43.8 %collective-permute-start.8 = (bf16[512,1664]{1,0:T(8,128)(2,1)S(1)}, bf16[512,1664]{1,0:T(8,128)(2,1)S(1)}, u32[]{:S(2)}, u32[]{:S(2)}) collective-permute-start(bf16[512,1664]{1,0:T(8,128)(2,1)S(1)} %constant_dynamic-update-slice_fusion.refs_0_), channel_id=1, source_target_pairs={{0,2},{2,6},{6,4},{4,0},{1,3},{3,7},{7,5},{5,1},{8,10},{10,14},{14... | collective-permute-start | bytes 5111816 | tf_op jit(solution)/shard_map/ppermute | solution.py:48
  53.6 40.6 %collective-permute-start.9 = (bf16[64,2048]{1,0:T(8,128)(2,1)}, bf16[64,2048]{1,0:T(8,128)(2,1)S(1)}, u32[]{:S(2)}, u32[]{:S(2)}) collective-permute-start(bf16[64,2048]{1,0:T(8,128)(2,1)} %copy-done.42), channel_id=1, source_target_pairs={{0,2},{2,6},{6,4},{4,0},{1,3},{3,7},{7,5},{5,1},{8,10},{10,14},{14... | collective-permute-start | bytes 786440 | tf_op jit(solution)/shard_map/ppermute | solution.py:48
  58.7 38.8 %collective-permute-start.15 = (bf16[256,2176]{1,0:T(8,128)(2,1)}, bf16[256,2176]{1,0:T(8,128)(2,1)}, u32[]{:S(2)}, u32[]{:S(2)}) collective-permute-start(bf16[256,2176]{1,0:T(8,128)(2,1)} %fusion.25.refs_2_), channel_id=1, source_target_pairs={{0,1},{1,0},{2,3},{3,2},{4,5},{5,4},{6,7},{7,6},{8,9},{9,8},{10,11... | collective-permute-start | bytes 3342344 | tf_op jit(solution)/shard_map/ppermute | solution.py:48
  94.2 37.4 %collective-permute-start.13 = (bf16[512,1664]{1,0:T(8,128)(2,1)S(1)}, bf16[512,1664]{1,0:T(8,128)(2,1)}, u32[]{:S(2)}, u32[]{:S(2)}) collective-permute-start(bf16[512,1664]{1,0:T(8,128)(2,1)S(1)} %collective-permute-done.8.refs_1_), channel_id=1, source_target_pairs={{0,2},{2,6},{6,4},{4,0},{1,3},{3,7},{7,5},{5,1},{8,10},{10,14},{14... | collective-permute-start | bytes 5111816 | tf_op jit(solution)/shard_map/ppermute | solution.py:48
  95.3 32.9 %collective-permute-start.14 = (bf16[256,2048]{1,0:T(8,128)(2,1)S(1)}, bf16[256,2048]{1,0:T(8,128)(2,1)}, u32[]{:S(2)}, u32[]{:S(2)}) collective-permute-start(bf16[256,2048]{1,0:T(8,128)(2,1)S(1)} %constant_dynamic-update-slice_fusion.2), channel_id=1, source_target_pairs={{0,16},{16,0},{1,17},{17,1},{2,18},{18,2},{3,19},{19,3},{4,20},{20... | collective-permute-start | bytes 3145736 | tf_op jit(solution)/shard_map/ppermute | solution.py:48
  96.9 37.1 %collective-permute-start.11 = (bf16[256,2048]{1,0:T(8,128)(2,1)}, bf16[256,2048]{1,0:T(8,128)(2,1)}, u32[]{:S(2)}, u32[]{:S(2)}) collective-permute-start(bf16[256,2048]{1,0:T(8,128)(2,1)} %bitcast), channel_id=1, source_target_pairs={{0,8},{8,0},{1,9},{9,1},{2,10},{10,2},{3,11},{11,3},{4,12},{12,4},... | collective-permute-start | bytes 3145736 | tf_op jit(solution)/shard_map/ppermute | solution.py:574
  96.9 37.1 %collective-permute-start.12 = (bf16[256,2048]{1,0:T(8,128)(2,1)}, bf16[256,2048]{1,0:T(8,128)(2,1)}, u32[]{:S(2)}, u32[]{:S(2)}) collective-permute-start(bf16[256,2048]{1,0:T(8,128)(2,1)} %collective-permute-done.10), channel_id=1, source_target_pairs={{0,8},{8,0},{1,9},{9,1},{2,10},{10,2},{3,11},{11,3},{4,12},{12,4},... | collective-permute-start | bytes 3145736 | tf_op jit(solution)/shard_map/ppermute | solution.py:574
  97.5 35.1 %collective-permute-start.1 = (s32[2]{0:T(128)S(1)}, s32[2]{0:T(128)S(1)}, u32[]{:S(2)}, u32[]{:S(2)}) collective-permute-start(s32[2]{0:T(128)S(1)} %bitcast.233), channel_id=1, source_target_pairs={{0,1},{1,0},{2,3},{3,2},{4,5},{5,4},{6,7},{7,6},{8,9},{9,8},{10,11... | collective-permute-start | bytes 32 | tf_op jit(solution)/shard_map/ppermute | solution.py:48
  131.6 37.4 %collective-permute-start.16 = (bf16[512,1664]{1,0:T(8,128)(2,1)}, bf16[512,1664]{1,0:T(8,128)(2,1)}, u32[]{:S(2)}, u32[]{:S(2)}) collective-permute-start(bf16[512,1664]{1,0:T(8,128)(2,1)} %collective-permute-done.13.refs_2_), channel_id=1, source_target_pairs={{0,2},{2,6},{6,4},{4,0},{1,3},{3,7},{7,5},{5,1},{8,10},{10,14},{14... | collective-permute-start | bytes 5111816 | tf_op jit(solution)/shard_map/ppermute | solution.py:48
  134.0 608.2 %reduce-scatter.4.cloned.1.call-start = ((), (), s32[]{:S(2)}) async-start(), calls=%async_computation.6 | async-start | bytes 10485760 | tf_op jit(solution)/shard_map/reduce_scatter | solution.py:906
  139.5 52.6 %collective-permute-start.18 = (bf16[512,2048]{1,0:T(8,128)(2,1)S(1)}, bf16[512,2048]{1,0:T(8,128)(2,1)}, u32[]{:S(2)}, u32[]{:S(2)}) collective-permute-start(bf16[512,2048]{1,0:T(8,128)(2,1)S(1)} %constant_dynamic-update-slice_fusion.6.refs_0_), channel_id=1, source_target_pairs={{0,1},{1,0},{2,3},{3,2},{4,5},{5,4},{6,7},{7,6},{8,9},{9,8},{10,11... | collective-permute-start | bytes 6291464 | tf_op jit(solution)/shard_map/ppermute | solution.py:48
  179.7 24.0 %collective-permute-start.17 = (bf16[256,2176]{1,0:T(8,128)(2,1)}, bf16[256,2176]{1,0:T(8,128)(2,1)}, u32[]{:S(2)}, u32[]{:S(2)}) collective-permute-start(bf16[256,2176]{1,0:T(8,128)(2,1)} %fusion.25.refs_2_), channel_id=1, source_target_pairs={{0,2},{2,6},{6,4},{4,0},{1,3},{3,7},{7,5},{5,1},{8,10},{10,14},{14... | collective-permute-start | bytes 3342344 | tf_op jit(solution)/shard_map/ppermute | solution.py:48
  203.7 49.0 %collective-permute-start.20 = (bf16[256,2176]{1,0:T(8,128)(2,1)}, bf16[256,2176]{1,0:T(8,128)(2,1)}, u32[]{:S(2)}, u32[]{:S(2)}) collective-permute-start(bf16[256,2176]{1,0:T(8,128)(2,1)} %collective-permute-done.17.refs_2_), channel_id=1, source_target_pairs={{0,2},{2,6},{6,4},{4,0},{1,3},{3,7},{7,5},{5,1},{8,10},{10,14},{14... | collective-permute-start | bytes 3342344 | tf_op jit(solution)/shard_map/ppermute | solution.py:48
  216.2 36.5 %collective-permute-start.21 = (bf16[256,2176]{1,0:T(8,128)(2,1)}, bf16[256,2176]{1,0:T(8,128)(2,1)}, u32[]{:S(2)}, u32[]{:S(2)}) collective-permute-start(bf16[256,2176]{1,0:T(8,128)(2,1)} %collective-permute-done.17.refs_2_), channel_id=1, source_target_pairs={{0,1},{1,0},{2,3},{3,2},{4,5},{5,4},{6,7},{7,6},{8,9},{9,8},{10,11... | collective-permute-start | bytes 3342344 | tf_op jit(solution)/shard_map/ppermute | solution.py:48
  234.1 17.4 %collective-permute-start.19 = (bf16[512,512]{1,0:T(8,128)(2,1)}, bf16[512,512]{1,0:T(8,128)(2,1)}, u32[]{:S(2)}, u32[]{:S(2)}) collective-permute-start(bf16[512,512]{1,0:T(8,128)(2,1)} %get-tuple-element.416), channel_id=1, source_target_pairs={{0,1},{1,0},{2,3},{3,2},{4,5},{5,4},{6,7},{7,6},{8,9},{9,8},{10,11... | collective-permute-start | bytes 1572872 | tf_op jit(solution)/shard_map/ppermute | solution.py:48
  255.3 28.2 %collective-permute-start.23 = (bf16[256,2176]{1,0:T(8,128)(2,1)}, bf16[256,2176]{1,0:T(8,128)(2,1)}, u32[]{:S(2)}, u32[]{:S(2)}) collective-permute-start(bf16[256,2176]{1,0:T(8,128)(2,1)} %collective-permute-done.20.refs_2_), channel_id=1, source_target_pairs={{0,2},{2,6},{6,4},{4,0},{1,3},{3,7},{7,5},{5,1},{8,10},{10,14},{14... | collective-permute-start | bytes 3342344 | tf_op jit(solution)/shard_map/ppermute | solution.py:48
  257.6 27.0 %collective-permute-start.24 = (bf16[256,2176]{1,0:T(8,128)(2,1)}, bf16[256,2176]{1,0:T(8,128)(2,1)}, u32[]{:S(2)}, u32[]{:S(2)}) collective-permute-start(bf16[256,2176]{1,0:T(8,128)(2,1)} %collective-permute-done.20.refs_2_), channel_id=1, source_target_pairs={{0,1},{1,0},{2,3},{3,2},{4,5},{5,4},{6,7},{7,6},{8,9},{9,8},{10,11... | collective-permute-start | bytes 3342344 | tf_op jit(solution)/shard_map/ppermute | solution.py:48
  284.6 27.5 %collective-permute-start.25 = (bf16[256,2176]{1,0:T(8,128)(2,1)S(1)}, bf16[256,2176]{1,0:T(8,128)(2,1)S(1)}, u32[]{:S(2)}, u32[]{:S(2)}) collective-permute-start(bf16[256,2176]{1,0:T(8,128)(2,1)S(1)} %pad_maximum_fusion.4.refs_0_), channel_id=1, source_target_pairs={{0,1},{1,0},{2,3},{3,2},{4,5},{5,4},{6,7},{7,6},{8,9},{9,8},{10,11... | collective-permute-start | bytes 3342344 | tf_op jit(solution)/shard_map/ppermute | solution.py:48
  286.2 26.5 %collective-permute-start.26 = (bf16[256,2176]{1,0:T(8,128)(2,1)S(1)}, bf16[256,2176]{1,0:T(8,128)(2,1)}, u32[]{:S(2)}, u32[]{:S(2)}) collective-permute-start(bf16[256,2176]{1,0:T(8,128)(2,1)S(1)} %pad_maximum_fusion.4.refs_0_), channel_id=1, source_target_pairs={{0,2},{2,6},{6,4},{4,0},{1,3},{3,7},{7,5},{5,1},{8,10},{10,14},{14... | collective-permute-start | bytes 3342344 | tf_op jit(solution)/shard_map/ppermute | solution.py:48
  286.6 173.9 %collective-permute-start.34 = (bf16[256,2176]{1,0:T(8,128)(2,1)}, bf16[256,2176]{1,0:T(8,128)(2,1)}, u32[]{:S(2)}, u32[]{:S(2)}) collective-permute-start(bf16[256,2176]{1,0:T(8,128)(2,1)} %collective-permute-done.23.refs_2_), channel_id=1, source_target_pairs={{0,1},{1,0},{2,3},{3,2},{4,5},{5,4},{6,7},{7,6},{8,9},{9,8},{10,11... | collective-permute-start | bytes 3342344 | tf_op jit(solution)/shard_map/ppermute | solution.py:48
  313.1 45.2 %collective-permute-start.27 = (bf16[256,2176]{1,0:T(8,128)(2,1)}, bf16[256,2176]{1,0:T(8,128)(2,1)}, u32[]{:S(2)}, u32[]{:S(2)}) collective-permute-start(bf16[256,2176]{1,0:T(8,128)(2,1)} %collective-permute-done.26.refs_0_), channel_id=1, source_target_pairs={{0,1},{1,0},{2,3},{3,2},{4,5},{5,4},{6,7},{7,6},{8,9},{9,8},{10,11... | collective-permute-start | bytes 3342344 | tf_op jit(solution)/shard_map/ppermute | solution.py:48
  314.7 43.5 %collective-permute-start.28 = (bf16[256,2176]{1,0:T(8,128)(2,1)}, bf16[256,2176]{1,0:T(8,128)(2,1)S(1)}, u32[]{:S(2)}, u32[]{:S(2)}) collective-permute-start(bf16[256,2176]{1,0:T(8,128)(2,1)} %collective-permute-done.26.refs_0_), channel_id=1, source_target_pairs={{0,2},{2,6},{6,4},{4,0},{1,3},{3,7},{7,5},{5,1},{8,10},{10,14},{14... | collective-permute-start | bytes 3342344 | tf_op jit(solution)/shard_map/ppermute | solution.py:48
  358.3 37.8 %collective-permute-start.29 = (bf16[256,2176]{1,0:T(8,128)(2,1)S(1)}, bf16[256,2176]{1,0:T(8,128)(2,1)S(1)}, u32[]{:S(2)}, u32[]{:S(2)}) collective-permute-start(bf16[256,2176]{1,0:T(8,128)(2,1)S(1)} %collective-permute-done.28.refs_0_), channel_id=1, source_target_pairs={{0,1},{1,0},{2,3},{3,2},{4,5},{5,4},{6,7},{7,6},{8,9},{9,8},{10,11... | collective-permute-start | bytes 3342344 | tf_op jit(solution)/shard_map/ppermute | solution.py:48
  359.9 36.2 %collective-permute-start.30 = (bf16[256,2176]{1,0:T(8,128)(2,1)S(1)}, bf16[256,2176]{1,0:T(8,128)(2,1)}, u32[]{:S(2)}, u32[]{:S(2)}) collective-permute-start(bf16[256,2176]{1,0:T(8,128)(2,1)S(1)} %collective-permute-done.28.refs_0_), channel_id=1, source_target_pairs={{0,2},{2,6},{6,4},{4,0},{1,3},{3,7},{7,5},{5,1},{8,10},{10,14},{14... | collective-permute-start | bytes 3342344 | tf_op jit(solution)/shard_map/ppermute | solution.py:48
  360.5 49.1 %collective-permute-start.31 = (bf16[256,2176]{1,0:T(8,128)(2,1)}, bf16[256,2176]{1,0:T(8,128)(2,1)S(1)}, u32[]{:S(2)}, u32[]{:S(2)}) collective-permute-start(bf16[256,2176]{1,0:T(8,128)(2,1)} %get-tuple-element.200), channel_id=1, source_target_pairs={{0,1},{1,0},{2,3},{3,2},{4,5},{5,4},{6,7},{7,6},{8,9},{9,8},{10,11... | collective-permute-start | bytes 3342344 | tf_op jit(solution)/shard_map/ppermute | solution.py:48
  394.3 51.0 %collective-permute-start.33 = (bf16[256,2176]{1,0:T(8,128)(2,1)}, bf16[256,2176]{1,0:T(8,128)(2,1)}, u32[]{:S(2)}, u32[]{:S(2)}) collective-permute-start(bf16[256,2176]{1,0:T(8,128)(2,1)} %get-tuple-element.216), channel_id=1, source_target_pairs={{0,1},{1,0},{2,3},{3,2},{4,5},{5,4},{6,7},{7,6},{8,9},{9,8},{10,11... | collective-permute-start | bytes 3342344 | tf_op jit(solution)/shard_map/ppermute | solution.py:48
  409.7 47.8 %collective-permute-start.32 = (bf16[256,2176]{1,0:T(8,128)(2,1)}, bf16[256,2176]{1,0:T(8,128)(2,1)}, u32[]{:S(2)}, u32[]{:S(2)}) collective-permute-start(bf16[256,2176]{1,0:T(8,128)(2,1)} %collective-permute-done.30.refs_0_), channel_id=1, source_target_pairs={{0,1},{1,0},{2,3},{3,2},{4,5},{5,4},{6,7},{7,6},{8,9},{9,8},{10,11... | collective-permute-start | bytes 3342344 | tf_op jit(solution)/shard_map/ppermute | solution.py:48
  444.5 51.2 %collective-permute-start.35 = (bf16[256,2176]{1,0:T(8,128)(2,1)}, bf16[256,2176]{1,0:T(8,128)(2,1)S(1)}, u32[]{:S(2)}, u32[]{:S(2)}) collective-permute-start(bf16[256,2176]{1,0:T(8,128)(2,1)} %get-tuple-element.233), channel_id=1, source_target_pairs={{0,1},{1,0},{2,3},{3,2},{4,5},{5,4},{6,7},{7,6},{8,9},{9,8},{10,11... | collective-permute-start | bytes 3342344 | tf_op jit(solution)/shard_map/ppermute | solution.py:48
  460.0 35.7 %collective-permute-start.36 = (bf16[256,2176]{1,0:T(8,128)(2,1)}, bf16[256,2176]{1,0:T(8,128)(2,1)S(1)}, u32[]{:S(2)}, u32[]{:S(2)}) collective-permute-start(bf16[256,2176]{1,0:T(8,128)(2,1)} %add_convert_fusion.2), channel_id=1, source_target_pairs={{0,2},{2,6},{6,4},{4,0},{1,3},{3,7},{7,5},{5,1},{8,10},{10,14},{14... | collective-permute-start | bytes 3342344 | tf_op jit(solution)/shard_map/ppermute | solution.py:48
  493.9 22.2 %collective-permute-start.37 = (bf16[256,2176]{1,0:T(8,128)(2,1)}, bf16[256,2176]{1,0:T(8,128)(2,1)}, u32[]{:S(2)}, u32[]{:S(2)}) collective-permute-start(bf16[256,2176]{1,0:T(8,128)(2,1)} %get-tuple-element.241), channel_id=1, source_target_pairs={{0,1},{1,0},{2,3},{3,2},{4,5},{5,4},{6,7},{7,6},{8,9},{9,8},{10,11... | collective-permute-start | bytes 3342344 | tf_op jit(solution)/shard_map/ppermute | solution.py:48
  497.1 22.4 %collective-permute-start.38 = (bf16[256,2176]{1,0:T(8,128)(2,1)}, bf16[256,2176]{1,0:T(8,128)(2,1)S(1)}, u32[]{:S(2)}, u32[]{:S(2)}) collective-permute-start(bf16[256,2176]{1,0:T(8,128)(2,1)} %add_convert_fusion.1), channel_id=1, source_target_pairs={{0,2},{2,6},{6,4},{4,0},{1,3},{3,7},{7,5},{5,1},{8,10},{10,14},{14... | collective-permute-start | bytes 3342344 | tf_op jit(solution)/shard_map/ppermute | solution.py:48
  519.5 226.8 %reduce-scatter.6.cloned.1.call-start = ((), (), s32[]{:S(2)}) async-start(), calls=%async_computation.7 | async-start | bytes 10485760 | tf_op jit(solution)/shard_map/reduce_scatter | solution.py:906
  519.6 22.9 %collective-permute-start.40 = (bf16[256,2048]{1,0:T(8,128)(2,1)}, bf16[256,2048]{1,0:T(8,128)(2,1)}, u32[]{:S(2)}, u32[]{:S(2)}) collective-permute-start(bf16[256,2048]{1,0:T(8,128)(2,1)} %get-tuple-element.193), channel_id=1, source_target_pairs={{0,1},{1,0},{2,3},{3,2},{4,5},{5,4},{6,7},{7,6},{8,9},{9,8},{10,11... | collective-permute-start | bytes 3145736 | tf_op jit(solution)/shard_map/ppermute | solution.py:48
  522.6 21.2 %collective-permute-start.39 = (bf16[256,2176]{1,0:T(8,128)(2,1)}, bf16[256,2176]{1,0:T(8,128)(2,1)S(1)}, u32[]{:S(2)}, u32[]{:S(2)}) collective-permute-start(bf16[256,2176]{1,0:T(8,128)(2,1)} %add_convert_fusion), channel_id=1, source_target_pairs={{0,2},{2,6},{6,4},{4,0},{1,3},{3,7},{7,5},{5,1},{8,10},{10,14},{14... | collective-permute-start | bytes 3342344 | tf_op jit(solution)/shard_map/ppermute | solution.py:48
  543.9 261.8 %reduce-scatter.8.cloned.1.call-start = ((), (), s32[]{:S(2)}) async-start(), calls=%async_computation.8 | async-start | bytes 10485760 | tf_op jit(solution)/shard_map/reduce_scatter | solution.py:906
  558.7 14.1 %collective-permute-start.42 = (bf16[512,512]{1,0:T(8,128)(2,1)S(1)}, bf16[512,512]{1,0:T(8,128)(2,1)S(1)}, u32[]{:S(2)}, u32[]{:S(2)}) collective-permute-start(bf16[512,512]{1,0:T(8,128)(2,1)S(1)} %get-tuple-element.415), channel_id=1, source_target_pairs={{0,1},{1,0},{2,3},{3,2},{4,5},{5,4},{6,7},{7,6},{8,9},{9,8},{10,11... | collective-permute-start | bytes 1572872 | tf_op jit(solution)/shard_map/ppermute | solution.py:48
  562.3 34.3 %collective-permute-start.44 = (bf16[256,2048]{1,0:T(8,128)(2,1)S(1)}, bf16[256,2048]{1,0:T(8,128)(2,1)S(1)}, u32[]{:S(2)}, u32[]{:S(2)}) collective-permute-start(bf16[256,2048]{1,0:T(8,128)(2,1)S(1)} %add_convert_fusion.6), channel_id=1, source_target_pairs={{0,2},{2,6},{6,4},{4,0},{1,3},{3,7},{7,5},{5,1},{8,10},{10,14},{14... | collective-permute-start | bytes 3145736 | tf_op jit(solution)/shard_map/ppermute | solution.py:48
  572.8 24.6 %collective-permute-start.43 = (bf16[256,2048]{1,0:T(8,128)(2,1)S(1)}, bf16[256,2048]{1,0:T(8,128)(2,1)S(1)}, u32[]{:S(2)}, u32[]{:S(2)}) collective-permute-start(bf16[256,2048]{1,0:T(8,128)(2,1)S(1)} %copy-done.58), channel_id=1, source_target_pairs={{0,1},{1,0},{2,3},{3,2},{4,5},{5,4},{6,7},{7,6},{8,9},{9,8},{10,11... | collective-permute-start | bytes 3145736 | tf_op jit(solution)/shard_map/ppermute | solution.py:48
  598.0 25.0 %collective-permute-start.48 = (bf16[256,2048]{1,0:T(8,128)(2,1)S(1)}, bf16[256,2048]{1,0:T(8,128)(2,1)S(1)}, u32[]{:S(2)}, u32[]{:S(2)}) collective-permute-start(bf16[256,2048]{1,0:T(8,128)(2,1)S(1)} %add_convert_fusion.5), channel_id=1, source_target_pairs={{0,2},{2,6},{6,4},{4,0},{1,3},{3,7},{7,5},{5,1},{8,10},{10,14},{14... | collective-permute-start | bytes 3145736 | tf_op jit(solution)/shard_map/ppermute | solution.py:48
  599.3 23.8 %collective-permute-start.47 = (bf16[256,2048]{1,0:T(8,128)(2,1)}, bf16[256,2048]{1,0:T(8,128)(2,1)S(1)}, u32[]{:S(2)}, u32[]{:S(2)}) collective-permute-start(bf16[256,2048]{1,0:T(8,128)(2,1)} %get-tuple-element.257), channel_id=1, source_target_pairs={{0,1},{1,0},{2,3},{3,2},{4,5},{5,4},{6,7},{7,6},{8,9},{9,8},{10,11... | collective-permute-start | bytes 3145736 | tf_op jit(solution)/shard_map/ppermute | solution.py:48
  608.8 9.4 %collective-permute-start.45 = (bf16[256,2048]{1,0:T(8,128)(2,1)}, bf16[256,2048]{1,0:T(8,128)(2,1)S(1)}, u32[]{:S(2)}, u32[]{:S(2)}) collective-permute-start(bf16[256,2048]{1,0:T(8,128)(2,1)} %get-tuple-element.411), channel_id=1, source_target_pairs={{0,8},{8,0},{1,9},{9,1},{2,10},{10,2},{3,11},{11,3},{4,12},{12,4},... | collective-permute-start | bytes 3145736 | tf_op jit(solution)/shard_map/ppermute | solution.py:48
  608.8 9.4 %collective-permute-start.46 = (bf16[256,2048]{1,0:T(8,128)(2,1)S(1)}, bf16[256,2048]{1,0:T(8,128)(2,1)S(1)}, u32[]{:S(2)}, u32[]{:S(2)}) collective-permute-start(bf16[256,2048]{1,0:T(8,128)(2,1)S(1)} %get-tuple-element.410), channel_id=1, source_target_pairs={{0,8},{8,0},{1,9},{9,1},{2,10},{10,2},{3,11},{11,3},{4,12},{12,4},... | collective-permute-start | bytes 3145736 | tf_op jit(solution)/shard_map/ppermute | solution.py:48
  623.1 26.4 %collective-permute-start.52 = (bf16[256,2048]{1,0:T(8,128)(2,1)}, bf16[256,2048]{1,0:T(8,128)(2,1)}, u32[]{:S(2)}, u32[]{:S(2)}) collective-permute-start(bf16[256,2048]{1,0:T(8,128)(2,1)} %get-tuple-element.270), channel_id=1, source_target_pairs={{0,1},{1,0},{2,3},{3,2},{4,5},{5,4},{6,7},{7,6},{8,9},{9,8},{10,11... | collective-permute-start | bytes 3145736 | tf_op jit(solution)/shard_map/ppermute | solution.py:48
  625.8 57.2 %collective-permute-start.51 = (bf16[2,2,2,64,1536]{4,3,2,1,0:T(8,128)(2,1)}, bf16[2,2,2,64,1536]{4,3,2,1,0:T(8,128)(2,1)}, u32[]{:S(2)}, u32[]{:S(2)}) collective-permute-start(bf16[2,2,2,64,1536]{4,3,2,1,0:T(8,128)(2,1)} %dynamic-slice_bitcast_fusion.1), channel_id=1, source_target_pairs={{0,2},{2,6},{6,4},{4,0},{1,3},{3,7},{7,5},{5,1},{8,10},{10,14},{14... | collective-permute-start | bytes 4718600 | tf_op jit(solution)/shard_map/ppermute | solution.py:48
  628.4 54.6 %collective-permute-start.50 = (bf16[256,2048]{1,0:T(8,128)(2,1)}, bf16[256,2048]{1,0:T(8,128)(2,1)}, u32[]{:S(2)}, u32[]{:S(2)}) collective-permute-start(bf16[256,2048]{1,0:T(8,128)(2,1)} %add_convert_fusion.4), channel_id=1, source_target_pairs={{0,2},{2,6},{6,4},{4,0},{1,3},{3,7},{7,5},{5,1},{8,10},{10,14},{14... | collective-permute-start | bytes 3145736 | tf_op jit(solution)/shard_map/ppermute | solution.py:48
  631.0 52.0 %collective-permute-start.49 = (bf16[256,2048]{1,0:T(8,128)(2,1)}, bf16[256,2048]{1,0:T(8,128)(2,1)}, u32[]{:S(2)}, u32[]{:S(2)}) collective-permute-start(bf16[256,2048]{1,0:T(8,128)(2,1)} %get-tuple-element.262), channel_id=1, source_target_pairs={{0,1},{1,0},{2,3},{3,2},{4,5},{5,4},{6,7},{7,6},{8,9},{9,8},{10,11... | collective-permute-start | bytes 3145736 | tf_op jit(solution)/shard_map/ppermute | solution.py:48
  693.9 43.8 %collective-permute-start.55 = (bf16[2,4,64,2048]{3,2,1,0:T(8,128)(2,1)}, bf16[2,4,64,2048]{3,2,1,0:T(8,128)(2,1)}, u32[]{:S(2)}, u32[]{:S(2)}) collective-permute-start(bf16[2,4,64,2048]{3,2,1,0:T(8,128)(2,1)} %dynamic-slice_bitcast_fusion), channel_id=1, source_target_pairs={{0,1},{1,0},{2,3},{3,2},{4,5},{5,4},{6,7},{7,6},{8,9},{9,8},{10,11... | collective-permute-start | bytes 6291464 | tf_op jit(solution)/shard_map/ppermute | solution.py:48
  694.4 56.0 %collective-permute-start.53 = (bf16[2,2,2,64,1536]{4,3,2,1,0:T(8,128)(2,1)}, bf16[2,2,2,64,1536]{4,3,2,1,0:T(8,128)(2,1)}, u32[]{:S(2)}, u32[]{:S(2)}) collective-permute-start(bf16[2,2,2,64,1536]{4,3,2,1,0:T(8,128)(2,1)} %convert_add_fusion.1), channel_id=1, source_target_pairs={{0,2},{2,6},{6,4},{4,0},{1,3},{3,7},{7,5},{5,1},{8,10},{10,14},{14... | collective-permute-start | bytes 4718600 | tf_op jit(solution)/shard_map/ppermute | solution.py:48
  698.1 52.4 %collective-permute-start.54 = (bf16[2,2,2,64,128]{4,3,2,1,0:T(8,128)(2,1)S(1)}, bf16[2,2,2,64,128]{4,3,2,1,0:T(8,128)(2,1)S(1)}, u32[]{:S(2)}, u32[]{:S(2)}) collective-permute-start(bf16[2,2,2,64,128]{4,3,2,1,0:T(8,128)(2,1)S(1)} %dynamic-slice_bitcast_fusion.7), channel_id=1, source_target_pairs={{0,2},{2,6},{6,4},{4,0},{1,3},{3,7},{7,5},{5,1},{8,10},{10,14},{14... | collective-permute-start | bytes 393224 | tf_op jit(solution)/shard_map/ppermute | solution.py:48
  754.1 35.3 %collective-permute-start.56 = (bf16[2,2,2,64,1536]{4,3,2,1,0:T(8,128)(2,1)}, bf16[2,2,2,64,1536]{4,3,2,1,0:T(8,128)(2,1)}, u32[]{:S(2)}, u32[]{:S(2)}) collective-permute-start(bf16[2,2,2,64,1536]{4,3,2,1,0:T(8,128)(2,1)} %fusion.8), channel_id=1, source_target_pairs={{0,2},{2,6},{6,4},{4,0},{1,3},{3,7},{7,5},{5,1},{8,10},{10,14},{14... | collective-permute-start | bytes 4718600 | tf_op jit(solution)/shard_map/ppermute | solution.py:48
  755.2 20.4 %collective-permute-start.58 = (bf16[4,64,2048]{2,1,0:T(8,128)(2,1)}, bf16[4,64,2048]{2,1,0:T(8,128)(2,1)}, u32[]{:S(2)}, u32[]{:S(2)}) collective-permute-start(bf16[4,64,2048]{2,1,0:T(8,128)(2,1)} %dynamic-slice_bitcast_fusion.2), channel_id=1, source_target_pairs={{0,16},{16,0},{1,17},{17,1},{2,18},{18,2},{3,19},{19,3},{4,20},{20... | collective-permute-start | bytes 3145736 | tf_op jit(solution)/shard_map/ppermute | solution.py:48
  755.2 34.1 %collective-permute-start.57 = (bf16[2,2,2,64,128]{4,3,2,1,0:T(8,128)(2,1)S(1)}, bf16[2,2,2,64,128]{4,3,2,1,0:T(8,128)(2,1)S(1)}, u32[]{:S(2)}, u32[]{:S(2)}) collective-permute-start(bf16[2,2,2,64,128]{4,3,2,1,0:T(8,128)(2,1)S(1)} %fusion.41), channel_id=1, source_target_pairs={{0,2},{2,6},{6,4},{4,0},{1,3},{3,7},{7,5},{5,1},{8,10},{10,14},{14... | collective-permute-start | bytes 393224 | tf_op jit(solution)/shard_map/ppermute | solution.py:48
  791.7 13.7 %collective-permute-start.59 = (bf16[2,2,64,1536]{3,2,1,0:T(8,128)(2,1)S(1)}, bf16[2,2,64,1536]{3,2,1,0:T(8,128)(2,1)S(1)}, u32[]{:S(2)}, u32[]{:S(2)}) collective-permute-start(bf16[2,2,64,1536]{3,2,1,0:T(8,128)(2,1)S(1)} %dynamic-slice_bitcast_fusion.3), channel_id=1, source_target_pairs={{0,16},{16,0},{1,17},{17,1},{2,18},{18,2},{3,19},{19,3},{4,20},{20... | collective-permute-start | bytes 2359304 | tf_op jit(solution)/shard_map/ppermute | solution.py:48
  797.8 12.0 %collective-permute-start.60 = (bf16[2,2,2,64,128]{4,3,2,1,0:T(8,128)(2,1)S(1)}, bf16[2,2,2,64,128]{4,3,2,1,0:T(8,128)(2,1)S(1)}, u32[]{:S(2)}, u32[]{:S(2)}) collective-permute-start(bf16[2,2,2,64,128]{4,3,2,1,0:T(8,128)(2,1)S(1)} %fusion.40), channel_id=1, source_target_pairs={{0,2},{2,6},{6,4},{4,0},{1,3},{3,7},{7,5},{5,1},{8,10},{10,14},{14... | collective-permute-start | bytes 393224 | tf_op jit(solution)/shard_map/ppermute | solution.py:48
  797.9 11.9 %collective-permute-start.61 = (bf16[64,2048]{1,0:T(8,128)(2,1)S(1)}, bf16[64,2048]{1,0:T(8,128)(2,1)S(1)}, u32[]{:S(2)}, u32[]{:S(2)}) collective-permute-start(bf16[64,2048]{1,0:T(8,128)(2,1)S(1)} %dynamic-slice_bitcast_fusion.6), channel_id=1, source_target_pairs={{0,2},{2,6},{6,4},{4,0},{1,3},{3,7},{7,5},{5,1},{8,10},{10,14},{14... | collective-permute-start | bytes 786440 | tf_op jit(solution)/shard_map/ppermute | solution.py:48
  811.2 8.7 %collective-permute-start.65 = (bf16[64,2048]{1,0:T(8,128)(2,1)S(1)}, bf16[64,2048]{1,0:T(8,128)(2,1)S(1)}, u32[]{:S(2)}, u32[]{:S(2)}) collective-permute-start(bf16[64,2048]{1,0:T(8,128)(2,1)S(1)} %fusion.26), channel_id=1, source_target_pairs={{0,2},{2,6},{6,4},{4,0},{1,3},{3,7},{7,5},{5,1},{8,10},{10,14},{14... | collective-permute-start | bytes 786440 | tf_op jit(solution)/shard_map/ppermute | solution.py:48
  815.2 8.2 collective-permute-start.63
  (73 other events, 1298.1 us)
Sparse Core Ops, SparseCore 0:
  47.9 69.0 all-gather.3
  118.6 59.6 all-gather.5
  179.8 58.2 all-gather.7
  519.7 68.9 reduce-scatter.3
  591.3 74.3 reduce-scatter.5
  683.2 70.7 reduce-scatter.7
